TPU v7x, 512 devices: a whole 4x4x16 slice. The times are simulated.
512 devices in a mesh: seq: 64 (over x, z), tensor: 8 (over y, core).
Axes of the slice: x: 4, y: 4, z: 16, core: 2. Of those that a mesh axis runs over, the one named last changes fastest.
Arguments:
- layer_entry_vectors: bfloat16 [1024, 4, 2048], P('seq'), may hold values from -6 to 6
- tally_of_tokens: int32 [1024], P('seq'), may hold values from 1 to 4, as said below
- prior_slot_lookup: int32 [1024], P('seq'), may hold values from 0 to 1023, as said below
- memory_matrices: float32 [1024, 32, 4096], P('seq', 'tensor'), may hold values from -6 to 6
- previous_standardized_entries: float32 [1024, 2048], P('seq'), may hold values from -6 to 6
- entry_standardize_scale: float32 [2048], replicated, may hold values from 0.1 to 1.9
- blend_coefficients: float32 [4, 2048], replicated, may hold values from 0 to 1
- acceptance_projection_matrix: bfloat16 [2048, 2048], P(None, 'tensor'), may hold values from -0.125 to 0.125
- lookup_projection_matrix: bfloat16 [2048, 2048], P(None, 'tensor'), may hold values from -0.125 to 0.125
- payload_projection_matrix: bfloat16 [2048, 2048], P(None, 'tensor'), may hold values from -0.125 to 0.125
- forget_map_left_matrix: bfloat16 [2048, 64], P('tensor'), may hold values from -0.125 to 0.125
- forget_map_right_matrix: bfloat16 [64, 2048], P(None, 'tensor'), may hold values from -0.75 to 0.75
- feature_forget_logloglevel: float32 [2048], P('tensor'), may hold values from -6 to 1
- present_token_boost: float32 [2048], P('tensor'), may hold values from -3 to 3
- team_standardize_scale: float32 [2048], P('tensor'), may hold values from 0.1 to 1.9
- final_projection_matrix: bfloat16 [2048, 2048], P('tensor'), may hold values from -0.125 to 0.125
Outputs:
- mixed: bfloat16 [1024, 4, 2048], P('seq')
- new_states: float32 [1024, 32, 4096], P('seq', 'tensor')
- new_shifts: float32 [1024, 2048], P('seq')
Inputs may be any that keep to these rules, and one draw needn't show every extreme that they name: `tally_of_tokens`: valid tokens of a request, at least one; some request has all 4, some has one. `prior_slot_lookup`: each former slot appears once. The 16 new slots of one index of seq take exactly one former slot of the index before it along seq, exactly one of the index after it (cyclically), and the rest from their own former slots.
All inputs are finite; a program needn't handle non-finite values.
Results may differ from a plain program's by a relative error of at most 0.015.
Values may be sent and summed in bfloat16 or wider, within the bound.
No kernel may reach another device: no remote copies, remote signals or barrier semaphores. Data moves between devices by JAX's collectives and lax.ppermute only.
A program may use at most 64 MiB of HBM per device.

v0:
```python
import jax
import jax.numpy as jnp
from jax import lax
from jax.sharding import PartitionSpec as P

TEAM_DIMENSION = 64


EPS = 1e-05


def padded(cells, sides, width):
    for axis, dim in sides:
        count = lax.axis_size(axis)
        head = lax.slice_in_dim(cells, 0, width, axis=dim)
        tail = lax.slice_in_dim(cells, cells.shape[dim] - width, cells.shape[dim], axis=dim)
        cells = jnp.concatenate(
            [
                lax.ppermute(tail, axis, [(i, (i + 1) % count) for i in range(count)]),
                cells,
                lax.ppermute(head, axis, [((i + 1) % count, i) for i in range(count)]),
            ],
            axis=dim,
        )
    return cells


def layer_norm(values, gain):
    center = values - jnp.mean(values, axis=-1, keepdims=True)
    spread = jnp.mean(center * center, axis=-1, keepdims=True)
    return center * lax.rsqrt(spread + EPS) * gain


def shards(
    layer_entry_vectors,
    tally_of_tokens,
    prior_slot_lookup,
    memory_matrices,
    previous_standardized_entries,
    entry_standardize_scale,
    blend_coefficients,
    acceptance_projection_matrix,
    lookup_projection_matrix,
    payload_projection_matrix,
    forget_map_left_matrix,
    forget_map_right_matrix,
    feature_forget_logloglevel,
    present_token_boost,
    team_standardize_scale,
    final_projection_matrix,
):
    slots = tally_of_tokens.shape[0]
    length = layer_entry_vectors.shape[1]
    width = layer_entry_vectors.shape[2]
    local_attention_teams = memory_matrices.shape[1]
    devices = lax.axis_size("seq")
    device = lax.axis_index("seq")
    state_cols = local_attention_teams * TEAM_DIMENSION * TEAM_DIMENSION
    packed = jnp.concatenate(
        [memory_matrices.reshape(slots, state_cols), previous_standardized_entries], axis=1
    )
    extended = padded(packed, (("seq", 0),), slots)
    relative = jnp.mod(prior_slot_lookup - (device - 1) * slots, devices * slots)
    moved = jnp.take(extended, relative, axis=0)
    state = moved[:, :state_cols].reshape(
        slots, local_attention_teams, TEAM_DIMENSION, TEAM_DIMENSION
    )
    shift_in = moved[:, state_cols:]
    inputs = layer_entry_vectors.astype(jnp.float32)
    normed = layer_norm(inputs, entry_standardize_scale)
    before = jnp.concatenate([shift_in[:, None, :], normed[:, :-1]], axis=1)
    change = before - normed
    row_count = slots * length

    def shifted_mix_rows(which):
        return (
            (normed + change * blend_coefficients[which])
            .astype(jnp.bfloat16)
            .reshape(row_count, width)
        )

    def project(which, weight):
        return jnp.dot(shifted_mix_rows(which), weight, preferred_element_type=jnp.float32).reshape(
            slots, length, local_attention_teams, TEAM_DIMENSION
        )

    recept = project(0, acceptance_projection_matrix)
    keys = project(1, lookup_projection_matrix)
    values = project(2, payload_projection_matrix)
    decay_rows_in = shifted_mix_rows(3)
    shared_portion = forget_map_left_matrix.shape[0]
    incoming_piece = lax.dynamic_slice_in_dim(
        decay_rows_in, lax.axis_index("tensor") * shared_portion, shared_portion, 1
    )
    prenorm_output = lax.psum(
        jnp.dot(incoming_piece, forget_map_left_matrix, preferred_element_type=jnp.float32),
        "tensor",
    )
    decay_lowrank = jnp.tanh(prenorm_output).astype(jnp.bfloat16)
    decay_factor = jnp.exp(
        -jnp.exp(
            feature_forget_logloglevel
            + jnp.dot(decay_lowrank, forget_map_right_matrix, preferred_element_type=jnp.float32)
        )
    )
    decay_factor = decay_factor.reshape(slots, length, local_attention_teams, TEAM_DIMENSION)
    team_boost_vectors = present_token_boost.reshape(local_attention_teams, TEAM_DIMENSION)
    outputs = []
    for step in range(length):
        valid = (tally_of_tokens > step)[:, None, None, None]
        current_receptance = recept[:, step]
        current_key = keys[:, step]
        current_value = values[:, step]
        state_readout = jnp.einsum(
            "rhi,rhij->rhj", current_receptance, state, precision=lax.Precision.HIGHEST
        )
        state_readout = (
            state_readout
            + jnp.sum(current_receptance * team_boost_vectors * current_key, axis=-1, keepdims=True)
            * current_value
        )
        outputs.append(state_readout)
        updated = (
            decay_factor[:, step][..., None] * state
            + current_key[..., None] * current_value[..., None, :]
        )
        state = jnp.where(valid, updated, state)
    heads_out = jnp.stack(outputs, axis=1)
    center = heads_out - jnp.mean(heads_out, axis=-1, keepdims=True)
    spread = jnp.mean(center * center, axis=-1, keepdims=True)
    normal_out = (center * lax.rsqrt(spread + EPS)).reshape(
        slots, length, local_attention_teams * TEAM_DIMENSION
    ) * team_standardize_scale
    normal_out = normal_out.astype(jnp.bfloat16).reshape(
        row_count, local_attention_teams * TEAM_DIMENSION
    )
    partial_value = jnp.dot(normal_out, final_projection_matrix, preferred_element_type=jnp.float32)
    proj = (
        lax.psum(partial_value.astype(jnp.bfloat16), "tensor")
        .astype(jnp.float32)
        .reshape(slots, length, width)
    )
    positions = jnp.arange(length, dtype=jnp.int32)
    valid_slots = tally_of_tokens[:, None] > positions[None, :]
    mixed = jnp.where(valid_slots[..., None], inputs + proj, 0.0).astype(jnp.bfloat16)
    last_slot = (positions[None, :] == tally_of_tokens[:, None] - 1)[..., None]
    new_shifts = jnp.sum(jnp.where(last_slot, normed, 0.0), axis=1)
    return (
        mixed,
        state.reshape(slots, local_attention_teams, TEAM_DIMENSION * TEAM_DIMENSION),
        new_shifts,
    )


def solution(mesh):
    in_specs = (
        P("seq", None, None),
        P("seq"),
        P("seq"),
        P("seq", "tensor", None),
        P("seq", None),
        P(),
        P(),
        P(None, "tensor"),
        P(None, "tensor"),
        P(None, "tensor"),
        P("tensor", None),
        P(None, "tensor"),
        P("tensor"),
        P("tensor"),
        P("tensor"),
        P("tensor", None),
    )
    out_specs = (P("seq", None, None), P("seq", "tensor", None), P("seq", None))
    return jax.shard_map(shards, mesh=mesh, in_specs=in_specs, out_specs=out_specs, check_vma=False)
```

profile of v0, /device:TPU:1, one launch (start us, length us, event | category | flops | bytes accessed | tf_op | source)
XLA Modules:
  0.0 221.2 jit_solution(10115790613157569189)
XLA Ops:
  7.3 2.0 copy.96
  9.4 14.1 %collective-permute-start.1 = (f32[16,18432]{1,0:T(8,128)S(1)}, f32[16,18432]{1,0:T(8,128)}, u32[]{:S(2)}, u32[]{:S(2)}) collective-permute-start(f32[16,18432]{1,0:T(8,128)S(1)} %constant_dynamic-update-slice_fusion), channel_id=1, source_target_pairs={{8,0},{16,8},{24,16},{32,24},{40,32},{48,40},{56,48},{64,56},{72,6... | collective-permute-start | bytes 3538952 | tf_op jit(solution)/shard_map/ppermute | solution.py:21
  23.5 1.9 collective-permute-start
  25.5 0.7 iota_compare_fusion.1
  26.7 0.6 iota_compare_fusion
  27.6 0.9 fusion.12
  29.6 0.7 mul.296
  30.3 1.5 copy.57
  31.8 2.4 %copy.59 = bf16[2048,256]{0,1:T(8,128)(2,1)} copy(bf16[2048,256]{1,0:T(8,128)(2,1)} %param.24) | data formatting | bytes 2097152 | tf_op args[8]
  34.1 1.4 copy.61
  35.5 0.7 add_rsqrt_fusion.1
  36.3 1.5 fusion.61
  37.8 1.9 fusion.13
  39.7 8.5 %collective-permute-done.1 = f32[16,18432]{1,0:T(8,128)} collective-permute-done((f32[16,18432]{1,0:T(8,128)S(1)}, f32[16,18432]{1,0:T(8,128)}, u32[]{:S(2)}, u32[]{:S(2)}) %collective-permute-start.1) | collective-permute-done | bytes 1179680 | tf_op jit(solution)/shard_map/ppermute | solution.py:21
  48.2 7.2 %collective-permute-done = f32[16,18432]{1,0:T(8,128)} collective-permute-done((f32[16,18432]{1,0:T(8,128)S(1)}, f32[16,18432]{1,0:T(8,128)}, u32[]{:S(2)}, u32[]{:S(2)}) %collective-permute-start) | collective-permute-done | bytes 1179680 | tf_op jit(solution)/shard_map/ppermute | solution.py:19
  55.4 3.6 %pad_maximum_fusion = f32[48,18432]{1,0:T(8,128)} fusion(f32[16,18432]{1,0:T(8,128)} %collective-permute-done.1, f32[16,18432]{1,0:T(8,128)S(1)} %constant_dynamic-update-slice_fusion, f32[16,18432]{1,0:T(8,128)} %collective-permute-done), kind=kLoop, calls=%fused_computation.1 | loop fusion | flops 1769472 | bytes 7077888 | tf_op jit(solution)/shard_map/concatenate | solution.py:17
  59.0 3.6 %gather_fusion = f32[16,18432]{1,0:T(8,128)S(1)} fusion(f32[48,18432]{1,0:T(8,128)} %pad_maximum_fusion, s32[1024]{0:T(1024)} %pad_clamp_fusion), kind=kCustom, calls=%fused_computation | custom fusion | bytes 2359360 | tf_op jit(solution)/shard_map/jit(_take)/gather | solution.py:64
  62.8 1.7 reshape.180
  64.5 2.2 reshape.175
  66.9 3.5 %fusion.16 = (bf16[16,4,2048,1]{2,1,0,3:T(4,128)(2,1)S(1)}, bf16[16,4,2048,1]{2,1,0,3:T(4,128)(2,1)S(1)}, bf16[16,4,2048,1]{2,1,0,3:T(4,128)(2,1)S(1)}, bf16[16,4,2048]{2,1,0:T(4,128)(2,1)}, f32[16,2048]{1,0:T(8,128)}) fusion(f32[2048]{0:T(1024)} %bitcast.159, f32[16,3,2048]{2,1,0:T(4,128)} %bitcast.149, f32[16,1,2048]{2,1,0:T(1,128)S(1)} %copy.56, ...), kind=kLoop, calls=%fused_computation.37 | loop fusion | flops 2588672 | bytes 2007616 | tf_op jit(solution)/shard_map/convert_element_type | solution.py:78
  70.3 0.6 fusion.23
  71.0 0.7 slice_bitcast_fusion.16
  71.7 0.6 fusion.21
  73.0 0.6 copy.64
  74.3 0.6 copy.70
  74.9 0.6 fusion.19
  75.6 0.6 copy-done.7
  77.4 0.6 copy.68
  78.1 0.6 copy.71
  78.7 1.7 reshape.176
  80.4 1.5 fusion.45
  81.9 24.3 %psum.14 = f32[64,64]{1,0:T(8,128)} all-reduce(f32[64,64]{1,0:T(8,128)} %fusion.45), channel_id=1, replica_groups=mesh['seq'=64,'tensor'=8] {'tensor'}, use_global_device_ids=true, to_apply=%region_3.4 | all-reduce | flops 4096 | bytes 32768 | tf_op jit(solution)/shard_map/psum | solution.py:95
  106.2 1.6 fusion.6
  107.8 1.6 reshape.177
  109.4 1.4 slice_bitcast_fusion.1
  110.9 4.8 %fusion.39 = f32[16,4,1,64]{3,2,1,0:T(1,128)S(1)} fusion(f32[16,4,64,1]{2,0,1,3:T(8,128)} %get-tuple-element.24, f32[16,4,64]{2,1,0:T(4,128)S(1)} %get-tuple-element.12, pred[16]{0:T(512)(128)(4,1)S(1)} %copy-done.43, f32[16,4,64,64]{3,2,1,0:T(8,128)S(1)} %copy-done.1, f32[16,4,64]{2,1,0:T(4,128)} %copy.65, f32[16,4,64]{2,1,0:T(4,128)} %copy.64, ...), kind=kOutput, calls=%fused_computation.85 | convolution fusion | flops 5242880 | bytes 1179680 | tf_op jit(solution)/shard_map/rhi,rhij->rhj/dot_general | solution.py:114
  115.9 6.2 %fusion = f32[16,4,1,64]{3,2,1,0:T(1,128)S(1)} fusion(f32[16,4,64]{2,1,0:T(4,128)S(1)} %get-tuple-element.11, pred[16]{0:T(512)(128)(4,1)S(1)} %copy-done.41, f32[16,4,64]{2,1,0:T(4,128)S(1)} %copy-done.19, f32[16,4,64]{2,1,0:T(4,128)S(1)} %copy-done.15, f32[16,4,64,1]{2,0,1,3:T(8,128)S(1)} %copy-done.38, f32[16,4,64]{2,1,0:T(4,128)S(1)} %get-tuple-element.12, ...), kind=kOutput, calls=%fused_computation.3 | convolution fusion | flops 6291456 | bytes 1228848 | tf_op jit(solution)/shard_map/rhi,rhij->rhj/dot_general | solution.py:114
  122.8 2.8 %fusion.9 = f32[16,4,1,64]{3,2,1,0:T(1,128)S(1)} fusion(f32[16,4,64,64]{3,2,1,0:T(8,128)S(1)} %copy-done.1, f32[16,4,64]{2,1,0:T(4,128)S(1)} %get-tuple-element.13, pred[16]{0:T(512)(128)(4,1)S(1)} %copy-done.45, f32[16,4,64]{2,1,0:T(4,128)S(1)} %copy-done.22, f32[16,4,64]{2,1,0:T(4,128)S(1)} %copy-done.18, f32[16,4,64,1]{2,0,1,3:T(8,128)S(1)} %copy-done.37), kind=kOutput, calls=%fused_computation.23 | convolution fusion | flops 4194304 | bytes 1130512 | tf_op jit(solution)/shard_map/rhi,rhij->rhj/dot_general | solution.py:114
  125.7 1.9 fusion.42
  128.6 0.7 copy.95
  129.4 0.8 copy.69
  130.1 0.8 copy.72
  130.9 1.4 broadcast_multiply_fusion.3
  132.4 2.8 %broadcast_multiply_fusion.2 = f32[16,4,64,64]{3,2,1,0:T(8,128)} fusion(f32[16,4,64]{2,1,0:T(4,128)} %copy.68, f32[16,4,64]{2,1,0:T(4,128)} %copy.67), kind=kLoop, calls=%fused_computation.17 | loop fusion | flops 262144 | bytes 1081344 | tf_op jit(solution)/shard_map/mul | solution.py:125
  135.1 1.9 broadcast_multiply_fusion.1
  138.3 0.7 copy.75
  139.4 0.7 stack.32
  140.1 0.9 sub.43.clone
  141.0 0.8 sub.44
  141.8 0.9 mul.343
  142.7 0.8 mul.344
  143.4 1.9 convolution_convert_fusion
  145.3 1.8 reshape.178
  147.1 1.8 mul.355
  148.9 3.1 %mul.357 = f32[16,4,4096]{2,1,0:T(4,128)} reshape(f32[16,4,64,64]{3,2,1,0:T(8,128)} %broadcast_multiply_fusion.2) | data formatting | bytes 2097152 | tf_op jit(solution)/shard_map/mul | solution.py:125
  152.1 1.8 mul.359
  154.6 1.8 mul.364
  157.0 1.8 mul.353
  159.4 1.8 mul.352
  161.9 1.8 mul.351
  164.3 1.9 mul.350
  166.3 6.9 %add_select_fusion.2 = f32[16,4,4096]{2,1,0:T(4,128)} fusion(f32[16,4,4096]{2,1,0:T(4,128)} %mul.364, f32[16,4,4096]{2,1,0:T(4,128)} %mul.350, f32[16,4,4096]{2,1,0:T(4,128)} %mul.359, f32[16,4,4096]{2,1,0:T(4,128)} %mul.351, f32[16,4,4096]{2,1,0:T(4,128)} %mul.357, f32[16,4,4096]{2,1,0:T(4,128)} %mul.352, f32[16,4,4096]{2,1,0:T(4,128)} %reshape.180, ...), kind=kLoop, calls=%fused_computation.13 | loop fusion | flops 3145728 | bytes 10485824 | tf_op jit(solution)/shard_map/jit(_where)/select_n | solution.py:127
  173.2 39.3 %all-reduce.2.cloned.1.call-done = bf16[16,4,2048]{2,1,0:T(4,128)(2,1)} async-done(((bf16[16,4,2048]{2,1,0:T(4,128)(2,1)}), bf16[16,4,2048]{2,1,0:T(4,128)(2,1)}) %all-reduce.2.cloned.1.call-update) | async-done | bytes 262160 | tf_op jit(solution)/shard_map/psum | solution.py:139
  212.6 1.8 fusion.15
  (144 shorter events, 11.5 us)
Async XLA Ops:
  7.2 136.3 %copy-start = (bf16[256,2048]{1,0:T(8,128)(2,1)S(1)}, bf16[256,2048]{1,0:T(8,128)(2,1)}, u32[]{:S(2)}) copy-start(bf16[256,2048]{1,0:T(8,128)(2,1)} %param.31) | copy-start | bytes 3145732
  7.2 205.4 %all-reduce.2.cloned.1.call-start = ((), (), s32[]{:S(2)}) async-start(), calls=%async_computation | async-start | bytes 524288 | tf_op jit(solution)/shard_map/psum | solution.py:139
  7.2 2.1 copy-start.33
  7.2 18.2 %copy-start.48 = (s32[16]{0:T(128)S(1)}, s32[16]{0:T(128)}, u32[]{:S(2)}) copy-start(s32[16]{0:T(128)} %param.17) | copy-start | bytes 196
  7.2 20.1 %copy-start.3 = (bf16[16,4,2048]{2,1,0:T(4,128)(2,1)S(1)}, bf16[16,4,2048]{2,1,0:T(4,128)(2,1)}, u32[]{:S(2)}) copy-start(bf16[16,4,2048]{2,1,0:T(4,128)(2,1)} %param.16) | copy-start | bytes 786436
  7.3 21.2 %copy-start.51 = (s32[16]{0:T(128)S(1)}, s32[16]{0:T(128)}, u32[]{:S(2)}) copy-start(s32[16]{0:T(128)} %param.18) | copy-start | bytes 196
  7.3 22.4 %copy-start.50 = (f32[256]{0:T(256)S(1)}, f32[256]{0:T(256)}, u32[]{:S(2)}) copy-start(f32[256]{0:T(256)} %param.29) | copy-start | bytes 3076
  7.3 23.0 %copy-start.11 = (bf16[2048,256]{1,0:T(8,128)(2,1)S(1)}, bf16[2048,256]{1,0:T(8,128)(2,1)}, u32[]{:S(2)}) copy-start(bf16[2048,256]{1,0:T(8,128)(2,1)} %param.23) | copy-start | bytes 3145732
  9.4 38.8 %collective-permute-start.1 = (f32[16,18432]{1,0:T(8,128)S(1)}, f32[16,18432]{1,0:T(8,128)}, u32[]{:S(2)}, u32[]{:S(2)}) collective-permute-start(f32[16,18432]{1,0:T(8,128)S(1)} %constant_dynamic-update-slice_fusion), channel_id=1, source_target_pairs={{8,0},{16,8},{24,16},{32,24},{40,32},{48,40},{56,48},{64,56},{72,6... | collective-permute-start | bytes 3538952 | tf_op jit(solution)/shard_map/ppermute | solution.py:21
  23.5 31.8 %collective-permute-start = (f32[16,18432]{1,0:T(8,128)S(1)}, f32[16,18432]{1,0:T(8,128)}, u32[]{:S(2)}, u32[]{:S(2)}) collective-permute-start(f32[16,18432]{1,0:T(8,128)S(1)} %constant_dynamic-update-slice_fusion), channel_id=1, source_target_pairs={{0,8},{8,16},{16,24},{24,32},{32,40},{40,48},{48,56},{56,64},{64,7... | collective-permute-start | bytes 3538952 | tf_op jit(solution)/shard_map/ppermute | solution.py:19
  31.8 2.4 %copy-start.12 = (bf16[2048,256]{1,0:T(8,128)(2,1)S(1)}, bf16[2048,256]{1,0:T(8,128)(2,1)}, u32[]{:S(2)}) copy-start(bf16[2048,256]{1,0:T(8,128)(2,1)} %param.25) | copy-start | bytes 3145732
  59.0 3.6 %copy-start.47 = (pred[16]{0:T(512)(128)(4,1)S(1)}, pred[16]{0:T(512)(128)(4,1)}, u32[]{:S(2)}) copy-start(pred[16]{0:T(512)(128)(4,1)} %get-tuple-element.3) | copy-start | bytes 52
  64.5 5.8 %copy-start.6 = (bf16[2048,256]{0,1:T(8,128)(2,1)S(1)}, bf16[2048,256]{0,1:T(8,128)(2,1)}, u32[]{:S(2)}) copy-start(bf16[2048,256]{0,1:T(8,128)(2,1)} %copy.57) | copy-start | bytes 3145732
  66.7 5.0 %copy-start.5 = (bf16[2048,256]{0,1:T(8,128)(2,1)S(1)}, bf16[2048,256]{0,1:T(8,128)(2,1)}, u32[]{:S(2)}) copy-start(bf16[2048,256]{0,1:T(8,128)(2,1)} %copy.59) | copy-start | bytes 3145732
  70.3 4.6 %copy-start.4 = (bf16[2048,256]{0,1:T(8,128)(2,1)S(1)}, bf16[2048,256]{0,1:T(8,128)(2,1)}, u32[]{:S(2)}) copy-start(bf16[2048,256]{0,1:T(8,128)(2,1)} %copy.61) | copy-start | bytes 3145732
  71.0 3.9 %copy-start.9 = (f32[16,4,4,64]{3,0,2,1:T(8,128)}, f32[16,4,4,64]{3,0,2,1:T(8,128)S(1)}, u32[]{:S(2)}) copy-start(f32[16,4,4,64]{3,0,2,1:T(8,128)S(1)} %fusion.23) | copy-start | bytes 196612
  71.7 34.5 %copy-start.49 = (f32[256]{0:T(256)S(1)}, f32[256]{0:T(256)}, u32[]{:S(2)}) copy-start(f32[256]{0:T(256)} %param.28) | copy-start | bytes 3076
  72.4 38.5 %copy-start.1 = (f32[16,4,64,64]{3,2,1,0:T(8,128)S(1)}, f32[16,4,64,64]{3,2,1,0:T(8,128)}, u32[]{:S(2)}) copy-start(f32[16,4,64,64]{3,2,1,0:T(8,128)} %reshape.175) | copy-start | bytes 3145732
  72.4 38.5 %copy-start.43 = (pred[16]{0:T(512)(128)(4,1)S(1)}, pred[16]{0:T(512)(128)(4,1)}, u32[]{:S(2)}) copy-start(pred[16]{0:T(512)(128)(4,1)} %get-tuple-element.32) | copy-start | bytes 52
  72.4 38.5 %copy-start.45 = (pred[16]{0:T(512)(128)(4,1)S(1)}, pred[16]{0:T(512)(128)(4,1)}, u32[]{:S(2)}) copy-start(pred[16]{0:T(512)(128)(4,1)} %get-tuple-element.33) | copy-start | bytes 52
  75.5 0.7 copy-start.7
  110.8 4.9 %copy-start.26 = (f32[16,4,64]{2,1,0:T(4,128)}, f32[16,4,64]{2,1,0:T(4,128)S(1)}, u32[]{:S(2)}) copy-start(f32[16,4,64]{2,1,0:T(4,128)S(1)} %get-tuple-element.11) | copy-start | bytes 49156
  110.8 4.9 %copy-start.28 = (f32[16,4,64]{2,1,0:T(4,128)}, f32[16,4,64]{2,1,0:T(4,128)S(1)}, u32[]{:S(2)}) copy-start(f32[16,4,64]{2,1,0:T(4,128)S(1)} %get-tuple-element.12) | copy-start | bytes 49156
  110.8 12.0 %copy-start.30 = (f32[16,4,64]{2,1,0:T(4,128)}, f32[16,4,64]{2,1,0:T(4,128)S(1)}, u32[]{:S(2)}) copy-start(f32[16,4,64]{2,1,0:T(4,128)S(1)} %get-tuple-element.13) | copy-start | bytes 49156
  110.8 4.9 %copy-start.15 = (f32[16,4,64]{2,1,0:T(4,128)S(1)}, f32[16,4,64]{2,1,0:T(4,128)}, u32[]{:S(2)}) copy-start(f32[16,4,64]{2,1,0:T(4,128)} %copy.70) | copy-start | bytes 49156
  110.9 4.9 %copy-start.17 = (f32[16,4,64]{2,1,0:T(4,128)S(1)}, f32[16,4,64]{2,1,0:T(4,128)}, u32[]{:S(2)}) copy-start(f32[16,4,64]{2,1,0:T(4,128)} %copy.67) | copy-start | bytes 49156
  110.9 4.9 %copy-start.18 = (f32[16,4,64]{2,1,0:T(4,128)S(1)}, f32[16,4,64]{2,1,0:T(4,128)}, u32[]{:S(2)}) copy-start(f32[16,4,64]{2,1,0:T(4,128)} %copy.64) | copy-start | bytes 49156
  110.9 4.9 %copy-start.19 = (f32[16,4,64]{2,1,0:T(4,128)S(1)}, f32[16,4,64]{2,1,0:T(4,128)}, u32[]{:S(2)}) copy-start(f32[16,4,64]{2,1,0:T(4,128)} %copy.71) | copy-start | bytes 49156
  110.9 4.9 %copy-start.21 = (f32[16,4,64]{2,1,0:T(4,128)S(1)}, f32[16,4,64]{2,1,0:T(4,128)}, u32[]{:S(2)}) copy-start(f32[16,4,64]{2,1,0:T(4,128)} %copy.68) | copy-start | bytes 49156
  110.9 4.9 %copy-start.22 = (f32[16,4,64]{2,1,0:T(4,128)S(1)}, f32[16,4,64]{2,1,0:T(4,128)}, u32[]{:S(2)}) copy-start(f32[16,4,64]{2,1,0:T(4,128)} %copy.65) | copy-start | bytes 49156
  110.9 4.9 %copy-start.38 = (f32[16,4,64,1]{2,0,1,3:T(8,128)S(1)}, f32[16,4,64,1]{2,0,1,3:T(8,128)}, u32[]{:S(2)}) copy-start(f32[16,4,64,1]{2,0,1,3:T(8,128)} %get-tuple-element.25) | copy-start | bytes 49156
  110.9 4.9 %copy-start.41 = (pred[16]{0:T(512)(128)(4,1)S(1)}, pred[16]{0:T(512)(128)(4,1)}, u32[]{:S(2)}) copy-start(pred[16]{0:T(512)(128)(4,1)} %get-tuple-element.31) | copy-start | bytes 52
  115.8 6.2 %copy-start.8 = (f32[16,4,4,64]{3,0,2,1:T(8,128)S(1)}, f32[16,4,4,64]{3,0,2,1:T(8,128)}, u32[]{:S(2)}) copy-start(f32[16,4,4,64]{3,0,2,1:T(8,128)} %copy-done.7) | copy-start | bytes 196612
  115.8 6.2 %copy-start.10 = (f32[16,4,4,64]{3,0,2,1:T(8,128)S(1)}, f32[16,4,4,64]{3,0,2,1:T(8,128)}, u32[]{:S(2)}) copy-start(f32[16,4,4,64]{3,0,2,1:T(8,128)} %copy-done.9) | copy-start | bytes 196612
  115.9 6.2 %copy-start.36 = (f32[4,64]{1,0:T(4,128)S(1)}, f32[4,64]{1,0:T(4,128)}, u32[]{:S(2)}) copy-start(f32[4,64]{1,0:T(4,128)} %mul.296) | copy-start | bytes 3076
  115.9 6.9 %copy-start.37 = (f32[16,4,64,1]{2,0,1,3:T(8,128)S(1)}, f32[16,4,64,1]{2,0,1,3:T(8,128)}, u32[]{:S(2)}) copy-start(f32[16,4,64,1]{2,0,1,3:T(8,128)} %get-tuple-element.23) | copy-start | bytes 49156
  122.1 3.6 %copy-start.32 = (f32[16,4,64,1]{2,0,1,3:T(8,128)S(1)}, f32[16,4,64,1]{2,0,1,3:T(8,128)}, u32[]{:S(2)}) copy-start(f32[16,4,64,1]{2,0,1,3:T(8,128)} %get-tuple-element.22) | copy-start | bytes 49156
  122.5 5.9 %copy-start.13 = (f32[16,4,64]{2,0,1:T(8,128)}, f32[16,4,64]{2,0,1:T(8,128)S(1)}, u32[]{:S(2)}) copy-start(f32[16,4,64]{2,0,1:T(8,128)S(1)} %bitcast_add_fusion) | copy-start | bytes 49156
  122.8 5.6 %copy-start.14 = (f32[16,4,64]{2,0,1:T(8,128)}, f32[16,4,64]{2,0,1:T(8,128)S(1)}, u32[]{:S(2)}) copy-start(f32[16,4,64]{2,0,1:T(8,128)S(1)} %bitcast_add_fusion.1) | copy-start | bytes 49156
  130.9 4.2 %copy-start.16 = (f32[16,4,64]{2,1,0:T(4,128)S(1)}, f32[16,4,64]{2,1,0:T(4,128)}, u32[]{:S(2)}) copy-start(f32[16,4,64]{2,1,0:T(4,128)} %copy.70) | copy-start | bytes 49156
  130.9 4.2 %copy-start.20 = (f32[16,4,64]{2,1,0:T(4,128)S(1)}, f32[16,4,64]{2,1,0:T(4,128)}, u32[]{:S(2)}) copy-start(f32[16,4,64]{2,1,0:T(4,128)} %copy.71) | copy-start | bytes 49156
  132.3 4.7 %copy-start.34 = (f32[16,4,64]{2,0,1:T(8,128)S(1)}, f32[16,4,64]{2,0,1:T(8,128)}, u32[]{:S(2)}) copy-start(f32[16,4,64]{2,0,1:T(8,128)} %get-tuple-element.14) | copy-start | bytes 49156
  132.3 5.3 %copy-start.35 = (f32[16,4,64]{2,0,1:T(8,128)S(1)}, f32[16,4,64]{2,0,1:T(8,128)}, u32[]{:S(2)}) copy-start(f32[16,4,64]{2,0,1:T(8,128)} %get-tuple-element.18) | copy-start | bytes 49156
  148.9 3.1 %copy-start.2 = (f32[16,4,64,64]{3,2,1,0:T(8,128)S(1)}, f32[16,4,64,64]{3,2,1,0:T(8,128)}, u32[]{:S(2)}) copy-start(f32[16,4,64,64]{3,2,1,0:T(8,128)} %broadcast_multiply_fusion.1) | copy-start | bytes 3145732
  152.1 1.8 copy-start.23
  152.1 1.8 copy-start.24
  154.5 1.8 copy-start.31
  157.0 1.8 copy-start.29
  159.4 1.9 copy-start.27
  161.9 1.8 copy-start.25
  164.3 2.0 copy-start.40
  164.3 2.0 copy-start.42
  164.3 1.9 copy-start.44
  164.3 1.9 copy-start.46
  166.3 46.3 %copy-start.39 = (pred[16,4]{1,0:T(8,128)(4,1)S(1)}, pred[16,4]{1,0:T(8,128)(4,1)}, u32[]{:S(2)}) copy-start(pred[16,4]{1,0:T(8,128)(4,1)} %iota_compare_fusion.1) | copy-start | bytes 196
Sparse Core Ops, SparseCore 0:
  147.3 65.2 all-reduce.1
where the time goes:
time: 223 us; the launch traced here: 221 us
  local copies, waits for them, and re-layouts  57.4 us (26%)
  waiting for transfers between devices  55 us (25%)
  other arithmetic  31.1 us (14%)
  blocking collectives  24.3 us (11%)
  matrix products  22.6 us (10%)
  starting transfers between devices  16.1 us (7%)
  between operations  14.7 us (7%)
    psum x1, waiting for transfers between devices, shards(): lax.psum(partial_value.astype(jnp.bfloat16), 'tensor').astype(jnp.float32)  39.3 us
    psum x1, blocking collectives, shards(): lax.psum(jnp.dot(incoming_piece, forget_map_left_matrix, preferred_elemen...  24.3 us
    dot_general x4, matrix products, shards(): jnp.einsum('rhi,rhij->rhj', current_receptance, state, precision=lax.Prec...  15.7 us
    ppermute x1, starting transfers between devices, padded(): lax.ppermute(head, axis, [((i + 1) % count, i) for i in range(count)])  14.1 us
    mul x9, local copies, waits for them, and re-layouts, shards(): decay_factor[:, step][..., None] * state  11.2 us
    unnamed x110, local copies, waits for them, and re-layouts  8.88 us
    mul x4, local copies, waits for them, and re-layouts, shards(): current_key[..., None] * current_value[..., None, :]  8.6 us
    ppermute x1, waiting for transfers between devices, padded(): lax.ppermute(head, axis, [((i + 1) % count, i) for i in range(count)])  8.48 us
  transfers between devices with their start and end apart: 3, of which 3 were waited for; matrix products, arithmetic and copies ran while one was open for 18% of the time, Pallas kernels for 0%

commit v1 on v0

v1 whole, which is shorter than its diff:
```python
import functools

import jax
import jax.numpy as jnp
from jax import lax
from jax.experimental import pallas as pl
from jax.experimental.pallas import tpu as pltpu
from jax.sharding import PartitionSpec as P

EPS = 1e-05
F32 = jnp.float32
BF16 = jnp.bfloat16
HEAD = 64
SLOTS = 16
STEPS = 4
WIDTH = 2048
HEADS = 4
LOCAL = HEADS * HEAD
TILES = WIDTH // 128
ROWS = SLOTS * STEPS
STATE_ROWS = HEADS * HEAD * HEAD // 128
PIECE = STATE_ROWS + TILES
PACK_ROWS = 2 * PIECE + 8


def vmem(count):
    return [pl.BlockSpec(memory_space=pltpu.VMEM)] * count


def smem(count):
    return [pl.BlockSpec(memory_space=pltpu.SMEM)] * count


def dot(a, b):
    return jnp.dot(a, b, preferred_element_type=F32)


def dot_rows(a, b):
    return lax.dot_general(a, b, (((0,), (0,)), ((), ())), preferred_element_type=F32)


def split(a):
    hi = a.astype(BF16)
    return hi, (a - hi.astype(F32)).astype(BF16)


def dot_split(a, b):
    hi, lo = split(a)
    return dot(hi, b) + dot(lo, b)


def iota(shape, dim):
    return lax.broadcasted_iota(jnp.int32, shape, dim)


def column_of(tally_ref, shape):
    rows = iota(shape, 0)
    out = jnp.zeros(shape, jnp.int32)
    for q in range(SLOTS):
        out = jnp.where(rows == q, tally_ref[q], out)
    return out


def row_of(ref):
    return jnp.concatenate([ref[i : i + 1, :] for i in range(ref.shape[0])], axis=1)


def pack_kernel(where_ref, lookup_ref, mem_ref, prev_ref, out_ref):
    first = where_ref[0] * SLOTS
    kept = jnp.int32(0)
    for q in range(SLOTS):
        at = lookup_ref[q] - first
        own = (at >= 0) & (at < SLOTS)
        kept = kept | jnp.where(own, jnp.int32(1) << jnp.where(own, at, 0), 0)
    low, high = jnp.int32(0), jnp.int32(0)
    for s in range(SLOTS):
        high = jnp.where((kept >> s) & 1 == 0, s, high)
        low = jnp.where((kept >> (SLOTS - 1 - s)) & 1 == 0, SLOTS - 1 - s, low)
    for n, slot in enumerate((low, high)):
        base = n * PIECE
        out_ref[base : base + STATE_ROWS, :] = mem_ref[pl.ds(slot * STATE_ROWS, STATE_ROWS), :]
        row = prev_ref[pl.ds(slot, 1), :]
        for c in range(TILES):
            out_ref[base + STATE_ROWS + c : base + STATE_ROWS + c + 1, :] = row[:, c * 128 : (c + 1) * 128]
    ids = jnp.where(iota((8, 128), 0) == 0, first + low, first + high)
    out_ref[2 * PIECE : 2 * PIECE + 8, :] = ids.astype(F32)


def pick(recv_ref, wanted, start, count):
    is_low = recv_ref[2 * PIECE : 2 * PIECE + 1, :] == wanted.astype(F32)
    return jnp.where(is_low, recv_ref[start : start + count, :], recv_ref[PIECE + start : PIECE + start + count, :])


def sources(where_ref, lookup_ref, q):
    wanted = lookup_ref[q]
    owner = wanted // SLOTS
    own = owner == where_ref[0]
    before = owner == where_ref[1]
    at = jnp.where(own, wanted - where_ref[0] * SLOTS, 0)
    return wanted, own, before, at


def project_kernel(
    where_ref, lookup_ref, tally_ref, x_ref, prev_ref, from_before, from_after, gain_ref, blend_ref, wr_ref, wk_ref, wv_ref,
    r_ref, k_ref, v_ref, mixed_ref, last_ref, x32, shift,
):
    x32[...] = x_ref[...].astype(F32)
    gain = row_of(gain_ref)
    normed = []
    for t in range(STEPS):
        row = jnp.concatenate([x32[pl.ds(c * STEPS + t, SLOTS, stride=STEPS * TILES), :] for c in range(TILES)], axis=1)
        center = row - jnp.mean(row, axis=-1, keepdims=True)
        spread = jnp.mean(center * center, axis=-1, keepdims=True)
        normed.append(center * lax.rsqrt(spread + EPS) * gain)
    tally = column_of(tally_ref, (SLOTS, 128))[:, :1]
    last = normed[0]
    for t in range(1, STEPS):
        last = jnp.where(tally == t + 1, normed[t], last)
    last_ref[...] = last
    for q in range(SLOTS):
        wanted, own, before, at = sources(where_ref, lookup_ref, q)

        @pl.when(own)
        def _():
            shift[q : q + 1, :] = prev_ref[pl.ds(at, 1), :]

        @pl.when(jnp.logical_not(own))
        def _():
            rows = jnp.where(
                before, pick(from_before, wanted, STATE_ROWS, TILES), pick(from_after, wanted, STATE_ROWS, TILES)
            )
            for c in range(TILES):
                shift[q : q + 1, c * 128 : (c + 1) * 128] = rows[c : c + 1, :]

    xn = jnp.concatenate(normed, axis=0)
    change = jnp.concatenate([shift[...]] + normed[:-1], axis=0) - xn

    def mix(which):
        return (xn + change * blend_ref[which : which + 1, :]).astype(BF16)

    r_ref[...] = dot(mix(0), wr_ref[...])
    k_ref[...] = dot(mix(1), wk_ref[...])
    v_ref[...] = dot(mix(2), wv_ref[...])
    mixed_ref[...] = mix(3)


def step_kernel(
    where_ref, lookup_ref, tally_ref, mixed_ref, left_ref, right_ref, base_ref, boost_ref, gain_ref, r_ref, k_ref, v_ref,
    mem_ref, from_before, from_after, final_ref,
    part_ref, new_ref, state, reads, keys, vals, decays, heads, part,
):
    for q in range(SLOTS):
        wanted, own, before, at = sources(where_ref, lookup_ref, q)
        here = slice(q * STATE_ROWS, (q + 1) * STATE_ROWS)

        @pl.when(own)
        def _():
            state[here, :] = mem_ref[pl.ds(at * STATE_ROWS, STATE_ROWS), :]

        @pl.when(jnp.logical_not(own) & before)
        def _():
            state[here, :] = pick(from_before, wanted, 0, STATE_ROWS)

        @pl.when(jnp.logical_not(own) & jnp.logical_not(before))
        def _():
            state[here, :] = pick(from_after, wanted, 0, STATE_ROWS)

    pre = jnp.zeros((ROWS, left_ref.shape[1]), F32)
    chunk = left_ref.shape[2]
    for n in range(left_ref.shape[0]):
        pre = pre + lax.dot_general(
            mixed_ref[:, n * chunk : (n + 1) * chunk], left_ref[n], (((1,), (1,)), ((), ())), preferred_element_type=F32
        )
    lora = jnp.tanh(pre).astype(BF16)
    decay = jnp.exp(-jnp.exp(row_of(base_ref) + dot(lora, right_ref[...])))
    tally = column_of(tally_ref, (SLOTS, 128))[:, :1]
    cut = lambda a, t: a[t * SLOTS : (t + 1) * SLOTS, :]
    r = [cut(r_ref[...], t) for t in range(STEPS)]
    k = [cut(k_ref[...], t) for t in range(STEPS)]
    v = [cut(v_ref[...], t) for t in range(STEPS)]
    d = [jnp.where(tally > t, cut(decay, t), 1.0) for t in range(STEPS)]
    kept = [jnp.where(tally > t, k[t], 0.0) for t in range(STEPS)]
    boost = row_of(boost_ref)

    run, reach = r[0] * 0.0 + 1.0, []
    for t in range(STEPS):
        reach.append(r[t] * run)
        run = run * d[t]
    tail, coefs = None, [None] * STEPS
    for t in reversed(range(STEPS)):
        coefs[t] = kept[t] if tail is None else kept[t] * tail
        tail = d[t] if tail is None else tail * d[t]
    pairs, terms = [], []
    for t in range(STEPS):
        pairs.append((t, t))
        terms.append(r[t] * boost * k[t])
        weight = r[t]
        for s in reversed(range(t)):
            pairs.append((t, s))
            terms.append(weight * kept[s])
            weight = weight * d[s]
    row256, col256 = iota((LOCAL, LOCAL), 0), iota((LOCAL, LOCAL), 1)
    same_head = (row256 // HEAD == col256 // HEAD).astype(BF16)
    sums = dot_split(jnp.concatenate(terms, axis=0), same_head)
    within = [None] * STEPS
    for n, (t, s) in enumerate(pairs):
        term = cut(sums, n) * v[s]
        within[t] = term if within[t] is None else within[t] + term

    source = (col256 % HEADS) * HEAD + ((col256 // HEADS) % (HEAD // 2)) * 2 + col256 // 128
    reorder = (row256 == source).astype(BF16)
    moved = dot_split(jnp.concatenate(reach + coefs + [run], axis=0), reorder)
    rowd, cold = iota((LOCAL, HEADS * 128), 0), iota((LOCAL, HEADS * 128), 1)
    double = (rowd == (cold // 128) * HEAD + cold % HEAD).astype(BF16)
    doubled = dot(v_ref[...].astype(BF16), double)

    lane = iota((SLOTS, 128), 1)
    for h in range(HEADS):
        head_lane = lane % HEADS == h
        for p in range(2):
            half = lane // HEAD == p
            for t in range(STEPS):
                at = pl.ds(t * 8 + p * HEADS + h, SLOTS, stride=STEPS * 8)
                cols = slice(p * 128, (p + 1) * 128)
                reads[at, :] = jnp.where(head_lane, cut(moved, t)[:, cols], 0.0)
                keys[at, :] = jnp.where(head_lane, cut(moved, STEPS + t)[:, cols], 0.0)
                vals[at, :] = jnp.where(half, cut(doubled, t)[:, h * 128 : (h + 1) * 128], 0.0)
            whole = jnp.where(head_lane, cut(moved, 2 * STEPS)[:, cols], 0.0)
            high = whole.astype(BF16).astype(F32)
            decays[pl.ds(p * HEADS + h, SLOTS, stride=16), :] = high
            decays[pl.ds(8 + p * HEADS + h, SLOTS, stride=16), :] = whole - high
    ones = ((iota((16, 128), 0) // HEADS) % 2 == iota((16, 128), 1) // HEAD).astype(BF16)
    for q in range(SLOTS):
        here = slice(q * STATE_ROWS, (q + 1) * STATE_ROWS)
        rows = slice(q * STEPS * 8, (q + 1) * STEPS * 8)
        now = state[here, :]
        heads[rows, :] = dot(reads[rows, :].astype(BF16), now.astype(BF16))
        fade = dot_rows(decays[q * 16 : (q + 1) * 16, :].astype(BF16), ones)
        grown = dot_rows(keys[rows, :].astype(BF16), vals[rows, :].astype(BF16))
        new_ref[here, :] = fade * now + grown

    outs = []
    left_half = lane < HEAD
    for t in range(STEPS):
        def read(p, h):
            return heads[pl.ds(t * 8 + p * HEADS + h, SLOTS, stride=STEPS * 8), :]

        cols = []
        for h in range(0, HEADS, 2):
            a, b, c, e = read(0, h), read(1, h), read(0, h + 1), read(1, h + 1)
            cols.append(jnp.where(left_half, a, e) + pltpu.roll(jnp.where(left_half, c, b), HEAD, 1))
        outs.append(jnp.concatenate(cols, axis=1) + within[t])
    y = jnp.concatenate(outs, axis=0)
    center = y - dot_split(y, same_head) * (1.0 / HEAD)
    spread = dot_split(center * center, same_head) * (1.0 / HEAD)
    g = (center * lax.rsqrt(spread + EPS) * row_of(gain_ref)).astype(BF16)
    proj = dot(g, final_ref[...])
    for t in range(STEPS):
        for c in range(TILES):
            part[pl.ds(c * STEPS + t, SLOTS, stride=STEPS * TILES), :] = cut(proj, t)[:, c * 128 : (c + 1) * 128]
    part_ref[...] = part[...].astype(BF16)


def finish_kernel(tally_ref, x_ref, proj_ref, out_ref):
    step = iota((STEPS * TILES, 128), 0) % STEPS
    for q in range(SLOTS):
        here = slice(q * STEPS * TILES, (q + 1) * STEPS * TILES)
        total = x_ref[here, :].astype(F32) + proj_ref[here, :].astype(F32)
        out_ref[here, :] = jnp.where(step < tally_ref[q], total, 0.0).astype(BF16)


def cost(flops, bytes_accessed):
    return pl.CostEstimate(flops=flops, bytes_accessed=bytes_accessed, transcendentals=0)


def tiles_view(a):
    lead, mid, width = a.shape
    return a.reshape(lead, mid, width // 128, 128).transpose(0, 2, 1, 3).reshape(lead * width // 128 * mid, 128)


def tiles_back(a, lead, mid, width):
    return a.reshape(lead, width // 128, mid, 128).transpose(0, 2, 1, 3).reshape(lead, mid, width)


def shards(
    layer_entry_vectors,
    tally_of_tokens,
    prior_slot_lookup,
    memory_matrices,
    previous_standardized_entries,
    entry_standardize_scale,
    blend_coefficients,
    acceptance_projection_matrix,
    lookup_projection_matrix,
    payload_projection_matrix,
    forget_map_left_matrix,
    forget_map_right_matrix,
    feature_forget_logloglevel,
    present_token_boost,
    team_standardize_scale,
    final_projection_matrix,
):
    rings = lax.axis_size("seq")
    teams = lax.axis_size("tensor")
    device = lax.axis_index("seq")
    where = jnp.stack([device, (device + rings - 1) % rings]).astype(jnp.int32)
    x = tiles_view(layer_entry_vectors)
    mem = tiles_view(memory_matrices)
    params = pltpu.CompilerParams(vmem_limit_bytes=24 << 20)

    left_t = forget_map_left_matrix.T
    left = lax.all_to_all(jnp.broadcast_to(left_t[None], (teams,) + left_t.shape), "tensor", 0, 0)

    packed = pl.pallas_call(
        pack_kernel,
        out_shape=jax.ShapeDtypeStruct((PACK_ROWS, 128), F32),
        in_specs=smem(2) + vmem(2),
        out_specs=vmem(1)[0],
        compiler_params=params,
        cost_estimate=cost(0, 1 << 20),
        name="pack",
    )(where, prior_slot_lookup, mem, previous_standardized_entries)
    from_before = lax.ppermute(packed, "seq", [(i, (i + 1) % rings) for i in range(rings)])
    from_after = lax.ppermute(packed, "seq", [((i + 1) % rings, i) for i in range(rings)])

    r, k, v, mixed3, new_shifts = pl.pallas_call(
        project_kernel,
        out_shape=[jax.ShapeDtypeStruct((ROWS, LOCAL), F32)] * 3
        + [jax.ShapeDtypeStruct((ROWS, WIDTH), BF16), jax.ShapeDtypeStruct((SLOTS, WIDTH), F32)],
        in_specs=smem(3) + vmem(9),
        out_specs=vmem(5),
        scratch_shapes=[pltpu.VMEM((ROWS * TILES, 128), F32), pltpu.VMEM((SLOTS, WIDTH), F32)],
        compiler_params=params,
        cost_estimate=cost(6 * ROWS * WIDTH * LOCAL, 4 << 20),
        name="project",
    )(
        where, prior_slot_lookup, tally_of_tokens, x, previous_standardized_entries, from_before, from_after,
        entry_standardize_scale.reshape(TILES, 128), blend_coefficients,
        acceptance_projection_matrix, lookup_projection_matrix, payload_projection_matrix,
    )

    part, new_states = pl.pallas_call(
        step_kernel,
        out_shape=[
            jax.ShapeDtypeStruct((ROWS * TILES, 128), BF16),
            jax.ShapeDtypeStruct((SLOTS * STATE_ROWS, 128), F32),
        ],
        in_specs=smem(3) + vmem(13),
        out_specs=vmem(2),
        scratch_shapes=[
            pltpu.VMEM((SLOTS * STATE_ROWS, 128), F32),
            pltpu.VMEM((SLOTS * STEPS * 8, 128), F32),
            pltpu.VMEM((SLOTS * STEPS * 8, 128), F32),
            pltpu.VMEM((SLOTS * STEPS * 8, 128), F32),
            pltpu.VMEM((SLOTS * 16, 128), F32),
            pltpu.VMEM((SLOTS * STEPS * 8, 128), F32),
            pltpu.VMEM((ROWS * TILES, 128), F32),
        ],
        compiler_params=params,
        cost_estimate=cost(2 * ROWS * WIDTH * LOCAL, 4 << 20),
        name="step",
    )(
        where, prior_slot_lookup, tally_of_tokens, mixed3, left, forget_map_right_matrix,
        feature_forget_logloglevel.reshape(2, 128), present_token_boost.reshape(2, 128),
        team_standardize_scale.reshape(2, 128), r, k, v, mem, from_before, from_after, final_projection_matrix,
    )

    pairs = [[2 * i, 2 * i + 1] for i in range(teams // 2)]
    chips = [[2 * i + c for i in range(teams // 2)] for c in range(2)]
    half = ROWS * TILES // 2
    both = lax.all_gather(part, "tensor", axis_index_groups=pairs, tiled=False)
    core = lax.axis_index("tensor") % 2
    mine = lax.dynamic_slice_in_dim(both, core * half, half, 1).astype(F32).sum(0).astype(BF16)
    spread = lax.all_to_all(
        jnp.broadcast_to(mine[None], (teams // 2,) + mine.shape), "tensor", 0, 0, axis_index_groups=chips
    )
    total = spread.astype(F32).sum(0).astype(BF16)
    proj = lax.all_gather(total, "tensor", axis_index_groups=pairs, tiled=True)

    mixed = pl.pallas_call(
        finish_kernel,
        out_shape=jax.ShapeDtypeStruct((ROWS * TILES, 128), BF16),
        in_specs=smem(1) + vmem(2),
        out_specs=vmem(1)[0],
        compiler_params=params,
        cost_estimate=cost(0, 1 << 19),
        name="finish",
    )(tally_of_tokens, x, proj)
    return (
        tiles_back(mixed, SLOTS, STEPS, WIDTH),
        tiles_back(new_states, SLOTS, HEADS, HEAD * HEAD),
        new_shifts,
    )


def solution(mesh):
    in_specs = (
        P("seq", None, None),
        P("seq"),
        P("seq"),
        P("seq", "tensor", None),
        P("seq", None),
        P(),
        P(),
        P(None, "tensor"),
        P(None, "tensor"),
        P(None, "tensor"),
        P("tensor", None),
        P(None, "tensor"),
        P("tensor"),
        P("tensor"),
        P("tensor"),
        P("tensor", None),
    )
    out_specs = (P("seq", None, None), P("seq", "tensor", None), P("seq", None))
    return jax.shard_map(shards, mesh=mesh, in_specs=in_specs, out_specs=out_specs, check_vma=False)
```

time: 223 us -> 79.9 us (0.36)
  waiting for transfers between devices: 55 us -> 7.84 us
  local copies, waits for them, and re-layouts: 57.4 us -> 21.1 us
  other arithmetic: 31.1 us -> 0.19 us
  matrix products: 22.6 us -> 0 us
  between operations: 14.7 us -> 0.74 us
  Pallas kernels: 0 us -> 8.76 us
  blocking collectives: 24.3 us -> 18.9 us
  starting transfers between devices: 16.1 us -> 21.3 us
    psum x1 -> x0, waiting for transfers between devices: 39.3 us -> none  [shards(): lax.psum(partial_value.astype(jnp.bfloat16), 'tensor').astype(jnp.float32)]
    psum x1 -> x0, blocking collectives: 24.3 us -> none  [shards(): lax.psum(jnp.dot(incoming_piece, forget_map_left_matrix, preferred_elemen...]
    dot_general x10 -> x0, matrix products: 22.6 us -> none  [the longest x4 15.7 us: shards(): jnp.einsum('rhi,rhij->rhj', current_receptance, state, precision=lax.Prec...]
    mul x16 -> x0, local copies, waits for them, and re-layouts: 22.1 us -> none  [the longest x9 11.2 us: shards(): decay_factor[:, step][..., None] * state]
    all_to_all x0 -> x1, blocking collectives: none -> 12.6 us  [shards(): lax.all_to_all(jnp.broadcast_to(mine[None], (teams // 2,) + mine.shape),...]
    all_to_all x0 -> x1, starting transfers between devices: none -> 10.9 us  [shards(): lax.all_to_all(jnp.broadcast_to(left_t[None], (teams,) + left_t.shape), '...]
    unnamed x110 -> x62, local copies, waits for them, and re-layouts: 8.88 us -> 19.5 us
    mul x9 -> x0, other arithmetic: 9.97 us -> none  [the longest x4 6.68 us: shards(): current_key[..., None] * current_value[..., None, :]]
  transfers between devices with their start and end apart: 3 -> 3, of which waited for: 3 -> 2; matrix products, arithmetic and copies ran while one was open for 18% -> 0% of each run, Pallas kernels for 0% -> 4%
where the time goes in v1:
time: 79.9 us; the launch traced here: 78.9 us
  starting transfers between devices  21.3 us (27%)
  local copies, waits for them, and re-layouts  21.1 us (26%)
  blocking collectives  18.9 us (24%)
  Pallas kernels  8.76 us (11%)
  waiting for transfers between devices  7.84 us (10%)
    unnamed x62, local copies, waits for them, and re-layouts  19.5 us
    all_to_all x1, blocking collectives, shards(): lax.all_to_all(jnp.broadcast_to(mine[None], (teams // 2,) + mine.shape),...  12.6 us
    all_to_all x1, starting transfers between devices, shards(): lax.all_to_all(jnp.broadcast_to(left_t[None], (teams,) + left_t.shape), '...  10.9 us
    ppermute x1, starting transfers between devices, shards(): lax.ppermute(packed, 'seq', [((i + 1) % rings, i) for i in range(rings)])  8.49 us
    ppermute x1, waiting for transfers between devices, shards(): lax.ppermute(packed, 'seq', [(i, (i + 1) % rings) for i in range(rings)])  6.45 us
    pallas_call x1, Pallas kernels, shards(): pl.pallas_call(step_kernel, out_shape=[jax.ShapeDtypeStruct((ROWS * TILES...  4.21 us
    all_gather x1, blocking collectives, shards(): proj = lax.all_gather(total, 'tensor', axis_index_groups=pairs, tiled=True)  3.45 us
    all_gather x1, blocking collectives, shards(): both = lax.all_gather(part, 'tensor', axis_index_groups=pairs, tiled=False)  2.9 us
  transfers between devices with their start and end apart: 3, of which 2 were waited for; matrix products, arithmetic and copies ran while one was open for 0% of the time, Pallas kernels for 4%

profile of v1, /device:TPU:1, one launch (start us, length us, event | category | flops | bytes accessed | tf_op | source)
XLA Modules:
  0.0 78.9 jit_solution(10620411635417870254)
XLA Ops:
  0.6 1.5 %broadcast_in_dim.4 = bf16[8,64,256]{2,1,0:T(8,128)(2,1)} broadcast(bf16[64,256]{1,0:T(8,128)(2,1)} %bitcast.38), dimensions={1,2} | broadcast | bytes 294912 | tf_op jit(solution)/shard_map/broadcast_in_dim | solution.py:312
  2.1 0.0 copy-start.13
  2.1 10.9 %all-to-all-start = ((bf16[8,64,256]{2,1,0:T(8,128)(2,1)}), bf16[8,64,256]{2,1,0:T(8,128)(2,1)}, u32[]{:S(2)}, u32[]{:S(2)}) async-start(bf16[8,64,256]{2,1,0:T(8,128)(2,1)} %broadcast_in_dim.4), calls=%async_computation | async-start | bytes 524288 | tf_op jit(solution)/shard_map/all_to_all | solution.py:312
  13.0 0.1 pad_add_fusion.where_ref
  13.1 0.0 copy-start.25
  13.1 0.0 copy-done.13
  13.1 0.7 copy-done.25
  13.8 0.0 copy-start
  13.8 1.2 %copy-done = f32[16,4,4096]{2,1,0:T(4,128)S(1)} copy-done((f32[16,4,4096]{2,1,0:T(4,128)S(1)}, f32[16,4,4096]{2,1,0:T(4,128)}, u32[]{:S(2)}) %copy-start) | copy-done | bytes 1048600
  15.0 0.0 copy-start.2
  15.0 0.0 copy-start.5
  15.0 0.6 pack.1
  15.6 8.5 %collective-permute-start.1 = (f32[296,128]{1,0:T(8,128)S(1)}, f32[296,128]{1,0:T(8,128)S(1)}, u32[]{:S(2)}, u32[]{:S(2)}) collective-permute-start(f32[296,128]{1,0:T(8,128)S(1)} %pack.1), channel_id=1, source_target_pairs={{8,0},{16,8},{24,16},{32,24},{40,32},{48,40},{56,48},{64,56},{72,6... | collective-permute-start | bytes 454664 | tf_op jit(solution)/shard_map/ppermute | solution.py:324
  24.1 1.9 %collective-permute-start = (f32[296,128]{1,0:T(8,128)S(1)}, f32[296,128]{1,0:T(8,128)S(1)}, u32[]{:S(2)}, u32[]{:S(2)}) collective-permute-start(f32[296,128]{1,0:T(8,128)S(1)} %pack.1), channel_id=1, source_target_pairs={{0,8},{8,16},{16,24},{24,32},{32,40},{40,48},{48,56},{56,64},{64,7... | collective-permute-start | bytes 454664 | tf_op jit(solution)/shard_map/ppermute | solution.py:323
  26.1 0.0 copy-start.24
  26.1 1.4 %collective-permute-done.1.from_after = f32[296,128]{1,0:T(8,128)S(1)} collective-permute-done((f32[296,128]{1,0:T(8,128)S(1)}, f32[296,128]{1,0:T(8,128)S(1)}, u32[]{:S(2)}, u32[]{:S(2)}) %collective-permute-start.1) | collective-permute-done | bytes 151584 | tf_op jit(solution)/shard_map/ppermute | solution.py:324
  27.5 0.0 copy-start.7
  27.5 0.7 copy-done.7
  28.1 6.5 %collective-permute-done.from_before = f32[296,128]{1,0:T(8,128)S(1)} collective-permute-done((f32[296,128]{1,0:T(8,128)S(1)}, f32[296,128]{1,0:T(8,128)S(1)}, u32[]{:S(2)}, u32[]{:S(2)}) %collective-permute-start) | collective-permute-done | bytes 151584 | tf_op jit(solution)/shard_map/ppermute | solution.py:323
  34.6 0.0 copy-start.10
  34.6 0.7 copy-done.10
  35.3 0.0 copy-start.26
  35.3 0.0 copy-done.2
  35.3 0.0 copy-done.5
  35.3 0.0 copy-done.24
  35.3 0.6 copy-done.26
  35.9 0.0 copy-start.3
  35.9 1.2 %copy-done.3 = bf16[2048,256]{1,0:T(8,128)(2,1)S(1)} copy-done((bf16[2048,256]{1,0:T(8,128)(2,1)S(1)}, bf16[2048,256]{1,0:T(8,128)(2,1)}, u32[]{:S(2)}) %copy-start.3) | copy-done | bytes 1048600
  37.1 0.0 copy-start.4
  37.1 1.2 %copy-done.4 = bf16[2048,256]{1,0:T(8,128)(2,1)S(1)} copy-done((bf16[2048,256]{1,0:T(8,128)(2,1)S(1)}, bf16[2048,256]{1,0:T(8,128)(2,1)}, u32[]{:S(2)}) %copy-start.4) | copy-done | bytes 1048600
  38.4 0.0 copy-start.8
  38.4 0.9 %copy-done.8 = f32[296,128]{1,0:T(8,128)S(1)} copy-done((f32[296,128]{1,0:T(8,128)S(1)}, f32[296,128]{1,0:T(8,128)}, u32[]{:S(2)}) %copy-start.8) | copy-done | bytes 151576
  39.3 0.0 copy-start.11
  39.3 0.9 %copy-done.11 = f32[296,128]{1,0:T(8,128)S(1)} copy-done((f32[296,128]{1,0:T(8,128)S(1)}, f32[296,128]{1,0:T(8,128)}, u32[]{:S(2)}) %copy-start.11) | copy-done | bytes 151576
  40.2 0.8 copy-done.22
  41.0 0.0 copy-start.1
  41.0 0.0 copy-start.6
  41.0 2.6 %project.1 = (f32[64,256]{1,0:T(8,128)S(1)}, f32[64,256]{1,0:T(8,128)S(1)}, f32[64,256]{1,0:T(8,128)S(1)}, bf16[64,2048]{1,0:T(8,128)(2,1)S(1)}, f32[16,2048]{1,0:T(8,128)}) custom-call(s32[2]{0:T(128)S(1)} %pad_add_fusion.where_ref, s32[16]{0:T(128)S(1)} %copy-done.25, s32[16]{0:T(128)S(1)} %copy-done.26, bf16[1024,128]{1,0:T(8,128)(2,1)S(1)} %bitcast.30, ...), custom_call_target="tpu_custom_call" | custom-call | flops 201326592 | bytes 4194304 | tf_op jit(solution)/shard_map/project/pallas_call | solution.py:326
  43.5 0.0 copy-start.14
  43.5 0.7 copy-done.14
  44.2 0.6 copy-done.16
  44.8 0.6 copy-done.18
  45.5 0.6 copy-done.20
  46.1 0.0 all-to-all-done.left_ref
  46.1 0.0 copy-done.1
  46.1 0.0 copy-done.6
  46.1 0.6 copy-done.27
  46.7 0.0 copy-done.28
  46.8 0.9 %copy-done.9 = f32[296,128]{1,0:T(8,128)S(1)} copy-done((f32[296,128]{1,0:T(8,128)S(1)}, f32[296,128]{1,0:T(8,128)}, u32[]{:S(2)}) %copy-start.9) | copy-done | bytes 151576
  47.7 0.9 %copy-done.12 = f32[296,128]{1,0:T(8,128)S(1)} copy-done((f32[296,128]{1,0:T(8,128)S(1)}, f32[296,128]{1,0:T(8,128)}, u32[]{:S(2)}) %copy-start.12) | copy-done | bytes 151576
  48.6 0.9 %copy-done.15 = bf16[64,2048]{1,0:T(8,128)(2,1)S(1)} copy-done((bf16[64,2048]{1,0:T(8,128)(2,1)S(1)}, bf16[64,2048]{1,0:T(8,128)(2,1)}, u32[]{:S(2)}) %copy-start.15) | copy-done | bytes 262168
  49.6 0.8 %copy-done.17 = f32[64,256]{1,0:T(8,128)S(1)} copy-done((f32[64,256]{1,0:T(8,128)S(1)}, f32[64,256]{1,0:T(8,128)}, u32[]{:S(2)}) %copy-start.17) | copy-done | bytes 65560
  50.4 0.8 %copy-done.19 = f32[64,256]{1,0:T(8,128)S(1)} copy-done((f32[64,256]{1,0:T(8,128)S(1)}, f32[64,256]{1,0:T(8,128)}, u32[]{:S(2)}) %copy-start.19) | copy-done | bytes 65560
  51.2 0.8 %copy-done.21 = f32[64,256]{1,0:T(8,128)S(1)} copy-done((f32[64,256]{1,0:T(8,128)S(1)}, f32[64,256]{1,0:T(8,128)}, u32[]{:S(2)}) %copy-start.21) | copy-done | bytes 65560
  52.1 0.8 copy-done.23
  52.8 0.7 copy-done.29
  53.5 0.7 copy-done.30
  54.2 4.2 %step.1 = (bf16[1024,128]{1,0:T(8,128)(2,1)S(1)}, f32[2048,128]{1,0:T(8,128)}) custom-call(s32[2]{0:T(128)S(1)} %pad_add_fusion.where_ref, s32[16]{0:T(128)S(1)} %copy-done.25, s32[16]{0:T(128)S(1)} %copy-done.27, bf16[64,2048]{1,0:T(8,128)(2,1)S(1)} %copy-done.15, bf16[8,64,256]{2,1,0:T(8,128)(2,1)} %all-to-all-done.left_ref, ...), custom_call_target="tpu_custom_call" | custom-call | flops 67108864 | bytes 4194304 | tf_op jit(solution)/shard_map/step/pallas_call | solution.py:342
  58.4 2.9 %all-gather = bf16[2048,128]{1,0:T(8,128)(2,1)S(1)} all-gather(bf16[1024,128]{1,0:T(8,128)(2,1)S(1)} %get-tuple-element.14), channel_id=2, replica_groups={{0,1},{2,3},{4,5},{6,7},{8,9},{10,11},{12,13},{14,15},{16,17},{18,19},{..., dimensions={0}, use_global_device_ids=true | all-gather | bytes 786432 | tf_op jit(solution)/shard_map/all_gather | solution.py:371
  61.3 0.1 broadcast_in_dim.5
  61.4 12.6 %all_to_all.10 = bf16[4,512,128]{2,1,0:T(8,128)(2,1)S(1)} all-to-all(bf16[4,512,128]{2,1,0:T(8,128)(2,1)S(1)} %broadcast_in_dim.5), channel_id=1, replica_groups={{0,2,4,6},{1,3,5,7},{8,10,12,14},{9,11,13,15},{16,18,20,22},{17,19,21,2..., dimensions={0} | all-to-all | bytes 1048576 | tf_op jit(solution)/shard_map/all_to_all | solution.py:374
  74.0 0.1 reduce_sum.25
  74.1 3.4 %all_gather.11.proj_ref = bf16[1024,128]{1,0:T(8,128)(2,1)S(1)} all-gather(bf16[512,128]{1,0:T(8,128)(2,1)S(1)} %reduce_sum.25), channel_id=1, replica_groups={{0,1},{2,3},{4,5},{6,7},{8,9},{10,11},{12,13},{14,15},{16,17},{18,19},{..., dimensions={0}, use_global_device_ids=true | all-gather | bytes 393216 | tf_op jit(solution)/shard_map/all_gather | solution.py:378
  77.5 1.3 %finish.1 = bf16[1024,128]{1,0:T(8,128)(2,1)} custom-call(s32[16]{0:T(128)S(1)} %copy-done.27, bf16[1024,128]{1,0:T(8,128)(2,1)S(1)} %bitcast.31, bf16[1024,128]{1,0:T(8,128)(2,1)S(1)} %all_gather.11.proj_ref), custom_call_target="tpu_custom_call" | custom-call | bytes 524288 | tf_op jit(solution)/shard_map/finish/pallas_call | solution.py:380
  (16 shorter events, 0.1 us)
Async XLA Ops:
  2.1 11.0 %copy-start.13 = (f32[16,2048]{1,0:T(8,128)S(1)}, f32[16,2048]{1,0:T(8,128)}, u32[]{:S(2)}) copy-start(f32[16,2048]{1,0:T(8,128)} %prev_ref.3) | copy-start | bytes 393220
  2.1 44.0 %all-to-all-start = ((bf16[8,64,256]{2,1,0:T(8,128)(2,1)}), bf16[8,64,256]{2,1,0:T(8,128)(2,1)}, u32[]{:S(2)}, u32[]{:S(2)}) async-start(bf16[8,64,256]{2,1,0:T(8,128)(2,1)} %broadcast_in_dim.4), calls=%async_computation | async-start | bytes 524288 | tf_op jit(solution)/shard_map/all_to_all | solution.py:312
  13.1 0.7 copy-start.25
  13.8 1.2 %copy-start = (f32[16,4,4096]{2,1,0:T(4,128)S(1)}, f32[16,4,4096]{2,1,0:T(4,128)}, u32[]{:S(2)}) copy-start(f32[16,4,4096]{2,1,0:T(4,128)} %param.19) | copy-start | bytes 3145732
  15.0 20.3 %copy-start.2 = (bf16[2048,256]{1,0:T(8,128)(2,1)S(1)}, bf16[2048,256]{1,0:T(8,128)(2,1)}, u32[]{:S(2)}) copy-start(bf16[2048,256]{1,0:T(8,128)(2,1)} %wr_ref.1) | copy-start | bytes 3145732
  15.0 20.3 %copy-start.5 = (bf16[16,4,2048]{2,1,0:T(4,128)(2,1)S(1)}, bf16[16,4,2048]{2,1,0:T(4,128)(2,1)}, u32[]{:S(2)}) copy-start(bf16[16,4,2048]{2,1,0:T(4,128)(2,1)} %param.16) | copy-start | bytes 786436
  15.6 11.8 %collective-permute-start.1 = (f32[296,128]{1,0:T(8,128)S(1)}, f32[296,128]{1,0:T(8,128)S(1)}, u32[]{:S(2)}, u32[]{:S(2)}) collective-permute-start(f32[296,128]{1,0:T(8,128)S(1)} %pack.1), channel_id=1, source_target_pairs={{8,0},{16,8},{24,16},{32,24},{40,32},{48,40},{56,48},{64,56},{72,6... | collective-permute-start | bytes 454664 | tf_op jit(solution)/shard_map/ppermute | solution.py:324
  24.1 10.5 %collective-permute-start = (f32[296,128]{1,0:T(8,128)S(1)}, f32[296,128]{1,0:T(8,128)S(1)}, u32[]{:S(2)}, u32[]{:S(2)}) collective-permute-start(f32[296,128]{1,0:T(8,128)S(1)} %pack.1), channel_id=1, source_target_pairs={{0,8},{8,16},{16,24},{24,32},{32,40},{40,48},{48,56},{56,64},{64,7... | collective-permute-start | bytes 454664 | tf_op jit(solution)/shard_map/ppermute | solution.py:323
  26.1 9.2 %copy-start.24 = (f32[2048]{0:T(1024)S(1)}, f32[2048]{0:T(1024)}, u32[]{:S(2)}) copy-start(f32[2048]{0:T(1024)} %param.21) | copy-start | bytes 24580
  27.5 0.7 copy-start.7
  34.6 0.7 copy-start.10
  35.3 0.7 copy-start.26
  35.9 1.2 %copy-start.3 = (bf16[2048,256]{1,0:T(8,128)(2,1)S(1)}, bf16[2048,256]{1,0:T(8,128)(2,1)}, u32[]{:S(2)}) copy-start(bf16[2048,256]{1,0:T(8,128)(2,1)} %wk_ref.1) | copy-start | bytes 3145732
  37.1 1.2 %copy-start.4 = (bf16[2048,256]{1,0:T(8,128)(2,1)S(1)}, bf16[2048,256]{1,0:T(8,128)(2,1)}, u32[]{:S(2)}) copy-start(bf16[2048,256]{1,0:T(8,128)(2,1)} %wv_ref.1) | copy-start | bytes 3145732
  38.4 0.9 %copy-start.8 = (f32[296,128]{1,0:T(8,128)S(1)}, f32[296,128]{1,0:T(8,128)}, u32[]{:S(2)}) copy-start(f32[296,128]{1,0:T(8,128)} %copy-done.7) | copy-start | bytes 454660
  39.3 0.9 %copy-start.11 = (f32[296,128]{1,0:T(8,128)S(1)}, f32[296,128]{1,0:T(8,128)}, u32[]{:S(2)}) copy-start(f32[296,128]{1,0:T(8,128)} %copy-done.10) | copy-start | bytes 454660
  40.2 0.8 copy-start.22
  41.0 5.1 %copy-start.1 = (f32[16,4,4096]{2,1,0:T(4,128)S(1)}, f32[16,4,4096]{2,1,0:T(4,128)}, u32[]{:S(2)}) copy-start(f32[16,4,4096]{2,1,0:T(4,128)} %param.19) | copy-start | bytes 3145732
  41.0 5.1 %copy-start.6 = (bf16[256,2048]{1,0:T(8,128)(2,1)S(1)}, bf16[256,2048]{1,0:T(8,128)(2,1)}, u32[]{:S(2)}) copy-start(bf16[256,2048]{1,0:T(8,128)(2,1)} %final_ref.1) | copy-start | bytes 3145732
  43.5 0.7 copy-start.14
  44.2 0.6 copy-start.16
  44.8 0.6 copy-start.18
  45.5 0.6 copy-start.20
  46.1 0.7 copy-start.27
  46.1 0.7 copy-start.28
  46.8 0.9 %copy-start.9 = (f32[296,128]{1,0:T(8,128)S(1)}, f32[296,128]{1,0:T(8,128)}, u32[]{:S(2)}) copy-start(f32[296,128]{1,0:T(8,128)} %copy-done.7) | copy-start | bytes 454660
  47.7 0.9 %copy-start.12 = (f32[296,128]{1,0:T(8,128)S(1)}, f32[296,128]{1,0:T(8,128)}, u32[]{:S(2)}) copy-start(f32[296,128]{1,0:T(8,128)} %copy-done.10) | copy-start | bytes 454660
  48.6 0.9 %copy-start.15 = (bf16[64,2048]{1,0:T(8,128)(2,1)S(1)}, bf16[64,2048]{1,0:T(8,128)(2,1)}, u32[]{:S(2)}) copy-start(bf16[64,2048]{1,0:T(8,128)(2,1)} %copy-done.14) | copy-start | bytes 786436
  49.6 0.8 %copy-start.17 = (f32[64,256]{1,0:T(8,128)S(1)}, f32[64,256]{1,0:T(8,128)}, u32[]{:S(2)}) copy-start(f32[64,256]{1,0:T(8,128)} %copy-done.16) | copy-start | bytes 196612
  50.4 0.8 %copy-start.19 = (f32[64,256]{1,0:T(8,128)S(1)}, f32[64,256]{1,0:T(8,128)}, u32[]{:S(2)}) copy-start(f32[64,256]{1,0:T(8,128)} %copy-done.18) | copy-start | bytes 196612
  51.2 0.8 %copy-start.21 = (f32[64,256]{1,0:T(8,128)S(1)}, f32[64,256]{1,0:T(8,128)}, u32[]{:S(2)}) copy-start(f32[64,256]{1,0:T(8,128)} %copy-done.20) | copy-start | bytes 196612
  52.1 0.8 copy-start.23
  52.8 0.7 copy-start.29
  53.5 0.7 copy-start.30

commit v2 on v1

v2 whole, which is shorter than its diff:
```python
import functools

import jax
import jax.numpy as jnp
from jax import lax
from jax.experimental import pallas as pl
from jax.experimental.pallas import tpu as pltpu
from jax.sharding import PartitionSpec as P

EPS = 1e-05
F32 = jnp.float32
BF16 = jnp.bfloat16
HEAD = 64
SLOTS = 16
STEPS = 4
WIDTH = 2048
HEADS = 4
LOCAL = HEADS * HEAD
TILES = WIDTH // 128
ROWS = SLOTS * STEPS
STATE_ROWS = HEADS * HEAD * HEAD // 128
PIECE = STATE_ROWS + TILES
PACK_ROWS = 2 * PIECE + 8
TALLY, OWNER = SLOTS, 2 * SLOTS


def spec(space, count):
    return [pl.BlockSpec(memory_space=space)] * count


def dot(a, b):
    return jnp.dot(a, b, preferred_element_type=F32)


def dot_rows(a, b):
    return lax.dot_general(a, b, (((0,), (0,)), ((), ())), preferred_element_type=F32)


def split(a):
    hi = a.astype(BF16)
    return hi, (a - hi.astype(F32)).astype(BF16)


def dot_split(a, b):
    hi, lo = split(a)
    return dot(hi, b) + dot(lo, b)


def iota(shape, dim):
    return lax.broadcasted_iota(jnp.int32, shape, dim)


def column_of(meta_ref, shape):
    rows = iota(shape, 0)
    out = jnp.zeros(shape, jnp.int32)
    for q in range(SLOTS):
        out = jnp.where(rows == q, meta_ref[TALLY + q], out)
    return out


def row_of(ref):
    return jnp.concatenate([ref[i : i + 1, :] for i in range(ref.shape[0])], axis=1)


def start(copies):
    for copy in copies:
        copy.start()


def pack_kernel(meta_ref, mem_ref, prev_ref, left_ref, out_ref, left_out, prev, row_tile, sems):
    first = meta_ref[OWNER] * SLOTS
    load = pltpu.make_async_copy(prev_ref, prev, sems.at[0])
    load.start()
    spread = [
        pltpu.make_async_copy(left_ref, left_out.at[n], sems.at[8 + n]) for n in range(left_out.shape[0])
    ]
    start(spread)
    kept = jnp.int32(0)
    for q in range(SLOTS):
        at = meta_ref[q] - first
        own = (at >= 0) & (at < SLOTS)
        kept = kept | jnp.where(own, jnp.int32(1) << jnp.where(own, at, 0), 0)
    low, high = jnp.int32(0), jnp.int32(0)
    for s in range(SLOTS):
        high = jnp.where((kept >> s) & 1 == 0, s, high)
        low = jnp.where((kept >> (SLOTS - 1 - s)) & 1 == 0, SLOTS - 1 - s, low)
    moves = [
        pltpu.make_async_copy(
            mem_ref.at[pl.ds(pl.multiple_of(slot * STATE_ROWS, STATE_ROWS), STATE_ROWS), :],
            out_ref.at[pl.ds(n * PIECE, STATE_ROWS), :],
            sems.at[1 + n],
        )
        for n, slot in enumerate((low, high))
    ]
    start(moves)
    row_tile[2 * TILES :, :] = jnp.where(iota((8, 128), 0) == 0, first + low, first + high).astype(F32)
    load.wait()
    for n, slot in enumerate((low, high)):
        row = prev[pl.ds(slot, 1), :]
        for c in range(TILES):
            row_tile[n * TILES + c : n * TILES + c + 1, :] = row[:, c * 128 : (c + 1) * 128]
    rows = [
        pltpu.make_async_copy(
            row_tile.at[pl.ds(0, TILES), :], out_ref.at[pl.ds(STATE_ROWS, TILES), :], sems.at[3]
        ),
        pltpu.make_async_copy(
            row_tile.at[pl.ds(TILES, TILES + 8), :], out_ref.at[pl.ds(PIECE + STATE_ROWS, TILES + 8), :], sems.at[4]
        ),
    ]
    start(rows)
    for copy in moves + rows + spread:
        copy.wait()


def pick(recv_ref, wanted, begin, count):
    is_low = recv_ref[2 * PIECE : 2 * PIECE + 1, :] == wanted.astype(F32)
    return jnp.where(is_low, recv_ref[begin : begin + count, :], recv_ref[PIECE + begin : PIECE + begin + count, :])


def sources(meta_ref, q):
    wanted = meta_ref[q]
    owner = wanted // SLOTS
    own = owner == meta_ref[OWNER]
    before = owner == meta_ref[OWNER + 1]
    at = jnp.where(own, wanted - meta_ref[OWNER] * SLOTS, 0)
    return wanted, own, before, at


def main_kernel(*refs):
    meta_ref, mem_hbm = refs[:2]
    hbm = refs[2:17]
    part_ref, new_hbm, last_ref = refs[17:20]
    bufs = refs[20:35]
    x32, shift, state, reads, keys, vals, decays, heads, part, mixed_ref, fresh, sems, state_sems, new_sems = refs[35:]
    loads = [pltpu.make_async_copy(src, dst, sems.at[n]) for n, (src, dst) in enumerate(zip(hbm, bufs))]
    start(loads)
    state_loads = []
    for q in range(SLOTS):
        at = sources(meta_ref, q)[3]
        state_loads.append(
            pltpu.make_async_copy(
                mem_hbm.at[pl.ds(pl.multiple_of(at * STATE_ROWS, STATE_ROWS), STATE_ROWS), :],
                state.at[pl.ds(q * STATE_ROWS, STATE_ROWS), :],
                state_sems.at[q],
            )
        )
    start(state_loads)
    (
        x_ref, gain_ref, prev_ref, from_before, from_after, blend_ref, wr_ref, wk_ref, wv_ref,
        left_ref, right_ref, base_ref, boost_ref, team_ref, final_ref,
    ) = bufs
    arrive = lambda *which: [loads[n].wait() for n in which]

    arrive(0, 1)
    x32[...] = x_ref[...].astype(F32)
    gain = row_of(gain_ref)
    normed = []
    for t in range(STEPS):
        row = jnp.concatenate([x32[pl.ds(c * STEPS + t, SLOTS, stride=STEPS * TILES), :] for c in range(TILES)], axis=1)
        center = row - jnp.mean(row, axis=-1, keepdims=True)
        spread = jnp.mean(center * center, axis=-1, keepdims=True)
        normed.append(center * lax.rsqrt(spread + EPS) * gain)
    tally = column_of(meta_ref, (SLOTS, 128))[:, :1]
    last = normed[0]
    for t in range(1, STEPS):
        last = jnp.where(tally == t + 1, normed[t], last)
    last_ref[...] = last
    arrive(2, 3, 4, 5)
    for q in range(SLOTS):
        wanted, own, before, at = sources(meta_ref, q)

        @pl.when(own)
        def _():
            shift[q : q + 1, :] = prev_ref[pl.ds(at, 1), :]

        @pl.when(jnp.logical_not(own))
        def _():
            rows = jnp.where(
                before, pick(from_before, wanted, STATE_ROWS, TILES), pick(from_after, wanted, STATE_ROWS, TILES)
            )
            for c in range(TILES):
                shift[q : q + 1, c * 128 : (c + 1) * 128] = rows[c : c + 1, :]

    xn = jnp.concatenate(normed, axis=0)
    change = jnp.concatenate([shift[...]] + normed[:-1], axis=0) - xn

    def mix(which):
        return (xn + change * blend_ref[which : which + 1, :]).astype(BF16)

    mixed_ref[...] = mix(3)
    arrive(6)
    r_all = dot(mix(0), wr_ref[...])
    arrive(7)
    k_all = dot(mix(1), wk_ref[...])
    arrive(8)
    v_all = dot(mix(2), wv_ref[...])

    arrive(9, 10, 11, 12, 13)
    pre = jnp.zeros((ROWS, left_ref.shape[1]), F32)
    chunk = left_ref.shape[2]
    for n in range(left_ref.shape[0]):
        pre = pre + lax.dot_general(
            mixed_ref[:, n * chunk : (n + 1) * chunk], left_ref[n], (((1,), (1,)), ((), ())), preferred_element_type=F32
        )
    lora = jnp.tanh(pre).astype(BF16)
    decay = jnp.exp(-jnp.exp(row_of(base_ref) + dot(lora, right_ref[...])))
    cut = lambda a, t: a[t * SLOTS : (t + 1) * SLOTS, :]
    r = [cut(r_all, t) for t in range(STEPS)]
    k = [cut(k_all, t) for t in range(STEPS)]
    v = [cut(v_all, t) for t in range(STEPS)]
    d = [jnp.where(tally > t, cut(decay, t), 1.0) for t in range(STEPS)]
    kept = [jnp.where(tally > t, k[t], 0.0) for t in range(STEPS)]
    boost = row_of(boost_ref)

    run, reach = r[0] * 0.0 + 1.0, []
    for t in range(STEPS):
        reach.append(r[t] * run)
        run = run * d[t]
    tail, coefs = None, [None] * STEPS
    for t in reversed(range(STEPS)):
        coefs[t] = kept[t] if tail is None else kept[t] * tail
        tail = d[t] if tail is None else tail * d[t]
    pairs, terms = [], []
    for t in range(STEPS):
        pairs.append((t, t))
        terms.append(r[t] * boost * k[t])
        weight = r[t]
        for s in reversed(range(t)):
            pairs.append((t, s))
            terms.append(weight * kept[s])
            weight = weight * d[s]
    row256, col256 = iota((LOCAL, LOCAL), 0), iota((LOCAL, LOCAL), 1)
    same_head = (row256 // HEAD == col256 // HEAD).astype(BF16)
    sums = dot_split(jnp.concatenate(terms, axis=0), same_head)
    within = [None] * STEPS
    for n, (t, s) in enumerate(pairs):
        term = cut(sums, n) * v[s]
        within[t] = term if within[t] is None else within[t] + term

    source = (col256 % HEADS) * HEAD + ((col256 // HEADS) % (HEAD // 2)) * 2 + col256 // 128
    reorder = (row256 == source).astype(BF16)
    moved = dot_split(jnp.concatenate(reach + coefs + [run], axis=0), reorder)
    rowd, cold = iota((LOCAL, HEADS * 128), 0), iota((LOCAL, HEADS * 128), 1)
    double = (rowd == (cold // 128) * HEAD + cold % HEAD).astype(BF16)
    doubled = dot(v_all.astype(BF16), double)

    lane = iota((SLOTS, 128), 1)
    for h in range(HEADS):
        head_lane = lane % HEADS == h
        for p in range(2):
            half = lane // HEAD == p
            for t in range(STEPS):
                at = pl.ds(t * 8 + p * HEADS + h, SLOTS, stride=STEPS * 8)
                cols = slice(p * 128, (p + 1) * 128)
                reads[at, :] = jnp.where(head_lane, cut(moved, t)[:, cols], 0.0)
                keys[at, :] = jnp.where(head_lane, cut(moved, STEPS + t)[:, cols], 0.0)
                vals[at, :] = jnp.where(half, cut(doubled, t)[:, h * 128 : (h + 1) * 128], 0.0)
            whole = jnp.where(head_lane, cut(moved, 2 * STEPS)[:, cols], 0.0)
            high = whole.astype(BF16).astype(F32)
            decays[pl.ds(p * HEADS + h, SLOTS, stride=16), :] = high
            decays[pl.ds(8 + p * HEADS + h, SLOTS, stride=16), :] = whole - high
    ones = ((iota((16, 128), 0) // HEADS) % 2 == iota((16, 128), 1) // HEAD).astype(BF16)
    news = []
    for q in range(SLOTS):
        state_loads[q].wait()
        wanted, own, before, _ = sources(meta_ref, q)
        here = slice(q * STATE_ROWS, (q + 1) * STATE_ROWS)

        @pl.when(jnp.logical_not(own) & before)
        def _():
            state[here, :] = pick(from_before, wanted, 0, STATE_ROWS)

        @pl.when(jnp.logical_not(own) & jnp.logical_not(before))
        def _():
            state[here, :] = pick(from_after, wanted, 0, STATE_ROWS)

    for q in range(SLOTS):
        here = slice(q * STATE_ROWS, (q + 1) * STATE_ROWS)
        rows = slice(q * STEPS * 8, (q + 1) * STEPS * 8)
        now = state[here, :]
        heads[rows, :] = dot(reads[rows, :].astype(BF16), now.astype(BF16))
        fade = dot_rows(decays[q * 16 : (q + 1) * 16, :].astype(BF16), ones)
        grown = dot_rows(keys[rows, :].astype(BF16), vals[rows, :].astype(BF16))
        fresh[here, :] = fade * now + grown
        news.append(pltpu.make_async_copy(fresh.at[here, :], new_hbm.at[here, :], new_sems.at[q]))
        news[-1].start()

    outs = []
    left_half = lane < HEAD
    for t in range(STEPS):
        def read(p, h):
            return heads[pl.ds(t * 8 + p * HEADS + h, SLOTS, stride=STEPS * 8), :]

        cols = []
        for h in range(0, HEADS, 2):
            a, b, c, e = read(0, h), read(1, h), read(0, h + 1), read(1, h + 1)
            cols.append(jnp.where(left_half, a, e) + pltpu.roll(jnp.where(left_half, c, b), HEAD, 1))
        outs.append(jnp.concatenate(cols, axis=1) + within[t])
    y = jnp.concatenate(outs, axis=0)
    center = y - dot_split(y, same_head) * (1.0 / HEAD)
    spread = dot_split(center * center, same_head) * (1.0 / HEAD)
    g = (center * lax.rsqrt(spread + EPS) * row_of(team_ref)).astype(BF16)
    arrive(14)
    proj = dot(g, final_ref[...])
    for t in range(STEPS):
        for c in range(TILES):
            part[pl.ds(c * STEPS + t, SLOTS, stride=STEPS * TILES), :] = cut(proj, t)[:, c * 128 : (c + 1) * 128]
    part_ref[...] = part[...].astype(BF16)
    for copy in news:
        copy.wait()


def finish_kernel(meta_ref, x_hbm, parts_ref, out_ref, x_ref, sem):
    rows = out_ref.shape[0]
    begin = meta_ref[OWNER + 2] * rows
    load = pltpu.make_async_copy(x_hbm.at[pl.ds(pl.multiple_of(begin, rows), rows), :], x_ref, sem)
    load.start()
    step = iota((STEPS * TILES, 128), 0) % STEPS
    load.wait()
    for q in range(rows // (STEPS * TILES)):
        here = slice(q * STEPS * TILES, (q + 1) * STEPS * TILES)
        total = x_ref[here, :].astype(F32)
        for n in range(parts_ref.shape[0]):
            total = total + parts_ref[n, here, :].astype(F32)
        tally = meta_ref[TALLY + meta_ref[OWNER + 2] * (rows // (STEPS * TILES)) + q]
        out_ref[here, :] = jnp.where(step < tally, total, 0.0).astype(BF16)


def cost(flops, bytes_accessed):
    return pl.CostEstimate(flops=flops, bytes_accessed=bytes_accessed, transcendentals=0)


def tiles_view(a):
    lead, mid, width = a.shape
    return a.reshape(lead, mid, width // 128, 128).transpose(0, 2, 1, 3).reshape(lead * width // 128 * mid, 128)


def tiles_back(a, lead, mid, width):
    return a.reshape(lead, width // 128, mid, 128).transpose(0, 2, 1, 3).reshape(lead, mid, width)


def shards(
    layer_entry_vectors,
    tally_of_tokens,
    prior_slot_lookup,
    memory_matrices,
    previous_standardized_entries,
    entry_standardize_scale,
    blend_coefficients,
    acceptance_projection_matrix,
    lookup_projection_matrix,
    payload_projection_matrix,
    forget_map_left_matrix,
    forget_map_right_matrix,
    feature_forget_logloglevel,
    present_token_boost,
    team_standardize_scale,
    final_projection_matrix,
):
    rings = lax.axis_size("seq")
    teams = lax.axis_size("tensor")
    device = lax.axis_index("seq")
    core = lax.axis_index("tensor") % 2
    meta = jnp.concatenate(
        [prior_slot_lookup, tally_of_tokens, jnp.stack([device, (device + rings - 1) % rings, core]).astype(jnp.int32)]
    )
    x = tiles_view(layer_entry_vectors)
    mem = tiles_view(memory_matrices)
    prev = previous_standardized_entries
    left_t = forget_map_left_matrix.T
    shape, scratch, dma = jax.ShapeDtypeStruct, pltpu.VMEM, pltpu.SemaphoreType.DMA

    packed, left = pl.pallas_call(
        pack_kernel,
        out_shape=[shape((PACK_ROWS, 128), F32), shape((teams,) + left_t.shape, BF16)],
        in_specs=spec(pltpu.SMEM, 1) + spec(pl.ANY, 3),
        out_specs=spec(pl.ANY, 2),
        scratch_shapes=[scratch(prev.shape, F32), scratch((2 * TILES + 8, 128), F32), dma((8 + teams,))],
        cost_estimate=cost(0, 1 << 20),
        compiler_params=pltpu.CompilerParams(vmem_limit_bytes=60 << 20),
        name="pack",
    )(meta, mem, prev, left_t)
    from_before = lax.ppermute(packed, "seq", [(i, (i + 1) % rings) for i in range(rings)])
    from_after = lax.ppermute(packed, "seq", [((i + 1) % rings, i) for i in range(rings)])
    left = lax.all_to_all(left, "tensor", 0, 0)

    operands = [
        x, entry_standardize_scale.reshape(TILES, 128), prev, from_before, from_after, blend_coefficients,
        acceptance_projection_matrix, lookup_projection_matrix, payload_projection_matrix,
        left, forget_map_right_matrix, feature_forget_logloglevel.reshape(2, 128),
        present_token_boost.reshape(2, 128), team_standardize_scale.reshape(2, 128), final_projection_matrix,
    ]
    part, new_states, new_shifts = pl.pallas_call(
        main_kernel,
        out_shape=[
            shape((ROWS * TILES, 128), BF16),
            shape((SLOTS * STATE_ROWS, 128), F32),
            shape((SLOTS, WIDTH), F32),
        ],
        in_specs=spec(pltpu.SMEM, 1) + spec(pl.ANY, 1 + len(operands)),
        out_specs=spec(pltpu.VMEM, 1) + spec(pl.ANY, 1) + spec(pltpu.VMEM, 1),
        scratch_shapes=[scratch(a.shape, a.dtype) for a in operands]
        + [
            scratch((ROWS * TILES, 128), F32),
            scratch((SLOTS, WIDTH), F32),
            scratch((SLOTS * STATE_ROWS, 128), F32),
            scratch((SLOTS * STEPS * 8, 128), F32),
            scratch((SLOTS * STEPS * 8, 128), F32),
            scratch((SLOTS * STEPS * 8, 128), F32),
            scratch((SLOTS * 16, 128), F32),
            scratch((SLOTS * STEPS * 8, 128), F32),
            scratch((ROWS * TILES, 128), F32),
            scratch((ROWS, WIDTH), BF16),
            scratch((SLOTS * STATE_ROWS, 128), F32),
            dma((len(operands),)),
            dma((SLOTS,)),
            dma((SLOTS,)),
        ],
        cost_estimate=cost(8 * ROWS * WIDTH * LOCAL, 8 << 20),
        compiler_params=pltpu.CompilerParams(vmem_limit_bytes=52 << 20),
        name="main",
    )(meta, mem, *operands)

    pairs = [[2 * i, 2 * i + 1] for i in range(teams // 2)]
    chips = [[2 * i + c for i in range(teams // 2)] for c in range(2)]
    half = ROWS * TILES // 2
    both = lax.all_gather(part, "tensor", axis_index_groups=pairs, tiled=False)
    mine = lax.dynamic_slice_in_dim(both, core * half, half, 1).astype(F32).sum(0).astype(BF16)
    spread = lax.all_to_all(
        jnp.broadcast_to(mine[None], (teams // 2,) + mine.shape), "tensor", 0, 0, axis_index_groups=chips
    )
    mixed = pl.pallas_call(
        finish_kernel,
        out_shape=shape((half, 128), BF16),
        in_specs=spec(pltpu.SMEM, 1) + spec(pl.ANY, 1) + spec(pltpu.VMEM, 1),
        out_specs=spec(pltpu.VMEM, 1)[0],
        scratch_shapes=[scratch((half, 128), BF16), dma],
        cost_estimate=cost(0, 1 << 19),
        compiler_params=pltpu.CompilerParams(vmem_limit_bytes=8 << 20),
        name="finish",
    )(meta, x, spread)
    mixed = tiles_back(mixed, SLOTS // 2, STEPS, WIDTH)
    mixed = lax.all_gather(mixed, "tensor", axis_index_groups=pairs, tiled=True)
    return (
        mixed,
        tiles_back(new_states, SLOTS, HEADS, HEAD * HEAD),
        new_shifts,
    )


def solution(mesh):
    in_specs = (
        P("seq", None, None),
        P("seq"),
        P("seq"),
        P("seq", "tensor", None),
        P("seq", None),
        P(),
        P(),
        P(None, "tensor"),
        P(None, "tensor"),
        P(None, "tensor"),
        P("tensor", None),
        P(None, "tensor"),
        P("tensor"),
        P("tensor"),
        P("tensor"),
        P("tensor", None),
    )
    out_specs = (P("seq", None, None), P("seq", "tensor", None), P("seq", None))
    return jax.shard_map(shards, mesh=mesh, in_specs=in_specs, out_specs=out_specs, check_vma=False)
```

time: 79.9 us -> 75.3 us (0.942)
  local copies, waits for them, and re-layouts: 21.1 us -> 2.75 us
  Pallas kernels: 8.76 us -> 22.3 us
  waiting for transfers between devices: 7.84 us -> 8.73 us
    unnamed x62 -> x23, local copies, waits for them, and re-layouts: 19.5 us -> 2.02 us
    pallas_call x4 -> x3, Pallas kernels: 8.76 us -> 22.3 us  [the longest x1 13.8 us: shards(): pl.pallas_call(pack_kernel, out_shape=[shape((PACK_ROWS, 128), F32), shap...]
    broadcast_in_dim x1 -> x0, local copies, waits for them, and re-layouts: 1.48 us -> none  [shards(): jnp.broadcast_to(left_t[None], (teams,) + left_t.shape)]
  transfers between devices with their start and end apart: 3 -> 3, of which waited for: 2 -> 2; matrix products, arithmetic and copies ran while one was open for 0% -> 0% of each run, Pallas kernels for 4% -> 0%
where the time goes in v2:
time: 75.3 us; the launch traced here: 75 us
  Pallas kernels  22.3 us (30%)
  starting transfers between devices  21.3 us (28%)
  blocking collectives  18.9 us (25%)
  waiting for transfers between devices  8.73 us (12%)
  local copies, waits for them, and re-layouts  2.75 us (4%)
  between operations  0.84 us (1%)
    pallas_call x1, Pallas kernels, shards(): pl.pallas_call(pack_kernel, out_shape=[shape((PACK_ROWS, 128), F32), shap...  13.8 us
    all_to_all x1, blocking collectives, shards(): lax.all_to_all(jnp.broadcast_to(mine[None], (teams // 2,) + mine.shape),...  12.6 us
    all_to_all x1, starting transfers between devices, shards(): left = lax.all_to_all(left, 'tensor', 0, 0)  10.3 us
    ppermute x1, starting transfers between devices, shards(): lax.ppermute(packed, 'seq', [((i + 1) % rings, i) for i in range(rings)])  9.08 us
    pallas_call x1, Pallas kernels, shards(): pl.pallas_call(main_kernel, out_shape=[shape((ROWS * TILES, 128), BF16),...  7.68 us
    ppermute x1, waiting for transfers between devices, shards(): lax.ppermute(packed, 'seq', [(i, (i + 1) % rings) for i in range(rings)])  7.01 us
    all_gather x1, blocking collectives, shards(): mixed = lax.all_gather(mixed, 'tensor', axis_index_groups=pairs, tiled=True)  3.45 us
    all_gather x1, blocking collectives, shards(): both = lax.all_gather(part, 'tensor', axis_index_groups=pairs, tiled=False)  2.91 us
  transfers between devices with their start and end apart: 3, of which 2 were waited for; matrix products, arithmetic and copies ran while one was open for 0% of the time, Pallas kernels for 0%

profile of v2, /device:TPU:1, one launch (start us, length us, event | category | flops | bytes accessed | tf_op | source)
XLA Modules:
  0.0 75.0 jit_solution(11675152973770947373)
XLA Ops:
  0.7 0.0 copy-start.9
  0.7 0.0 copy-start.10
  0.7 0.6 copy-done.9
  1.3 0.0 copy-done.10
  1.3 0.7 concatenate.3.meta_ref.refs_0_
  2.0 13.8 %pack.1 = (f32[296,128]{1,0:T(8,128)}, bf16[8,64,256]{2,1,0:T(8,128)(2,1)}) custom-call(s32[35]{0:T(128)} %concatenate.3.meta_ref.refs_0_, f32[2048,128]{1,0:T(8,128)} %bitcast.36, f32[16,2048]{1,0:T(8,128)} %refs_4_.1, bf16[64,256]{1,0:T(8,128)(2,1)} %bitcast.39), custom_call_target="tpu_custom_call" | custom-call | bytes 1048576 | tf_op jit(solution)/shard_map/pack/pallas_call | solution.py:373
  15.8 0.0 copy-start
  15.8 0.0 copy-start.1
  15.8 0.0 copy-start.2
  15.9 0.0 copy-start.3
  15.9 0.0 copy-start.7
  15.9 0.0 copy-start.8
  15.9 10.3 %all-to-all-start = ((bf16[8,64,256]{2,1,0:T(8,128)(2,1)}), bf16[8,64,256]{2,1,0:T(8,128)(2,1)S(1)}, u32[]{:S(2)}, u32[]{:S(2)}) async-start(bf16[8,64,256]{2,1,0:T(8,128)(2,1)} %get-tuple-element.9), calls=%async_computation | async-start | bytes 524288 | tf_op jit(solution)/shard_map/all_to_all | solution.py:385
  26.2 9.1 %collective-permute-start.1 = (f32[296,128]{1,0:T(8,128)}, f32[296,128]{1,0:T(8,128)S(1)}, u32[]{:S(2)}, u32[]{:S(2)}) collective-permute-start(f32[296,128]{1,0:T(8,128)} %get-tuple-element.8), channel_id=1, source_target_pairs={{8,0},{16,8},{24,16},{32,24},{40,32},{48,40},{56,48},{64,56},{72,6... | collective-permute-start | bytes 454664 | tf_op jit(solution)/shard_map/ppermute | solution.py:384
  35.3 1.9 %collective-permute-start = (f32[296,128]{1,0:T(8,128)}, f32[296,128]{1,0:T(8,128)S(1)}, u32[]{:S(2)}, u32[]{:S(2)}) collective-permute-start(f32[296,128]{1,0:T(8,128)} %get-tuple-element.8), channel_id=1, source_target_pairs={{0,8},{8,16},{16,24},{24,32},{32,40},{40,48},{48,56},{56,64},{64,7... | collective-permute-start | bytes 454664 | tf_op jit(solution)/shard_map/ppermute | solution.py:383
  37.3 0.0 copy-start.4
  37.3 1.7 %collective-permute-done.1.refs_6_ = f32[296,128]{1,0:T(8,128)S(1)} collective-permute-done((f32[296,128]{1,0:T(8,128)}, f32[296,128]{1,0:T(8,128)S(1)}, u32[]{:S(2)}, u32[]{:S(2)}) %collective-permute-start.1) | collective-permute-done | bytes 151584 | tf_op jit(solution)/shard_map/ppermute | solution.py:384
  39.0 7.0 %collective-permute-done.refs_5_ = f32[296,128]{1,0:T(8,128)S(1)} collective-permute-done((f32[296,128]{1,0:T(8,128)}, f32[296,128]{1,0:T(8,128)S(1)}, u32[]{:S(2)}, u32[]{:S(2)}) %collective-permute-start) | collective-permute-done | bytes 151584 | tf_op jit(solution)/shard_map/ppermute | solution.py:383
  46.0 0.0 all-to-all-done.refs_11_
  46.0 0.0 copy-start.5
  46.0 0.0 copy-start.6
  46.0 0.0 copy-done
  46.0 0.0 copy-done.1
  46.0 0.0 copy-done.2
  46.0 0.0 copy-done.3
  46.0 0.0 copy-done.7
  46.0 0.0 copy-done.8
  46.1 0.0 copy-done.4
  46.1 0.6 copy-done.5
  46.7 0.0 copy-done.6
  46.7 7.7 %main.1 = (bf16[1024,128]{1,0:T(8,128)(2,1)S(1)}, f32[2048,128]{1,0:T(8,128)}, f32[16,2048]{1,0:T(8,128)}) custom-call(s32[35]{0:T(128)S(1)} %copy-done.5, f32[2048,128]{1,0:T(8,128)} %bitcast.37, bf16[1024,128]{1,0:T(8,128)(2,1)S(1)} %bitcast.29, f32[16,128]{1,0:T(8,128)S(1)} %bitcast.32, f32[16,2048]{1,0:T(8,128)S(1)} %copy-done.1, ...), custom_call_target="tpu_custom_call" | custom-call | flops 268435456 | bytes 8388608 | tf_op jit(solution)/shard_map/main/pallas_call | solution.py:393
  54.4 2.9 %all-gather = bf16[2048,128]{1,0:T(8,128)(2,1)S(1)} all-gather(bf16[1024,128]{1,0:T(8,128)(2,1)S(1)} %get-tuple-element.10), channel_id=2, replica_groups={{0,1},{2,3},{4,5},{6,7},{8,9},{10,11},{12,13},{14,15},{16,17},{18,19},{..., dimensions={0}, use_global_device_ids=true | all-gather | bytes 786432 | tf_op jit(solution)/shard_map/all_gather | solution.py:427
  57.3 0.1 broadcast_in_dim.2
  57.4 12.6 %all_to_all.10.parts_ref = bf16[4,512,128]{2,1,0:T(8,128)(2,1)S(1)} all-to-all(bf16[4,512,128]{2,1,0:T(8,128)(2,1)S(1)} %broadcast_in_dim.2), channel_id=1, replica_groups={{0,2,4,6},{1,3,5,7},{8,10,12,14},{9,11,13,15},{16,18,20,22},{17,19,21,2..., dimensions={0} | all-to-all | bytes 1048576 | tf_op jit(solution)/shard_map/all_to_all | solution.py:429
  70.0 0.8 %finish.1 = bf16[512,128]{1,0:T(8,128)(2,1)S(1)} custom-call(s32[35]{0:T(128)S(1)} %copy-done.5, bf16[1024,128]{1,0:T(8,128)(2,1)S(1)} %bitcast.30, bf16[4,512,128]{2,1,0:T(8,128)(2,1)S(1)} %all_to_all.10.parts_ref), custom_call_target="tpu_custom_call" | custom-call | bytes 524288 | tf_op jit(solution)/shard_map/finish/pallas_call | solution.py:432
  70.8 3.4 %all_gather.11 = bf16[16,4,2048]{2,1,0:T(4,128)(2,1)S(1)} all-gather(bf16[8,4,2048]{2,1,0:T(4,128)(2,1)S(1)} %bitcast.31), channel_id=1, replica_groups={{0,1},{2,3},{4,5},{6,7},{8,9},{10,11},{12,13},{14,15},{16,17},{18,19},{..., dimensions={0}, use_global_device_ids=true | all-gather | bytes 393216 | tf_op jit(solution)/shard_map/all_gather | solution.py:443
  74.3 0.7 copy.27
  (1 shorter events, 0.0 us)
Async XLA Ops:
  0.7 0.7 copy-start.9
  0.7 0.7 copy-start.10
  15.8 30.2 %copy-start = (bf16[16,4,2048]{2,1,0:T(4,128)(2,1)S(1)}, bf16[16,4,2048]{2,1,0:T(4,128)(2,1)}, u32[]{:S(2)}) copy-start(bf16[16,4,2048]{2,1,0:T(4,128)(2,1)} %param.16) | copy-start | bytes 786436
  15.8 30.2 %copy-start.1 = (f32[16,2048]{1,0:T(8,128)S(1)}, f32[16,2048]{1,0:T(8,128)}, u32[]{:S(2)}) copy-start(f32[16,2048]{1,0:T(8,128)} %refs_4_.1) | copy-start | bytes 393220
  15.8 30.2 %copy-start.2 = (f32[4,2048]{1,0:T(4,128)S(1)}, f32[4,2048]{1,0:T(4,128)}, u32[]{:S(2)}) copy-start(f32[4,2048]{1,0:T(4,128)} %refs_7_.1) | copy-start | bytes 98308
  15.9 30.2 %copy-start.3 = (bf16[64,256]{1,0:T(8,128)(2,1)S(1)}, bf16[64,256]{1,0:T(8,128)(2,1)}, u32[]{:S(2)}) copy-start(bf16[64,256]{1,0:T(8,128)(2,1)} %refs_12_.1) | copy-start | bytes 98308
  15.9 30.2 %copy-start.7 = (f32[256]{0:T(256)S(1)}, f32[256]{0:T(256)}, u32[]{:S(2)}) copy-start(f32[256]{0:T(256)} %param.29) | copy-start | bytes 3076
  15.9 30.2 %copy-start.8 = (f32[256]{0:T(256)S(1)}, f32[256]{0:T(256)}, u32[]{:S(2)}) copy-start(f32[256]{0:T(256)} %param.30) | copy-start | bytes 3076
  15.9 30.1 %all-to-all-start = ((bf16[8,64,256]{2,1,0:T(8,128)(2,1)}), bf16[8,64,256]{2,1,0:T(8,128)(2,1)S(1)}, u32[]{:S(2)}, u32[]{:S(2)}) async-start(bf16[8,64,256]{2,1,0:T(8,128)(2,1)} %get-tuple-element.9), calls=%async_computation | async-start | bytes 524288 | tf_op jit(solution)/shard_map/all_to_all | solution.py:385
  26.2 12.8 %collective-permute-start.1 = (f32[296,128]{1,0:T(8,128)}, f32[296,128]{1,0:T(8,128)S(1)}, u32[]{:S(2)}, u32[]{:S(2)}) collective-permute-start(f32[296,128]{1,0:T(8,128)} %get-tuple-element.8), channel_id=1, source_target_pairs={{8,0},{16,8},{24,16},{32,24},{40,32},{48,40},{56,48},{64,56},{72,6... | collective-permute-start | bytes 454664 | tf_op jit(solution)/shard_map/ppermute | solution.py:384
  35.3 10.7 %collective-permute-start = (f32[296,128]{1,0:T(8,128)}, f32[296,128]{1,0:T(8,128)S(1)}, u32[]{:S(2)}, u32[]{:S(2)}) collective-permute-start(f32[296,128]{1,0:T(8,128)} %get-tuple-element.8), channel_id=1, source_target_pairs={{0,8},{8,16},{16,24},{24,32},{32,40},{40,48},{48,56},{56,64},{64,7... | collective-permute-start | bytes 454664 | tf_op jit(solution)/shard_map/ppermute | solution.py:383
  37.3 8.8 %copy-start.4 = (f32[2048]{0:T(1024)S(1)}, f32[2048]{0:T(1024)}, u32[]{:S(2)}) copy-start(f32[2048]{0:T(1024)} %param.21) | copy-start | bytes 24580
  46.0 0.7 copy-start.5
  46.0 0.7 copy-start.6

commit v3 on v2

v3 whole, which is shorter than its diff:
```python
import functools

import jax
import jax.numpy as jnp
from jax import lax
from jax.experimental import pallas as pl
from jax.experimental.pallas import tpu as pltpu
from jax.sharding import PartitionSpec as P

EPS = 1e-05
F32 = jnp.float32
BF16 = jnp.bfloat16
HEAD = 64
SLOTS = 16
STEPS = 4
WIDTH = 2048
HEADS = 4
LOCAL = HEADS * HEAD
TILES = WIDTH // 128
ROWS = SLOTS * STEPS
STATE_ROWS = HEADS * HEAD * HEAD // 128
PIECE = STATE_ROWS + TILES
PACK_ROWS = 2 * PIECE + 8
PACK_MIB, MAIN_MIB = 60, 52


def spec(space, count):
    return [pl.BlockSpec(memory_space=space)] * count


def dot(a, b):
    return jnp.dot(a, b, preferred_element_type=F32)


def dot_rows(a, b):
    return lax.dot_general(a, b, (((0,), (0,)), ((), ())), preferred_element_type=F32)


def split(a):
    hi = a.astype(BF16)
    return hi, (a - hi.astype(F32)).astype(BF16)


def dot_split(a, b):
    hi, lo = split(a)
    return dot(hi, b) + dot(lo, b)


def iota(shape, dim):
    return lax.broadcasted_iota(jnp.int32, shape, dim)


def column_of(tally_ref, shape):
    rows = iota(shape, 0)
    out = jnp.zeros(shape, jnp.int32)
    for q in range(SLOTS):
        out = jnp.where(rows == q, tally_ref[q], out)
    return out


def row_of(ref):
    return jnp.concatenate([ref[i : i + 1, :] for i in range(ref.shape[0])], axis=1)


def start(items):
    for copy in items:
        copy.start()


def pack_kernel(where_ref, lookup_hbm, mem_ref, prev_ref, left_ref, out_ref, left_out, lookup_ref, prev, left, tile, sems):
    loads = [
        pltpu.make_async_copy(lookup_hbm, lookup_ref, sems.at[0]),
        pltpu.make_async_copy(prev_ref, prev, sems.at[1]),
        pltpu.make_async_copy(left_ref, left, sems.at[2]),
    ]
    start(loads)
    first = where_ref[0] * SLOTS
    loads[0].wait()
    kept = jnp.int32(0)
    for q in range(SLOTS):
        at = lookup_ref[q] - first
        own = (at >= 0) & (at < SLOTS)
        kept = kept | jnp.where(own, jnp.int32(1) << jnp.where(own, at, 0), 0)
    low, high = jnp.int32(0), jnp.int32(0)
    for s in range(SLOTS):
        high = jnp.where((kept >> s) & 1 == 0, s, high)
        low = jnp.where((kept >> (SLOTS - 1 - s)) & 1 == 0, SLOTS - 1 - s, low)
    moves = [
        pltpu.make_async_copy(
            mem_ref.at[pl.ds(pl.multiple_of(slot * STATE_ROWS, STATE_ROWS), STATE_ROWS), :],
            tile.at[pl.ds(n * PIECE, STATE_ROWS), :],
            sems.at[3 + n],
        )
        for n, slot in enumerate((low, high))
    ]
    start(moves)
    loads[2].wait()
    spread = [pltpu.make_async_copy(left, left_out.at[n], sems.at[8 + n]) for n in range(left_out.shape[0])]
    start(spread)
    tile[2 * PIECE :, :] = jnp.where(iota((8, 128), 0) == 0, first + low, first + high).astype(F32)
    loads[1].wait()
    for n, slot in enumerate((low, high)):
        row = prev[pl.ds(slot, 1), :]
        at = n * PIECE + STATE_ROWS
        for c in range(TILES):
            tile[at + c : at + c + 1, :] = row[:, c * 128 : (c + 1) * 128]
    moves[0].wait()
    moves[1].wait()
    done = pltpu.make_async_copy(tile, out_ref, sems.at[5])
    done.start()
    done.wait()
    for copy in spread:
        copy.wait()


def pick(recv_ref, wanted, begin, count):
    is_low = recv_ref[2 * PIECE : 2 * PIECE + 1, :] == wanted.astype(F32)
    return jnp.where(is_low, recv_ref[begin : begin + count, :], recv_ref[PIECE + begin : PIECE + begin + count, :])


def sources(where_ref, lookup_ref, q):
    wanted = lookup_ref[q]
    owner = wanted // SLOTS
    own = owner == where_ref[0]
    before = owner == where_ref[1]
    at = jnp.where(own, wanted - where_ref[0] * SLOTS, 0)
    return wanted, own, before, at


def copies(sources_, targets, sems):
    return [pltpu.make_async_copy(a, b, sems.at[n]) for n, (a, b) in enumerate(zip(sources_, targets))]


def state_copies(where_ref, lookup_ref, mem_hbm, state, sems):
    out = []
    for q in range(SLOTS):
        at = sources(where_ref, lookup_ref, q)[3]
        out.append(
            pltpu.make_async_copy(
                mem_hbm.at[pl.ds(pl.multiple_of(at * STATE_ROWS, STATE_ROWS), STATE_ROWS), :],
                state.at[pl.ds(q * STATE_ROWS, STATE_ROWS), :],
                sems.at[q],
            )
        )
    return out


def place_received(where_ref, lookup_ref, from_before, from_after, state):
    for q in range(SLOTS):
        wanted, own, before, _ = sources(where_ref, lookup_ref, q)
        here = slice(q * STATE_ROWS, (q + 1) * STATE_ROWS)

        @pl.when(jnp.logical_not(own) & before)
        def _():
            state[here, :] = pick(from_before, wanted, 0, STATE_ROWS)

        @pl.when(jnp.logical_not(own) & jnp.logical_not(before))
        def _():
            state[here, :] = pick(from_after, wanted, 0, STATE_ROWS)


def cut(a, t):
    return a[t * SLOTS : (t + 1) * SLOTS, :]


def project_kernel(where_ref, lookup_ref, tally_ref, *refs):
    count = 9
    hbm, (rkv_ref, mixed_ref, last_ref), bufs = refs[:count], refs[count : count + 3], refs[count + 3 : 2 * count + 3]
    x32, shift, sems = refs[2 * count + 3 :]
    loads = copies(hbm, bufs, sems)
    start(loads)
    x_ref, gain_ref, prev_ref, from_before, from_after, blend_ref = bufs[:6]
    loads[0].wait()
    loads[1].wait()
    x32[...] = x_ref[...].astype(F32)
    gain = row_of(gain_ref)
    normed = []
    for t in range(STEPS):
        row = jnp.concatenate([x32[pl.ds(c * STEPS + t, SLOTS, stride=STEPS * TILES), :] for c in range(TILES)], axis=1)
        center = row - jnp.mean(row, axis=-1, keepdims=True)
        spread = jnp.mean(center * center, axis=-1, keepdims=True)
        normed.append(center * lax.rsqrt(spread + EPS) * gain)
    tally = column_of(tally_ref, (SLOTS, 128))[:, :1]
    last = normed[0]
    for t in range(1, STEPS):
        last = jnp.where(tally == t + 1, normed[t], last)
    last_ref[...] = last
    for n in range(2, 6):
        loads[n].wait()
    for q in range(SLOTS):
        wanted, own, before, at = sources(where_ref, lookup_ref, q)

        @pl.when(own)
        def _():
            shift[q : q + 1, :] = prev_ref[pl.ds(at, 1), :]

        @pl.when(jnp.logical_not(own))
        def _():
            rows = jnp.where(
                before, pick(from_before, wanted, STATE_ROWS, TILES), pick(from_after, wanted, STATE_ROWS, TILES)
            )
            for c in range(TILES):
                shift[q : q + 1, c * 128 : (c + 1) * 128] = rows[c : c + 1, :]

    xn = jnp.concatenate(normed, axis=0)
    change = jnp.concatenate([shift[...]] + normed[:-1], axis=0) - xn

    def mix(which):
        return (xn + change * blend_ref[which : which + 1, :]).astype(BF16)

    mixed_ref[...] = mix(3)
    for n in range(3):
        loads[6 + n].wait()
        rkv_ref[n] = dot(mix(n), bufs[6 + n][...])


def step_kernel(where_ref, lookup_ref, tally_ref, mem_hbm, *refs):
    count = 10
    hbm, (part_ref, moved_ref, doubled_ref) = refs[:count], refs[count : count + 3]
    bufs = refs[count + 3 : 2 * count + 3]
    state, reads, heads, part, sems, state_sems = refs[2 * count + 3 :]
    loads = copies(hbm, bufs, sems)
    start(loads)
    state_loads = state_copies(where_ref, lookup_ref, mem_hbm, state, state_sems)
    start(state_loads)
    (
        mixed_ref, left_ref, right_ref, base_ref, boost_ref, team_ref, rkv_ref, from_before, from_after, final_ref,
    ) = bufs
    for n in range(7):
        loads[n].wait()
    tally = column_of(tally_ref, (SLOTS, 128))[:, :1]
    pre = jnp.zeros((ROWS, left_ref.shape[1]), F32)
    chunk = left_ref.shape[2]
    for n in range(left_ref.shape[0]):
        pre = pre + lax.dot_general(
            mixed_ref[:, n * chunk : (n + 1) * chunk], left_ref[n], (((1,), (1,)), ((), ())), preferred_element_type=F32
        )
    lora = jnp.tanh(pre).astype(BF16)
    decay = jnp.exp(-jnp.exp(row_of(base_ref) + dot(lora, right_ref[...])))
    r = [cut(rkv_ref[0], t) for t in range(STEPS)]
    k = [cut(rkv_ref[1], t) for t in range(STEPS)]
    v = [cut(rkv_ref[2], t) for t in range(STEPS)]
    d = [jnp.where(tally > t, cut(decay, t), 1.0) for t in range(STEPS)]
    kept = [jnp.where(tally > t, k[t], 0.0) for t in range(STEPS)]
    boost = row_of(boost_ref)

    run, reach = r[0] * 0.0 + 1.0, []
    for t in range(STEPS):
        reach.append(r[t] * run)
        run = run * d[t]
    tail, coefs = None, [None] * STEPS
    for t in reversed(range(STEPS)):
        coefs[t] = kept[t] if tail is None else kept[t] * tail
        tail = d[t] if tail is None else tail * d[t]
    pairs, terms = [], []
    for t in range(STEPS):
        pairs.append((t, t))
        terms.append(r[t] * boost * k[t])
        weight = r[t]
        for s in reversed(range(t)):
            pairs.append((t, s))
            terms.append(weight * kept[s])
            weight = weight * d[s]
    row256, col256 = iota((LOCAL, LOCAL), 0), iota((LOCAL, LOCAL), 1)
    same_head = (row256 // HEAD == col256 // HEAD).astype(BF16)
    sums = dot_split(jnp.concatenate(terms, axis=0), same_head)
    within = [None] * STEPS
    for n, (t, s) in enumerate(pairs):
        term = cut(sums, n) * v[s]
        within[t] = term if within[t] is None else within[t] + term

    source = (col256 % HEADS) * HEAD + ((col256 // HEADS) % (HEAD // 2)) * 2 + col256 // 128
    reorder = (row256 == source).astype(BF16)
    moved = dot_split(jnp.concatenate(reach + coefs + [run], axis=0), reorder)
    moved_ref[...] = moved[STEPS * SLOTS :, :]
    rowd, cold = iota((LOCAL, HEADS * 128), 0), iota((LOCAL, HEADS * 128), 1)
    double = (rowd == (cold // 128) * HEAD + cold % HEAD).astype(BF16)
    doubled_ref[...] = dot(rkv_ref[2].astype(BF16), double)

    lane = iota((SLOTS, 128), 1)
    for h in range(HEADS):
        head_lane = lane % HEADS == h
        for p in range(2):
            for t in range(STEPS):
                at = pl.ds(t * 8 + p * HEADS + h, SLOTS, stride=STEPS * 8)
                reads[at, :] = jnp.where(head_lane, cut(moved, t)[:, p * 128 : (p + 1) * 128], 0.0)
    for copy in loads[7:9] + state_loads:
        copy.wait()
    place_received(where_ref, lookup_ref, from_before, from_after, state)
    for q in range(SLOTS):
        rows = slice(q * STEPS * 8, (q + 1) * STEPS * 8)
        now = state[q * STATE_ROWS : (q + 1) * STATE_ROWS, :]
        heads[rows, :] = dot(reads[rows, :].astype(BF16), now.astype(BF16))

    outs = []
    left_half = lane < HEAD
    for t in range(STEPS):
        def read(p, h):
            return heads[pl.ds(t * 8 + p * HEADS + h, SLOTS, stride=STEPS * 8), :]

        cols = []
        for h in range(0, HEADS, 2):
            a, b, c, e = read(0, h), read(1, h), read(0, h + 1), read(1, h + 1)
            cols.append(jnp.where(left_half, a, e) + pltpu.roll(jnp.where(left_half, c, b), HEAD, 1))
        outs.append(jnp.concatenate(cols, axis=1) + within[t])
    y = jnp.concatenate(outs, axis=0)
    center = y - dot_split(y, same_head) * (1.0 / HEAD)
    spread = dot_split(center * center, same_head) * (1.0 / HEAD)
    g = (center * lax.rsqrt(spread + EPS) * row_of(team_ref)).astype(BF16)
    loads[9].wait()
    proj = dot(g, final_ref[...])
    for t in range(STEPS):
        for c in range(TILES):
            part[pl.ds(c * STEPS + t, SLOTS, stride=STEPS * TILES), :] = cut(proj, t)[:, c * 128 : (c + 1) * 128]
    part_ref[...] = part[...].astype(BF16)


def update_kernel(where_ref, lookup_ref, mem_hbm, *refs):
    count = 4
    hbm, new_hbm, bufs = refs[:count], refs[count], refs[count + 1 : 2 * count + 1]
    state, keys, vals, decays, fresh, sems, state_sems, new_sems = refs[2 * count + 1 :]
    loads = copies(hbm, bufs, sems)
    start(loads)
    state_loads = state_copies(where_ref, lookup_ref, mem_hbm, state, state_sems)
    start(state_loads)
    moved_ref, doubled_ref, from_before, from_after = bufs
    loads[0].wait()
    loads[1].wait()
    lane = iota((SLOTS, 128), 1)
    for h in range(HEADS):
        head_lane = lane % HEADS == h
        for p in range(2):
            half = lane // HEAD == p
            cols = slice(p * 128, (p + 1) * 128)
            for t in range(STEPS):
                at = pl.ds(t * 8 + p * HEADS + h, SLOTS, stride=STEPS * 8)
                keys[at, :] = jnp.where(head_lane, cut(moved_ref, t)[:, cols], 0.0)
                vals[at, :] = jnp.where(half, cut(doubled_ref, t)[:, h * 128 : (h + 1) * 128], 0.0)
            whole = jnp.where(head_lane, cut(moved_ref, STEPS)[:, cols], 0.0)
            high = whole.astype(BF16).astype(F32)
            decays[pl.ds(p * HEADS + h, SLOTS, stride=16), :] = high
            decays[pl.ds(8 + p * HEADS + h, SLOTS, stride=16), :] = whole - high
    ones = ((iota((16, 128), 0) // HEADS) % 2 == iota((16, 128), 1) // HEAD).astype(BF16)
    for copy in loads[2:] + state_loads:
        copy.wait()
    place_received(where_ref, lookup_ref, from_before, from_after, state)
    news = []
    for q in range(SLOTS):
        here = slice(q * STATE_ROWS, (q + 1) * STATE_ROWS)
        rows = slice(q * STEPS * 8, (q + 1) * STEPS * 8)
        fade = dot_rows(decays[q * 16 : (q + 1) * 16, :].astype(BF16), ones)
        grown = dot_rows(keys[rows, :].astype(BF16), vals[rows, :].astype(BF16))
        fresh[here, :] = fade * state[here, :] + grown
        news.append(pltpu.make_async_copy(fresh.at[here, :], new_hbm.at[here, :], new_sems.at[q]))
        news[-1].start()
    for copy in news:
        copy.wait()


def finish_kernel(where_ref, tally_ref, x_hbm, parts_ref, out_ref, x_ref, sem):
    rows = out_ref.shape[0]
    begin = where_ref[2] * rows
    load = pltpu.make_async_copy(x_hbm.at[pl.ds(pl.multiple_of(begin, rows), rows), :], x_ref, sem)
    load.start()
    step = iota((STEPS * TILES, 128), 0) % STEPS
    load.wait()
    for q in range(rows // (STEPS * TILES)):
        here = slice(q * STEPS * TILES, (q + 1) * STEPS * TILES)
        total = x_ref[here, :].astype(F32)
        for n in range(parts_ref.shape[0]):
            total = total + parts_ref[n, here, :].astype(F32)
        tally = tally_ref[where_ref[2] * (rows // (STEPS * TILES)) + q]
        out_ref[here, :] = jnp.where(step < tally, total, 0.0).astype(BF16)


def cost(flops, bytes_accessed):
    return pl.CostEstimate(flops=flops, bytes_accessed=bytes_accessed, transcendentals=0)


def tiles_view(a):
    lead, mid, width = a.shape
    return a.reshape(lead, mid, width // 128, 128).transpose(0, 2, 1, 3).reshape(lead * width // 128 * mid, 128)


def tiles_back(a, lead, mid, width):
    return a.reshape(lead, width // 128, mid, 128).transpose(0, 2, 1, 3).reshape(lead, mid, width)


def shards(
    layer_entry_vectors,
    tally_of_tokens,
    prior_slot_lookup,
    memory_matrices,
    previous_standardized_entries,
    entry_standardize_scale,
    blend_coefficients,
    acceptance_projection_matrix,
    lookup_projection_matrix,
    payload_projection_matrix,
    forget_map_left_matrix,
    forget_map_right_matrix,
    feature_forget_logloglevel,
    present_token_boost,
    team_standardize_scale,
    final_projection_matrix,
):
    rings = lax.axis_size("seq")
    teams = lax.axis_size("tensor")
    device = lax.axis_index("seq")
    core = lax.axis_index("tensor") % 2
    where = jnp.stack([device, (device + rings - 1) % rings, core]).astype(jnp.int32)
    x = tiles_view(layer_entry_vectors)
    mem = tiles_view(memory_matrices)
    prev = previous_standardized_entries
    lookup, tally = prior_slot_lookup, tally_of_tokens
    left_t = forget_map_left_matrix.T
    shape, scratch, dma = jax.ShapeDtypeStruct, pltpu.VMEM, pltpu.SemaphoreType.DMA
    params = lambda mib: pltpu.CompilerParams(vmem_limit_bytes=mib << 20)
    like = lambda items: [scratch(a.shape, a.dtype) for a in items]
    state_buf = scratch((SLOTS * STATE_ROWS, 128), F32)
    rows_buf = scratch((SLOTS * STEPS * 8, 128), F32)

    packed, left = pl.pallas_call(
        pack_kernel,
        out_shape=[shape((PACK_ROWS, 128), F32), shape((teams,) + left_t.shape, BF16)],
        in_specs=spec(pltpu.SMEM, 1) + spec(pl.ANY, 4),
        out_specs=spec(pl.ANY, 2),
        scratch_shapes=[
            pltpu.SMEM(lookup.shape, jnp.int32), scratch(prev.shape, F32), scratch(left_t.shape, BF16),
            scratch((PACK_ROWS, 128), F32), dma((8 + teams,)),
        ],
        compiler_params=params(PACK_MIB),
        cost_estimate=cost(0, 1 << 20),
        name="pack",
    )(where, lookup, mem, prev, left_t)
    from_before = lax.ppermute(packed, "seq", [(i, (i + 1) % rings) for i in range(rings)])
    from_after = lax.ppermute(packed, "seq", [((i + 1) % rings, i) for i in range(rings)])
    left = lax.all_to_all(left, "tensor", 0, 0)

    operands = [
        x, entry_standardize_scale.reshape(TILES, 128), prev, from_before, from_after, blend_coefficients,
        acceptance_projection_matrix, lookup_projection_matrix, payload_projection_matrix,
    ]
    rkv, mixed_rows, new_shifts = pl.pallas_call(
        project_kernel,
        out_shape=[shape((3, ROWS, LOCAL), F32), shape((ROWS, WIDTH), BF16), shape((SLOTS, WIDTH), F32)],
        in_specs=spec(pltpu.SMEM, 3) + spec(pl.ANY, len(operands)),
        out_specs=spec(pltpu.VMEM, 3),
        scratch_shapes=like(operands)
        + [scratch((ROWS * TILES, 128), F32), scratch((SLOTS, WIDTH), F32), dma((len(operands),))],
        compiler_params=params(MAIN_MIB),
        cost_estimate=cost(6 * ROWS * WIDTH * LOCAL, 8 << 20),
        name="project",
    )(where, lookup, tally, *operands)

    operands = [
        mixed_rows, left, forget_map_right_matrix, feature_forget_logloglevel.reshape(2, 128),
        present_token_boost.reshape(2, 128), team_standardize_scale.reshape(2, 128), rkv, from_before, from_after,
        final_projection_matrix,
    ]
    part, moved, doubled = pl.pallas_call(
        step_kernel,
        out_shape=[
            shape((ROWS * TILES, 128), BF16), shape((ROWS + SLOTS, LOCAL), F32), shape((ROWS, HEADS * 128), F32),
        ],
        in_specs=spec(pltpu.SMEM, 3) + spec(pl.ANY, 1 + len(operands)),
        out_specs=spec(pltpu.VMEM, 3),
        scratch_shapes=like(operands)
        + [state_buf, rows_buf, rows_buf, scratch((ROWS * TILES, 128), F32), dma((len(operands),)), dma((SLOTS,))],
        compiler_params=params(MAIN_MIB),
        cost_estimate=cost(2 * ROWS * WIDTH * LOCAL, 4 << 20),
        name="step",
    )(where, lookup, tally, mem, *operands)

    operands = [moved, doubled, from_before, from_after]
    new_states = pl.pallas_call(
        update_kernel,
        out_shape=shape((SLOTS * STATE_ROWS, 128), F32),
        in_specs=spec(pltpu.SMEM, 2) + spec(pl.ANY, 1 + len(operands)),
        out_specs=spec(pl.ANY, 1)[0],
        scratch_shapes=like(operands)
        + [state_buf, rows_buf, rows_buf, scratch((SLOTS * 16, 128), F32), state_buf]
        + [dma((len(operands),)), dma((SLOTS,)), dma((SLOTS,))],
        compiler_params=params(MAIN_MIB),
        cost_estimate=cost(1 << 24, 8 << 20),
        name="update",
    )(where, lookup, mem, *operands)

    pairs = [[2 * i, 2 * i + 1] for i in range(teams // 2)]
    chips = [[2 * i + c for i in range(teams // 2)] for c in range(2)]
    half = ROWS * TILES // 2
    both = lax.all_gather(part, "tensor", axis_index_groups=pairs, tiled=False)
    mine = lax.dynamic_slice_in_dim(both, core * half, half, 1).astype(F32).sum(0).astype(BF16)
    spread = lax.all_to_all(
        jnp.broadcast_to(mine[None], (teams // 2,) + mine.shape), "tensor", 0, 0, axis_index_groups=chips
    )
    mixed = pl.pallas_call(
        finish_kernel,
        out_shape=shape((half, 128), BF16),
        in_specs=spec(pltpu.SMEM, 2) + spec(pl.ANY, 1) + spec(pltpu.VMEM, 1),
        out_specs=spec(pltpu.VMEM, 1)[0],
        scratch_shapes=[scratch((half, 128), BF16), dma],
        compiler_params=params(8),
        cost_estimate=cost(0, 1 << 19),
        name="finish",
    )(where, tally, x, spread)
    mixed = tiles_back(mixed, SLOTS // 2, STEPS, WIDTH)
    mixed = lax.all_gather(mixed, "tensor", axis_index_groups=pairs, tiled=True)
    return (
        mixed,
        tiles_back(new_states, SLOTS, HEADS, HEAD * HEAD),
        new_shifts,
    )


def solution(mesh):
    in_specs = (
        P("seq", None, None),
        P("seq"),
        P("seq"),
        P("seq", "tensor", None),
        P("seq", None),
        P(),
        P(),
        P(None, "tensor"),
        P(None, "tensor"),
        P(None, "tensor"),
        P("tensor", None),
        P(None, "tensor"),
        P("tensor"),
        P("tensor"),
        P("tensor"),
        P("tensor", None),
    )
    out_specs = (P("seq", None, None), P("seq", "tensor", None), P("seq", None))
    return jax.shard_map(shards, mesh=mesh, in_specs=in_specs, out_specs=out_specs, check_vma=False)
```

time: 75.3 us -> 66.5 us (0.88)
  blocking collectives: 18.9 us -> 5.94 us
  Pallas kernels: 22.3 us -> 17.3 us
  starting transfers between devices: 21.3 us -> 25.6 us
  waiting for transfers between devices: 8.73 us -> 12.8 us
    all_to_all x1 -> x0, blocking collectives: 12.6 us -> none  [shards(): lax.all_to_all(jnp.broadcast_to(mine[None], (teams // 2,) + mine.shape),...]
    pallas_call x1, Pallas kernels: 13.8 us -> 3.09 us  [shards(): pl.pallas_call(pack_kernel, out_shape=[shape((PACK_ROWS, 128), F32), shap...]
    pallas_call x1 -> x3, Pallas kernels: 7.68 us -> 13.3 us  [the longest x1 5.02 us: shards(): pl.pallas_call(update_kernel, out_shape=shape((SLOTS * STATE_ROWS, 128),...]
    all_to_all x0 -> x1, starting transfers between devices: none -> 4.16 us  [shards(): lax.all_to_all(jnp.broadcast_to(mine[None], (teams // 2,) + mine.shape),...]
    all_to_all x0 -> x1, waiting for transfers between devices: none -> 3.88 us  [shards(): lax.all_to_all(jnp.broadcast_to(mine[None], (teams // 2,) + mine.shape),...]
    broadcast_in_dim x1, local copies, waits for them, and re-layouts: 0.07 us -> 0.88 us  [shards(): jnp.broadcast_to(mine[None], (teams // 2,) + mine.shape)]
    unnamed x23 -> x25, local copies, waits for them, and re-layouts: 2.02 us -> 2.03 us
  transfers between devices with their start and end apart: 3 -> 4, of which waited for: 2 -> 3; matrix products, arithmetic and copies ran while one was open for 0% -> 0% of each run, Pallas kernels for 0% -> 13%
where the time goes in v3:
time: 66.5 us; the launch traced here: 66 us
  starting transfers between devices  25.6 us (38%)
  Pallas kernels  17.3 us (26%)
  waiting for transfers between devices  12.8 us (19%)
  blocking collectives  5.94 us (9%)
  local copies, waits for them, and re-layouts  2.91 us (4%)
  between operations  0.83 us (1%)
  other arithmetic  0.7 us (1%)
    all_to_all x1, starting transfers between devices, shards(): left = lax.all_to_all(left, 'tensor', 0, 0)  10.3 us
    ppermute x1, starting transfers between devices, shards(): lax.ppermute(packed, 'seq', [((i + 1) % rings, i) for i in range(rings)])  9.21 us
    ppermute x1, waiting for transfers between devices, shards(): lax.ppermute(packed, 'seq', [(i, (i + 1) % rings) for i in range(rings)])  7.01 us
    pallas_call x1, Pallas kernels, shards(): pl.pallas_call(update_kernel, out_shape=shape((SLOTS * STATE_ROWS, 128),...  5.02 us
    pallas_call x1, Pallas kernels, shards(): pl.pallas_call(step_kernel, out_shape=[shape((ROWS * TILES, 128), BF16),...  4.44 us
    all_to_all x1, starting transfers between devices, shards(): lax.all_to_all(jnp.broadcast_to(mine[None], (teams // 2,) + mine.shape),...  4.16 us
    pallas_call x1, Pallas kernels, shards(): pl.pallas_call(project_kernel, out_shape=[shape((3, ROWS, LOCAL), F32), s...  3.88 us
    all_to_all x1, waiting for transfers between devices, shards(): lax.all_to_all(jnp.broadcast_to(mine[None], (teams // 2,) + mine.shape),...  3.88 us
  transfers between devices with their start and end apart: 4, of which 3 were waited for; matrix products, arithmetic and copies ran while one was open for 0% of the time, Pallas kernels for 13%

profile of v3, /device:TPU:1, one launch (start us, length us, event | category | flops | bytes accessed | tf_op | source)
XLA Modules:
  0.0 66.0 jit_solution(14118790105007532537)
XLA Ops:
  0.6 0.7 %pad_add_fusion.where_ref = s32[3]{0:T(128)} fusion(s32[1]{0:T(128)} %bitcast.2, s32[1]{0:T(128)} %bitcast.1, s32[1]{0:T(128)} %bitcast), kind=kLoop, calls=%fused_computation.1 | loop fusion | flops 6 | bytes 24 | tf_op jit(solution)/shard_map/stack | solution.py:411
  1.3 3.1 %pack.1 = (f32[296,128]{1,0:T(8,128)}, bf16[8,64,256]{2,1,0:T(8,128)(2,1)}) custom-call(s32[3]{0:T(128)} %pad_add_fusion.where_ref, s32[16]{0:T(128)} %lookup_ref.5, f32[2048,128]{1,0:T(8,128)} %bitcast.29, f32[16,2048]{1,0:T(8,128)} %refs_2_.2, bf16[64,256]{1,0:T(8,128)(2,1)} %bitcast.41), custom_call_target="tpu_custom_call" | custom-call | bytes 1048576 | tf_op jit(solution)/shard_map/pack/pallas_call | solution.py:423
  4.4 0.0 copy-start.1
  4.4 0.0 copy-start.2
  4.4 0.0 copy-start.3
  4.5 10.3 %all-to-all-start = ((bf16[8,64,256]{2,1,0:T(8,128)(2,1)}), bf16[8,64,256]{2,1,0:T(8,128)(2,1)S(1)}, u32[]{:S(2)}, u32[]{:S(2)}) async-start(bf16[8,64,256]{2,1,0:T(8,128)(2,1)} %get-tuple-element.13), calls=%async_computation | async-start | bytes 524288 | tf_op jit(solution)/shard_map/all_to_all | solution.py:438
  14.8 0.0 copy-start.6
  14.8 9.2 %collective-permute-start.1 = (f32[296,128]{1,0:T(8,128)}, f32[296,128]{1,0:T(8,128)S(1)}, u32[]{:S(2)}, u32[]{:S(2)}) collective-permute-start(f32[296,128]{1,0:T(8,128)} %get-tuple-element.11), channel_id=1, source_target_pairs={{8,0},{16,8},{24,16},{32,24},{40,32},{48,40},{56,48},{64,56},{72,6... | collective-permute-start | bytes 454664 | tf_op jit(solution)/shard_map/ppermute | solution.py:437
  24.0 1.9 %collective-permute-start = (f32[296,128]{1,0:T(8,128)}, f32[296,128]{1,0:T(8,128)S(1)}, u32[]{:S(2)}, u32[]{:S(2)}) collective-permute-start(f32[296,128]{1,0:T(8,128)} %get-tuple-element.11), channel_id=1, source_target_pairs={{0,8},{8,16},{16,24},{24,32},{32,40},{40,48},{48,56},{56,64},{64,7... | collective-permute-start | bytes 454664 | tf_op jit(solution)/shard_map/ppermute | solution.py:436
  25.9 1.9 %collective-permute-done.1.refs_4_.refs_8_.refs_3_ = f32[296,128]{1,0:T(8,128)S(1)} collective-permute-done((f32[296,128]{1,0:T(8,128)}, f32[296,128]{1,0:T(8,128)S(1)}, u32[]{:S(2)}, u32[]{:S(2)}) %collective-permute-start.1) | collective-permute-done | bytes 151584 | tf_op jit(solution)/shard_map/ppermute | solution.py:437
  27.8 7.0 %collective-permute-done.refs_3_.refs_7_.refs_2_ = f32[296,128]{1,0:T(8,128)S(1)} collective-permute-done((f32[296,128]{1,0:T(8,128)}, f32[296,128]{1,0:T(8,128)S(1)}, u32[]{:S(2)}, u32[]{:S(2)}) %collective-permute-start) | collective-permute-done | bytes 151584 | tf_op jit(solution)/shard_map/ppermute | solution.py:436
  34.8 0.0 copy-start.5
  34.8 0.0 copy-start.7
  34.8 0.0 copy-start.8
  34.8 0.0 copy-done.1
  34.8 0.0 copy-done.2
  34.8 0.0 copy-done.3
  34.8 0.0 copy-done.6
  34.9 0.6 copy-done.5
  35.5 0.0 copy-done.7
  35.5 0.0 copy-done.8
  35.5 0.0 copy-start.4
  35.5 0.0 copy-start.10
  35.5 0.0 copy-start.11
  35.5 3.9 %project.1 = (f32[3,64,256]{2,1,0:T(8,128)S(1)}, bf16[64,2048]{1,0:T(8,128)(2,1)S(1)}, f32[16,2048]{1,0:T(8,128)}) custom-call(s32[3]{0:T(128)S(1)} %copy-done.5, s32[16]{0:T(128)S(1)} %copy-done.7, s32[16]{0:T(128)S(1)} %copy-done.8, bf16[1024,128]{1,0:T(8,128)(2,1)S(1)} %bitcast.32, f32[16,128]{1,0:T(8,128)S(1)} %bitcast.35, f32[16,2048]{1,0:T(8,128)S(1)} %copy-done.2, ...), custom_call_target="tpu_custom_call" | custom-call | flops 201326592 | bytes 8388608 | tf_op jit(solution)/shard_map/project/pallas_call | solution.py:444
  39.4 0.0 all-to-all-done.refs_1_
  39.4 0.0 copy-start.9
  39.4 0.0 copy-done.4
  39.4 0.0 copy-done.10
  39.5 0.0 copy-done.11
  39.5 0.6 copy-done.9
  40.1 4.4 %step.1 = (bf16[1024,128]{1,0:T(8,128)(2,1)S(1)}, f32[80,256]{1,0:T(8,128)S(1)}, f32[64,512]{1,0:T(8,128)S(1)}) custom-call(s32[3]{0:T(128)S(1)} %copy-done.5, s32[16]{0:T(128)S(1)} %copy-done.7, s32[16]{0:T(128)S(1)} %copy-done.8, f32[2048,128]{1,0:T(8,128)} %bitcast.30, bf16[64,2048]{1,0:T(8,128)(2,1)S(1)} %get-tuple-element.12.refs_0_, ...), custom_call_target="tpu_custom_call" | custom-call | flops 67108864 | bytes 4194304 | tf_op jit(solution)/shard_map/step/pallas_call | solution.py:461
  44.6 2.8 %all-gather = bf16[2048,128]{1,0:T(8,128)(2,1)S(1)} all-gather(bf16[1024,128]{1,0:T(8,128)(2,1)S(1)} %get-tuple-element.15), channel_id=2, replica_groups={{0,1},{2,3},{4,5},{6,7},{8,9},{10,11},{12,13},{14,15},{16,17},{18,19},{..., dimensions={0}, use_global_device_ids=true | all-gather | bytes 786432 | tf_op jit(solution)/shard_map/all_gather | solution.py:492
  47.3 0.0 copy-start
  47.4 0.9 %broadcast_in_dim.2 = bf16[4,512,128]{2,1,0:T(8,128)(2,1)} broadcast(bf16[512,128]{1,0:T(8,128)(2,1)S(1)} %dynamic-slice_reduce_fusion), dimensions={1,2} | broadcast | bytes 655360 | tf_op jit(solution)/shard_map/broadcast_in_dim | solution.py:495
  48.3 4.2 %all-to-all-start.1 = ((bf16[4,512,128]{2,1,0:T(8,128)(2,1)}), bf16[4,512,128]{2,1,0:T(8,128)(2,1)S(1)}, u32[]{:S(2)}, u32[]{:S(2)}) async-start(bf16[4,512,128]{2,1,0:T(8,128)(2,1)} %broadcast_in_dim.2), calls=%async_computation.1 | async-start | bytes 1048576 | tf_op jit(solution)/shard_map/all_to_all | solution.py:494
  52.4 0.0 copy-done
  52.4 5.0 %update.1 = f32[2048,128]{1,0:T(8,128)} custom-call(s32[3]{0:T(128)S(1)} %copy-done.5, s32[16]{0:T(128)S(1)} %copy-done.7, f32[2048,128]{1,0:T(8,128)S(1)} %bitcast.31, f32[80,256]{1,0:T(8,128)S(1)} %get-tuple-element.16.refs_0_, f32[64,512]{1,0:T(8,128)S(1)} %get-tuple-element.17.refs_1_, f32[296,128]{1,0:T(8,128)S(1)} %collective-permute-done.refs_3_.refs_7_.refs_2_, ...), custom_call_target="tpu_custom_call" | custom-call | flops 16777216 | bytes 8388608 | tf_op jit(solution)/shard_map/update/pallas_call | solution.py:476
  57.4 3.9 %all-to-all-done.1.parts_ref = bf16[4,512,128]{2,1,0:T(8,128)(2,1)S(1)} async-done(((bf16[4,512,128]{2,1,0:T(8,128)(2,1)}), bf16[4,512,128]{2,1,0:T(8,128)(2,1)S(1)}, u32[]{:S(2)}, u32[]{:S(2)}) %all-to-all-start.1) | async-done | bytes 524320 | tf_op jit(solution)/shard_map/all_to_all | solution.py:494
  61.3 0.8 %finish.1 = bf16[512,128]{1,0:T(8,128)(2,1)S(1)} custom-call(s32[3]{0:T(128)S(1)} %copy-done.5, s32[16]{0:T(128)S(1)} %copy-done.8, bf16[1024,128]{1,0:T(8,128)(2,1)S(1)} %bitcast.33, bf16[4,512,128]{2,1,0:T(8,128)(2,1)S(1)} %all-to-all-done.1.parts_ref), custom_call_target="tpu_custom_call" | custom-call | bytes 524288 | tf_op jit(solution)/shard_map/finish/pallas_call | solution.py:497
  62.2 3.2 %all_gather.11 = bf16[16,4,2048]{2,1,0:T(4,128)(2,1)S(1)} all-gather(bf16[8,4,2048]{2,1,0:T(4,128)(2,1)S(1)} %bitcast.34), channel_id=1, replica_groups={{0,1},{2,3},{4,5},{6,7},{8,9},{10,11},{12,13},{14,15},{16,17},{18,19},{..., dimensions={0}, use_global_device_ids=true | all-gather | bytes 393216 | tf_op jit(solution)/shard_map/all_gather | solution.py:508
  65.3 0.7 %copy.27 = bf16[16,4,2048]{2,1,0:T(4,128)(2,1)} copy(bf16[16,4,2048]{2,1,0:T(4,128)(2,1)S(1)} %all_gather.11) | data formatting | bytes 524288
  (1 shorter events, 0.0 us)
Async XLA Ops:
  4.4 30.4 %copy-start.1 = (bf16[16,4,2048]{2,1,0:T(4,128)(2,1)S(1)}, bf16[16,4,2048]{2,1,0:T(4,128)(2,1)}, u32[]{:S(2)}) copy-start(bf16[16,4,2048]{2,1,0:T(4,128)(2,1)} %param.16) | copy-start | bytes 786436
  4.4 30.4 %copy-start.2 = (f32[16,2048]{1,0:T(8,128)S(1)}, f32[16,2048]{1,0:T(8,128)}, u32[]{:S(2)}) copy-start(f32[16,2048]{1,0:T(8,128)} %refs_2_.2) | copy-start | bytes 393220
  4.4 30.4 %copy-start.3 = (f32[4,2048]{1,0:T(4,128)S(1)}, f32[4,2048]{1,0:T(4,128)}, u32[]{:S(2)}) copy-start(f32[4,2048]{1,0:T(4,128)} %refs_5_.1) | copy-start | bytes 98308
  4.5 35.0 %all-to-all-start = ((bf16[8,64,256]{2,1,0:T(8,128)(2,1)}), bf16[8,64,256]{2,1,0:T(8,128)(2,1)S(1)}, u32[]{:S(2)}, u32[]{:S(2)}) async-start(bf16[8,64,256]{2,1,0:T(8,128)(2,1)} %get-tuple-element.13), calls=%async_computation | async-start | bytes 524288 | tf_op jit(solution)/shard_map/all_to_all | solution.py:438
  14.8 20.1 %copy-start.6 = (f32[2048]{0:T(1024)S(1)}, f32[2048]{0:T(1024)}, u32[]{:S(2)}) copy-start(f32[2048]{0:T(1024)} %param.21) | copy-start | bytes 24580
  14.8 13.0 %collective-permute-start.1 = (f32[296,128]{1,0:T(8,128)}, f32[296,128]{1,0:T(8,128)S(1)}, u32[]{:S(2)}, u32[]{:S(2)}) collective-permute-start(f32[296,128]{1,0:T(8,128)} %get-tuple-element.11), channel_id=1, source_target_pairs={{8,0},{16,8},{24,16},{32,24},{40,32},{48,40},{56,48},{64,56},{72,6... | collective-permute-start | bytes 454664 | tf_op jit(solution)/shard_map/ppermute | solution.py:437
  24.0 10.8 %collective-permute-start = (f32[296,128]{1,0:T(8,128)}, f32[296,128]{1,0:T(8,128)S(1)}, u32[]{:S(2)}, u32[]{:S(2)}) collective-permute-start(f32[296,128]{1,0:T(8,128)} %get-tuple-element.11), channel_id=1, source_target_pairs={{0,8},{8,16},{16,24},{24,32},{32,40},{40,48},{48,56},{56,64},{64,7... | collective-permute-start | bytes 454664 | tf_op jit(solution)/shard_map/ppermute | solution.py:436
  34.8 0.7 %copy-start.5 = (s32[3]{0:T(128)S(1)}, s32[3]{0:T(128)}, u32[]{:S(2)}) copy-start(s32[3]{0:T(128)} %pad_add_fusion.where_ref) | copy-start | bytes 40
  34.8 0.7 %copy-start.7 = (s32[16]{0:T(128)S(1)}, s32[16]{0:T(128)}, u32[]{:S(2)}) copy-start(s32[16]{0:T(128)} %lookup_ref.5) | copy-start | bytes 196
  34.8 0.7 %copy-start.8 = (s32[16]{0:T(128)S(1)}, s32[16]{0:T(128)}, u32[]{:S(2)}) copy-start(s32[16]{0:T(128)} %tally_ref.5) | copy-start | bytes 196
  35.5 3.9 %copy-start.4 = (bf16[64,256]{1,0:T(8,128)(2,1)S(1)}, bf16[64,256]{1,0:T(8,128)(2,1)}, u32[]{:S(2)}) copy-start(bf16[64,256]{1,0:T(8,128)(2,1)} %refs_2_.3) | copy-start | bytes 98308
  35.5 3.9 %copy-start.10 = (f32[256]{0:T(256)S(1)}, f32[256]{0:T(256)}, u32[]{:S(2)}) copy-start(f32[256]{0:T(256)} %param.29) | copy-start | bytes 3076
  35.5 3.9 %copy-start.11 = (f32[256]{0:T(256)S(1)}, f32[256]{0:T(256)}, u32[]{:S(2)}) copy-start(f32[256]{0:T(256)} %param.30) | copy-start | bytes 3076
  39.4 0.7 %copy-start.9 = (f32[256]{0:T(256)S(1)}, f32[256]{0:T(256)}, u32[]{:S(2)}) copy-start(f32[256]{0:T(256)} %param.28) | copy-start | bytes 3076
  47.3 5.1 %copy-start = (f32[16,4,4096]{2,1,0:T(4,128)S(1)}, f32[16,4,4096]{2,1,0:T(4,128)}, u32[]{:S(2)}) copy-start(f32[16,4,4096]{2,1,0:T(4,128)} %param.19) | copy-start | bytes 3145732
  48.3 13.1 %all-to-all-start.1 = ((bf16[4,512,128]{2,1,0:T(8,128)(2,1)}), bf16[4,512,128]{2,1,0:T(8,128)(2,1)S(1)}, u32[]{:S(2)}, u32[]{:S(2)}) async-start(bf16[4,512,128]{2,1,0:T(8,128)(2,1)} %broadcast_in_dim.2), calls=%async_computation.1 | async-start | bytes 1048576 | tf_op jit(solution)/shard_map/all_to_all | solution.py:494

commit v4 on v3

--- a/solution.py
+++ b/solution.py
@@ -67,14 +67,21 @@
         copy.start()
 
 
-def pack_kernel(where_ref, lookup_hbm, mem_ref, prev_ref, left_ref, out_ref, left_out, lookup_ref, prev, left, tile, sems):
-    loads = [
-        pltpu.make_async_copy(lookup_hbm, lookup_ref, sems.at[0]),
-        pltpu.make_async_copy(prev_ref, prev, sems.at[1]),
-        pltpu.make_async_copy(left_ref, left, sems.at[2]),
-    ]
+def place():
+    count = lax.axis_size("seq")
+    me = lax.axis_index("seq")
+    return me, jnp.where(me == 0, count - 1, me - 1)
+
+
+def pack_kernel(lookup_hbm, mem_hbm, prev_hbm, left_hbm, out_ref, left_out, lookup_ref, mem, prev, left, sems):
+    loads = copies(
+        (lookup_hbm, left_hbm, prev_hbm, mem_hbm), (lookup_ref, left, prev, mem), sems
+    )
     start(loads)
-    first = where_ref[0] * SLOTS
+    first = place()[0] * SLOTS
+    loads[1].wait()
+    spread = [pltpu.make_async_copy(left, left_out.at[n], sems.at[4 + n]) for n in range(left_out.shape[0])]
+    start(spread)
     loads[0].wait()
     kept = jnp.int32(0)
     for q in range(SLOTS):
@@ -85,30 +92,17 @@
     for s in range(SLOTS):
         high = jnp.where((kept >> s) & 1 == 0, s, high)
         low = jnp.where((kept >> (SLOTS - 1 - s)) & 1 == 0, SLOTS - 1 - s, low)
-    moves = [
-        pltpu.make_async_copy(
-            mem_ref.at[pl.ds(pl.multiple_of(slot * STATE_ROWS, STATE_ROWS), STATE_ROWS), :],
-            tile.at[pl.ds(n * PIECE, STATE_ROWS), :],
-            sems.at[3 + n],
-        )
-        for n, slot in enumerate((low, high))
-    ]
-    start(moves)
+    out_ref[2 * PIECE :, :] = jnp.where(iota((8, 128), 0) == 0, first + low, first + high).astype(F32)
     loads[2].wait()
-    spread = [pltpu.make_async_copy(left, left_out.at[n], sems.at[8 + n]) for n in range(left_out.shape[0])]
-    start(spread)
-    tile[2 * PIECE :, :] = jnp.where(iota((8, 128), 0) == 0, first + low, first + high).astype(F32)
-    loads[1].wait()
     for n, slot in enumerate((low, high)):
         row = prev[pl.ds(slot, 1), :]
         at = n * PIECE + STATE_ROWS
         for c in range(TILES):
-            tile[at + c : at + c + 1, :] = row[:, c * 128 : (c + 1) * 128]
-    moves[0].wait()
-    moves[1].wait()
-    done = pltpu.make_async_copy(tile, out_ref, sems.at[5])
-    done.start()
-    done.wait()
+            out_ref[at + c : at + c + 1, :] = row[:, c * 128 : (c + 1) * 128]
+    loads[3].wait()
+    for n, slot in enumerate((low, high)):
+        begin = pl.multiple_of(slot * STATE_ROWS, STATE_ROWS)
+        out_ref[n * PIECE : n * PIECE + STATE_ROWS, :] = mem[pl.ds(begin, STATE_ROWS), :]
     for copy in spread:
         copy.wait()
 
@@ -118,12 +112,12 @@
     return jnp.where(is_low, recv_ref[begin : begin + count, :], recv_ref[PIECE + begin : PIECE + begin + count, :])
 
 
-def sources(where_ref, lookup_ref, q):
+def sources(where, lookup_ref, q):
     wanted = lookup_ref[q]
     owner = wanted // SLOTS
-    own = owner == where_ref[0]
-    before = owner == where_ref[1]
-    at = jnp.where(own, wanted - where_ref[0] * SLOTS, 0)
+    own = owner == where[0]
+    before = owner == where[1]
+    at = jnp.where(own, wanted - where[0] * SLOTS, 0)
     return wanted, own, before, at
 
 
@@ -131,10 +125,10 @@
     return [pltpu.make_async_copy(a, b, sems.at[n]) for n, (a, b) in enumerate(zip(sources_, targets))]
 
 
-def state_copies(where_ref, lookup_ref, mem_hbm, state, sems):
+def state_copies(where, lookup_ref, mem_hbm, state, sems):
     out = []
     for q in range(SLOTS):
-        at = sources(where_ref, lookup_ref, q)[3]
+        at = sources(where, lookup_ref, q)[3]
         out.append(
             pltpu.make_async_copy(
                 mem_hbm.at[pl.ds(pl.multiple_of(at * STATE_ROWS, STATE_ROWS), STATE_ROWS), :],
@@ -145,9 +139,9 @@
     return out
 
 
-def place_received(where_ref, lookup_ref, from_before, from_after, state):
-    for q in range(SLOTS):
-        wanted, own, before, _ = sources(where_ref, lookup_ref, q)
+def place_received(where, lookup_ref, from_before, from_after, state):
+    for q in range(SLOTS):
+        wanted, own, before, _ = sources(where, lookup_ref, q)
         here = slice(q * STATE_ROWS, (q + 1) * STATE_ROWS)
 
         @pl.when(jnp.logical_not(own) & before)
@@ -163,13 +157,9 @@
     return a[t * SLOTS : (t + 1) * SLOTS, :]
 
 
-def project_kernel(where_ref, lookup_ref, tally_ref, *refs):
-    count = 9
-    hbm, (rkv_ref, mixed_ref, last_ref), bufs = refs[:count], refs[count : count + 3], refs[count + 3 : 2 * count + 3]
-    x32, shift, sems = refs[2 * count + 3 :]
-    loads = copies(hbm, bufs, sems)
+def norm_kernel(tally_ref, x_hbm, gain_hbm, xn_ref, last_ref, x_ref, gain_ref, x32, sems):
+    loads = copies((x_hbm, gain_hbm), (x_ref, gain_ref), sems)
     start(loads)
-    x_ref, gain_ref, prev_ref, from_before, from_after, blend_ref = bufs[:6]
     loads[0].wait()
     loads[1].wait()
     x32[...] = x_ref[...].astype(F32)
@@ -185,10 +175,28 @@
     for t in range(1, STEPS):
         last = jnp.where(tally == t + 1, normed[t], last)
     last_ref[...] = last
-    for n in range(2, 6):
+    for t in range(STEPS):
+        xn_ref[t * SLOTS : (t + 1) * SLOTS, :] = normed[t]
+
+
+def main_kernel(lookup_ref, tally_ref, mem_hbm, *refs):
+    count = 14
+    hbm, (part_ref, moved_ref, doubled_ref) = refs[:count], refs[count : count + 3]
+    bufs = refs[count + 3 : 2 * count + 3]
+    shift, state, reads, heads, part, sems, state_sems = refs[2 * count + 3 :]
+    where = place()
+    loads = copies(hbm, bufs, sems)
+    start(loads[:-1])
+    state_loads = state_copies(where, lookup_ref, mem_hbm, state, state_sems)
+    start(state_loads)
+    loads[-1].start()
+    xn_ref, prev_ref, from_before, from_after, blend_ref = bufs[:5]
+    left_ref, right_ref, base_ref, boost_ref, team_ref, final_ref = bufs[8:]
+    tally = column_of(tally_ref, (SLOTS, 128))[:, :1]
+    for n in range(5):
         loads[n].wait()
     for q in range(SLOTS):
-        wanted, own, before, at = sources(where_ref, lookup_ref, q)
+        wanted, own, before, at = sources(where, lookup_ref, q)
 
         @pl.when(own)
         def _():
@@ -202,44 +210,30 @@
             for c in range(TILES):
                 shift[q : q + 1, c * 128 : (c + 1) * 128] = rows[c : c + 1, :]
 
-    xn = jnp.concatenate(normed, axis=0)
-    change = jnp.concatenate([shift[...]] + normed[:-1], axis=0) - xn
+    xn = xn_ref[...]
+    change = jnp.concatenate([shift[...], xn[: (STEPS - 1) * SLOTS, :]], axis=0) - xn
 
     def mix(which):
         return (xn + change * blend_ref[which : which + 1, :]).astype(BF16)
 
-    mixed_ref[...] = mix(3)
+    mixed_rows = mix(3)
+    rkv = []
     for n in range(3):
-        loads[6 + n].wait()
-        rkv_ref[n] = dot(mix(n), bufs[6 + n][...])
-
-
-def step_kernel(where_ref, lookup_ref, tally_ref, mem_hbm, *refs):
-    count = 10
-    hbm, (part_ref, moved_ref, doubled_ref) = refs[:count], refs[count : count + 3]
-    bufs = refs[count + 3 : 2 * count + 3]
-    state, reads, heads, part, sems, state_sems = refs[2 * count + 3 :]
-    loads = copies(hbm, bufs, sems)
-    start(loads)
-    state_loads = state_copies(where_ref, lookup_ref, mem_hbm, state, state_sems)
-    start(state_loads)
-    (
-        mixed_ref, left_ref, right_ref, base_ref, boost_ref, team_ref, rkv_ref, from_before, from_after, final_ref,
-    ) = bufs
-    for n in range(7):
+        loads[5 + n].wait()
+        rkv.append(dot(mix(n), bufs[5 + n][...]))
+    for n in range(8, 13):
         loads[n].wait()
-    tally = column_of(tally_ref, (SLOTS, 128))[:, :1]
     pre = jnp.zeros((ROWS, left_ref.shape[1]), F32)
     chunk = left_ref.shape[2]
     for n in range(left_ref.shape[0]):
         pre = pre + lax.dot_general(
-            mixed_ref[:, n * chunk : (n + 1) * chunk], left_ref[n], (((1,), (1,)), ((), ())), preferred_element_type=F32
+            mixed_rows[:, n * chunk : (n + 1) * chunk], left_ref[n], (((1,), (1,)), ((), ())), preferred_element_type=F32
         )
     lora = jnp.tanh(pre).astype(BF16)
     decay = jnp.exp(-jnp.exp(row_of(base_ref) + dot(lora, right_ref[...])))
-    r = [cut(rkv_ref[0], t) for t in range(STEPS)]
-    k = [cut(rkv_ref[1], t) for t in range(STEPS)]
-    v = [cut(rkv_ref[2], t) for t in range(STEPS)]
+    r = [cut(rkv[0], t) for t in range(STEPS)]
+    k = [cut(rkv[1], t) for t in range(STEPS)]
+    v = [cut(rkv[2], t) for t in range(STEPS)]
     d = [jnp.where(tally > t, cut(decay, t), 1.0) for t in range(STEPS)]
     kept = [jnp.where(tally > t, k[t], 0.0) for t in range(STEPS)]
     boost = row_of(boost_ref)
@@ -275,7 +269,7 @@
     moved_ref[...] = moved[STEPS * SLOTS :, :]
     rowd, cold = iota((LOCAL, HEADS * 128), 0), iota((LOCAL, HEADS * 128), 1)
     double = (rowd == (cold // 128) * HEAD + cold % HEAD).astype(BF16)
-    doubled_ref[...] = dot(rkv_ref[2].astype(BF16), double)
+    doubled_ref[...] = dot(rkv[2].astype(BF16), double)
 
     lane = iota((SLOTS, 128), 1)
     for h in range(HEADS):
@@ -284,9 +278,9 @@
             for t in range(STEPS):
                 at = pl.ds(t * 8 + p * HEADS + h, SLOTS, stride=STEPS * 8)
                 reads[at, :] = jnp.where(head_lane, cut(moved, t)[:, p * 128 : (p + 1) * 128], 0.0)
-    for copy in loads[7:9] + state_loads:
+    for copy in state_loads:
         copy.wait()
-    place_received(where_ref, lookup_ref, from_before, from_after, state)
+    place_received(where, lookup_ref, from_before, from_after, state)
     for q in range(SLOTS):
         rows = slice(q * STEPS * 8, (q + 1) * STEPS * 8)
         now = state[q * STATE_ROWS : (q + 1) * STATE_ROWS, :]
@@ -307,7 +301,7 @@
     center = y - dot_split(y, same_head) * (1.0 / HEAD)
     spread = dot_split(center * center, same_head) * (1.0 / HEAD)
     g = (center * lax.rsqrt(spread + EPS) * row_of(team_ref)).astype(BF16)
-    loads[9].wait()
+    loads[13].wait()
     proj = dot(g, final_ref[...])
     for t in range(STEPS):
         for c in range(TILES):
@@ -315,13 +309,14 @@
     part_ref[...] = part[...].astype(BF16)
 
 
-def update_kernel(where_ref, lookup_ref, mem_hbm, *refs):
+def update_kernel(lookup_ref, mem_hbm, *refs):
     count = 4
     hbm, new_hbm, bufs = refs[:count], refs[count], refs[count + 1 : 2 * count + 1]
     state, keys, vals, decays, fresh, sems, state_sems, new_sems = refs[2 * count + 1 :]
+    where = place()
     loads = copies(hbm, bufs, sems)
     start(loads)
-    state_loads = state_copies(where_ref, lookup_ref, mem_hbm, state, state_sems)
+    state_loads = state_copies(where, lookup_ref, mem_hbm, state, state_sems)
     start(state_loads)
     moved_ref, doubled_ref, from_before, from_after = bufs
     loads[0].wait()
@@ -343,7 +338,7 @@
     ones = ((iota((16, 128), 0) // HEADS) % 2 == iota((16, 128), 1) // HEAD).astype(BF16)
     for copy in loads[2:] + state_loads:
         copy.wait()
-    place_received(where_ref, lookup_ref, from_before, from_after, state)
+    place_received(where, lookup_ref, from_before, from_after, state)
     news = []
     for q in range(SLOTS):
         here = slice(q * STATE_ROWS, (q + 1) * STATE_ROWS)
@@ -357,9 +352,10 @@
         copy.wait()
 
 
-def finish_kernel(where_ref, tally_ref, x_hbm, parts_ref, out_ref, x_ref, sem):
+def finish_kernel(tally_ref, x_hbm, parts_ref, out_ref, x_ref, sem):
     rows = out_ref.shape[0]
-    begin = where_ref[2] * rows
+    core = lax.axis_index("tensor") % 2
+    begin = core * rows
     load = pltpu.make_async_copy(x_hbm.at[pl.ds(pl.multiple_of(begin, rows), rows), :], x_ref, sem)
     load.start()
     step = iota((STEPS * TILES, 128), 0) % STEPS
@@ -369,7 +365,7 @@
         total = x_ref[here, :].astype(F32)
         for n in range(parts_ref.shape[0]):
             total = total + parts_ref[n, here, :].astype(F32)
-        tally = tally_ref[where_ref[2] * (rows // (STEPS * TILES)) + q]
+        tally = tally_ref[core * (rows // (STEPS * TILES)) + q]
         out_ref[here, :] = jnp.where(step < tally, total, 0.0).astype(BF16)
 
 
@@ -406,9 +402,7 @@
 ):
     rings = lax.axis_size("seq")
     teams = lax.axis_size("tensor")
-    device = lax.axis_index("seq")
     core = lax.axis_index("tensor") % 2
-    where = jnp.stack([device, (device + rings - 1) % rings, core]).astype(jnp.int32)
     x = tiles_view(layer_entry_vectors)
     mem = tiles_view(memory_matrices)
     prev = previous_standardized_entries
@@ -423,60 +417,55 @@
     packed, left = pl.pallas_call(
         pack_kernel,
         out_shape=[shape((PACK_ROWS, 128), F32), shape((teams,) + left_t.shape, BF16)],
-        in_specs=spec(pltpu.SMEM, 1) + spec(pl.ANY, 4),
-        out_specs=spec(pl.ANY, 2),
-        scratch_shapes=[
-            pltpu.SMEM(lookup.shape, jnp.int32), scratch(prev.shape, F32), scratch(left_t.shape, BF16),
-            scratch((PACK_ROWS, 128), F32), dma((8 + teams,)),
-        ],
+        in_specs=spec(pl.ANY, 4),
+        out_specs=spec(pltpu.VMEM, 1) + spec(pl.ANY, 1),
+        scratch_shapes=[pltpu.SMEM(lookup.shape, jnp.int32)] + like([mem, prev, left_t]) + [dma((4 + teams,))],
         compiler_params=params(PACK_MIB),
         cost_estimate=cost(0, 1 << 20),
         name="pack",
-    )(where, lookup, mem, prev, left_t)
+    )(lookup, mem, prev, left_t)
     from_before = lax.ppermute(packed, "seq", [(i, (i + 1) % rings) for i in range(rings)])
     from_after = lax.ppermute(packed, "seq", [((i + 1) % rings, i) for i in range(rings)])
     left = lax.all_to_all(left, "tensor", 0, 0)
 
+    gain = entry_standardize_scale.reshape(TILES, 128)
+    xn, new_shifts = pl.pallas_call(
+        norm_kernel,
+        out_shape=[shape((ROWS, WIDTH), F32), shape((SLOTS, WIDTH), F32)],
+        in_specs=spec(pltpu.SMEM, 1) + spec(pl.ANY, 2),
+        out_specs=spec(pltpu.VMEM, 2),
+        scratch_shapes=like([x, gain]) + [scratch((ROWS * TILES, 128), F32), dma((2,))],
+        compiler_params=params(MAIN_MIB),
+        cost_estimate=cost(0, 4 << 20),
+        name="norm",
+    )(tally, x, gain)
+
     operands = [
-        x, entry_standardize_scale.reshape(TILES, 128), prev, from_before, from_after, blend_coefficients,
+        xn, prev, from_before, from_after, blend_coefficients,
         acceptance_projection_matrix, lookup_projection_matrix, payload_projection_matrix,
-    ]
-    rkv, mixed_rows, new_shifts = pl.pallas_call(
-        project_kernel,
-        out_shape=[shape((3, ROWS, LOCAL), F32), shape((ROWS, WIDTH), BF16), shape((SLOTS, WIDTH), F32)],
-        in_specs=spec(pltpu.SMEM, 3) + spec(pl.ANY, len(operands)),
-        out_specs=spec(pltpu.VMEM, 3),
-        scratch_shapes=like(operands)
-        + [scratch((ROWS * TILES, 128), F32), scratch((SLOTS, WIDTH), F32), dma((len(operands),))],
-        compiler_params=params(MAIN_MIB),
-        cost_estimate=cost(6 * ROWS * WIDTH * LOCAL, 8 << 20),
-        name="project",
-    )(where, lookup, tally, *operands)
-
-    operands = [
-        mixed_rows, left, forget_map_right_matrix, feature_forget_logloglevel.reshape(2, 128),
-        present_token_boost.reshape(2, 128), team_standardize_scale.reshape(2, 128), rkv, from_before, from_after,
-        final_projection_matrix,
+        left, forget_map_right_matrix, feature_forget_logloglevel.reshape(2, 128),
+        present_token_boost.reshape(2, 128), team_standardize_scale.reshape(2, 128), final_projection_matrix,
     ]
     part, moved, doubled = pl.pallas_call(
-        step_kernel,
+        main_kernel,
         out_shape=[
             shape((ROWS * TILES, 128), BF16), shape((ROWS + SLOTS, LOCAL), F32), shape((ROWS, HEADS * 128), F32),
         ],
-        in_specs=spec(pltpu.SMEM, 3) + spec(pl.ANY, 1 + len(operands)),
+        in_specs=spec(pltpu.SMEM, 2) + spec(pl.ANY, 1 + len(operands)),
         out_specs=spec(pltpu.VMEM, 3),
         scratch_shapes=like(operands)
-        + [state_buf, rows_buf, rows_buf, scratch((ROWS * TILES, 128), F32), dma((len(operands),)), dma((SLOTS,))],
+        + [scratch((SLOTS, WIDTH), F32), state_buf, rows_buf, rows_buf, scratch((ROWS * TILES, 128), F32)]
+        + [dma((len(operands),)), dma((SLOTS,))],
         compiler_params=params(MAIN_MIB),
-        cost_estimate=cost(2 * ROWS * WIDTH * LOCAL, 4 << 20),
-        name="step",
-    )(where, lookup, tally, mem, *operands)
+        cost_estimate=cost(8 * ROWS * WIDTH * LOCAL, 8 << 20),
+        name="main",
+    )(lookup, tally, mem, *operands)
 
     operands = [moved, doubled, from_before, from_after]
     new_states = pl.pallas_call(
         update_kernel,
         out_shape=shape((SLOTS * STATE_ROWS, 128), F32),
-        in_specs=spec(pltpu.SMEM, 2) + spec(pl.ANY, 1 + len(operands)),
+        in_specs=spec(pltpu.SMEM, 1) + spec(pl.ANY, 1 + len(operands)),
         out_specs=spec(pl.ANY, 1)[0],
         scratch_shapes=like(operands)
         + [state_buf, rows_buf, rows_buf, scratch((SLOTS * 16, 128), F32), state_buf]
@@ -484,7 +473,7 @@
         compiler_params=params(MAIN_MIB),
         cost_estimate=cost(1 << 24, 8 << 20),
         name="update",
-    )(where, lookup, mem, *operands)
+    )(lookup, mem, *operands)
 
     pairs = [[2 * i, 2 * i + 1] for i in range(teams // 2)]
     chips = [[2 * i + c for i in range(teams // 2)] for c in range(2)]
@@ -497,13 +486,13 @@
     mixed = pl.pallas_call(
         finish_kernel,
         out_shape=shape((half, 128), BF16),
-        in_specs=spec(pltpu.SMEM, 2) + spec(pl.ANY, 1) + spec(pltpu.VMEM, 1),
+        in_specs=spec(pltpu.SMEM, 1) + spec(pl.ANY, 1) + spec(pltpu.VMEM, 1),
         out_specs=spec(pltpu.VMEM, 1)[0],
         scratch_shapes=[scratch((half, 128), BF16), dma],
         compiler_params=params(8),
         cost_estimate=cost(0, 1 << 19),
         name="finish",
-    )(where, tally, x, spread)
+    )(tally, x, spread)
     mixed = tiles_back(mixed, SLOTS // 2, STEPS, WIDTH)
     mixed = lax.all_gather(mixed, "tensor", axis_index_groups=pairs, tiled=True)
     return (

time: 66.5 us -> 61.9 us (0.931)
  waiting for transfers between devices: 12.8 us -> 9.87 us
  Pallas kernels: 17.3 us -> 16.2 us
    ppermute x1, waiting for transfers between devices: 1.86 us -> 0.01 us  [shards(): lax.ppermute(packed, 'seq', [((i + 1) % rings, i) for i in range(rings)])]
    ppermute x1, waiting for transfers between devices: 7.01 us -> 5.99 us  [shards(): lax.ppermute(packed, 'seq', [(i, (i + 1) % rings) for i in range(rings)])]
    pallas_call x1, Pallas kernels: 3.09 us -> 2.22 us  [shards(): pl.pallas_call(pack_kernel, out_shape=[shape((PACK_ROWS, 128), F32), shap...]
    another operation x1 -> x0, other arithmetic: 0.67 us -> none  [shards(): jnp.stack([device, (device + rings - 1) % rings, core]).astype(jnp.int32)]
  transfers between devices with their start and end apart: 4 -> 4, of which waited for: 3 -> 2; matrix products, arithmetic and copies ran while one was open for 0% -> 0% of each run, Pallas kernels for 13% -> 11%
where the time goes in v4:
time: 61.9 us; the launch traced here: 61.4 us
  starting transfers between devices  25.5 us (41%)
  Pallas kernels  16.2 us (26%)
  waiting for transfers between devices  9.87 us (16%)
  blocking collectives  6.09 us (10%)
  local copies, waits for them, and re-layouts  2.93 us (5%)
  between operations  0.81 us (1%)
    all_to_all x1, starting transfers between devices, shards(): left = lax.all_to_all(left, 'tensor', 0, 0)  10.3 us
    ppermute x1, starting transfers between devices, shards(): lax.ppermute(packed, 'seq', [((i + 1) % rings, i) for i in range(rings)])  9.08 us
    pallas_call x1, Pallas kernels, shards(): pl.pallas_call(main_kernel, out_shape=[shape((ROWS * TILES, 128), BF16),...  6.36 us
    ppermute x1, waiting for transfers between devices, shards(): lax.ppermute(packed, 'seq', [(i, (i + 1) % rings) for i in range(rings)])  5.99 us
    pallas_call x1, Pallas kernels, shards(): pl.pallas_call(update_kernel, out_shape=shape((SLOTS * STATE_ROWS, 128),...  5.02 us
    all_to_all x1, starting transfers between devices, shards(): lax.all_to_all(jnp.broadcast_to(mine[None], (teams // 2,) + mine.shape),...  4.16 us
    all_to_all x1, waiting for transfers between devices, shards(): lax.all_to_all(jnp.broadcast_to(mine[None], (teams // 2,) + mine.shape),...  3.87 us
    all_gather x1, blocking collectives, shards(): mixed = lax.all_gather(mixed, 'tensor', axis_index_groups=pairs, tiled=True)  3.16 us
  transfers between devices with their start and end apart: 4, of which 2 were waited for; matrix products, arithmetic and copies ran while one was open for 0% of the time, Pallas kernels for 11%

profile of v4, /device:TPU:1, one launch (start us, length us, event | category | flops | bytes accessed | tf_op | source)
XLA Modules:
  0.0 61.4 jit_solution(15271184363941478458)
XLA Ops:
  0.6 2.2 %pack.1 = (f32[296,128]{1,0:T(8,128)}, bf16[8,64,256]{2,1,0:T(8,128)(2,1)}) custom-call(s32[16]{0:T(128)} %lookup_ref.3, f32[2048,128]{1,0:T(8,128)} %bitcast.26, f32[16,2048]{1,0:T(8,128)} %refs_1_.1, bf16[64,256]{1,0:T(8,128)(2,1)} %bitcast.38), custom_call_target="tpu_custom_call" | custom-call | bytes 1048576 | tf_op jit(solution)/shard_map/pack/pallas_call | solution.py:417
  2.9 0.0 copy-start.11
  2.9 0.0 copy-start.1
  2.9 10.3 %all-to-all-start = ((bf16[8,64,256]{2,1,0:T(8,128)(2,1)}), bf16[8,64,256]{2,1,0:T(8,128)(2,1)S(1)}, u32[]{:S(2)}, u32[]{:S(2)}) async-start(bf16[8,64,256]{2,1,0:T(8,128)(2,1)} %get-tuple-element.12), calls=%async_computation | async-start | bytes 524288 | tf_op jit(solution)/shard_map/all_to_all | solution.py:429
  13.2 0.0 copy-done.11
  13.2 9.1 %collective-permute-start.1 = (f32[296,128]{1,0:T(8,128)S(1)}, f32[296,128]{1,0:T(8,128)S(1)}, u32[]{:S(2)}, u32[]{:S(2)}) collective-permute-start(f32[296,128]{1,0:T(8,128)S(1)} %copy-done.11), channel_id=1, source_target_pairs={{8,0},{16,8},{24,16},{32,24},{40,32},{48,40},{56,48},{64,56},{72,6... | collective-permute-start | bytes 454664 | tf_op jit(solution)/shard_map/ppermute | solution.py:428
  22.3 1.9 %collective-permute-start = (f32[296,128]{1,0:T(8,128)S(1)}, f32[296,128]{1,0:T(8,128)S(1)}, u32[]{:S(2)}, u32[]{:S(2)}) collective-permute-start(f32[296,128]{1,0:T(8,128)S(1)} %copy-done.11), channel_id=1, source_target_pairs={{0,8},{8,16},{16,24},{24,32},{32,40},{40,48},{48,56},{56,64},{64,7... | collective-permute-start | bytes 454664 | tf_op jit(solution)/shard_map/ppermute | solution.py:427
  24.2 0.0 copy-start.5
  24.3 0.0 copy-start.6
  24.3 0.0 copy-done.1
  24.3 0.7 %copy-done.5 = f32[2048]{0:T(1024)S(1)} copy-done((f32[2048]{0:T(1024)S(1)}, f32[2048]{0:T(1024)}, u32[]{:S(2)}) %copy-start.5) | copy-done | bytes 8216
  24.9 0.0 copy-done.6
  24.9 0.0 copy-start.2
  24.9 0.0 copy-start.3
  25.0 0.0 copy-start.4
  25.0 0.0 copy-start.9
  25.0 0.0 copy-start.10
  25.0 1.8 %norm.1 = (f32[64,2048]{1,0:T(8,128)S(1)}, f32[16,2048]{1,0:T(8,128)}) custom-call(s32[16]{0:T(128)S(1)} %copy-done.6, bf16[1024,128]{1,0:T(8,128)(2,1)S(1)} %bitcast.29, f32[16,128]{1,0:T(8,128)S(1)} %bitcast.32), custom_call_target="tpu_custom_call" | custom-call | bytes 4194304 | tf_op jit(solution)/shard_map/norm/pallas_call | solution.py:432
  26.8 0.0 collective-permute-done.1.refs_3_
  26.8 6.0 %collective-permute-done.refs_2_ = f32[296,128]{1,0:T(8,128)S(1)} collective-permute-done((f32[296,128]{1,0:T(8,128)S(1)}, f32[296,128]{1,0:T(8,128)S(1)}, u32[]{:S(2)}, u32[]{:S(2)}) %collective-permute-start) | collective-permute-done | bytes 151584 | tf_op jit(solution)/shard_map/ppermute | solution.py:427
  32.8 0.0 all-to-all-done.refs_8_
  32.8 0.0 copy-start.7
  32.8 0.0 copy-start.8
  32.8 0.0 copy-done.2
  32.8 0.0 copy-done.3
  32.8 0.0 copy-done.4
  32.8 0.0 copy-done.9
  32.8 0.0 copy-done.10
  32.8 0.6 copy-done.7
  33.4 0.0 copy-done.8
  33.5 6.4 %main.1 = (bf16[1024,128]{1,0:T(8,128)(2,1)S(1)}, f32[80,256]{1,0:T(8,128)S(1)}, f32[64,512]{1,0:T(8,128)S(1)}) custom-call(s32[16]{0:T(128)S(1)} %copy-done.7, s32[16]{0:T(128)S(1)} %copy-done.6, f32[2048,128]{1,0:T(8,128)} %bitcast.27, f32[64,2048]{1,0:T(8,128)S(1)} %get-tuple-element.10.refs_0_, f32[16,2048]{1,0:T(8,128)S(1)} %copy-done.2, ...), custom_call_target="tpu_custom_call" | custom-call | flops 268435456 | bytes 8388608 | tf_op jit(solution)/shard_map/main/pallas_call | solution.py:449
  39.8 2.9 %all-gather = bf16[2048,128]{1,0:T(8,128)(2,1)S(1)} all-gather(bf16[1024,128]{1,0:T(8,128)(2,1)S(1)} %get-tuple-element.13), channel_id=2, replica_groups={{0,1},{2,3},{4,5},{6,7},{8,9},{10,11},{12,13},{14,15},{16,17},{18,19},{..., dimensions={0}, use_global_device_ids=true | all-gather | bytes 786432 | tf_op jit(solution)/shard_map/all_gather | solution.py:481
  42.8 0.0 copy-start
  42.8 0.9 %broadcast_in_dim.2 = bf16[4,512,128]{2,1,0:T(8,128)(2,1)} broadcast(bf16[512,128]{1,0:T(8,128)(2,1)S(1)} %dynamic-slice_reduce_fusion), dimensions={1,2} | broadcast | bytes 655360 | tf_op jit(solution)/shard_map/broadcast_in_dim | solution.py:484
  43.7 4.2 %all-to-all-start.1 = ((bf16[4,512,128]{2,1,0:T(8,128)(2,1)}), bf16[4,512,128]{2,1,0:T(8,128)(2,1)S(1)}, u32[]{:S(2)}, u32[]{:S(2)}) async-start(bf16[4,512,128]{2,1,0:T(8,128)(2,1)} %broadcast_in_dim.2), calls=%async_computation.1 | async-start | bytes 1048576 | tf_op jit(solution)/shard_map/all_to_all | solution.py:483
  47.8 0.0 copy-done
  47.8 5.0 %update.1 = f32[2048,128]{1,0:T(8,128)} custom-call(s32[16]{0:T(128)S(1)} %copy-done.7, f32[2048,128]{1,0:T(8,128)S(1)} %bitcast.28, f32[80,256]{1,0:T(8,128)S(1)} %get-tuple-element.14.refs_0_, f32[64,512]{1,0:T(8,128)S(1)} %get-tuple-element.15.refs_1_, f32[296,128]{1,0:T(8,128)S(1)} %collective-permute-done.refs_2_, ...), custom_call_target="tpu_custom_call" | custom-call | flops 16777216 | bytes 8388608 | tf_op jit(solution)/shard_map/update/pallas_call | solution.py:465
  52.9 3.9 %all-to-all-done.1.parts_ref = bf16[4,512,128]{2,1,0:T(8,128)(2,1)S(1)} async-done(((bf16[4,512,128]{2,1,0:T(8,128)(2,1)}), bf16[4,512,128]{2,1,0:T(8,128)(2,1)S(1)}, u32[]{:S(2)}, u32[]{:S(2)}) %all-to-all-start.1) | async-done | bytes 524320 | tf_op jit(solution)/shard_map/all_to_all | solution.py:483
  56.7 0.8 %finish.1 = bf16[512,128]{1,0:T(8,128)(2,1)S(1)} custom-call(s32[16]{0:T(128)S(1)} %copy-done.6, bf16[1024,128]{1,0:T(8,128)(2,1)S(1)} %bitcast.30, bf16[4,512,128]{2,1,0:T(8,128)(2,1)S(1)} %all-to-all-done.1.parts_ref), custom_call_target="tpu_custom_call" | custom-call | bytes 524288 | tf_op jit(solution)/shard_map/finish/pallas_call | solution.py:486
  57.6 3.2 %all_gather.11 = bf16[16,4,2048]{2,1,0:T(4,128)(2,1)S(1)} all-gather(bf16[8,4,2048]{2,1,0:T(4,128)(2,1)S(1)} %bitcast.31), channel_id=1, replica_groups={{0,1},{2,3},{4,5},{6,7},{8,9},{10,11},{12,13},{14,15},{16,17},{18,19},{..., dimensions={0}, use_global_device_ids=true | all-gather | bytes 393216 | tf_op jit(solution)/shard_map/all_gather | solution.py:497
  60.7 0.7 %copy.27 = bf16[16,4,2048]{2,1,0:T(4,128)(2,1)} copy(bf16[16,4,2048]{2,1,0:T(4,128)(2,1)S(1)} %all_gather.11) | data formatting | bytes 524288
  (1 shorter events, 0.0 us)
Async XLA Ops:
  2.9 10.4 %copy-start.11 = (f32[296,128]{1,0:T(8,128)S(1)}, f32[296,128]{1,0:T(8,128)}, u32[]{:S(2)}) copy-start(f32[296,128]{1,0:T(8,128)} %get-tuple-element.11) | copy-start | bytes 454660
  2.9 21.4 %copy-start.1 = (bf16[16,4,2048]{2,1,0:T(4,128)(2,1)S(1)}, bf16[16,4,2048]{2,1,0:T(4,128)(2,1)}, u32[]{:S(2)}) copy-start(bf16[16,4,2048]{2,1,0:T(4,128)(2,1)} %param.16) | copy-start | bytes 786436
  2.9 29.9 %all-to-all-start = ((bf16[8,64,256]{2,1,0:T(8,128)(2,1)}), bf16[8,64,256]{2,1,0:T(8,128)(2,1)S(1)}, u32[]{:S(2)}, u32[]{:S(2)}) async-start(bf16[8,64,256]{2,1,0:T(8,128)(2,1)} %get-tuple-element.12), calls=%async_computation | async-start | bytes 524288 | tf_op jit(solution)/shard_map/all_to_all | solution.py:429
  13.2 13.5 %collective-permute-start.1 = (f32[296,128]{1,0:T(8,128)S(1)}, f32[296,128]{1,0:T(8,128)S(1)}, u32[]{:S(2)}, u32[]{:S(2)}) collective-permute-start(f32[296,128]{1,0:T(8,128)S(1)} %copy-done.11), channel_id=1, source_target_pairs={{8,0},{16,8},{24,16},{32,24},{40,32},{48,40},{56,48},{64,56},{72,6... | collective-permute-start | bytes 454664 | tf_op jit(solution)/shard_map/ppermute | solution.py:428
  22.3 10.4 %collective-permute-start = (f32[296,128]{1,0:T(8,128)S(1)}, f32[296,128]{1,0:T(8,128)S(1)}, u32[]{:S(2)}, u32[]{:S(2)}) collective-permute-start(f32[296,128]{1,0:T(8,128)S(1)} %copy-done.11), channel_id=1, source_target_pairs={{0,8},{8,16},{16,24},{24,32},{32,40},{40,48},{48,56},{56,64},{64,7... | collective-permute-start | bytes 454664 | tf_op jit(solution)/shard_map/ppermute | solution.py:427
  24.2 0.7 %copy-start.5 = (f32[2048]{0:T(1024)S(1)}, f32[2048]{0:T(1024)}, u32[]{:S(2)}) copy-start(f32[2048]{0:T(1024)} %param.21) | copy-start | bytes 24580
  24.3 0.7 %copy-start.6 = (s32[16]{0:T(128)S(1)}, s32[16]{0:T(128)}, u32[]{:S(2)}) copy-start(s32[16]{0:T(128)} %tally_ref.5) | copy-start | bytes 196
  24.9 7.8 %copy-start.2 = (f32[16,2048]{1,0:T(8,128)S(1)}, f32[16,2048]{1,0:T(8,128)}, u32[]{:S(2)}) copy-start(f32[16,2048]{1,0:T(8,128)} %refs_1_.1) | copy-start | bytes 393220
  24.9 7.8 %copy-start.3 = (f32[4,2048]{1,0:T(4,128)S(1)}, f32[4,2048]{1,0:T(4,128)}, u32[]{:S(2)}) copy-start(f32[4,2048]{1,0:T(4,128)} %refs_4_.1) | copy-start | bytes 98308
  25.0 7.8 %copy-start.4 = (bf16[64,256]{1,0:T(8,128)(2,1)S(1)}, bf16[64,256]{1,0:T(8,128)(2,1)}, u32[]{:S(2)}) copy-start(bf16[64,256]{1,0:T(8,128)(2,1)} %refs_9_.1) | copy-start | bytes 98308
  25.0 7.8 %copy-start.9 = (f32[256]{0:T(256)S(1)}, f32[256]{0:T(256)}, u32[]{:S(2)}) copy-start(f32[256]{0:T(256)} %param.29) | copy-start | bytes 3076
  25.0 7.8 %copy-start.10 = (f32[256]{0:T(256)S(1)}, f32[256]{0:T(256)}, u32[]{:S(2)}) copy-start(f32[256]{0:T(256)} %param.30) | copy-start | bytes 3076
  32.8 0.7 %copy-start.7 = (s32[16]{0:T(128)S(1)}, s32[16]{0:T(128)}, u32[]{:S(2)}) copy-start(s32[16]{0:T(128)} %lookup_ref.3) | copy-start | bytes 196
  32.8 0.7 %copy-start.8 = (f32[256]{0:T(256)S(1)}, f32[256]{0:T(256)}, u32[]{:S(2)}) copy-start(f32[256]{0:T(256)} %param.28) | copy-start | bytes 3076
  42.8 5.1 %copy-start = (f32[16,4,4096]{2,1,0:T(4,128)S(1)}, f32[16,4,4096]{2,1,0:T(4,128)}, u32[]{:S(2)}) copy-start(f32[16,4,4096]{2,1,0:T(4,128)} %param.19) | copy-start | bytes 3145732
  43.7 13.1 %all-to-all-start.1 = ((bf16[4,512,128]{2,1,0:T(8,128)(2,1)}), bf16[4,512,128]{2,1,0:T(8,128)(2,1)S(1)}, u32[]{:S(2)}, u32[]{:S(2)}) async-start(bf16[4,512,128]{2,1,0:T(8,128)(2,1)} %broadcast_in_dim.2), calls=%async_computation.1 | async-start | bytes 1048576 | tf_op jit(solution)/shard_map/all_to_all | solution.py:483

commit v5 on v4

--- a/solution.py
+++ b/solution.py
@@ -20,7 +20,7 @@
 ROWS = SLOTS * STEPS
 STATE_ROWS = HEADS * HEAD * HEAD // 128
 PIECE = STATE_ROWS + TILES
-PACK_ROWS = 2 * PIECE + 8
+PACK_ROWS = 2 * PIECE + 16
 PACK_MIB, MAIN_MIB = 60, 52
 
 
@@ -73,15 +73,13 @@
     return me, jnp.where(me == 0, count - 1, me - 1)
 
 
-def pack_kernel(lookup_hbm, mem_hbm, prev_hbm, left_hbm, out_ref, left_out, lookup_ref, mem, prev, left, sems):
-    loads = copies(
-        (lookup_hbm, left_hbm, prev_hbm, mem_hbm), (lookup_ref, left, prev, mem), sems
-    )
+def pack_kernel(lookup_hbm, prev_hbm, mem_hbm, left_hbm, out_ref, left_out, lookup_ref, prev, mem, left, tile, sems):
+    loads = copies((lookup_hbm, prev_hbm, mem_hbm, left_hbm), (lookup_ref, prev, mem, left), sems)
     start(loads)
     first = place()[0] * SLOTS
-    loads[1].wait()
-    spread = [pltpu.make_async_copy(left, left_out.at[n], sems.at[4 + n]) for n in range(left_out.shape[0])]
-    start(spread)
+    loads[3].wait()
+    sends = [pltpu.make_async_copy(left, left_out.at[n], sems.at[4 + n]) for n in range(left_out.shape[0])]
+    start(sends)
     loads[0].wait()
     kept = jnp.int32(0)
     for q in range(SLOTS):
@@ -92,24 +90,26 @@
     for s in range(SLOTS):
         high = jnp.where((kept >> s) & 1 == 0, s, high)
         low = jnp.where((kept >> (SLOTS - 1 - s)) & 1 == 0, SLOTS - 1 - s, low)
-    out_ref[2 * PIECE :, :] = jnp.where(iota((8, 128), 0) == 0, first + low, first + high).astype(F32)
+    out_ref[2 * PIECE :, :] = jnp.full((16, 128), low, jnp.int32).astype(F32).astype(BF16)
+    loads[1].wait()
+    for n, slot in enumerate((low, high)):
+        row = prev[pl.ds(slot, 1), :]
+        for c in range(TILES):
+            tile[n * TILES + c : n * TILES + c + 1, :] = row[:, c * 128 : (c + 1) * 128]
     loads[2].wait()
     for n, slot in enumerate((low, high)):
-        row = prev[pl.ds(slot, 1), :]
-        at = n * PIECE + STATE_ROWS
-        for c in range(TILES):
-            out_ref[at + c : at + c + 1, :] = row[:, c * 128 : (c + 1) * 128]
-    loads[3].wait()
-    for n, slot in enumerate((low, high)):
         begin = pl.multiple_of(slot * STATE_ROWS, STATE_ROWS)
-        out_ref[n * PIECE : n * PIECE + STATE_ROWS, :] = mem[pl.ds(begin, STATE_ROWS), :]
-    for copy in spread:
+        out_ref[n * PIECE : n * PIECE + STATE_ROWS, :] = mem[pl.ds(begin, STATE_ROWS), :].astype(BF16)
+        out_ref[n * PIECE + STATE_ROWS : (n + 1) * PIECE, :] = tile[n * TILES : (n + 1) * TILES, :].astype(BF16)
+    for copy in sends:
         copy.wait()
 
 
 def pick(recv_ref, wanted, begin, count):
-    is_low = recv_ref[2 * PIECE : 2 * PIECE + 1, :] == wanted.astype(F32)
-    return jnp.where(is_low, recv_ref[begin : begin + count, :], recv_ref[PIECE + begin : PIECE + begin + count, :])
+    low = recv_ref[2 * PIECE :, :].astype(F32)[:1, :]
+    is_low = low == (wanted % SLOTS).astype(F32)
+    rows = [recv_ref[at : at + count, :].astype(F32) for at in (begin, PIECE + begin)]
+    return jnp.where(is_low, rows[0], rows[1])
 
 
 def sources(where, lookup_ref, q):
@@ -181,7 +181,7 @@
 
 def main_kernel(lookup_ref, tally_ref, mem_hbm, *refs):
     count = 14
-    hbm, (part_ref, moved_ref, doubled_ref) = refs[:count], refs[count : count + 3]
+    hbm, (part_ref, moved_ref, vals_ref) = refs[:count], refs[count : count + 3]
     bufs = refs[count + 3 : 2 * count + 3]
     shift, state, reads, heads, part, sems, state_sems = refs[2 * count + 3 :]
     where = place()
@@ -190,7 +190,7 @@
     state_loads = state_copies(where, lookup_ref, mem_hbm, state, state_sems)
     start(state_loads)
     loads[-1].start()
-    xn_ref, prev_ref, from_before, from_after, blend_ref = bufs[:5]
+    xn_ref, prev_ref, from_after, from_before, blend_ref = bufs[:5]
     left_ref, right_ref, base_ref, boost_ref, team_ref, final_ref = bufs[8:]
     tally = column_of(tally_ref, (SLOTS, 128))[:, :1]
     for n in range(5):
@@ -267,9 +267,7 @@
     reorder = (row256 == source).astype(BF16)
     moved = dot_split(jnp.concatenate(reach + coefs + [run], axis=0), reorder)
     moved_ref[...] = moved[STEPS * SLOTS :, :]
-    rowd, cold = iota((LOCAL, HEADS * 128), 0), iota((LOCAL, HEADS * 128), 1)
-    double = (rowd == (cold // 128) * HEAD + cold % HEAD).astype(BF16)
-    doubled_ref[...] = dot(rkv[2].astype(BF16), double)
+    vals_ref[...] = rkv[2]
 
     lane = iota((SLOTS, 128), 1)
     for h in range(HEADS):
@@ -318,9 +316,12 @@
     start(loads)
     state_loads = state_copies(where, lookup_ref, mem_hbm, state, state_sems)
     start(state_loads)
-    moved_ref, doubled_ref, from_before, from_after = bufs
+    moved_ref, vals_ref, from_after, from_before = bufs
     loads[0].wait()
     loads[1].wait()
+    rowd, cold = iota((LOCAL, HEADS * 128), 0), iota((LOCAL, HEADS * 128), 1)
+    double = (rowd == (cold // 128) * HEAD + cold % HEAD).astype(BF16)
+    doubled = dot(vals_ref[...].astype(BF16), double)
     lane = iota((SLOTS, 128), 1)
     for h in range(HEADS):
         head_lane = lane % HEADS == h
@@ -330,7 +331,7 @@
             for t in range(STEPS):
                 at = pl.ds(t * 8 + p * HEADS + h, SLOTS, stride=STEPS * 8)
                 keys[at, :] = jnp.where(head_lane, cut(moved_ref, t)[:, cols], 0.0)
-                vals[at, :] = jnp.where(half, cut(doubled_ref, t)[:, h * 128 : (h + 1) * 128], 0.0)
+                vals[at, :] = jnp.where(half, cut(doubled, t)[:, h * 128 : (h + 1) * 128], 0.0)
             whole = jnp.where(head_lane, cut(moved_ref, STEPS)[:, cols], 0.0)
             high = whole.astype(BF16).astype(F32)
             decays[pl.ds(p * HEADS + h, SLOTS, stride=16), :] = high
@@ -416,16 +417,18 @@
 
     packed, left = pl.pallas_call(
         pack_kernel,
-        out_shape=[shape((PACK_ROWS, 128), F32), shape((teams,) + left_t.shape, BF16)],
+        out_shape=[shape((PACK_ROWS, 128), BF16), shape((teams,) + left_t.shape, BF16)],
         in_specs=spec(pl.ANY, 4),
         out_specs=spec(pltpu.VMEM, 1) + spec(pl.ANY, 1),
-        scratch_shapes=[pltpu.SMEM(lookup.shape, jnp.int32)] + like([mem, prev, left_t]) + [dma((4 + teams,))],
+        scratch_shapes=[pltpu.SMEM(lookup.shape, jnp.int32)]
+        + like([prev, mem, left_t])
+        + [scratch((2 * TILES, 128), F32), dma((4 + teams,))],
         compiler_params=params(PACK_MIB),
         cost_estimate=cost(0, 1 << 20),
         name="pack",
-    )(lookup, mem, prev, left_t)
+    )(lookup, prev, mem, left_t)
+    from_after = lax.ppermute(packed, "seq", [((i + 1) % rings, i) for i in range(rings)])
     from_before = lax.ppermute(packed, "seq", [(i, (i + 1) % rings) for i in range(rings)])
-    from_after = lax.ppermute(packed, "seq", [((i + 1) % rings, i) for i in range(rings)])
     left = lax.all_to_all(left, "tensor", 0, 0)
 
     gain = entry_standardize_scale.reshape(TILES, 128)
@@ -441,15 +444,15 @@
     )(tally, x, gain)
 
     operands = [
-        xn, prev, from_before, from_after, blend_coefficients,
+        xn, prev, from_after, from_before, blend_coefficients,
         acceptance_projection_matrix, lookup_projection_matrix, payload_projection_matrix,
         left, forget_map_right_matrix, feature_forget_logloglevel.reshape(2, 128),
         present_token_boost.reshape(2, 128), team_standardize_scale.reshape(2, 128), final_projection_matrix,
     ]
-    part, moved, doubled = pl.pallas_call(
+    part, moved, values = pl.pallas_call(
         main_kernel,
         out_shape=[
-            shape((ROWS * TILES, 128), BF16), shape((ROWS + SLOTS, LOCAL), F32), shape((ROWS, HEADS * 128), F32),
+            shape((ROWS * TILES, 128), BF16), shape((ROWS + SLOTS, LOCAL), F32), shape((ROWS, LOCAL), F32),
         ],
         in_specs=spec(pltpu.SMEM, 2) + spec(pl.ANY, 1 + len(operands)),
         out_specs=spec(pltpu.VMEM, 3),
@@ -461,7 +464,7 @@
         name="main",
     )(lookup, tally, mem, *operands)
 
-    operands = [moved, doubled, from_before, from_after]
+    operands = [moved, values, from_after, from_before]
     new_states = pl.pallas_call(
         update_kernel,
         out_shape=shape((SLOTS * STATE_ROWS, 128), F32),

time: 61.9 us -> 55.6 us (0.90)
  waiting for transfers between devices: 9.87 us -> 4.12 us
  blocking collectives: 6.09 us -> 5.34 us
    ppermute x1, waiting for transfers between devices: 5.99 us -> 0.01 us  [shards(): lax.ppermute(packed, 'seq', [(i, (i + 1) % rings) for i in range(rings)])]
    all_gather x1, blocking collectives: 2.93 us -> 2.18 us  [shards(): both = lax.all_gather(part, 'tensor', axis_index_groups=pairs, tiled=False)]
  transfers between devices with their start and end apart: 4 -> 4, of which waited for: 2 -> 1; matrix products, arithmetic and copies ran while one was open for 0% -> 0% of each run, Pallas kernels for 11% -> 12%
where the time goes in v5:
time: 55.6 us; the launch traced here: 55.2 us
  starting transfers between devices  25.8 us (46%)
  Pallas kernels  16.1 us (29%)
  blocking collectives  5.34 us (10%)
  waiting for transfers between devices  4.12 us (7%)
  local copies, waits for them, and re-layouts  2.92 us (5%)
  between operations  0.85 us (2%)
    all_to_all x1, starting transfers between devices, shards(): left = lax.all_to_all(left, 'tensor', 0, 0)  10.3 us
    ppermute x1, starting transfers between devices, shards(): lax.ppermute(packed, 'seq', [((i + 1) % rings, i) for i in range(rings)])  9.1 us
    pallas_call x1, Pallas kernels, shards(): pl.pallas_call(main_kernel, out_shape=[shape((ROWS * TILES, 128), BF16),...  6.18 us
    pallas_call x1, Pallas kernels, shards(): pl.pallas_call(update_kernel, out_shape=shape((SLOTS * STATE_ROWS, 128),...  4.78 us
    all_to_all x1, starting transfers between devices, shards(): lax.all_to_all(jnp.broadcast_to(mine[None], (teams // 2,) + mine.shape),...  4.43 us
    all_to_all x1, waiting for transfers between devices, shards(): lax.all_to_all(jnp.broadcast_to(mine[None], (teams // 2,) + mine.shape),...  4.11 us
    all_gather x1, blocking collectives, shards(): mixed = lax.all_gather(mixed, 'tensor', axis_index_groups=pairs, tiled=True)  3.16 us
    pallas_call x1, Pallas kernels, shards(): pl.pallas_call(pack_kernel, out_shape=[shape((PACK_ROWS, 128), BF16), sha...  2.57 us
  transfers between devices with their start and end apart: 4, of which 1 were waited for; matrix products, arithmetic and copies ran while one was open for 0% of the time, Pallas kernels for 12%

profile of v5, /device:TPU:1, one launch (start us, length us, event | category | flops | bytes accessed | tf_op | source)
XLA Modules:
  0.0 55.2 jit_solution(11280062755517033866)
XLA Ops:
  0.6 2.6 %pack.1 = (bf16[304,128]{1,0:T(8,128)(2,1)}, bf16[8,64,256]{2,1,0:T(8,128)(2,1)}) custom-call(s32[16]{0:T(128)} %lookup_ref.3, f32[16,2048]{1,0:T(8,128)} %refs_1_.1, f32[2048,128]{1,0:T(8,128)} %bitcast.26, bf16[64,256]{1,0:T(8,128)(2,1)} %bitcast.38), custom_call_target="tpu_custom_call" | custom-call | bytes 1048576 | tf_op jit(solution)/shard_map/pack/pallas_call | solution.py:418
  3.2 0.0 copy-start.11
  3.2 0.0 copy-start.1
  3.2 10.3 %all-to-all-start = ((bf16[8,64,256]{2,1,0:T(8,128)(2,1)}), bf16[8,64,256]{2,1,0:T(8,128)(2,1)S(1)}, u32[]{:S(2)}, u32[]{:S(2)}) async-start(bf16[8,64,256]{2,1,0:T(8,128)(2,1)} %get-tuple-element.12), calls=%async_computation | async-start | bytes 524288 | tf_op jit(solution)/shard_map/all_to_all | solution.py:432
  13.6 0.0 copy-done.11
  13.6 1.9 %collective-permute-start.1 = (bf16[304,128]{1,0:T(8,128)(2,1)S(1)}, bf16[304,128]{1,0:T(8,128)(2,1)S(1)}, u32[]{:S(2)}, u32[]{:S(2)}) collective-permute-start(bf16[304,128]{1,0:T(8,128)(2,1)S(1)} %copy-done.11), channel_id=1, source_target_pairs={{0,8},{8,16},{16,24},{24,32},{32,40},{40,48},{48,56},{56,64},{64,7... | collective-permute-start | bytes 233480 | tf_op jit(solution)/shard_map/ppermute | solution.py:431
  15.5 9.1 %collective-permute-start = (bf16[304,128]{1,0:T(8,128)(2,1)S(1)}, bf16[304,128]{1,0:T(8,128)(2,1)S(1)}, u32[]{:S(2)}, u32[]{:S(2)}) collective-permute-start(bf16[304,128]{1,0:T(8,128)(2,1)S(1)} %copy-done.11), channel_id=1, source_target_pairs={{8,0},{16,8},{24,16},{32,24},{40,32},{48,40},{56,48},{64,56},{72,6... | collective-permute-start | bytes 233480 | tf_op jit(solution)/shard_map/ppermute | solution.py:430
  24.6 0.0 copy-start.5
  24.6 0.0 copy-start.6
  24.6 0.0 copy-done.1
  24.6 0.7 %copy-done.5 = f32[2048]{0:T(1024)S(1)} copy-done((f32[2048]{0:T(1024)S(1)}, f32[2048]{0:T(1024)}, u32[]{:S(2)}) %copy-start.5) | copy-done | bytes 8216
  25.3 0.0 copy-done.6
  25.3 0.0 copy-start.2
  25.3 0.0 copy-start.3
  25.3 0.0 copy-start.4
  25.3 0.0 copy-start.9
  25.3 0.0 copy-start.10
  25.3 1.8 %norm.1 = (f32[64,2048]{1,0:T(8,128)S(1)}, f32[16,2048]{1,0:T(8,128)}) custom-call(s32[16]{0:T(128)S(1)} %copy-done.6, bf16[1024,128]{1,0:T(8,128)(2,1)S(1)} %bitcast.29, f32[16,128]{1,0:T(8,128)S(1)} %bitcast.32), custom_call_target="tpu_custom_call" | custom-call | bytes 4194304 | tf_op jit(solution)/shard_map/norm/pallas_call | solution.py:435
  27.1 0.0 collective-permute-done.1.refs_3_
  27.1 0.0 collective-permute-done.refs_2_
  27.1 0.0 all-to-all-done.refs_8_
  27.1 0.0 copy-start.7
  27.1 0.0 copy-start.8
  27.2 0.0 copy-done.2
  27.2 0.0 copy-done.3
  27.2 0.0 copy-done.4
  27.2 0.0 copy-done.9
  27.2 0.0 copy-done.10
  27.2 0.6 %copy-done.7 = s32[16]{0:T(128)S(1)} copy-done((s32[16]{0:T(128)S(1)}, s32[16]{0:T(128)}, u32[]{:S(2)}) %copy-start.7) | copy-done | bytes 88
  27.8 0.0 copy-done.8
  27.8 6.2 %main.1 = (bf16[1024,128]{1,0:T(8,128)(2,1)S(1)}, f32[80,256]{1,0:T(8,128)S(1)}, f32[64,256]{1,0:T(8,128)S(1)}) custom-call(s32[16]{0:T(128)S(1)} %copy-done.7, s32[16]{0:T(128)S(1)} %copy-done.6, f32[2048,128]{1,0:T(8,128)} %bitcast.27, f32[64,2048]{1,0:T(8,128)S(1)} %get-tuple-element.10.refs_0_, f32[16,2048]{1,0:T(8,128)S(1)} %copy-done.2, ...), custom_call_target="tpu_custom_call" | custom-call | flops 268435456 | bytes 8388608 | tf_op jit(solution)/shard_map/main/pallas_call | solution.py:452
  34.0 2.2 %all-gather = bf16[2048,128]{1,0:T(8,128)(2,1)S(1)} all-gather(bf16[1024,128]{1,0:T(8,128)(2,1)S(1)} %get-tuple-element.13), channel_id=2, replica_groups={{0,1},{2,3},{4,5},{6,7},{8,9},{10,11},{12,13},{14,15},{16,17},{18,19},{..., dimensions={0}, use_global_device_ids=true | all-gather | bytes 786432 | tf_op jit(solution)/shard_map/all_gather | solution.py:484
  36.2 0.0 copy-start
  36.2 0.9 %broadcast_in_dim.2 = bf16[4,512,128]{2,1,0:T(8,128)(2,1)} broadcast(bf16[512,128]{1,0:T(8,128)(2,1)S(1)} %dynamic-slice_reduce_fusion), dimensions={1,2} | broadcast | bytes 655360 | tf_op jit(solution)/shard_map/broadcast_in_dim | solution.py:487
  37.1 4.4 %all-to-all-start.1 = ((bf16[4,512,128]{2,1,0:T(8,128)(2,1)}), bf16[4,512,128]{2,1,0:T(8,128)(2,1)S(1)}, u32[]{:S(2)}, u32[]{:S(2)}) async-start(bf16[4,512,128]{2,1,0:T(8,128)(2,1)} %broadcast_in_dim.2), calls=%async_computation.1 | async-start | bytes 1048576 | tf_op jit(solution)/shard_map/all_to_all | solution.py:486
  41.6 0.0 copy-done
  41.6 4.8 %update.1 = f32[2048,128]{1,0:T(8,128)} custom-call(s32[16]{0:T(128)S(1)} %copy-done.7, f32[2048,128]{1,0:T(8,128)S(1)} %bitcast.28, f32[80,256]{1,0:T(8,128)S(1)} %get-tuple-element.14.refs_0_, f32[64,256]{1,0:T(8,128)S(1)} %get-tuple-element.15.refs_1_, bf16[304,128]{1,0:T(8,128)(2,1)S(1)} %collective-permute-done.refs_2_, ...), custom_call_target="tpu_custom_call" | custom-call | flops 16777216 | bytes 8388608 | tf_op jit(solution)/shard_map/update/pallas_call | solution.py:468
  46.3 4.1 %all-to-all-done.1.parts_ref = bf16[4,512,128]{2,1,0:T(8,128)(2,1)S(1)} async-done(((bf16[4,512,128]{2,1,0:T(8,128)(2,1)}), bf16[4,512,128]{2,1,0:T(8,128)(2,1)S(1)}, u32[]{:S(2)}, u32[]{:S(2)}) %all-to-all-start.1) | async-done | bytes 524320 | tf_op jit(solution)/shard_map/all_to_all | solution.py:486
  50.5 0.8 %finish.1 = bf16[512,128]{1,0:T(8,128)(2,1)S(1)} custom-call(s32[16]{0:T(128)S(1)} %copy-done.6, bf16[1024,128]{1,0:T(8,128)(2,1)S(1)} %bitcast.30, bf16[4,512,128]{2,1,0:T(8,128)(2,1)S(1)} %all-to-all-done.1.parts_ref), custom_call_target="tpu_custom_call" | custom-call | bytes 524288 | tf_op jit(solution)/shard_map/finish/pallas_call | solution.py:489
  51.3 3.2 %all_gather.11 = bf16[16,4,2048]{2,1,0:T(4,128)(2,1)S(1)} all-gather(bf16[8,4,2048]{2,1,0:T(4,128)(2,1)S(1)} %bitcast.31), channel_id=1, replica_groups={{0,1},{2,3},{4,5},{6,7},{8,9},{10,11},{12,13},{14,15},{16,17},{18,19},{..., dimensions={0}, use_global_device_ids=true | all-gather | bytes 393216 | tf_op jit(solution)/shard_map/all_gather | solution.py:500
  54.5 0.7 %copy.27 = bf16[16,4,2048]{2,1,0:T(4,128)(2,1)} copy(bf16[16,4,2048]{2,1,0:T(4,128)(2,1)S(1)} %all_gather.11) | data formatting | bytes 524288
  (1 shorter events, 0.0 us)
Async XLA Ops:
  3.2 10.4 %copy-start.11 = (bf16[304,128]{1,0:T(8,128)(2,1)S(1)}, bf16[304,128]{1,0:T(8,128)(2,1)}, u32[]{:S(2)}) copy-start(bf16[304,128]{1,0:T(8,128)(2,1)} %get-tuple-element.11) | copy-start | bytes 233476
  3.2 21.4 %copy-start.1 = (bf16[16,4,2048]{2,1,0:T(4,128)(2,1)S(1)}, bf16[16,4,2048]{2,1,0:T(4,128)(2,1)}, u32[]{:S(2)}) copy-start(bf16[16,4,2048]{2,1,0:T(4,128)(2,1)} %param.16) | copy-start | bytes 786436
  3.2 23.9 %all-to-all-start = ((bf16[8,64,256]{2,1,0:T(8,128)(2,1)}), bf16[8,64,256]{2,1,0:T(8,128)(2,1)S(1)}, u32[]{:S(2)}, u32[]{:S(2)}) async-start(bf16[8,64,256]{2,1,0:T(8,128)(2,1)} %get-tuple-element.12), calls=%async_computation | async-start | bytes 524288 | tf_op jit(solution)/shard_map/all_to_all | solution.py:432
  13.6 13.5 %collective-permute-start.1 = (bf16[304,128]{1,0:T(8,128)(2,1)S(1)}, bf16[304,128]{1,0:T(8,128)(2,1)S(1)}, u32[]{:S(2)}, u32[]{:S(2)}) collective-permute-start(bf16[304,128]{1,0:T(8,128)(2,1)S(1)} %copy-done.11), channel_id=1, source_target_pairs={{0,8},{8,16},{16,24},{24,32},{32,40},{40,48},{48,56},{56,64},{64,7... | collective-permute-start | bytes 233480 | tf_op jit(solution)/shard_map/ppermute | solution.py:431
  15.5 11.6 %collective-permute-start = (bf16[304,128]{1,0:T(8,128)(2,1)S(1)}, bf16[304,128]{1,0:T(8,128)(2,1)S(1)}, u32[]{:S(2)}, u32[]{:S(2)}) collective-permute-start(bf16[304,128]{1,0:T(8,128)(2,1)S(1)} %copy-done.11), channel_id=1, source_target_pairs={{8,0},{16,8},{24,16},{32,24},{40,32},{48,40},{56,48},{64,56},{72,6... | collective-permute-start | bytes 233480 | tf_op jit(solution)/shard_map/ppermute | solution.py:430
  24.6 0.7 %copy-start.5 = (f32[2048]{0:T(1024)S(1)}, f32[2048]{0:T(1024)}, u32[]{:S(2)}) copy-start(f32[2048]{0:T(1024)} %param.21) | copy-start | bytes 24580
  24.6 0.7 %copy-start.6 = (s32[16]{0:T(128)S(1)}, s32[16]{0:T(128)}, u32[]{:S(2)}) copy-start(s32[16]{0:T(128)} %tally_ref.5) | copy-start | bytes 196
  25.3 1.9 %copy-start.2 = (f32[16,2048]{1,0:T(8,128)S(1)}, f32[16,2048]{1,0:T(8,128)}, u32[]{:S(2)}) copy-start(f32[16,2048]{1,0:T(8,128)} %refs_1_.1) | copy-start | bytes 393220
  25.3 1.9 %copy-start.3 = (f32[4,2048]{1,0:T(4,128)S(1)}, f32[4,2048]{1,0:T(4,128)}, u32[]{:S(2)}) copy-start(f32[4,2048]{1,0:T(4,128)} %refs_4_.1) | copy-start | bytes 98308
  25.3 1.9 %copy-start.4 = (bf16[64,256]{1,0:T(8,128)(2,1)S(1)}, bf16[64,256]{1,0:T(8,128)(2,1)}, u32[]{:S(2)}) copy-start(bf16[64,256]{1,0:T(8,128)(2,1)} %refs_9_.1) | copy-start | bytes 98308
  25.3 1.9 %copy-start.9 = (f32[256]{0:T(256)S(1)}, f32[256]{0:T(256)}, u32[]{:S(2)}) copy-start(f32[256]{0:T(256)} %param.29) | copy-start | bytes 3076
  25.3 1.9 %copy-start.10 = (f32[256]{0:T(256)S(1)}, f32[256]{0:T(256)}, u32[]{:S(2)}) copy-start(f32[256]{0:T(256)} %param.30) | copy-start | bytes 3076
  27.1 0.7 %copy-start.7 = (s32[16]{0:T(128)S(1)}, s32[16]{0:T(128)}, u32[]{:S(2)}) copy-start(s32[16]{0:T(128)} %lookup_ref.3) | copy-start | bytes 196
  27.1 0.7 %copy-start.8 = (f32[256]{0:T(256)S(1)}, f32[256]{0:T(256)}, u32[]{:S(2)}) copy-start(f32[256]{0:T(256)} %param.28) | copy-start | bytes 3076
  36.2 5.4 %copy-start = (f32[16,4,4096]{2,1,0:T(4,128)S(1)}, f32[16,4,4096]{2,1,0:T(4,128)}, u32[]{:S(2)}) copy-start(f32[16,4,4096]{2,1,0:T(4,128)} %param.19) | copy-start | bytes 3145732
  37.1 13.3 %all-to-all-start.1 = ((bf16[4,512,128]{2,1,0:T(8,128)(2,1)}), bf16[4,512,128]{2,1,0:T(8,128)(2,1)S(1)}, u32[]{:S(2)}, u32[]{:S(2)}) async-start(bf16[4,512,128]{2,1,0:T(8,128)(2,1)} %broadcast_in_dim.2), calls=%async_computation.1 | async-start | bytes 1048576 | tf_op jit(solution)/shard_map/all_to_all | solution.py:486

commit v6 on v5

--- a/solution.py
+++ b/solution.py
@@ -157,9 +157,19 @@
     return a[t * SLOTS : (t + 1) * SLOTS, :]
 
 
-def norm_kernel(tally_ref, x_hbm, gain_hbm, xn_ref, last_ref, x_ref, gain_ref, x32, sems):
-    loads = copies((x_hbm, gain_hbm), (x_ref, gain_ref), sems)
-    start(loads)
+def main_kernel(lookup_ref, tally_ref, mem_hbm, *refs):
+    count = 15
+    hbm, (part_ref, moved_ref, vals_ref, last_ref) = refs[:count], refs[count : count + 4]
+    bufs = refs[count + 4 : 2 * count + 4]
+    x32, shift, state, reads, heads, part, sems, state_sems = refs[2 * count + 4 :]
+    where = place()
+    loads = copies(hbm, bufs, sems)
+    start(loads[:-1])
+    state_loads = state_copies(where, lookup_ref, mem_hbm, state, state_sems)
+    start(state_loads)
+    loads[-1].start()
+    x_ref, gain_ref, prev_ref, from_after, from_before, blend_ref = bufs[:6]
+    left_ref, right_ref, base_ref, boost_ref, team_ref, final_ref = bufs[9:]
     loads[0].wait()
     loads[1].wait()
     x32[...] = x_ref[...].astype(F32)
@@ -175,25 +185,7 @@
     for t in range(1, STEPS):
         last = jnp.where(tally == t + 1, normed[t], last)
     last_ref[...] = last
-    for t in range(STEPS):
-        xn_ref[t * SLOTS : (t + 1) * SLOTS, :] = normed[t]
-
-
-def main_kernel(lookup_ref, tally_ref, mem_hbm, *refs):
-    count = 14
-    hbm, (part_ref, moved_ref, vals_ref) = refs[:count], refs[count : count + 3]
-    bufs = refs[count + 3 : 2 * count + 3]
-    shift, state, reads, heads, part, sems, state_sems = refs[2 * count + 3 :]
-    where = place()
-    loads = copies(hbm, bufs, sems)
-    start(loads[:-1])
-    state_loads = state_copies(where, lookup_ref, mem_hbm, state, state_sems)
-    start(state_loads)
-    loads[-1].start()
-    xn_ref, prev_ref, from_after, from_before, blend_ref = bufs[:5]
-    left_ref, right_ref, base_ref, boost_ref, team_ref, final_ref = bufs[8:]
-    tally = column_of(tally_ref, (SLOTS, 128))[:, :1]
-    for n in range(5):
+    for n in range(2, 6):
         loads[n].wait()
     for q in range(SLOTS):
         wanted, own, before, at = sources(where, lookup_ref, q)
@@ -210,8 +202,8 @@
             for c in range(TILES):
                 shift[q : q + 1, c * 128 : (c + 1) * 128] = rows[c : c + 1, :]
 
-    xn = xn_ref[...]
-    change = jnp.concatenate([shift[...], xn[: (STEPS - 1) * SLOTS, :]], axis=0) - xn
+    xn = jnp.concatenate(normed, axis=0)
+    change = jnp.concatenate([shift[...]] + normed[:-1], axis=0) - xn
 
     def mix(which):
         return (xn + change * blend_ref[which : which + 1, :]).astype(BF16)
@@ -219,9 +211,9 @@
     mixed_rows = mix(3)
     rkv = []
     for n in range(3):
-        loads[5 + n].wait()
-        rkv.append(dot(mix(n), bufs[5 + n][...]))
-    for n in range(8, 13):
+        loads[6 + n].wait()
+        rkv.append(dot(mix(n), bufs[6 + n][...]))
+    for n in range(9, 14):
         loads[n].wait()
     pre = jnp.zeros((ROWS, left_ref.shape[1]), F32)
     chunk = left_ref.shape[2]
@@ -299,7 +291,7 @@
     center = y - dot_split(y, same_head) * (1.0 / HEAD)
     spread = dot_split(center * center, same_head) * (1.0 / HEAD)
     g = (center * lax.rsqrt(spread + EPS) * row_of(team_ref)).astype(BF16)
-    loads[13].wait()
+    loads[14].wait()
     proj = dot(g, final_ref[...])
     for t in range(STEPS):
         for c in range(TILES):
@@ -353,23 +345,6 @@
         copy.wait()
 
 
-def finish_kernel(tally_ref, x_hbm, parts_ref, out_ref, x_ref, sem):
-    rows = out_ref.shape[0]
-    core = lax.axis_index("tensor") % 2
-    begin = core * rows
-    load = pltpu.make_async_copy(x_hbm.at[pl.ds(pl.multiple_of(begin, rows), rows), :], x_ref, sem)
-    load.start()
-    step = iota((STEPS * TILES, 128), 0) % STEPS
-    load.wait()
-    for q in range(rows // (STEPS * TILES)):
-        here = slice(q * STEPS * TILES, (q + 1) * STEPS * TILES)
-        total = x_ref[here, :].astype(F32)
-        for n in range(parts_ref.shape[0]):
-            total = total + parts_ref[n, here, :].astype(F32)
-        tally = tally_ref[core * (rows // (STEPS * TILES)) + q]
-        out_ref[here, :] = jnp.where(step < tally, total, 0.0).astype(BF16)
-
-
 def cost(flops, bytes_accessed):
     return pl.CostEstimate(flops=flops, bytes_accessed=bytes_accessed, transcendentals=0)
 
@@ -431,33 +406,22 @@
     from_before = lax.ppermute(packed, "seq", [(i, (i + 1) % rings) for i in range(rings)])
     left = lax.all_to_all(left, "tensor", 0, 0)
 
-    gain = entry_standardize_scale.reshape(TILES, 128)
-    xn, new_shifts = pl.pallas_call(
-        norm_kernel,
-        out_shape=[shape((ROWS, WIDTH), F32), shape((SLOTS, WIDTH), F32)],
-        in_specs=spec(pltpu.SMEM, 1) + spec(pl.ANY, 2),
-        out_specs=spec(pltpu.VMEM, 2),
-        scratch_shapes=like([x, gain]) + [scratch((ROWS * TILES, 128), F32), dma((2,))],
-        compiler_params=params(MAIN_MIB),
-        cost_estimate=cost(0, 4 << 20),
-        name="norm",
-    )(tally, x, gain)
-
     operands = [
-        xn, prev, from_after, from_before, blend_coefficients,
+        x, entry_standardize_scale.reshape(TILES, 128), prev, from_after, from_before, blend_coefficients,
         acceptance_projection_matrix, lookup_projection_matrix, payload_projection_matrix,
         left, forget_map_right_matrix, feature_forget_logloglevel.reshape(2, 128),
         present_token_boost.reshape(2, 128), team_standardize_scale.reshape(2, 128), final_projection_matrix,
     ]
-    part, moved, values = pl.pallas_call(
+    part, moved, values, new_shifts = pl.pallas_call(
         main_kernel,
         out_shape=[
             shape((ROWS * TILES, 128), BF16), shape((ROWS + SLOTS, LOCAL), F32), shape((ROWS, LOCAL), F32),
+            shape((SLOTS, WIDTH), F32),
         ],
         in_specs=spec(pltpu.SMEM, 2) + spec(pl.ANY, 1 + len(operands)),
-        out_specs=spec(pltpu.VMEM, 3),
+        out_specs=spec(pltpu.VMEM, 4),
         scratch_shapes=like(operands)
-        + [scratch((SLOTS, WIDTH), F32), state_buf, rows_buf, rows_buf, scratch((ROWS * TILES, 128), F32)]
+        + [scratch((ROWS * TILES, 128), F32), scratch((SLOTS, WIDTH), F32), state_buf, rows_buf, rows_buf, scratch((ROWS * TILES, 128), F32)]
         + [dma((len(operands),)), dma((SLOTS,))],
         compiler_params=params(MAIN_MIB),
         cost_estimate=cost(8 * ROWS * WIDTH * LOCAL, 8 << 20),
@@ -486,18 +450,10 @@
     spread = lax.all_to_all(
         jnp.broadcast_to(mine[None], (teams // 2,) + mine.shape), "tensor", 0, 0, axis_index_groups=chips
     )
-    mixed = pl.pallas_call(
-        finish_kernel,
-        out_shape=shape((half, 128), BF16),
-        in_specs=spec(pltpu.SMEM, 1) + spec(pl.ANY, 1) + spec(pltpu.VMEM, 1),
-        out_specs=spec(pltpu.VMEM, 1)[0],
-        scratch_shapes=[scratch((half, 128), BF16), dma],
-        compiler_params=params(8),
-        cost_estimate=cost(0, 1 << 19),
-        name="finish",
-    )(tally, x, spread)
-    mixed = tiles_back(mixed, SLOTS // 2, STEPS, WIDTH)
-    mixed = lax.all_gather(mixed, "tensor", axis_index_groups=pairs, tiled=True)
+    total = tiles_back(spread.astype(F32).sum(0).astype(BF16), SLOTS // 2, STEPS, WIDTH)
+    proj = lax.all_gather(total, "tensor", axis_index_groups=pairs, tiled=True)
+    valid = tally[:, None, None] > jnp.arange(STEPS, dtype=jnp.int32)[None, :, None]
+    mixed = jnp.where(valid, layer_entry_vectors.astype(F32) + proj.astype(F32), 0.0).astype(BF16)
     return (
         mixed,
         tiles_back(new_states, SLOTS, HEADS, HEAD * HEAD),

time: 55.6 us -> 54.8 us (0.986)
  Pallas kernels: 16.1 us -> 13.7 us
  waiting for transfers between devices: 4.12 us -> 5.87 us
  local copies, waits for them, and re-layouts: 2.92 us -> 1.51 us
  other arithmetic: 0.04 us -> 1.15 us
    pallas_call x2 -> x0, Pallas kernels: 2.6 us -> none  [the longest x1 1.76 us: shards(): pl.pallas_call(norm_kernel, out_shape=[shape((ROWS, WIDTH), F32), shape((...]
    unnamed x25 -> x24, local copies, waits for them, and re-layouts: 2.04 us -> 0.65 us
    ppermute x1, waiting for transfers between devices: 0.01 us -> 0.99 us  [shards(): lax.ppermute(packed, 'seq', [((i + 1) % rings, i) for i in range(rings)])]
    convert_element_type x0 -> x1, other arithmetic: none -> 0.96 us  [shards(): jnp.where(valid, layer_entry_vectors.astype(F32) + proj.astype(F32), 0.0)]
    ppermute x1, waiting for transfers between devices: 0.01 us -> 0.84 us  [shards(): lax.ppermute(packed, 'seq', [(i, (i + 1) % rings) for i in range(rings)])]
  transfers between devices with their start and end apart: 4 -> 4, of which waited for: 1 -> 3; matrix products, arithmetic and copies ran while one was open for 0% -> 0% of each run, Pallas kernels for 12% -> 9%
where the time goes in v6:
time: 54.8 us; the launch traced here: 54.4 us
  starting transfers between devices  25.7 us (47%)
  Pallas kernels  13.7 us (25%)
  waiting for transfers between devices  5.87 us (11%)
  blocking collectives  5.62 us (10%)
  local copies, waits for them, and re-layouts  1.51 us (3%)
  other arithmetic  1.15 us (2%)
  between operations  0.82 us (1%)
    all_to_all x1, starting transfers between devices, shards(): left = lax.all_to_all(left, 'tensor', 0, 0)  10.3 us
    ppermute x1, starting transfers between devices, shards(): lax.ppermute(packed, 'seq', [((i + 1) % rings, i) for i in range(rings)])  9.1 us
    pallas_call x1, Pallas kernels, shards(): pl.pallas_call(main_kernel, out_shape=[shape((ROWS * TILES, 128), BF16),...  6.32 us
    pallas_call x1, Pallas kernels, shards(): pl.pallas_call(update_kernel, out_shape=shape((SLOTS * STATE_ROWS, 128),...  4.79 us
    all_to_all x1, starting transfers between devices, shards(): lax.all_to_all(jnp.broadcast_to(mine[None], (teams // 2,) + mine.shape),...  4.25 us
    all_to_all x1, waiting for transfers between devices, shards(): lax.all_to_all(jnp.broadcast_to(mine[None], (teams // 2,) + mine.shape),...  4.04 us
    all_gather x1, blocking collectives, shards(): proj = lax.all_gather(total, 'tensor', axis_index_groups=pairs, tiled=True)  3.16 us
    pallas_call x1, Pallas kernels, shards(): pl.pallas_call(pack_kernel, out_shape=[shape((PACK_ROWS, 128), BF16), sha...  2.57 us
  transfers between devices with their start and end apart: 4, of which 3 were waited for; matrix products, arithmetic and copies ran while one was open for 0% of the time, Pallas kernels for 9%

profile of v6, /device:TPU:1, one launch (start us, length us, event | category | flops | bytes accessed | tf_op | source)
XLA Modules:
  0.0 54.4 jit_solution(5837850403908661519)
XLA Ops:
  0.6 2.6 %pack.1 = (bf16[304,128]{1,0:T(8,128)(2,1)}, bf16[8,64,256]{2,1,0:T(8,128)(2,1)}) custom-call(s32[16]{0:T(128)} %lookup_ref.3, f32[16,2048]{1,0:T(8,128)} %refs_2_.1, f32[2048,128]{1,0:T(8,128)} %bitcast.26, bf16[64,256]{1,0:T(8,128)(2,1)} %bitcast.37), custom_call_target="tpu_custom_call" | custom-call | bytes 1048576 | tf_op jit(solution)/shard_map/pack/pallas_call | solution.py:393
  3.2 0.0 copy-start.11
  3.2 0.0 copy-start.1
  3.2 0.0 copy-start.2
  3.2 0.0 copy-start.4
  3.3 10.3 %all-to-all-start = ((bf16[8,64,256]{2,1,0:T(8,128)(2,1)}), bf16[8,64,256]{2,1,0:T(8,128)(2,1)S(1)}, u32[]{:S(2)}, u32[]{:S(2)}) async-start(bf16[8,64,256]{2,1,0:T(8,128)(2,1)} %get-tuple-element.10), calls=%async_computation | async-start | bytes 524288 | tf_op jit(solution)/shard_map/all_to_all | solution.py:407
  13.6 0.0 copy-start.3
  13.6 0.0 copy-done.11
  13.6 2.0 %collective-permute-start.1 = (bf16[304,128]{1,0:T(8,128)(2,1)S(1)}, bf16[304,128]{1,0:T(8,128)(2,1)S(1)}, u32[]{:S(2)}, u32[]{:S(2)}) collective-permute-start(bf16[304,128]{1,0:T(8,128)(2,1)S(1)} %copy-done.11), channel_id=1, source_target_pairs={{0,8},{8,16},{16,24},{24,32},{32,40},{40,48},{48,56},{56,64},{64,7... | collective-permute-start | bytes 233480 | tf_op jit(solution)/shard_map/ppermute | solution.py:406
  15.6 9.1 %collective-permute-start = (bf16[304,128]{1,0:T(8,128)(2,1)S(1)}, bf16[304,128]{1,0:T(8,128)(2,1)S(1)}, u32[]{:S(2)}, u32[]{:S(2)}) collective-permute-start(bf16[304,128]{1,0:T(8,128)(2,1)S(1)} %copy-done.11), channel_id=1, source_target_pairs={{8,0},{16,8},{24,16},{32,24},{40,32},{48,40},{56,48},{64,56},{72,6... | collective-permute-start | bytes 233480 | tf_op jit(solution)/shard_map/ppermute | solution.py:405
  24.8 0.0 copy-start.8
  24.8 0.0 copy-start.9
  24.8 0.0 copy-start.10
  24.8 0.0 copy-start.5
  24.8 0.8 %collective-permute-done.1.refs_4_.refs_3_ = bf16[304,128]{1,0:T(8,128)(2,1)S(1)} collective-permute-done((bf16[304,128]{1,0:T(8,128)(2,1)S(1)}, bf16[304,128]{1,0:T(8,128)(2,1)S(1)}, u32[]{:S(2)}, u32[]{:S(2)}) %collective-permute-start.1) | collective-permute-done | bytes 77856 | tf_op jit(solution)/shard_map/ppermute | solution.py:406
  25.7 1.0 %collective-permute-done.refs_3_.refs_2_ = bf16[304,128]{1,0:T(8,128)(2,1)S(1)} collective-permute-done((bf16[304,128]{1,0:T(8,128)(2,1)S(1)}, bf16[304,128]{1,0:T(8,128)(2,1)S(1)}, u32[]{:S(2)}, u32[]{:S(2)}) %collective-permute-start) | collective-permute-done | bytes 77856 | tf_op jit(solution)/shard_map/ppermute | solution.py:405
  26.6 0.0 all-to-all-done.refs_9_
  26.7 0.0 copy-start.6
  26.7 0.0 copy-start.7
  26.7 0.0 copy-done.1
  26.7 0.0 copy-done.2
  26.7 0.0 copy-done.4
  26.7 0.0 copy-done.3
  26.7 0.0 copy-done.8
  26.7 0.0 copy-done.9
  26.7 0.0 copy-done.10
  26.7 0.0 copy-done.5
  26.7 0.6 %copy-done.6 = s32[16]{0:T(128)S(1)} copy-done((s32[16]{0:T(128)S(1)}, s32[16]{0:T(128)}, u32[]{:S(2)}) %copy-start.6) | copy-done | bytes 88
  27.3 0.0 copy-done.7
  27.3 6.3 %main.1 = (bf16[1024,128]{1,0:T(8,128)(2,1)S(1)}, f32[80,256]{1,0:T(8,128)S(1)}, f32[64,256]{1,0:T(8,128)S(1)}, f32[16,2048]{1,0:T(8,128)}) custom-call(s32[16]{0:T(128)S(1)} %copy-done.6, s32[16]{0:T(128)S(1)} %copy-done.7, f32[2048,128]{1,0:T(8,128)} %bitcast.27, bf16[1024,128]{1,0:T(8,128)(2,1)S(1)} %bitcast.29, f32[16,128]{1,0:T(8,128)S(1)} %bitcast.30, ...), custom_call_target="tpu_custom_call" | custom-call | flops 268435456 | bytes 8388608 | tf_op jit(solution)/shard_map/main/pallas_call | solution.py:415
  33.7 2.5 %all-gather = bf16[2048,128]{1,0:T(8,128)(2,1)S(1)} all-gather(bf16[1024,128]{1,0:T(8,128)(2,1)S(1)} %get-tuple-element.11), channel_id=2, replica_groups={{0,1},{2,3},{4,5},{6,7},{8,9},{10,11},{12,13},{14,15},{16,17},{18,19},{..., dimensions={0}, use_global_device_ids=true | all-gather | bytes 786432 | tf_op jit(solution)/shard_map/all_gather | solution.py:448
  36.1 0.0 copy-start
  36.2 0.9 %broadcast_in_dim.21 = bf16[4,512,128]{2,1,0:T(8,128)(2,1)} broadcast(bf16[512,128]{1,0:T(8,128)(2,1)S(1)} %dynamic-slice_reduce_fusion), dimensions={1,2} | broadcast | bytes 655360 | tf_op jit(solution)/shard_map/broadcast_in_dim | solution.py:451
  37.0 4.3 %all-to-all-start.1 = ((bf16[4,512,128]{2,1,0:T(8,128)(2,1)}), bf16[4,512,128]{2,1,0:T(8,128)(2,1)S(1)}, u32[]{:S(2)}, u32[]{:S(2)}) async-start(bf16[4,512,128]{2,1,0:T(8,128)(2,1)} %broadcast_in_dim.21), calls=%async_computation.1 | async-start | bytes 1048576 | tf_op jit(solution)/shard_map/all_to_all | solution.py:450
  41.3 0.1 iota_compare_fusion
  41.3 0.0 copy-done
  41.3 4.8 %update.1 = f32[2048,128]{1,0:T(8,128)} custom-call(s32[16]{0:T(128)S(1)} %copy-done.6, f32[2048,128]{1,0:T(8,128)S(1)} %bitcast.28, f32[80,256]{1,0:T(8,128)S(1)} %get-tuple-element.12.refs_0_, f32[64,256]{1,0:T(8,128)S(1)} %get-tuple-element.13.refs_1_, bf16[304,128]{1,0:T(8,128)(2,1)S(1)} %collective-permute-done.refs_3_.refs_2_, ...), custom_call_target="tpu_custom_call" | custom-call | flops 16777216 | bytes 8388608 | tf_op jit(solution)/shard_map/update/pallas_call | solution.py:432
  46.1 4.0 %all-to-all-done.1 = bf16[4,512,128]{2,1,0:T(8,128)(2,1)S(1)} async-done(((bf16[4,512,128]{2,1,0:T(8,128)(2,1)}), bf16[4,512,128]{2,1,0:T(8,128)(2,1)S(1)}, u32[]{:S(2)}, u32[]{:S(2)}) %all-to-all-start.1) | async-done | bytes 524320 | tf_op jit(solution)/shard_map/all_to_all | solution.py:450
  50.2 0.1 reduce_sum.25
  50.3 3.2 %all_gather.11 = bf16[16,4,2048]{2,1,0:T(4,128)(2,1)S(1)} all-gather(bf16[8,4,2048]{2,1,0:T(4,128)(2,1)S(1)} %bitcast.36), channel_id=1, replica_groups={{0,1},{2,3},{4,5},{6,7},{8,9},{10,11},{12,13},{14,15},{16,17},{18,19},{..., dimensions={0}, use_global_device_ids=true | all-gather | bytes 393216 | tf_op jit(solution)/shard_map/all_gather | solution.py:454
  53.4 1.0 %select_convert_fusion = bf16[16,4,2048]{2,1,0:T(4,128)(2,1)} fusion(bf16[16,4,2048]{2,1,0:T(4,128)(2,1)S(1)} %all_gather.11, bf16[16,4,2048]{2,1,0:T(4,128)(2,1)S(1)} %copy-done.1, pred[16,4]{1,0:T(8,128)(4,1)S(1)} %iota_compare_fusion), kind=kLoop, calls=%fused_computation | loop fusion | flops 655360 | bytes 786496 | tf_op jit(solution)/shard_map/convert_element_type | solution.py:456
  (1 shorter events, 0.0 us)
Async XLA Ops:
  3.2 10.4 %copy-start.11 = (bf16[304,128]{1,0:T(8,128)(2,1)S(1)}, bf16[304,128]{1,0:T(8,128)(2,1)}, u32[]{:S(2)}) copy-start(bf16[304,128]{1,0:T(8,128)(2,1)} %get-tuple-element.9) | copy-start | bytes 233476
  3.2 23.4 %copy-start.1 = (bf16[16,4,2048]{2,1,0:T(4,128)(2,1)S(1)}, bf16[16,4,2048]{2,1,0:T(4,128)(2,1)}, u32[]{:S(2)}) copy-start(bf16[16,4,2048]{2,1,0:T(4,128)(2,1)} %param.16) | copy-start | bytes 786436
  3.2 23.4 %copy-start.2 = (f32[16,2048]{1,0:T(8,128)S(1)}, f32[16,2048]{1,0:T(8,128)}, u32[]{:S(2)}) copy-start(f32[16,2048]{1,0:T(8,128)} %refs_2_.1) | copy-start | bytes 393220
  3.2 23.4 %copy-start.4 = (bf16[64,256]{1,0:T(8,128)(2,1)S(1)}, bf16[64,256]{1,0:T(8,128)(2,1)}, u32[]{:S(2)}) copy-start(bf16[64,256]{1,0:T(8,128)(2,1)} %refs_10_.1) | copy-start | bytes 98308
  3.3 23.4 %all-to-all-start = ((bf16[8,64,256]{2,1,0:T(8,128)(2,1)}), bf16[8,64,256]{2,1,0:T(8,128)(2,1)S(1)}, u32[]{:S(2)}, u32[]{:S(2)}) async-start(bf16[8,64,256]{2,1,0:T(8,128)(2,1)} %get-tuple-element.10), calls=%async_computation | async-start | bytes 524288 | tf_op jit(solution)/shard_map/all_to_all | solution.py:407
  13.6 13.1 %copy-start.3 = (f32[4,2048]{1,0:T(4,128)S(1)}, f32[4,2048]{1,0:T(4,128)}, u32[]{:S(2)}) copy-start(f32[4,2048]{1,0:T(4,128)} %refs_5_.1) | copy-start | bytes 98308
  13.6 12.1 %collective-permute-start.1 = (bf16[304,128]{1,0:T(8,128)(2,1)S(1)}, bf16[304,128]{1,0:T(8,128)(2,1)S(1)}, u32[]{:S(2)}, u32[]{:S(2)}) collective-permute-start(bf16[304,128]{1,0:T(8,128)(2,1)S(1)} %copy-done.11), channel_id=1, source_target_pairs={{0,8},{8,16},{16,24},{24,32},{32,40},{40,48},{48,56},{56,64},{64,7... | collective-permute-start | bytes 233480 | tf_op jit(solution)/shard_map/ppermute | solution.py:406
  15.6 11.0 %collective-permute-start = (bf16[304,128]{1,0:T(8,128)(2,1)S(1)}, bf16[304,128]{1,0:T(8,128)(2,1)S(1)}, u32[]{:S(2)}, u32[]{:S(2)}) collective-permute-start(bf16[304,128]{1,0:T(8,128)(2,1)S(1)} %copy-done.11), channel_id=1, source_target_pairs={{8,0},{16,8},{24,16},{32,24},{40,32},{48,40},{56,48},{64,56},{72,6... | collective-permute-start | bytes 233480 | tf_op jit(solution)/shard_map/ppermute | solution.py:405
  24.8 1.9 %copy-start.8 = (f32[256]{0:T(256)S(1)}, f32[256]{0:T(256)}, u32[]{:S(2)}) copy-start(f32[256]{0:T(256)} %param.28) | copy-start | bytes 3076
  24.8 1.9 %copy-start.9 = (f32[256]{0:T(256)S(1)}, f32[256]{0:T(256)}, u32[]{:S(2)}) copy-start(f32[256]{0:T(256)} %param.29) | copy-start | bytes 3076
  24.8 1.9 %copy-start.10 = (f32[256]{0:T(256)S(1)}, f32[256]{0:T(256)}, u32[]{:S(2)}) copy-start(f32[256]{0:T(256)} %param.30) | copy-start | bytes 3076
  24.8 1.9 %copy-start.5 = (f32[2048]{0:T(1024)S(1)}, f32[2048]{0:T(1024)}, u32[]{:S(2)}) copy-start(f32[2048]{0:T(1024)} %param.21) | copy-start | bytes 24580
  26.7 0.7 %copy-start.6 = (s32[16]{0:T(128)S(1)}, s32[16]{0:T(128)}, u32[]{:S(2)}) copy-start(s32[16]{0:T(128)} %lookup_ref.3) | copy-start | bytes 196
  26.7 0.7 %copy-start.7 = (s32[16]{0:T(128)S(1)}, s32[16]{0:T(128)}, u32[]{:S(2)}) copy-start(s32[16]{0:T(128)} %tally_ref.1) | copy-start | bytes 196
  36.1 5.2 %copy-start = (f32[16,4,4096]{2,1,0:T(4,128)S(1)}, f32[16,4,4096]{2,1,0:T(4,128)}, u32[]{:S(2)}) copy-start(f32[16,4,4096]{2,1,0:T(4,128)} %param.19) | copy-start | bytes 3145732
  37.0 13.2 %all-to-all-start.1 = ((bf16[4,512,128]{2,1,0:T(8,128)(2,1)}), bf16[4,512,128]{2,1,0:T(8,128)(2,1)S(1)}, u32[]{:S(2)}, u32[]{:S(2)}) async-start(bf16[4,512,128]{2,1,0:T(8,128)(2,1)} %broadcast_in_dim.21), calls=%async_computation.1 | async-start | bytes 1048576 | tf_op jit(solution)/shard_map/all_to_all | solution.py:450

commit v7 on v6

--- a/solution.py
+++ b/solution.py
@@ -21,6 +21,7 @@
 STATE_ROWS = HEADS * HEAD * HEAD // 128
 PIECE = STATE_ROWS + TILES
 PACK_ROWS = 2 * PIECE + 16
+CAME, TALLY, META = SLOTS, SLOTS + 16, 64
 PACK_MIB, MAIN_MIB = 60, 52
 
 
@@ -50,11 +51,11 @@
     return lax.broadcasted_iota(jnp.int32, shape, dim)
 
 
-def column_of(tally_ref, shape):
+def column_of(meta_ref, shape):
     rows = iota(shape, 0)
     out = jnp.zeros(shape, jnp.int32)
     for q in range(SLOTS):
-        out = jnp.where(rows == q, tally_ref[q], out)
+        out = jnp.where(rows == q, meta_ref[TALLY + q], out)
     return out
 
 
@@ -73,19 +74,35 @@
     return me, jnp.where(me == 0, count - 1, me - 1)
 
 
-def pack_kernel(lookup_hbm, prev_hbm, mem_hbm, left_hbm, out_ref, left_out, lookup_ref, prev, mem, left, tile, sems):
-    loads = copies((lookup_hbm, prev_hbm, mem_hbm, left_hbm), (lookup_ref, prev, mem, left), sems)
+def pack_kernel(
+    lookup_hbm, tally_hbm, prev_hbm, mem_hbm, left_hbm, out_ref, left_out, meta_ref,
+    lookup_ref, tally_ref, prev, mem, left, tile, sems,
+):
+    loads = copies(
+        (lookup_hbm, prev_hbm, mem_hbm, left_hbm, tally_hbm), (lookup_ref, prev, mem, left, tally_ref), sems
+    )
     start(loads)
-    first = place()[0] * SLOTS
+    me, behind = place()
+    first = me * SLOTS
     loads[3].wait()
-    sends = [pltpu.make_async_copy(left, left_out.at[n], sems.at[4 + n]) for n in range(left_out.shape[0])]
+    sends = [pltpu.make_async_copy(left, left_out.at[n], sems.at[5 + n]) for n in range(left_out.shape[0])]
     start(sends)
     loads[0].wait()
     kept = jnp.int32(0)
+    slots, wants = [jnp.int32(0)] * 2, [jnp.int32(0)] * 2
     for q in range(SLOTS):
         at = lookup_ref[q] - first
         own = (at >= 0) & (at < SLOTS)
-        kept = kept | jnp.where(own, jnp.int32(1) << jnp.where(own, at, 0), 0)
+        at = jnp.where(own, at, 0)
+        kept = kept | jnp.where(own, jnp.int32(1) << at, 0)
+        meta_ref[q] = at
+        owner = lookup_ref[q] >> (SLOTS.bit_length() - 1)
+        for n, mine in enumerate((jnp.logical_not(own) & (owner == behind), jnp.logical_not(own) & (owner != behind))):
+            slots[n] = jnp.where(mine, q, slots[n])
+            wants[n] = jnp.where(mine, lookup_ref[q] & (SLOTS - 1), wants[n])
+    for n in range(2):
+        meta_ref[CAME + n] = slots[n]
+        meta_ref[CAME + 2 + n] = wants[n]
     low, high = jnp.int32(0), jnp.int32(0)
     for s in range(SLOTS):
         high = jnp.where((kept >> s) & 1 == 0, s, high)
@@ -101,71 +118,53 @@
         begin = pl.multiple_of(slot * STATE_ROWS, STATE_ROWS)
         out_ref[n * PIECE : n * PIECE + STATE_ROWS, :] = mem[pl.ds(begin, STATE_ROWS), :].astype(BF16)
         out_ref[n * PIECE + STATE_ROWS : (n + 1) * PIECE, :] = tile[n * TILES : (n + 1) * TILES, :].astype(BF16)
+    loads[4].wait()
+    for q in range(SLOTS):
+        meta_ref[TALLY + q] = tally_ref[q]
     for copy in sends:
         copy.wait()
 
 
 def pick(recv_ref, wanted, begin, count):
     low = recv_ref[2 * PIECE :, :].astype(F32)[:1, :]
-    is_low = low == (wanted % SLOTS).astype(F32)
+    is_low = low == wanted.astype(F32)
     rows = [recv_ref[at : at + count, :].astype(F32) for at in (begin, PIECE + begin)]
     return jnp.where(is_low, rows[0], rows[1])
 
 
-def sources(where, lookup_ref, q):
-    wanted = lookup_ref[q]
-    owner = wanted // SLOTS
-    own = owner == where[0]
-    before = owner == where[1]
-    at = jnp.where(own, wanted - where[0] * SLOTS, 0)
-    return wanted, own, before, at
-
-
 def copies(sources_, targets, sems):
     return [pltpu.make_async_copy(a, b, sems.at[n]) for n, (a, b) in enumerate(zip(sources_, targets))]
 
 
-def state_copies(where, lookup_ref, mem_hbm, state, sems):
-    out = []
-    for q in range(SLOTS):
-        at = sources(where, lookup_ref, q)[3]
-        out.append(
-            pltpu.make_async_copy(
-                mem_hbm.at[pl.ds(pl.multiple_of(at * STATE_ROWS, STATE_ROWS), STATE_ROWS), :],
-                state.at[pl.ds(q * STATE_ROWS, STATE_ROWS), :],
-                sems.at[q],
-            )
-        )
-    return out
-
-
-def place_received(where, lookup_ref, from_before, from_after, state):
-    for q in range(SLOTS):
-        wanted, own, before, _ = sources(where, lookup_ref, q)
-        here = slice(q * STATE_ROWS, (q + 1) * STATE_ROWS)
-
-        @pl.when(jnp.logical_not(own) & before)
-        def _():
-            state[here, :] = pick(from_before, wanted, 0, STATE_ROWS)
-
-        @pl.when(jnp.logical_not(own) & jnp.logical_not(before))
-        def _():
-            state[here, :] = pick(from_after, wanted, 0, STATE_ROWS)
-
-
 def cut(a, t):
     return a[t * SLOTS : (t + 1) * SLOTS, :]
 
 
-def main_kernel(lookup_ref, tally_ref, mem_hbm, *refs):
+def state_copies(meta_ref, mem_hbm, state, sems):
+    return [
+        pltpu.make_async_copy(
+            mem_hbm.at[pl.ds(pl.multiple_of(meta_ref[q] * STATE_ROWS, STATE_ROWS), STATE_ROWS), :],
+            state.at[pl.ds(q * STATE_ROWS, STATE_ROWS), :],
+            sems.at[q],
+        )
+        for q in range(SLOTS)
+    ]
+
+
+def place_received(meta_ref, received, state):
+    for n, recv_ref in enumerate(received):
+        begin = pl.multiple_of(meta_ref[CAME + n] * STATE_ROWS, STATE_ROWS)
+        state[pl.ds(begin, STATE_ROWS), :] = pick(recv_ref, meta_ref[CAME + 2 + n], 0, STATE_ROWS)
+
+
+def main_kernel(meta_ref, mem_hbm, *refs):
     count = 15
     hbm, (part_ref, moved_ref, vals_ref, last_ref) = refs[:count], refs[count : count + 4]
     bufs = refs[count + 4 : 2 * count + 4]
     x32, shift, state, reads, heads, part, sems, state_sems = refs[2 * count + 4 :]
-    where = place()
     loads = copies(hbm, bufs, sems)
     start(loads[:-1])
-    state_loads = state_copies(where, lookup_ref, mem_hbm, state, state_sems)
+    state_loads = state_copies(meta_ref, mem_hbm, state, state_sems)
     start(state_loads)
     loads[-1].start()
     x_ref, gain_ref, prev_ref, from_after, from_before, blend_ref = bufs[:6]
@@ -180,7 +179,7 @@
         center = row - jnp.mean(row, axis=-1, keepdims=True)
         spread = jnp.mean(center * center, axis=-1, keepdims=True)
         normed.append(center * lax.rsqrt(spread + EPS) * gain)
-    tally = column_of(tally_ref, (SLOTS, 128))[:, :1]
+    tally = column_of(meta_ref, (SLOTS, 128))[:, :1]
     last = normed[0]
     for t in range(1, STEPS):
         last = jnp.where(tally == t + 1, normed[t], last)
@@ -188,22 +187,19 @@
     for n in range(2, 6):
         loads[n].wait()
     for q in range(SLOTS):
-        wanted, own, before, at = sources(where, lookup_ref, q)
-
-        @pl.when(own)
-        def _():
-            shift[q : q + 1, :] = prev_ref[pl.ds(at, 1), :]
-
-        @pl.when(jnp.logical_not(own))
-        def _():
-            rows = jnp.where(
-                before, pick(from_before, wanted, STATE_ROWS, TILES), pick(from_after, wanted, STATE_ROWS, TILES)
-            )
-            for c in range(TILES):
-                shift[q : q + 1, c * 128 : (c + 1) * 128] = rows[c : c + 1, :]
-
+        shift[q : q + 1, :] = prev_ref[pl.ds(meta_ref[q], 1), :]
+    slot = iota((SLOTS, 128), 0)
+    moved_rows = [
+        pick(recv_ref, meta_ref[CAME + 2 + n], STATE_ROWS, TILES) for n, recv_ref in enumerate((from_before, from_after))
+    ]
+    shift_in = []
+    for c in range(TILES):
+        col = shift[:, c * 128 : (c + 1) * 128]
+        for n, rows in enumerate(moved_rows):
+            col = jnp.where(slot == meta_ref[CAME + n], rows[c : c + 1, :], col)
+        shift_in.append(col)
     xn = jnp.concatenate(normed, axis=0)
-    change = jnp.concatenate([shift[...]] + normed[:-1], axis=0) - xn
+    change = jnp.concatenate([jnp.concatenate(shift_in, axis=1)] + normed[:-1], axis=0) - xn
 
     def mix(which):
         return (xn + change * blend_ref[which : which + 1, :]).astype(BF16)
@@ -270,7 +266,7 @@
                 reads[at, :] = jnp.where(head_lane, cut(moved, t)[:, p * 128 : (p + 1) * 128], 0.0)
     for copy in state_loads:
         copy.wait()
-    place_received(where, lookup_ref, from_before, from_after, state)
+    place_received(meta_ref, (from_before, from_after), state)
     for q in range(SLOTS):
         rows = slice(q * STEPS * 8, (q + 1) * STEPS * 8)
         now = state[q * STATE_ROWS : (q + 1) * STATE_ROWS, :]
@@ -299,14 +295,13 @@
     part_ref[...] = part[...].astype(BF16)
 
 
-def update_kernel(lookup_ref, mem_hbm, *refs):
+def update_kernel(meta_ref, mem_hbm, *refs):
     count = 4
     hbm, new_hbm, bufs = refs[:count], refs[count], refs[count + 1 : 2 * count + 1]
     state, keys, vals, decays, fresh, sems, state_sems, new_sems = refs[2 * count + 1 :]
-    where = place()
     loads = copies(hbm, bufs, sems)
     start(loads)
-    state_loads = state_copies(where, lookup_ref, mem_hbm, state, state_sems)
+    state_loads = state_copies(meta_ref, mem_hbm, state, state_sems)
     start(state_loads)
     moved_ref, vals_ref, from_after, from_before = bufs
     loads[0].wait()
@@ -331,7 +326,7 @@
     ones = ((iota((16, 128), 0) // HEADS) % 2 == iota((16, 128), 1) // HEAD).astype(BF16)
     for copy in loads[2:] + state_loads:
         copy.wait()
-    place_received(where, lookup_ref, from_before, from_after, state)
+    place_received(meta_ref, (from_before, from_after), state)
     news = []
     for q in range(SLOTS):
         here = slice(q * STATE_ROWS, (q + 1) * STATE_ROWS)
@@ -390,18 +385,20 @@
     state_buf = scratch((SLOTS * STATE_ROWS, 128), F32)
     rows_buf = scratch((SLOTS * STEPS * 8, 128), F32)
 
-    packed, left = pl.pallas_call(
+    packed, left, meta = pl.pallas_call(
         pack_kernel,
-        out_shape=[shape((PACK_ROWS, 128), BF16), shape((teams,) + left_t.shape, BF16)],
-        in_specs=spec(pl.ANY, 4),
-        out_specs=spec(pltpu.VMEM, 1) + spec(pl.ANY, 1),
-        scratch_shapes=[pltpu.SMEM(lookup.shape, jnp.int32)]
+        out_shape=[
+            shape((PACK_ROWS, 128), BF16), shape((teams,) + left_t.shape, BF16), shape((META,), jnp.int32),
+        ],
+        in_specs=spec(pl.ANY, 5),
+        out_specs=spec(pltpu.VMEM, 1) + spec(pl.ANY, 1) + spec(pltpu.SMEM, 1),
+        scratch_shapes=[pltpu.SMEM(lookup.shape, jnp.int32)] * 2
         + like([prev, mem, left_t])
-        + [scratch((2 * TILES, 128), F32), dma((4 + teams,))],
+        + [scratch((2 * TILES, 128), F32), dma((5 + teams,))],
         compiler_params=params(PACK_MIB),
         cost_estimate=cost(0, 1 << 20),
         name="pack",
-    )(lookup, prev, mem, left_t)
+    )(lookup, tally, prev, mem, left_t)
     from_after = lax.ppermute(packed, "seq", [((i + 1) % rings, i) for i in range(rings)])
     from_before = lax.ppermute(packed, "seq", [(i, (i + 1) % rings) for i in range(rings)])
     left = lax.all_to_all(left, "tensor", 0, 0)
@@ -418,7 +415,7 @@
             shape((ROWS * TILES, 128), BF16), shape((ROWS + SLOTS, LOCAL), F32), shape((ROWS, LOCAL), F32),
             shape((SLOTS, WIDTH), F32),
         ],
-        in_specs=spec(pltpu.SMEM, 2) + spec(pl.ANY, 1 + len(operands)),
+        in_specs=spec(pltpu.SMEM, 1) + spec(pl.ANY, 1 + len(operands)),
         out_specs=spec(pltpu.VMEM, 4),
         scratch_shapes=like(operands)
         + [scratch((ROWS * TILES, 128), F32), scratch((SLOTS, WIDTH), F32), state_buf, rows_buf, rows_buf, scratch((ROWS * TILES, 128), F32)]
@@ -426,7 +423,7 @@
         compiler_params=params(MAIN_MIB),
         cost_estimate=cost(8 * ROWS * WIDTH * LOCAL, 8 << 20),
         name="main",
-    )(lookup, tally, mem, *operands)
+    )(meta, mem, *operands)
 
     operands = [moved, values, from_after, from_before]
     new_states = pl.pallas_call(
@@ -440,7 +437,7 @@
         compiler_params=params(MAIN_MIB),
         cost_estimate=cost(1 << 24, 8 << 20),
         name="update",
-    )(lookup, mem, *operands)
+    )(meta, mem, *operands)
 
     pairs = [[2 * i, 2 * i + 1] for i in range(teams // 2)]
     chips = [[2 * i + c for i in range(teams // 2)] for c in range(2)]

time: 54.8 us -> 54.7 us (level)
  Pallas kernels: 13.7 us -> 12.9 us
  transfers between devices with their start and end apart: 4 -> 4, of which waited for: 3 -> 3; matrix products, arithmetic and copies ran while one was open for 0% -> 0% of each run, Pallas kernels for 9% -> 8%
where the time goes in v7:
time: 54.7 us; the launch traced here: 54.2 us
  starting transfers between devices  25.9 us (47%)
  Pallas kernels  12.9 us (24%)
  waiting for transfers between devices  6.31 us (12%)
  blocking collectives  5.61 us (10%)
  local copies, waits for them, and re-layouts  1.54 us (3%)
  other arithmetic  1.15 us (2%)
  between operations  0.81 us (1%)
    all_to_all x1, starting transfers between devices, shards(): left = lax.all_to_all(left, 'tensor', 0, 0)  10.3 us
    ppermute x1, starting transfers between devices, shards(): lax.ppermute(packed, 'seq', [((i + 1) % rings, i) for i in range(rings)])  9.1 us
    pallas_call x1, Pallas kernels, shards(): pl.pallas_call(main_kernel, out_shape=[shape((ROWS * TILES, 128), BF16),...  5.99 us
    all_to_all x1, waiting for transfers between devices, shards(): lax.all_to_all(jnp.broadcast_to(mine[None], (teams // 2,) + mine.shape),...  4.46 us
    all_to_all x1, starting transfers between devices, shards(): lax.all_to_all(jnp.broadcast_to(mine[None], (teams // 2,) + mine.shape),...  4.38 us
    pallas_call x1, Pallas kernels, shards(): pl.pallas_call(update_kernel, out_shape=shape((SLOTS * STATE_ROWS, 128),...  4.36 us
    all_gather x1, blocking collectives, shards(): proj = lax.all_gather(total, 'tensor', axis_index_groups=pairs, tiled=True)  3.16 us
    pallas_call x1, Pallas kernels, shards(): pl.pallas_call(pack_kernel, out_shape=[shape((PACK_ROWS, 128), BF16), sha...  2.58 us
  transfers between devices with their start and end apart: 4, of which 3 were waited for; matrix products, arithmetic and copies ran while one was open for 0% of the time, Pallas kernels for 8%

profile of v7, /device:TPU:1, one launch (start us, length us, event | category | flops | bytes accessed | tf_op | source)
XLA Modules:
  0.0 54.2 jit_solution(2805831020189692628)
XLA Ops:
  0.6 2.6 %pack.1 = (bf16[304,128]{1,0:T(8,128)(2,1)}, bf16[8,64,256]{2,1,0:T(8,128)(2,1)}, s32[64]{0:T(128)}) custom-call(s32[16]{0:T(128)} %lookup_hbm.1, s32[16]{0:T(128)} %tally_hbm.1, f32[16,2048]{1,0:T(8,128)} %refs_2_.1, f32[2048,128]{1,0:T(8,128)} %bitcast.26, bf16[64,256]{1,0:T(8,128)(2,1)} %bitcast.37), custom_call_target="tpu_custom_call" | custom-call | bytes 1048576 | tf_op jit(solution)/shard_map/pack/pallas_call | solution.py:388
  3.2 0.0 copy-start.11
  3.2 0.0 copy-start.1
  3.2 0.0 copy-start.2
  3.3 0.0 copy-start.4
  3.3 10.3 %all-to-all-start = ((bf16[8,64,256]{2,1,0:T(8,128)(2,1)}), bf16[8,64,256]{2,1,0:T(8,128)(2,1)S(1)}, u32[]{:S(2)}, u32[]{:S(2)}) async-start(bf16[8,64,256]{2,1,0:T(8,128)(2,1)} %get-tuple-element.12), calls=%async_computation | async-start | bytes 524288 | tf_op jit(solution)/shard_map/all_to_all | solution.py:404
  13.6 0.0 copy-start.3
  13.6 0.0 copy-done.11
  13.6 2.0 %collective-permute-start.1 = (bf16[304,128]{1,0:T(8,128)(2,1)S(1)}, bf16[304,128]{1,0:T(8,128)(2,1)S(1)}, u32[]{:S(2)}, u32[]{:S(2)}) collective-permute-start(bf16[304,128]{1,0:T(8,128)(2,1)S(1)} %copy-done.11), channel_id=1, source_target_pairs={{0,8},{8,16},{16,24},{24,32},{32,40},{40,48},{48,56},{56,64},{64,7... | collective-permute-start | bytes 233480 | tf_op jit(solution)/shard_map/ppermute | solution.py:403
  15.7 9.1 %collective-permute-start = (bf16[304,128]{1,0:T(8,128)(2,1)S(1)}, bf16[304,128]{1,0:T(8,128)(2,1)S(1)}, u32[]{:S(2)}, u32[]{:S(2)}) collective-permute-start(bf16[304,128]{1,0:T(8,128)(2,1)S(1)} %copy-done.11), channel_id=1, source_target_pairs={{8,0},{16,8},{24,16},{32,24},{40,32},{48,40},{56,48},{64,56},{72,6... | collective-permute-start | bytes 233480 | tf_op jit(solution)/shard_map/ppermute | solution.py:402
  24.8 0.0 copy-start.8
  24.8 0.0 copy-start.9
  24.8 0.0 copy-start.5
  24.8 0.8 %collective-permute-done.1.refs_4_.refs_3_ = bf16[304,128]{1,0:T(8,128)(2,1)S(1)} collective-permute-done((bf16[304,128]{1,0:T(8,128)(2,1)S(1)}, bf16[304,128]{1,0:T(8,128)(2,1)S(1)}, u32[]{:S(2)}, u32[]{:S(2)}) %collective-permute-start.1) | collective-permute-done | bytes 77856 | tf_op jit(solution)/shard_map/ppermute | solution.py:403
  25.7 1.0 %collective-permute-done.refs_3_.refs_2_ = bf16[304,128]{1,0:T(8,128)(2,1)S(1)} collective-permute-done((bf16[304,128]{1,0:T(8,128)(2,1)S(1)}, bf16[304,128]{1,0:T(8,128)(2,1)S(1)}, u32[]{:S(2)}, u32[]{:S(2)}) %collective-permute-start) | collective-permute-done | bytes 77856 | tf_op jit(solution)/shard_map/ppermute | solution.py:402
  26.7 0.0 all-to-all-done.refs_9_
  26.7 0.0 copy-start.6
  26.7 0.0 copy-start.7
  26.7 0.0 copy-done.1
  26.7 0.0 copy-done.2
  26.7 0.0 copy-done.4
  26.7 0.0 copy-done.3
  26.7 0.0 copy-done.8
  26.7 0.0 copy-done.9
  26.7 0.0 copy-done.5
  26.7 0.6 %copy-done.6 = s32[64]{0:T(128)S(1)} copy-done((s32[64]{0:T(128)S(1)}, s32[64]{0:T(128)}, u32[]{:S(2)}) %copy-start.6) | copy-done | bytes 280
  27.3 0.0 copy-done.7
  27.4 6.0 %main.1 = (bf16[1024,128]{1,0:T(8,128)(2,1)S(1)}, f32[80,256]{1,0:T(8,128)S(1)}, f32[64,256]{1,0:T(8,128)S(1)}, f32[16,2048]{1,0:T(8,128)}) custom-call(s32[64]{0:T(128)S(1)} %copy-done.6, f32[2048,128]{1,0:T(8,128)} %bitcast.27, bf16[1024,128]{1,0:T(8,128)(2,1)S(1)} %bitcast.29, f32[16,128]{1,0:T(8,128)S(1)} %bitcast.30, f32[16,2048]{1,0:T(8,128)S(1)} %copy-done.2, ...), custom_call_target="tpu_custom_call" | custom-call | flops 268435456 | bytes 8388608 | tf_op jit(solution)/shard_map/main/pallas_call | solution.py:412
  33.4 2.5 %all-gather = bf16[2048,128]{1,0:T(8,128)(2,1)S(1)} all-gather(bf16[1024,128]{1,0:T(8,128)(2,1)S(1)} %get-tuple-element.13), channel_id=2, replica_groups={{0,1},{2,3},{4,5},{6,7},{8,9},{10,11},{12,13},{14,15},{16,17},{18,19},{..., dimensions={0}, use_global_device_ids=true | all-gather | bytes 786432 | tf_op jit(solution)/shard_map/all_gather | solution.py:445
  35.8 0.0 copy-start
  35.9 0.9 %broadcast_in_dim.21 = bf16[4,512,128]{2,1,0:T(8,128)(2,1)} broadcast(bf16[512,128]{1,0:T(8,128)(2,1)S(1)} %dynamic-slice_reduce_fusion), dimensions={1,2} | broadcast | bytes 655360 | tf_op jit(solution)/shard_map/broadcast_in_dim | solution.py:448
  36.7 0.0 copy-start.10
  36.7 4.4 %all-to-all-start.1 = ((bf16[4,512,128]{2,1,0:T(8,128)(2,1)}), bf16[4,512,128]{2,1,0:T(8,128)(2,1)S(1)}, u32[]{:S(2)}, u32[]{:S(2)}) async-start(bf16[4,512,128]{2,1,0:T(8,128)(2,1)} %broadcast_in_dim.21), calls=%async_computation.1 | async-start | bytes 1048576 | tf_op jit(solution)/shard_map/all_to_all | solution.py:447
  41.1 0.0 copy-done.10
  41.1 0.1 iota_compare_fusion
  41.2 0.0 copy-done
  41.2 4.4 %update.1 = f32[2048,128]{1,0:T(8,128)} custom-call(s32[64]{0:T(128)S(1)} %copy-done.6, f32[2048,128]{1,0:T(8,128)S(1)} %bitcast.28, f32[80,256]{1,0:T(8,128)S(1)} %get-tuple-element.14.refs_0_, f32[64,256]{1,0:T(8,128)S(1)} %get-tuple-element.15.refs_1_, bf16[304,128]{1,0:T(8,128)(2,1)S(1)} %collective-permute-done.refs_3_.refs_2_, ...), custom_call_target="tpu_custom_call" | custom-call | flops 16777216 | bytes 8388608 | tf_op jit(solution)/shard_map/update/pallas_call | solution.py:429
  45.6 4.5 %all-to-all-done.1 = bf16[4,512,128]{2,1,0:T(8,128)(2,1)S(1)} async-done(((bf16[4,512,128]{2,1,0:T(8,128)(2,1)}), bf16[4,512,128]{2,1,0:T(8,128)(2,1)S(1)}, u32[]{:S(2)}, u32[]{:S(2)}) %all-to-all-start.1) | async-done | bytes 524320 | tf_op jit(solution)/shard_map/all_to_all | solution.py:447
  50.0 0.1 reduce_sum.25
  50.1 3.2 %all_gather.11 = bf16[16,4,2048]{2,1,0:T(4,128)(2,1)S(1)} all-gather(bf16[8,4,2048]{2,1,0:T(4,128)(2,1)S(1)} %bitcast.36), channel_id=1, replica_groups={{0,1},{2,3},{4,5},{6,7},{8,9},{10,11},{12,13},{14,15},{16,17},{18,19},{..., dimensions={0}, use_global_device_ids=true | all-gather | bytes 393216 | tf_op jit(solution)/shard_map/all_gather | solution.py:451
  53.3 1.0 %select_convert_fusion = bf16[16,4,2048]{2,1,0:T(4,128)(2,1)} fusion(bf16[16,4,2048]{2,1,0:T(4,128)(2,1)S(1)} %all_gather.11, bf16[16,4,2048]{2,1,0:T(4,128)(2,1)S(1)} %copy-done.1, pred[16,4]{1,0:T(8,128)(4,1)S(1)} %iota_compare_fusion), kind=kLoop, calls=%fused_computation | loop fusion | flops 655360 | bytes 786496 | tf_op jit(solution)/shard_map/convert_element_type | solution.py:453
  (1 shorter events, 0.0 us)
Async XLA Ops:
  3.2 10.4 %copy-start.11 = (bf16[304,128]{1,0:T(8,128)(2,1)S(1)}, bf16[304,128]{1,0:T(8,128)(2,1)}, u32[]{:S(2)}) copy-start(bf16[304,128]{1,0:T(8,128)(2,1)} %get-tuple-element.11) | copy-start | bytes 233476
  3.2 23.4 %copy-start.1 = (bf16[16,4,2048]{2,1,0:T(4,128)(2,1)S(1)}, bf16[16,4,2048]{2,1,0:T(4,128)(2,1)}, u32[]{:S(2)}) copy-start(bf16[16,4,2048]{2,1,0:T(4,128)(2,1)} %param.16) | copy-start | bytes 786436
  3.2 23.4 %copy-start.2 = (f32[16,2048]{1,0:T(8,128)S(1)}, f32[16,2048]{1,0:T(8,128)}, u32[]{:S(2)}) copy-start(f32[16,2048]{1,0:T(8,128)} %refs_2_.1) | copy-start | bytes 393220
  3.3 23.4 %copy-start.4 = (bf16[64,256]{1,0:T(8,128)(2,1)S(1)}, bf16[64,256]{1,0:T(8,128)(2,1)}, u32[]{:S(2)}) copy-start(bf16[64,256]{1,0:T(8,128)(2,1)} %refs_10_.1) | copy-start | bytes 98308
  3.3 23.4 %all-to-all-start = ((bf16[8,64,256]{2,1,0:T(8,128)(2,1)}), bf16[8,64,256]{2,1,0:T(8,128)(2,1)S(1)}, u32[]{:S(2)}, u32[]{:S(2)}) async-start(bf16[8,64,256]{2,1,0:T(8,128)(2,1)} %get-tuple-element.12), calls=%async_computation | async-start | bytes 524288 | tf_op jit(solution)/shard_map/all_to_all | solution.py:404
  13.6 13.1 %copy-start.3 = (f32[4,2048]{1,0:T(4,128)S(1)}, f32[4,2048]{1,0:T(4,128)}, u32[]{:S(2)}) copy-start(f32[4,2048]{1,0:T(4,128)} %refs_5_.1) | copy-start | bytes 98308
  13.6 12.1 %collective-permute-start.1 = (bf16[304,128]{1,0:T(8,128)(2,1)S(1)}, bf16[304,128]{1,0:T(8,128)(2,1)S(1)}, u32[]{:S(2)}, u32[]{:S(2)}) collective-permute-start(bf16[304,128]{1,0:T(8,128)(2,1)S(1)} %copy-done.11), channel_id=1, source_target_pairs={{0,8},{8,16},{16,24},{24,32},{32,40},{40,48},{48,56},{56,64},{64,7... | collective-permute-start | bytes 233480 | tf_op jit(solution)/shard_map/ppermute | solution.py:403
  15.7 11.0 %collective-permute-start = (bf16[304,128]{1,0:T(8,128)(2,1)S(1)}, bf16[304,128]{1,0:T(8,128)(2,1)S(1)}, u32[]{:S(2)}, u32[]{:S(2)}) collective-permute-start(bf16[304,128]{1,0:T(8,128)(2,1)S(1)} %copy-done.11), channel_id=1, source_target_pairs={{8,0},{16,8},{24,16},{32,24},{40,32},{48,40},{56,48},{64,56},{72,6... | collective-permute-start | bytes 233480 | tf_op jit(solution)/shard_map/ppermute | solution.py:402
  24.8 1.9 %copy-start.8 = (f32[256]{0:T(256)S(1)}, f32[256]{0:T(256)}, u32[]{:S(2)}) copy-start(f32[256]{0:T(256)} %param.29) | copy-start | bytes 3076
  24.8 1.9 %copy-start.9 = (f32[256]{0:T(256)S(1)}, f32[256]{0:T(256)}, u32[]{:S(2)}) copy-start(f32[256]{0:T(256)} %param.30) | copy-start | bytes 3076
  24.8 1.9 %copy-start.5 = (f32[2048]{0:T(1024)S(1)}, f32[2048]{0:T(1024)}, u32[]{:S(2)}) copy-start(f32[2048]{0:T(1024)} %param.21) | copy-start | bytes 24580
  26.7 0.7 %copy-start.6 = (s32[64]{0:T(128)S(1)}, s32[64]{0:T(128)}, u32[]{:S(2)}) copy-start(s32[64]{0:T(128)} %get-tuple-element.10.meta_ref) | copy-start | bytes 772
  26.7 0.7 %copy-start.7 = (f32[256]{0:T(256)S(1)}, f32[256]{0:T(256)}, u32[]{:S(2)}) copy-start(f32[256]{0:T(256)} %param.28) | copy-start | bytes 3076
  35.8 5.4 %copy-start = (f32[16,4,4096]{2,1,0:T(4,128)S(1)}, f32[16,4,4096]{2,1,0:T(4,128)}, u32[]{:S(2)}) copy-start(f32[16,4,4096]{2,1,0:T(4,128)} %param.19) | copy-start | bytes 3145732
  36.7 4.4 %copy-start.10 = (s32[16]{0:T(128)S(1)}, s32[16]{0:T(128)}, u32[]{:S(2)}) copy-start(s32[16]{0:T(128)} %tally_hbm.1) | copy-start | bytes 196
  36.7 13.3 %all-to-all-start.1 = ((bf16[4,512,128]{2,1,0:T(8,128)(2,1)}), bf16[4,512,128]{2,1,0:T(8,128)(2,1)S(1)}, u32[]{:S(2)}, u32[]{:S(2)}) async-start(bf16[4,512,128]{2,1,0:T(8,128)(2,1)} %broadcast_in_dim.21), calls=%async_computation.1 | async-start | bytes 1048576 | tf_op jit(solution)/shard_map/all_to_all | solution.py:447

commit v8 on v7

--- a/solution.py
+++ b/solution.py
@@ -100,13 +100,15 @@
         for n, mine in enumerate((jnp.logical_not(own) & (owner == behind), jnp.logical_not(own) & (owner != behind))):
             slots[n] = jnp.where(mine, q, slots[n])
             wants[n] = jnp.where(mine, lookup_ref[q] & (SLOTS - 1), wants[n])
-    for n in range(2):
-        meta_ref[CAME + n] = slots[n]
-        meta_ref[CAME + 2 + n] = wants[n]
     low, high = jnp.int32(0), jnp.int32(0)
     for s in range(SLOTS):
         high = jnp.where((kept >> s) & 1 == 0, s, high)
         low = jnp.where((kept >> (SLOTS - 1 - s)) & 1 == 0, SLOTS - 1 - s, low)
+    for n, free in enumerate((low, high)):
+        meta_ref[slots[n]] = free
+        meta_ref[CAME + n] = slots[n]
+        meta_ref[CAME + 2 + n] = wants[n]
+        meta_ref[CAME + 4 + n] = free
     out_ref[2 * PIECE :, :] = jnp.full((16, 128), low, jnp.int32).astype(F32).astype(BF16)
     loads[1].wait()
     for n, slot in enumerate((low, high)):
@@ -140,32 +142,25 @@
     return a[t * SLOTS : (t + 1) * SLOTS, :]
 
 
-def state_copies(meta_ref, mem_hbm, state, sems):
-    return [
-        pltpu.make_async_copy(
-            mem_hbm.at[pl.ds(pl.multiple_of(meta_ref[q] * STATE_ROWS, STATE_ROWS), STATE_ROWS), :],
-            state.at[pl.ds(q * STATE_ROWS, STATE_ROWS), :],
-            sems.at[q],
-        )
-        for q in range(SLOTS)
-    ]
-
-
 def place_received(meta_ref, received, state):
     for n, recv_ref in enumerate(received):
-        begin = pl.multiple_of(meta_ref[CAME + n] * STATE_ROWS, STATE_ROWS)
+        begin = pl.multiple_of(meta_ref[CAME + 4 + n] * STATE_ROWS, STATE_ROWS)
         state[pl.ds(begin, STATE_ROWS), :] = pick(recv_ref, meta_ref[CAME + 2 + n], 0, STATE_ROWS)
+
+
+def state_of(meta_ref, state, q):
+    return state[pl.ds(pl.multiple_of(meta_ref[q] * STATE_ROWS, STATE_ROWS), STATE_ROWS), :]
 
 
 def main_kernel(meta_ref, mem_hbm, *refs):
     count = 15
     hbm, (part_ref, moved_ref, vals_ref, last_ref) = refs[:count], refs[count : count + 4]
     bufs = refs[count + 4 : 2 * count + 4]
-    x32, shift, state, reads, heads, part, sems, state_sems = refs[2 * count + 4 :]
+    x32, shift, state, reads, heads, part, ordered, sems, state_sem = refs[2 * count + 4 :]
     loads = copies(hbm, bufs, sems)
     start(loads[:-1])
-    state_loads = state_copies(meta_ref, mem_hbm, state, state_sems)
-    start(state_loads)
+    state_load = pltpu.make_async_copy(mem_hbm, state, state_sem)
+    state_load.start()
     loads[-1].start()
     x_ref, gain_ref, prev_ref, from_after, from_before, blend_ref = bufs[:6]
     left_ref, right_ref, base_ref, boost_ref, team_ref, final_ref = bufs[9:]
@@ -264,12 +259,11 @@
             for t in range(STEPS):
                 at = pl.ds(t * 8 + p * HEADS + h, SLOTS, stride=STEPS * 8)
                 reads[at, :] = jnp.where(head_lane, cut(moved, t)[:, p * 128 : (p + 1) * 128], 0.0)
-    for copy in state_loads:
-        copy.wait()
+    state_load.wait()
     place_received(meta_ref, (from_before, from_after), state)
     for q in range(SLOTS):
         rows = slice(q * STEPS * 8, (q + 1) * STEPS * 8)
-        now = state[q * STATE_ROWS : (q + 1) * STATE_ROWS, :]
+        now = state_of(meta_ref, state, q)
         heads[rows, :] = dot(reads[rows, :].astype(BF16), now.astype(BF16))
 
     outs = []
@@ -286,23 +280,31 @@
     y = jnp.concatenate(outs, axis=0)
     center = y - dot_split(y, same_head) * (1.0 / HEAD)
     spread = dot_split(center * center, same_head) * (1.0 / HEAD)
-    g = (center * lax.rsqrt(spread + EPS) * row_of(team_ref)).astype(BF16)
+    g = center * lax.rsqrt(spread + EPS) * row_of(team_ref)
+    for t in range(STEPS):
+        for c in range(LOCAL // 128):
+            ordered[c, pl.ds(t, SLOTS, stride=STEPS), :] = cut(g, t)[:, c * 128 : (c + 1) * 128]
+    g = jnp.concatenate([ordered[c] for c in range(LOCAL // 128)], axis=1).astype(BF16)
     loads[14].wait()
     proj = dot(g, final_ref[...])
-    for t in range(STEPS):
-        for c in range(TILES):
-            part[pl.ds(c * STEPS + t, SLOTS, stride=STEPS * TILES), :] = cut(proj, t)[:, c * 128 : (c + 1) * 128]
+    for q in range(SLOTS):
+        rows = proj[q * STEPS : (q + 1) * STEPS, :]
+        for c in range(0, TILES, 2):
+            at = (q * TILES + c) * STEPS
+            part[at : at + 2 * STEPS, :] = jnp.concatenate(
+                [rows[:, c * 128 : (c + 1) * 128], rows[:, (c + 1) * 128 : (c + 2) * 128]], axis=0
+            )
     part_ref[...] = part[...].astype(BF16)
 
 
 def update_kernel(meta_ref, mem_hbm, *refs):
     count = 4
     hbm, new_hbm, bufs = refs[:count], refs[count], refs[count + 1 : 2 * count + 1]
-    state, keys, vals, decays, fresh, sems, state_sems, new_sems = refs[2 * count + 1 :]
+    state, keys, vals, decays, fresh, sems, state_sem, new_sems = refs[2 * count + 1 :]
     loads = copies(hbm, bufs, sems)
     start(loads)
-    state_loads = state_copies(meta_ref, mem_hbm, state, state_sems)
-    start(state_loads)
+    state_load = pltpu.make_async_copy(mem_hbm, state, state_sem)
+    state_load.start()
     moved_ref, vals_ref, from_after, from_before = bufs
     loads[0].wait()
     loads[1].wait()
@@ -324,7 +326,7 @@
             decays[pl.ds(p * HEADS + h, SLOTS, stride=16), :] = high
             decays[pl.ds(8 + p * HEADS + h, SLOTS, stride=16), :] = whole - high
     ones = ((iota((16, 128), 0) // HEADS) % 2 == iota((16, 128), 1) // HEAD).astype(BF16)
-    for copy in loads[2:] + state_loads:
+    for copy in loads[2:] + [state_load]:
         copy.wait()
     place_received(meta_ref, (from_before, from_after), state)
     news = []
@@ -333,7 +335,7 @@
         rows = slice(q * STEPS * 8, (q + 1) * STEPS * 8)
         fade = dot_rows(decays[q * 16 : (q + 1) * 16, :].astype(BF16), ones)
         grown = dot_rows(keys[rows, :].astype(BF16), vals[rows, :].astype(BF16))
-        fresh[here, :] = fade * state[here, :] + grown
+        fresh[here, :] = fade * state_of(meta_ref, state, q) + grown
         news.append(pltpu.make_async_copy(fresh.at[here, :], new_hbm.at[here, :], new_sems.at[q]))
         news[-1].start()
     for copy in news:
@@ -419,7 +421,7 @@
         out_specs=spec(pltpu.VMEM, 4),
         scratch_shapes=like(operands)
         + [scratch((ROWS * TILES, 128), F32), scratch((SLOTS, WIDTH), F32), state_buf, rows_buf, rows_buf, scratch((ROWS * TILES, 128), F32)]
-        + [dma((len(operands),)), dma((SLOTS,))],
+        + [scratch((LOCAL // 128, ROWS, 128), F32), dma((len(operands),)), dma],
         compiler_params=params(MAIN_MIB),
         cost_estimate=cost(8 * ROWS * WIDTH * LOCAL, 8 << 20),
         name="main",
@@ -433,7 +435,7 @@
         out_specs=spec(pl.ANY, 1)[0],
         scratch_shapes=like(operands)
         + [state_buf, rows_buf, rows_buf, scratch((SLOTS * 16, 128), F32), state_buf]
-        + [dma((len(operands),)), dma((SLOTS,)), dma((SLOTS,))],
+        + [dma((len(operands),)), dma, dma((SLOTS,))],
         compiler_params=params(MAIN_MIB),
         cost_estimate=cost(1 << 24, 8 << 20),
         name="update",

time: 54.7 us -> 54.5 us (level)
  Pallas kernels: 12.9 us -> 11.3 us
  waiting for transfers between devices: 6.31 us -> 7.76 us
    all_to_all x1, waiting for transfers between devices: 4.46 us -> 5.91 us  [shards(): lax.all_to_all(jnp.broadcast_to(mine[None], (teams // 2,) + mine.shape),...]
    pallas_call x1, Pallas kernels: 4.36 us -> 2.91 us  [shards(): pl.pallas_call(update_kernel, out_shape=shape((SLOTS * STATE_ROWS, 128),...]
  transfers between devices with their start and end apart: 4 -> 4, of which waited for: 3 -> 3; matrix products, arithmetic and copies ran while one was open for 0% -> 0% of each run, Pallas kernels for 8% -> 5%
where the time goes in v8:
time: 54.5 us; the launch traced here: 54.1 us
  starting transfers between devices  25.9 us (48%)
  Pallas kernels  11.3 us (21%)
  waiting for transfers between devices  7.76 us (14%)
  blocking collectives  5.62 us (10%)
  local copies, waits for them, and re-layouts  1.54 us (3%)
  other arithmetic  1.15 us (2%)
  between operations  0.81 us (1%)
    all_to_all x1, starting transfers between devices, shards(): left = lax.all_to_all(left, 'tensor', 0, 0)  10.3 us
    ppermute x1, starting transfers between devices, shards(): lax.ppermute(packed, 'seq', [((i + 1) % rings, i) for i in range(rings)])  9.1 us
    all_to_all x1, waiting for transfers between devices, shards(): lax.all_to_all(jnp.broadcast_to(mine[None], (teams // 2,) + mine.shape),...  5.91 us
    pallas_call x1, Pallas kernels, shards(): pl.pallas_call(main_kernel, out_shape=[shape((ROWS * TILES, 128), BF16),...  5.85 us
    all_to_all x1, starting transfers between devices, shards(): lax.all_to_all(jnp.broadcast_to(mine[None], (teams // 2,) + mine.shape),...  4.38 us
    all_gather x1, blocking collectives, shards(): proj = lax.all_gather(total, 'tensor', axis_index_groups=pairs, tiled=True)  3.16 us
    pallas_call x1, Pallas kernels, shards(): pl.pallas_call(update_kernel, out_shape=shape((SLOTS * STATE_ROWS, 128),...  2.91 us
    pallas_call x1, Pallas kernels, shards(): pl.pallas_call(pack_kernel, out_shape=[shape((PACK_ROWS, 128), BF16), sha...  2.58 us
  transfers between devices with their start and end apart: 4, of which 3 were waited for; matrix products, arithmetic and copies ran while one was open for 0% of the time, Pallas kernels for 5%

profile of v8, /device:TPU:1, one launch (start us, length us, event | category | flops | bytes accessed | tf_op | source)
XLA Modules:
  0.0 54.1 jit_solution(1751419369192589697)
XLA Ops:
  0.6 2.6 %pack.1 = (bf16[304,128]{1,0:T(8,128)(2,1)}, bf16[8,64,256]{2,1,0:T(8,128)(2,1)}, s32[64]{0:T(128)}) custom-call(s32[16]{0:T(128)} %lookup_hbm.1, s32[16]{0:T(128)} %tally_hbm.1, f32[16,2048]{1,0:T(8,128)} %refs_2_.1, f32[2048,128]{1,0:T(8,128)} %bitcast.26, bf16[64,256]{1,0:T(8,128)(2,1)} %bitcast.37), custom_call_target="tpu_custom_call" | custom-call | bytes 1048576 | tf_op jit(solution)/shard_map/pack/pallas_call | solution.py:390
  3.2 0.0 copy-start.11
  3.2 0.0 copy-start.1
  3.2 0.0 copy-start.2
  3.3 0.0 copy-start.4
  3.3 10.3 %all-to-all-start = ((bf16[8,64,256]{2,1,0:T(8,128)(2,1)}), bf16[8,64,256]{2,1,0:T(8,128)(2,1)S(1)}, u32[]{:S(2)}, u32[]{:S(2)}) async-start(bf16[8,64,256]{2,1,0:T(8,128)(2,1)} %get-tuple-element.12), calls=%async_computation | async-start | bytes 524288 | tf_op jit(solution)/shard_map/all_to_all | solution.py:406
  13.6 0.0 copy-start.3
  13.6 0.0 copy-done.11
  13.6 2.0 %collective-permute-start.1 = (bf16[304,128]{1,0:T(8,128)(2,1)S(1)}, bf16[304,128]{1,0:T(8,128)(2,1)S(1)}, u32[]{:S(2)}, u32[]{:S(2)}) collective-permute-start(bf16[304,128]{1,0:T(8,128)(2,1)S(1)} %copy-done.11), channel_id=1, source_target_pairs={{0,8},{8,16},{16,24},{24,32},{32,40},{40,48},{48,56},{56,64},{64,7... | collective-permute-start | bytes 233480 | tf_op jit(solution)/shard_map/ppermute | solution.py:405
  15.7 9.1 %collective-permute-start = (bf16[304,128]{1,0:T(8,128)(2,1)S(1)}, bf16[304,128]{1,0:T(8,128)(2,1)S(1)}, u32[]{:S(2)}, u32[]{:S(2)}) collective-permute-start(bf16[304,128]{1,0:T(8,128)(2,1)S(1)} %copy-done.11), channel_id=1, source_target_pairs={{8,0},{16,8},{24,16},{32,24},{40,32},{48,40},{56,48},{64,56},{72,6... | collective-permute-start | bytes 233480 | tf_op jit(solution)/shard_map/ppermute | solution.py:404
  24.8 0.0 copy-start.8
  24.8 0.0 copy-start.9
  24.8 0.0 copy-start.5
  24.8 0.8 %collective-permute-done.1.refs_4_.refs_3_ = bf16[304,128]{1,0:T(8,128)(2,1)S(1)} collective-permute-done((bf16[304,128]{1,0:T(8,128)(2,1)S(1)}, bf16[304,128]{1,0:T(8,128)(2,1)S(1)}, u32[]{:S(2)}, u32[]{:S(2)}) %collective-permute-start.1) | collective-permute-done | bytes 77856 | tf_op jit(solution)/shard_map/ppermute | solution.py:405
  25.7 1.0 %collective-permute-done.refs_3_.refs_2_ = bf16[304,128]{1,0:T(8,128)(2,1)S(1)} collective-permute-done((bf16[304,128]{1,0:T(8,128)(2,1)S(1)}, bf16[304,128]{1,0:T(8,128)(2,1)S(1)}, u32[]{:S(2)}, u32[]{:S(2)}) %collective-permute-start) | collective-permute-done | bytes 77856 | tf_op jit(solution)/shard_map/ppermute | solution.py:404
  26.7 0.0 all-to-all-done.refs_9_
  26.7 0.0 copy-start.6
  26.7 0.0 copy-start.7
  26.7 0.0 copy-done.1
  26.7 0.0 copy-done.2
  26.7 0.0 copy-done.4
  26.7 0.0 copy-done.3
  26.7 0.0 copy-done.8
  26.7 0.0 copy-done.9
  26.7 0.0 copy-done.5
  26.7 0.6 %copy-done.6 = s32[64]{0:T(128)S(1)} copy-done((s32[64]{0:T(128)S(1)}, s32[64]{0:T(128)}, u32[]{:S(2)}) %copy-start.6) | copy-done | bytes 280
  27.3 0.0 copy-done.7
  27.4 5.8 %main.1 = (bf16[1024,128]{1,0:T(8,128)(2,1)S(1)}, f32[80,256]{1,0:T(8,128)S(1)}, f32[64,256]{1,0:T(8,128)S(1)}, f32[16,2048]{1,0:T(8,128)}) custom-call(s32[64]{0:T(128)S(1)} %copy-done.6, f32[2048,128]{1,0:T(8,128)} %bitcast.27, bf16[1024,128]{1,0:T(8,128)(2,1)S(1)} %bitcast.29, f32[16,128]{1,0:T(8,128)S(1)} %bitcast.30, f32[16,2048]{1,0:T(8,128)S(1)} %copy-done.2, ...), custom_call_target="tpu_custom_call" | custom-call | flops 268435456 | bytes 8388608 | tf_op jit(solution)/shard_map/main/pallas_call | solution.py:414
  33.2 2.5 %all-gather = bf16[2048,128]{1,0:T(8,128)(2,1)S(1)} all-gather(bf16[1024,128]{1,0:T(8,128)(2,1)S(1)} %get-tuple-element.13), channel_id=2, replica_groups={{0,1},{2,3},{4,5},{6,7},{8,9},{10,11},{12,13},{14,15},{16,17},{18,19},{..., dimensions={0}, use_global_device_ids=true | all-gather | bytes 786432 | tf_op jit(solution)/shard_map/all_gather | solution.py:447
  35.7 0.0 copy-start
  35.7 0.9 %broadcast_in_dim.21 = bf16[4,512,128]{2,1,0:T(8,128)(2,1)} broadcast(bf16[512,128]{1,0:T(8,128)(2,1)S(1)} %dynamic-slice_reduce_fusion), dimensions={1,2} | broadcast | bytes 655360 | tf_op jit(solution)/shard_map/broadcast_in_dim | solution.py:450
  36.6 0.0 copy-start.10
  36.6 4.4 %all-to-all-start.1 = ((bf16[4,512,128]{2,1,0:T(8,128)(2,1)}), bf16[4,512,128]{2,1,0:T(8,128)(2,1)S(1)}, u32[]{:S(2)}, u32[]{:S(2)}) async-start(bf16[4,512,128]{2,1,0:T(8,128)(2,1)} %broadcast_in_dim.21), calls=%async_computation.1 | async-start | bytes 1048576 | tf_op jit(solution)/shard_map/all_to_all | solution.py:449
  41.0 0.0 copy-done.10
  41.0 0.1 iota_compare_fusion
  41.0 0.0 copy-done
  41.0 2.9 %update.1 = f32[2048,128]{1,0:T(8,128)} custom-call(s32[64]{0:T(128)S(1)} %copy-done.6, f32[2048,128]{1,0:T(8,128)S(1)} %bitcast.28, f32[80,256]{1,0:T(8,128)S(1)} %get-tuple-element.14.refs_0_, f32[64,256]{1,0:T(8,128)S(1)} %get-tuple-element.15.refs_1_, bf16[304,128]{1,0:T(8,128)(2,1)S(1)} %collective-permute-done.refs_3_.refs_2_, ...), custom_call_target="tpu_custom_call" | custom-call | flops 16777216 | bytes 8388608 | tf_op jit(solution)/shard_map/update/pallas_call | solution.py:431
  44.0 5.9 %all-to-all-done.1 = bf16[4,512,128]{2,1,0:T(8,128)(2,1)S(1)} async-done(((bf16[4,512,128]{2,1,0:T(8,128)(2,1)}), bf16[4,512,128]{2,1,0:T(8,128)(2,1)S(1)}, u32[]{:S(2)}, u32[]{:S(2)}) %all-to-all-start.1) | async-done | bytes 524320 | tf_op jit(solution)/shard_map/all_to_all | solution.py:449
  49.9 0.1 reduce_sum.25
  50.0 3.2 %all_gather.11 = bf16[16,4,2048]{2,1,0:T(4,128)(2,1)S(1)} all-gather(bf16[8,4,2048]{2,1,0:T(4,128)(2,1)S(1)} %bitcast.36), channel_id=1, replica_groups={{0,1},{2,3},{4,5},{6,7},{8,9},{10,11},{12,13},{14,15},{16,17},{18,19},{..., dimensions={0}, use_global_device_ids=true | all-gather | bytes 393216 | tf_op jit(solution)/shard_map/all_gather | solution.py:453
  53.1 1.0 %select_convert_fusion = bf16[16,4,2048]{2,1,0:T(4,128)(2,1)} fusion(bf16[16,4,2048]{2,1,0:T(4,128)(2,1)S(1)} %all_gather.11, bf16[16,4,2048]{2,1,0:T(4,128)(2,1)S(1)} %copy-done.1, pred[16,4]{1,0:T(8,128)(4,1)S(1)} %iota_compare_fusion), kind=kLoop, calls=%fused_computation | loop fusion | flops 655360 | bytes 786496 | tf_op jit(solution)/shard_map/convert_element_type | solution.py:455
  (1 shorter events, 0.0 us)
Async XLA Ops:
  3.2 10.4 %copy-start.11 = (bf16[304,128]{1,0:T(8,128)(2,1)S(1)}, bf16[304,128]{1,0:T(8,128)(2,1)}, u32[]{:S(2)}) copy-start(bf16[304,128]{1,0:T(8,128)(2,1)} %get-tuple-element.11) | copy-start | bytes 233476
  3.2 23.4 %copy-start.1 = (bf16[16,4,2048]{2,1,0:T(4,128)(2,1)S(1)}, bf16[16,4,2048]{2,1,0:T(4,128)(2,1)}, u32[]{:S(2)}) copy-start(bf16[16,4,2048]{2,1,0:T(4,128)(2,1)} %param.16) | copy-start | bytes 786436
  3.2 23.4 %copy-start.2 = (f32[16,2048]{1,0:T(8,128)S(1)}, f32[16,2048]{1,0:T(8,128)}, u32[]{:S(2)}) copy-start(f32[16,2048]{1,0:T(8,128)} %refs_2_.1) | copy-start | bytes 393220
  3.3 23.4 %copy-start.4 = (bf16[64,256]{1,0:T(8,128)(2,1)S(1)}, bf16[64,256]{1,0:T(8,128)(2,1)}, u32[]{:S(2)}) copy-start(bf16[64,256]{1,0:T(8,128)(2,1)} %refs_10_.1) | copy-start | bytes 98308
  3.3 23.4 %all-to-all-start = ((bf16[8,64,256]{2,1,0:T(8,128)(2,1)}), bf16[8,64,256]{2,1,0:T(8,128)(2,1)S(1)}, u32[]{:S(2)}, u32[]{:S(2)}) async-start(bf16[8,64,256]{2,1,0:T(8,128)(2,1)} %get-tuple-element.12), calls=%async_computation | async-start | bytes 524288 | tf_op jit(solution)/shard_map/all_to_all | solution.py:406
  13.6 13.1 %copy-start.3 = (f32[4,2048]{1,0:T(4,128)S(1)}, f32[4,2048]{1,0:T(4,128)}, u32[]{:S(2)}) copy-start(f32[4,2048]{1,0:T(4,128)} %refs_5_.1) | copy-start | bytes 98308
  13.6 12.1 %collective-permute-start.1 = (bf16[304,128]{1,0:T(8,128)(2,1)S(1)}, bf16[304,128]{1,0:T(8,128)(2,1)S(1)}, u32[]{:S(2)}, u32[]{:S(2)}) collective-permute-start(bf16[304,128]{1,0:T(8,128)(2,1)S(1)} %copy-done.11), channel_id=1, source_target_pairs={{0,8},{8,16},{16,24},{24,32},{32,40},{40,48},{48,56},{56,64},{64,7... | collective-permute-start | bytes 233480 | tf_op jit(solution)/shard_map/ppermute | solution.py:405
  15.7 11.0 %collective-permute-start = (bf16[304,128]{1,0:T(8,128)(2,1)S(1)}, bf16[304,128]{1,0:T(8,128)(2,1)S(1)}, u32[]{:S(2)}, u32[]{:S(2)}) collective-permute-start(bf16[304,128]{1,0:T(8,128)(2,1)S(1)} %copy-done.11), channel_id=1, source_target_pairs={{8,0},{16,8},{24,16},{32,24},{40,32},{48,40},{56,48},{64,56},{72,6... | collective-permute-start | bytes 233480 | tf_op jit(solution)/shard_map/ppermute | solution.py:404
  24.8 1.9 %copy-start.8 = (f32[256]{0:T(256)S(1)}, f32[256]{0:T(256)}, u32[]{:S(2)}) copy-start(f32[256]{0:T(256)} %param.29) | copy-start | bytes 3076
  24.8 1.9 %copy-start.9 = (f32[256]{0:T(256)S(1)}, f32[256]{0:T(256)}, u32[]{:S(2)}) copy-start(f32[256]{0:T(256)} %param.30) | copy-start | bytes 3076
  24.8 1.9 %copy-start.5 = (f32[2048]{0:T(1024)S(1)}, f32[2048]{0:T(1024)}, u32[]{:S(2)}) copy-start(f32[2048]{0:T(1024)} %param.21) | copy-start | bytes 24580
  26.7 0.7 %copy-start.6 = (s32[64]{0:T(128)S(1)}, s32[64]{0:T(128)}, u32[]{:S(2)}) copy-start(s32[64]{0:T(128)} %get-tuple-element.10.meta_ref) | copy-start | bytes 772
  26.7 0.7 %copy-start.7 = (f32[256]{0:T(256)S(1)}, f32[256]{0:T(256)}, u32[]{:S(2)}) copy-start(f32[256]{0:T(256)} %param.28) | copy-start | bytes 3076
  35.7 5.4 %copy-start = (f32[16,4,4096]{2,1,0:T(4,128)S(1)}, f32[16,4,4096]{2,1,0:T(4,128)}, u32[]{:S(2)}) copy-start(f32[16,4,4096]{2,1,0:T(4,128)} %param.19) | copy-start | bytes 3145732
  36.6 4.4 %copy-start.10 = (s32[16]{0:T(128)S(1)}, s32[16]{0:T(128)}, u32[]{:S(2)}) copy-start(s32[16]{0:T(128)} %tally_hbm.1) | copy-start | bytes 196
  36.6 13.3 %all-to-all-start.1 = ((bf16[4,512,128]{2,1,0:T(8,128)(2,1)}), bf16[4,512,128]{2,1,0:T(8,128)(2,1)S(1)}, u32[]{:S(2)}, u32[]{:S(2)}) async-start(bf16[4,512,128]{2,1,0:T(8,128)(2,1)} %broadcast_in_dim.21), calls=%async_computation.1 | async-start | bytes 1048576 | tf_op jit(solution)/shard_map/all_to_all | solution.py:449

commit v9 on v8

--- a/solution.py
+++ b/solution.py
@@ -152,18 +152,11 @@
     return state[pl.ds(pl.multiple_of(meta_ref[q] * STATE_ROWS, STATE_ROWS), STATE_ROWS), :]
 
 
-def main_kernel(meta_ref, mem_hbm, *refs):
-    count = 15
-    hbm, (part_ref, moved_ref, vals_ref, last_ref) = refs[:count], refs[count : count + 4]
-    bufs = refs[count + 4 : 2 * count + 4]
-    x32, shift, state, reads, heads, part, ordered, sems, state_sem = refs[2 * count + 4 :]
-    loads = copies(hbm, bufs, sems)
-    start(loads[:-1])
-    state_load = pltpu.make_async_copy(mem_hbm, state, state_sem)
-    state_load.start()
-    loads[-1].start()
-    x_ref, gain_ref, prev_ref, from_after, from_before, blend_ref = bufs[:6]
-    left_ref, right_ref, base_ref, boost_ref, team_ref, final_ref = bufs[9:]
+def norm_kernel(meta_ref, x_hbm, gain_hbm, *refs):
+    hbm, (xn_ref, last_ref, small_ref), (x_ref, gain_ref), bufs = refs[:3], refs[3:6], refs[6:8], refs[8:11]
+    x32, sems = refs[11:]
+    loads = copies((x_hbm, gain_hbm) + hbm, (x_ref, gain_ref) + bufs, sems)
+    start(loads)
     loads[0].wait()
     loads[1].wait()
     x32[...] = x_ref[...].astype(F32)
@@ -179,7 +172,28 @@
     for t in range(1, STEPS):
         last = jnp.where(tally == t + 1, normed[t], last)
     last_ref[...] = last
-    for n in range(2, 6):
+    for t in range(STEPS):
+        xn_ref[t * SLOTS : (t + 1) * SLOTS, :] = normed[t]
+    small_ref[6:8, :] = jnp.zeros((2, 128), F32)
+    for n in range(3):
+        loads[2 + n].wait()
+        small_ref[2 * n : 2 * n + 2, :] = bufs[n][...]
+
+
+def main_kernel(meta_ref, mem_hbm, *refs):
+    count = 12
+    hbm, (part_ref, moved_ref, vals_ref) = refs[:count], refs[count : count + 3]
+    bufs = refs[count + 3 : 2 * count + 3]
+    shift, state, reads, heads, part, ordered, sems, state_sem = refs[2 * count + 3 :]
+    loads = copies(hbm, bufs, sems)
+    start(loads[:-1])
+    state_load = pltpu.make_async_copy(mem_hbm, state, state_sem)
+    state_load.start()
+    loads[-1].start()
+    xn_ref, prev_ref, from_after, from_before, blend_ref = bufs[:5]
+    left_ref, right_ref, small_ref, final_ref = bufs[8:]
+    tally = column_of(meta_ref, (SLOTS, 128))[:, :1]
+    for n in range(5):
         loads[n].wait()
     for q in range(SLOTS):
         shift[q : q + 1, :] = prev_ref[pl.ds(meta_ref[q], 1), :]
@@ -193,8 +207,8 @@
         for n, rows in enumerate(moved_rows):
             col = jnp.where(slot == meta_ref[CAME + n], rows[c : c + 1, :], col)
         shift_in.append(col)
-    xn = jnp.concatenate(normed, axis=0)
-    change = jnp.concatenate([jnp.concatenate(shift_in, axis=1)] + normed[:-1], axis=0) - xn
+    xn = xn_ref[...]
+    change = jnp.concatenate([jnp.concatenate(shift_in, axis=1), xn[: (STEPS - 1) * SLOTS, :]], axis=0) - xn
 
     def mix(which):
         return (xn + change * blend_ref[which : which + 1, :]).astype(BF16)
@@ -202,9 +216,9 @@
     mixed_rows = mix(3)
     rkv = []
     for n in range(3):
-        loads[6 + n].wait()
-        rkv.append(dot(mix(n), bufs[6 + n][...]))
-    for n in range(9, 14):
+        loads[5 + n].wait()
+        rkv.append(dot(mix(n), bufs[5 + n][...]))
+    for n in range(8, 11):
         loads[n].wait()
     pre = jnp.zeros((ROWS, left_ref.shape[1]), F32)
     chunk = left_ref.shape[2]
@@ -213,13 +227,13 @@
             mixed_rows[:, n * chunk : (n + 1) * chunk], left_ref[n], (((1,), (1,)), ((), ())), preferred_element_type=F32
         )
     lora = jnp.tanh(pre).astype(BF16)
-    decay = jnp.exp(-jnp.exp(row_of(base_ref) + dot(lora, right_ref[...])))
+    decay = jnp.exp(-jnp.exp(row_of(small_ref[0:2, :]) + dot(lora, right_ref[...])))
     r = [cut(rkv[0], t) for t in range(STEPS)]
     k = [cut(rkv[1], t) for t in range(STEPS)]
     v = [cut(rkv[2], t) for t in range(STEPS)]
     d = [jnp.where(tally > t, cut(decay, t), 1.0) for t in range(STEPS)]
     kept = [jnp.where(tally > t, k[t], 0.0) for t in range(STEPS)]
-    boost = row_of(boost_ref)
+    boost = row_of(small_ref[2:4, :])
 
     run, reach = r[0] * 0.0 + 1.0, []
     for t in range(STEPS):
@@ -280,12 +294,12 @@
     y = jnp.concatenate(outs, axis=0)
     center = y - dot_split(y, same_head) * (1.0 / HEAD)
     spread = dot_split(center * center, same_head) * (1.0 / HEAD)
-    g = center * lax.rsqrt(spread + EPS) * row_of(team_ref)
+    g = center * lax.rsqrt(spread + EPS) * row_of(small_ref[4:6, :])
     for t in range(STEPS):
         for c in range(LOCAL // 128):
             ordered[c, pl.ds(t, SLOTS, stride=STEPS), :] = cut(g, t)[:, c * 128 : (c + 1) * 128]
     g = jnp.concatenate([ordered[c] for c in range(LOCAL // 128)], axis=1).astype(BF16)
-    loads[14].wait()
+    loads[11].wait()
     proj = dot(g, final_ref[...])
     for q in range(SLOTS):
         rows = proj[q * STEPS : (q + 1) * STEPS, :]
@@ -405,22 +419,35 @@
     from_before = lax.ppermute(packed, "seq", [(i, (i + 1) % rings) for i in range(rings)])
     left = lax.all_to_all(left, "tensor", 0, 0)
 
+    gain = entry_standardize_scale.reshape(TILES, 128)
+    vectors = [
+        v.reshape(2, 128) for v in (feature_forget_logloglevel, present_token_boost, team_standardize_scale)
+    ]
+    xn, new_shifts, small = pl.pallas_call(
+        norm_kernel,
+        out_shape=[shape((ROWS, WIDTH), F32), shape((SLOTS, WIDTH), F32), shape((8, 128), F32)],
+        in_specs=spec(pltpu.SMEM, 1) + spec(pl.ANY, 5),
+        out_specs=spec(pltpu.VMEM, 3),
+        scratch_shapes=like([x, gain] + vectors) + [scratch((ROWS * TILES, 128), F32), dma((5,))],
+        compiler_params=params(MAIN_MIB),
+        cost_estimate=cost(0, 4 << 20),
+        name="norm",
+    )(meta, x, gain, *vectors)
+
     operands = [
-        x, entry_standardize_scale.reshape(TILES, 128), prev, from_after, from_before, blend_coefficients,
+        xn, prev, from_after, from_before, blend_coefficients,
         acceptance_projection_matrix, lookup_projection_matrix, payload_projection_matrix,
-        left, forget_map_right_matrix, feature_forget_logloglevel.reshape(2, 128),
-        present_token_boost.reshape(2, 128), team_standardize_scale.reshape(2, 128), final_projection_matrix,
+        left, forget_map_right_matrix, small, final_projection_matrix,
     ]
-    part, moved, values, new_shifts = pl.pallas_call(
+    part, moved, values = pl.pallas_call(
         main_kernel,
         out_shape=[
             shape((ROWS * TILES, 128), BF16), shape((ROWS + SLOTS, LOCAL), F32), shape((ROWS, LOCAL), F32),
-            shape((SLOTS, WIDTH), F32),
         ],
         in_specs=spec(pltpu.SMEM, 1) + spec(pl.ANY, 1 + len(operands)),
-        out_specs=spec(pltpu.VMEM, 4),
+        out_specs=spec(pltpu.VMEM, 3),
         scratch_shapes=like(operands)
-        + [scratch((ROWS * TILES, 128), F32), scratch((SLOTS, WIDTH), F32), state_buf, rows_buf, rows_buf, scratch((ROWS * TILES, 128), F32)]
+        + [scratch((SLOTS, WIDTH), F32), state_buf, rows_buf, rows_buf, scratch((ROWS * TILES, 128), F32)]
         + [scratch((LOCAL // 128, ROWS, 128), F32), dma((len(operands),)), dma],
         compiler_params=params(MAIN_MIB),
         cost_estimate=cost(8 * ROWS * WIDTH * LOCAL, 8 << 20),

time: 54.5 us -> 53.8 us (0.987)
  waiting for transfers between devices: 7.76 us -> 5.92 us
  Pallas kernels: 11.3 us -> 12.7 us
    pallas_call x0 -> x1, Pallas kernels: none -> 1.8 us  [shards(): pl.pallas_call(norm_kernel, out_shape=[shape((ROWS, WIDTH), F32), shape((...]
    ppermute x1, waiting for transfers between devices: 0.99 us -> 0.01 us  [shards(): lax.ppermute(packed, 'seq', [((i + 1) % rings, i) for i in range(rings)])]
    ppermute x1, waiting for transfers between devices: 0.85 us -> 0.01 us  [shards(): lax.ppermute(packed, 'seq', [(i, (i + 1) % rings) for i in range(rings)])]
  transfers between devices with their start and end apart: 4 -> 4, of which waited for: 3 -> 1; matrix products, arithmetic and copies ran while one was open for 0% -> 0% of each run, Pallas kernels for 5% -> 9%
where the time goes in v9:
time: 53.8 us; the launch traced here: 53.4 us
  starting transfers between devices  25.9 us (48%)
  Pallas kernels  12.7 us (24%)
  waiting for transfers between devices  5.92 us (11%)
  blocking collectives  5.34 us (10%)
  local copies, waits for them, and re-layouts  1.58 us (3%)
  other arithmetic  1.15 us (2%)
  between operations  0.83 us (2%)
    all_to_all x1, starting transfers between devices, shards(): left = lax.all_to_all(left, 'tensor', 0, 0)  10.3 us
    ppermute x1, starting transfers between devices, shards(): lax.ppermute(packed, 'seq', [((i + 1) % rings, i) for i in range(rings)])  9.1 us
    all_to_all x1, waiting for transfers between devices, shards(): lax.all_to_all(jnp.broadcast_to(mine[None], (teams // 2,) + mine.shape),...  5.91 us
    pallas_call x1, Pallas kernels, shards(): pl.pallas_call(main_kernel, out_shape=[shape((ROWS * TILES, 128), BF16),...  5.44 us
    all_to_all x1, starting transfers between devices, shards(): lax.all_to_all(jnp.broadcast_to(mine[None], (teams // 2,) + mine.shape),...  4.56 us
    all_gather x1, blocking collectives, shards(): proj = lax.all_gather(total, 'tensor', axis_index_groups=pairs, tiled=True)  3.16 us
    pallas_call x1, Pallas kernels, shards(): pl.pallas_call(update_kernel, out_shape=shape((SLOTS * STATE_ROWS, 128),...  2.91 us
    pallas_call x1, Pallas kernels, shards(): pl.pallas_call(pack_kernel, out_shape=[shape((PACK_ROWS, 128), BF16), sha...  2.58 us
  transfers between devices with their start and end apart: 4, of which 1 were waited for; matrix products, arithmetic and copies ran while one was open for 0% of the time, Pallas kernels for 9%

profile of v9, /device:TPU:1, one launch (start us, length us, event | category | flops | bytes accessed | tf_op | source)
XLA Modules:
  0.0 53.4 jit_solution(9696322336974036167)
XLA Ops:
  0.6 2.6 %pack.1 = (bf16[304,128]{1,0:T(8,128)(2,1)}, bf16[8,64,256]{2,1,0:T(8,128)(2,1)}, s32[64]{0:T(128)}) custom-call(s32[16]{0:T(128)} %lookup_hbm.1, s32[16]{0:T(128)} %tally_hbm.1, f32[16,2048]{1,0:T(8,128)} %refs_1_.1, f32[2048,128]{1,0:T(8,128)} %bitcast.26, bf16[64,256]{1,0:T(8,128)(2,1)} %bitcast.37), custom_call_target="tpu_custom_call" | custom-call | bytes 1048576 | tf_op jit(solution)/shard_map/pack/pallas_call | solution.py:404
  3.2 0.0 copy-start.11
  3.2 0.0 copy-start.1
  3.2 10.3 %all-to-all-start = ((bf16[8,64,256]{2,1,0:T(8,128)(2,1)}), bf16[8,64,256]{2,1,0:T(8,128)(2,1)S(1)}, u32[]{:S(2)}, u32[]{:S(2)}) async-start(bf16[8,64,256]{2,1,0:T(8,128)(2,1)} %get-tuple-element.15), calls=%async_computation | async-start | bytes 524288 | tf_op jit(solution)/shard_map/all_to_all | solution.py:420
  13.6 0.0 copy-done.11
  13.6 1.9 %collective-permute-start.1 = (bf16[304,128]{1,0:T(8,128)(2,1)S(1)}, bf16[304,128]{1,0:T(8,128)(2,1)S(1)}, u32[]{:S(2)}, u32[]{:S(2)}) collective-permute-start(bf16[304,128]{1,0:T(8,128)(2,1)S(1)} %copy-done.11), channel_id=1, source_target_pairs={{0,8},{8,16},{16,24},{24,32},{32,40},{40,48},{48,56},{56,64},{64,7... | collective-permute-start | bytes 233480 | tf_op jit(solution)/shard_map/ppermute | solution.py:419
  15.5 9.1 %collective-permute-start = (bf16[304,128]{1,0:T(8,128)(2,1)S(1)}, bf16[304,128]{1,0:T(8,128)(2,1)S(1)}, u32[]{:S(2)}, u32[]{:S(2)}) collective-permute-start(bf16[304,128]{1,0:T(8,128)(2,1)S(1)} %copy-done.11), channel_id=1, source_target_pairs={{8,0},{16,8},{24,16},{32,24},{40,32},{48,40},{56,48},{64,56},{72,6... | collective-permute-start | bytes 233480 | tf_op jit(solution)/shard_map/ppermute | solution.py:418
  24.6 0.0 copy-start.8
  24.6 0.0 copy-start.9
  24.6 0.0 copy-start.5
  24.7 0.0 copy-start.6
  24.7 0.0 copy-start.7
  24.7 0.0 copy-done.1
  24.7 0.6 %copy-done.8 = f32[256]{0:T(256)S(1)} copy-done((f32[256]{0:T(256)S(1)}, f32[256]{0:T(256)}, u32[]{:S(2)}) %copy-start.8) | copy-done | bytes 1048
  25.3 0.0 copy-done.9
  25.3 0.0 copy-done.5
  25.3 0.0 copy-done.6
  25.3 0.0 copy-done.7
  25.4 0.0 copy-start.2
  25.4 0.0 copy-start.3
  25.4 0.0 copy-start.4
  25.4 1.8 %norm.1 = (f32[64,2048]{1,0:T(8,128)S(1)}, f32[16,2048]{1,0:T(8,128)}, f32[8,128]{1,0:T(8,128)S(1)}) custom-call(s32[64]{0:T(128)S(1)} %copy-done.6, bf16[1024,128]{1,0:T(8,128)(2,1)S(1)} %bitcast.29, f32[16,128]{1,0:T(8,128)S(1)} %bitcast.30, f32[2,128]{1,0:T(2,128)S(1)} %bitcast.31, f32[2,128]{1,0:T(2,128)S(1)} %bitcast.32, f32[2,128]{1,0:T(2,128)S(1)} %bitcast.33), custom_call_target="tpu_custom_call" | custom-call | bytes 4194304 | tf_op jit(solution)/shard_map/norm/pallas_call | solution.py:426
  27.2 0.0 collective-permute-done.1.refs_3_
  27.2 0.0 collective-permute-done.refs_2_
  27.2 0.0 all-to-all-done.refs_8_
  27.2 0.0 copy-done.2
  27.2 0.0 copy-done.3
  27.2 0.0 copy-done.4
  27.2 5.4 %main.1 = (bf16[1024,128]{1,0:T(8,128)(2,1)S(1)}, f32[80,256]{1,0:T(8,128)S(1)}, f32[64,256]{1,0:T(8,128)S(1)}) custom-call(s32[64]{0:T(128)S(1)} %copy-done.6, f32[2048,128]{1,0:T(8,128)} %bitcast.27, f32[64,2048]{1,0:T(8,128)S(1)} %get-tuple-element.13.refs_0_, f32[16,2048]{1,0:T(8,128)S(1)} %copy-done.2, ...), custom_call_target="tpu_custom_call" | custom-call | flops 268435456 | bytes 8388608 | tf_op jit(solution)/shard_map/main/pallas_call | solution.py:442
  32.7 2.2 %all-gather = bf16[2048,128]{1,0:T(8,128)(2,1)S(1)} all-gather(bf16[1024,128]{1,0:T(8,128)(2,1)S(1)} %get-tuple-element.17), channel_id=2, replica_groups={{0,1},{2,3},{4,5},{6,7},{8,9},{10,11},{12,13},{14,15},{16,17},{18,19},{..., dimensions={0}, use_global_device_ids=true | all-gather | bytes 786432 | tf_op jit(solution)/shard_map/all_gather | solution.py:474
  34.9 0.0 copy-start
  34.9 0.9 %broadcast_in_dim.21 = bf16[4,512,128]{2,1,0:T(8,128)(2,1)} broadcast(bf16[512,128]{1,0:T(8,128)(2,1)S(1)} %dynamic-slice_reduce_fusion), dimensions={1,2} | broadcast | bytes 655360 | tf_op jit(solution)/shard_map/broadcast_in_dim | solution.py:477
  35.8 0.0 copy-start.10
  35.8 4.6 %all-to-all-start.1 = ((bf16[4,512,128]{2,1,0:T(8,128)(2,1)}), bf16[4,512,128]{2,1,0:T(8,128)(2,1)S(1)}, u32[]{:S(2)}, u32[]{:S(2)}) async-start(bf16[4,512,128]{2,1,0:T(8,128)(2,1)} %broadcast_in_dim.21), calls=%async_computation.1 | async-start | bytes 1048576 | tf_op jit(solution)/shard_map/all_to_all | solution.py:476
  40.3 0.0 copy-done.10
  40.3 0.1 iota_compare_fusion
  40.4 0.0 copy-done
  40.4 2.9 %update.1 = f32[2048,128]{1,0:T(8,128)} custom-call(s32[64]{0:T(128)S(1)} %copy-done.6, f32[2048,128]{1,0:T(8,128)S(1)} %bitcast.28, f32[80,256]{1,0:T(8,128)S(1)} %get-tuple-element.18.refs_0_, f32[64,256]{1,0:T(8,128)S(1)} %get-tuple-element.19.refs_1_, bf16[304,128]{1,0:T(8,128)(2,1)S(1)} %collective-permute-done.refs_2_, ...), custom_call_target="tpu_custom_call" | custom-call | flops 16777216 | bytes 8388608 | tf_op jit(solution)/shard_map/update/pallas_call | solution.py:458
  43.3 5.9 %all-to-all-done.1 = bf16[4,512,128]{2,1,0:T(8,128)(2,1)S(1)} async-done(((bf16[4,512,128]{2,1,0:T(8,128)(2,1)}), bf16[4,512,128]{2,1,0:T(8,128)(2,1)S(1)}, u32[]{:S(2)}, u32[]{:S(2)}) %all-to-all-start.1) | async-done | bytes 524320 | tf_op jit(solution)/shard_map/all_to_all | solution.py:476
  49.2 0.1 reduce_sum.25
  49.3 3.2 %all_gather.11 = bf16[16,4,2048]{2,1,0:T(4,128)(2,1)S(1)} all-gather(bf16[8,4,2048]{2,1,0:T(4,128)(2,1)S(1)} %bitcast.36), channel_id=1, replica_groups={{0,1},{2,3},{4,5},{6,7},{8,9},{10,11},{12,13},{14,15},{16,17},{18,19},{..., dimensions={0}, use_global_device_ids=true | all-gather | bytes 393216 | tf_op jit(solution)/shard_map/all_gather | solution.py:480
  52.5 1.0 %select_convert_fusion = bf16[16,4,2048]{2,1,0:T(4,128)(2,1)} fusion(bf16[16,4,2048]{2,1,0:T(4,128)(2,1)S(1)} %all_gather.11, bf16[16,4,2048]{2,1,0:T(4,128)(2,1)S(1)} %copy-done.1, pred[16,4]{1,0:T(8,128)(4,1)S(1)} %iota_compare_fusion), kind=kLoop, calls=%fused_computation | loop fusion | flops 655360 | bytes 786496 | tf_op jit(solution)/shard_map/convert_element_type | solution.py:482
  (1 shorter events, 0.0 us)
Async XLA Ops:
  3.2 10.4 %copy-start.11 = (bf16[304,128]{1,0:T(8,128)(2,1)S(1)}, bf16[304,128]{1,0:T(8,128)(2,1)}, u32[]{:S(2)}) copy-start(bf16[304,128]{1,0:T(8,128)(2,1)} %get-tuple-element.14) | copy-start | bytes 233476
  3.2 21.4 %copy-start.1 = (bf16[16,4,2048]{2,1,0:T(4,128)(2,1)S(1)}, bf16[16,4,2048]{2,1,0:T(4,128)(2,1)}, u32[]{:S(2)}) copy-start(bf16[16,4,2048]{2,1,0:T(4,128)(2,1)} %param.16) | copy-start | bytes 786436
  3.2 24.0 %all-to-all-start = ((bf16[8,64,256]{2,1,0:T(8,128)(2,1)}), bf16[8,64,256]{2,1,0:T(8,128)(2,1)S(1)}, u32[]{:S(2)}, u32[]{:S(2)}) async-start(bf16[8,64,256]{2,1,0:T(8,128)(2,1)} %get-tuple-element.15), calls=%async_computation | async-start | bytes 524288 | tf_op jit(solution)/shard_map/all_to_all | solution.py:420
  13.6 13.6 %collective-permute-start.1 = (bf16[304,128]{1,0:T(8,128)(2,1)S(1)}, bf16[304,128]{1,0:T(8,128)(2,1)S(1)}, u32[]{:S(2)}, u32[]{:S(2)}) collective-permute-start(bf16[304,128]{1,0:T(8,128)(2,1)S(1)} %copy-done.11), channel_id=1, source_target_pairs={{0,8},{8,16},{16,24},{24,32},{32,40},{40,48},{48,56},{56,64},{64,7... | collective-permute-start | bytes 233480 | tf_op jit(solution)/shard_map/ppermute | solution.py:419
  15.5 11.7 %collective-permute-start = (bf16[304,128]{1,0:T(8,128)(2,1)S(1)}, bf16[304,128]{1,0:T(8,128)(2,1)S(1)}, u32[]{:S(2)}, u32[]{:S(2)}) collective-permute-start(bf16[304,128]{1,0:T(8,128)(2,1)S(1)} %copy-done.11), channel_id=1, source_target_pairs={{8,0},{16,8},{24,16},{32,24},{40,32},{48,40},{56,48},{64,56},{72,6... | collective-permute-start | bytes 233480 | tf_op jit(solution)/shard_map/ppermute | solution.py:418
  24.6 0.7 %copy-start.8 = (f32[256]{0:T(256)S(1)}, f32[256]{0:T(256)}, u32[]{:S(2)}) copy-start(f32[256]{0:T(256)} %param.29) | copy-start | bytes 3076
  24.6 0.7 %copy-start.9 = (f32[256]{0:T(256)S(1)}, f32[256]{0:T(256)}, u32[]{:S(2)}) copy-start(f32[256]{0:T(256)} %param.30) | copy-start | bytes 3076
  24.6 0.7 %copy-start.5 = (f32[2048]{0:T(1024)S(1)}, f32[2048]{0:T(1024)}, u32[]{:S(2)}) copy-start(f32[2048]{0:T(1024)} %param.21) | copy-start | bytes 24580
  24.7 0.7 %copy-start.6 = (s32[64]{0:T(128)S(1)}, s32[64]{0:T(128)}, u32[]{:S(2)}) copy-start(s32[64]{0:T(128)} %get-tuple-element.12.meta_ref) | copy-start | bytes 772
  24.7 0.7 %copy-start.7 = (f32[256]{0:T(256)S(1)}, f32[256]{0:T(256)}, u32[]{:S(2)}) copy-start(f32[256]{0:T(256)} %param.28) | copy-start | bytes 3076
  25.4 1.9 %copy-start.2 = (f32[16,2048]{1,0:T(8,128)S(1)}, f32[16,2048]{1,0:T(8,128)}, u32[]{:S(2)}) copy-start(f32[16,2048]{1,0:T(8,128)} %refs_1_.1) | copy-start | bytes 393220
  25.4 1.9 %copy-start.3 = (f32[4,2048]{1,0:T(4,128)S(1)}, f32[4,2048]{1,0:T(4,128)}, u32[]{:S(2)}) copy-start(f32[4,2048]{1,0:T(4,128)} %refs_4_.1) | copy-start | bytes 98308
  25.4 1.9 %copy-start.4 = (bf16[64,256]{1,0:T(8,128)(2,1)S(1)}, bf16[64,256]{1,0:T(8,128)(2,1)}, u32[]{:S(2)}) copy-start(bf16[64,256]{1,0:T(8,128)(2,1)} %refs_9_.1) | copy-start | bytes 98308
  34.9 5.5 %copy-start = (f32[16,4,4096]{2,1,0:T(4,128)S(1)}, f32[16,4,4096]{2,1,0:T(4,128)}, u32[]{:S(2)}) copy-start(f32[16,4,4096]{2,1,0:T(4,128)} %param.19) | copy-start | bytes 3145732
  35.8 4.6 %copy-start.10 = (s32[16]{0:T(128)S(1)}, s32[16]{0:T(128)}, u32[]{:S(2)}) copy-start(s32[16]{0:T(128)} %tally_hbm.1) | copy-start | bytes 196
  35.8 13.5 %all-to-all-start.1 = ((bf16[4,512,128]{2,1,0:T(8,128)(2,1)}), bf16[4,512,128]{2,1,0:T(8,128)(2,1)S(1)}, u32[]{:S(2)}, u32[]{:S(2)}) async-start(bf16[4,512,128]{2,1,0:T(8,128)(2,1)} %broadcast_in_dim.21), calls=%async_computation.1 | async-start | bytes 1048576 | tf_op jit(solution)/shard_map/all_to_all | solution.py:476

commit v10 on v9

--- a/solution.py
+++ b/solution.py
@@ -22,6 +22,7 @@
 PIECE = STATE_ROWS + TILES
 PACK_ROWS = 2 * PIECE + 16
 CAME, TALLY, META = SLOTS, SLOTS + 16, 64
+READ_STRIDE = STEPS * 8 + 8
 PACK_MIB, MAIN_MIB = 60, 52
 
 
@@ -186,7 +187,7 @@
     bufs = refs[count + 3 : 2 * count + 3]
     shift, state, reads, heads, part, ordered, sems, state_sem = refs[2 * count + 3 :]
     loads = copies(hbm, bufs, sems)
-    start(loads[:-1])
+    start(loads[5:8] + loads[:5] + loads[8:-1])
     state_load = pltpu.make_async_copy(mem_hbm, state, state_sem)
     state_load.start()
     loads[-1].start()
@@ -214,10 +215,6 @@
         return (xn + change * blend_ref[which : which + 1, :]).astype(BF16)
 
     mixed_rows = mix(3)
-    rkv = []
-    for n in range(3):
-        loads[5 + n].wait()
-        rkv.append(dot(mix(n), bufs[5 + n][...]))
     for n in range(8, 11):
         loads[n].wait()
     pre = jnp.zeros((ROWS, left_ref.shape[1]), F32)
@@ -228,6 +225,14 @@
         )
     lora = jnp.tanh(pre).astype(BF16)
     decay = jnp.exp(-jnp.exp(row_of(small_ref[0:2, :]) + dot(lora, right_ref[...])))
+    row256, col256 = iota((LOCAL, LOCAL), 0), iota((LOCAL, LOCAL), 1)
+    same_head = (row256 // HEAD == col256 // HEAD).astype(BF16)
+    source = (col256 % HEADS) * HEAD + ((col256 // HEADS) % (HEAD // 2)) * 2 + col256 // 128
+    reorder = (row256 == source).astype(BF16)
+    rkv = []
+    for n in range(3):
+        loads[5 + n].wait()
+        rkv.append(dot(mix(n), bufs[5 + n][...]))
     r = [cut(rkv[0], t) for t in range(STEPS)]
     k = [cut(rkv[1], t) for t in range(STEPS)]
     v = [cut(rkv[2], t) for t in range(STEPS)]
@@ -235,7 +240,7 @@
     kept = [jnp.where(tally > t, k[t], 0.0) for t in range(STEPS)]
     boost = row_of(small_ref[2:4, :])
 
-    run, reach = r[0] * 0.0 + 1.0, []
+    run, reach = jnp.ones_like(r[0]), []
     for t in range(STEPS):
         reach.append(r[t] * run)
         run = run * d[t]
@@ -252,16 +257,12 @@
             pairs.append((t, s))
             terms.append(weight * kept[s])
             weight = weight * d[s]
-    row256, col256 = iota((LOCAL, LOCAL), 0), iota((LOCAL, LOCAL), 1)
-    same_head = (row256 // HEAD == col256 // HEAD).astype(BF16)
     sums = dot_split(jnp.concatenate(terms, axis=0), same_head)
     within = [None] * STEPS
     for n, (t, s) in enumerate(pairs):
         term = cut(sums, n) * v[s]
         within[t] = term if within[t] is None else within[t] + term
 
-    source = (col256 % HEADS) * HEAD + ((col256 // HEADS) % (HEAD // 2)) * 2 + col256 // 128
-    reorder = (row256 == source).astype(BF16)
     moved = dot_split(jnp.concatenate(reach + coefs + [run], axis=0), reorder)
     moved_ref[...] = moved[STEPS * SLOTS :, :]
     vals_ref[...] = rkv[2]
@@ -271,12 +272,12 @@
         head_lane = lane % HEADS == h
         for p in range(2):
             for t in range(STEPS):
-                at = pl.ds(t * 8 + p * HEADS + h, SLOTS, stride=STEPS * 8)
+                at = pl.ds(t * 8 + p * HEADS + h, SLOTS, stride=READ_STRIDE)
                 reads[at, :] = jnp.where(head_lane, cut(moved, t)[:, p * 128 : (p + 1) * 128], 0.0)
     state_load.wait()
     place_received(meta_ref, (from_before, from_after), state)
     for q in range(SLOTS):
-        rows = slice(q * STEPS * 8, (q + 1) * STEPS * 8)
+        rows = slice(q * READ_STRIDE, q * READ_STRIDE + STEPS * 8)
         now = state_of(meta_ref, state, q)
         heads[rows, :] = dot(reads[rows, :].astype(BF16), now.astype(BF16))
 
@@ -284,7 +285,7 @@
     left_half = lane < HEAD
     for t in range(STEPS):
         def read(p, h):
-            return heads[pl.ds(t * 8 + p * HEADS + h, SLOTS, stride=STEPS * 8), :]
+            return heads[pl.ds(t * 8 + p * HEADS + h, SLOTS, stride=READ_STRIDE), :]
 
         cols = []
         for h in range(0, HEADS, 2):
@@ -400,6 +401,7 @@
     like = lambda items: [scratch(a.shape, a.dtype) for a in items]
     state_buf = scratch((SLOTS * STATE_ROWS, 128), F32)
     rows_buf = scratch((SLOTS * STEPS * 8, 128), F32)
+    read_buf = scratch((SLOTS * READ_STRIDE, 128), F32)
 
     packed, left, meta = pl.pallas_call(
         pack_kernel,
@@ -447,7 +449,7 @@
         in_specs=spec(pltpu.SMEM, 1) + spec(pl.ANY, 1 + len(operands)),
         out_specs=spec(pltpu.VMEM, 3),
         scratch_shapes=like(operands)
-        + [scratch((SLOTS, WIDTH), F32), state_buf, rows_buf, rows_buf, scratch((ROWS * TILES, 128), F32)]
+        + [scratch((SLOTS, WIDTH), F32), state_buf, read_buf, read_buf, scratch((ROWS * TILES, 128), F32)]
         + [scratch((LOCAL // 128, ROWS, 128), F32), dma((len(operands),)), dma],
         compiler_params=params(MAIN_MIB),
         cost_estimate=cost(8 * ROWS * WIDTH * LOCAL, 8 << 20),

time: 53.8 us -> 52.6 us (0.978)
  Pallas kernels: 12.7 us -> 11.5 us
    pallas_call x1, Pallas kernels: 5.44 us -> 4.2 us  [shards(): pl.pallas_call(main_kernel, out_shape=[shape((ROWS * TILES, 128), BF16),...]
where the time goes in v10:
time: 52.6 us; the launch traced here: 52.2 us
  starting transfers between devices  25.9 us (49%)
  Pallas kernels  11.5 us (22%)
  waiting for transfers between devices  5.92 us (11%)
  blocking collectives  5.34 us (10%)
  local copies, waits for them, and re-layouts  1.58 us (3%)
  other arithmetic  1.15 us (2%)
  between operations  0.83 us (2%)
    all_to_all x1, starting transfers between devices, shards(): left = lax.all_to_all(left, 'tensor', 0, 0)  10.3 us
    ppermute x1, starting transfers between devices, shards(): lax.ppermute(packed, 'seq', [((i + 1) % rings, i) for i in range(rings)])  9.1 us
    all_to_all x1, waiting for transfers between devices, shards(): lax.all_to_all(jnp.broadcast_to(mine[None], (teams // 2,) + mine.shape),...  5.91 us
    all_to_all x1, starting transfers between devices, shards(): lax.all_to_all(jnp.broadcast_to(mine[None], (teams // 2,) + mine.shape),...  4.56 us
    pallas_call x1, Pallas kernels, shards(): pl.pallas_call(main_kernel, out_shape=[shape((ROWS * TILES, 128), BF16),...  4.2 us
    all_gather x1, blocking collectives, shards(): proj = lax.all_gather(total, 'tensor', axis_index_groups=pairs, tiled=True)  3.16 us
    pallas_call x1, Pallas kernels, shards(): pl.pallas_call(update_kernel, out_shape=shape((SLOTS * STATE_ROWS, 128),...  2.91 us
    pallas_call x1, Pallas kernels, shards(): pl.pallas_call(pack_kernel, out_shape=[shape((PACK_ROWS, 128), BF16), sha...  2.58 us
  transfers between devices with their start and end apart: 4, of which 1 were waited for; matrix products, arithmetic and copies ran while one was open for 0% of the time, Pallas kernels for 9%

profile of v10, /device:TPU:1, one launch (start us, length us, event | category | flops | bytes accessed | tf_op | source)
XLA Modules:
  0.0 52.2 jit_solution(3076406988043927047)
XLA Ops:
  0.6 2.6 %pack.1 = (bf16[304,128]{1,0:T(8,128)(2,1)}, bf16[8,64,256]{2,1,0:T(8,128)(2,1)}, s32[64]{0:T(128)}) custom-call(s32[16]{0:T(128)} %lookup_hbm.1, s32[16]{0:T(128)} %tally_hbm.1, f32[16,2048]{1,0:T(8,128)} %refs_1_.1, f32[2048,128]{1,0:T(8,128)} %bitcast.26, bf16[64,256]{1,0:T(8,128)(2,1)} %bitcast.37), custom_call_target="tpu_custom_call" | custom-call | bytes 1048576 | tf_op jit(solution)/shard_map/pack/pallas_call | solution.py:406
  3.2 0.0 copy-start.11
  3.2 0.0 copy-start.1
  3.2 10.3 %all-to-all-start = ((bf16[8,64,256]{2,1,0:T(8,128)(2,1)}), bf16[8,64,256]{2,1,0:T(8,128)(2,1)S(1)}, u32[]{:S(2)}, u32[]{:S(2)}) async-start(bf16[8,64,256]{2,1,0:T(8,128)(2,1)} %get-tuple-element.15), calls=%async_computation | async-start | bytes 524288 | tf_op jit(solution)/shard_map/all_to_all | solution.py:422
  13.6 0.0 copy-done.11
  13.6 1.9 %collective-permute-start.1 = (bf16[304,128]{1,0:T(8,128)(2,1)S(1)}, bf16[304,128]{1,0:T(8,128)(2,1)S(1)}, u32[]{:S(2)}, u32[]{:S(2)}) collective-permute-start(bf16[304,128]{1,0:T(8,128)(2,1)S(1)} %copy-done.11), channel_id=1, source_target_pairs={{0,8},{8,16},{16,24},{24,32},{32,40},{40,48},{48,56},{56,64},{64,7... | collective-permute-start | bytes 233480 | tf_op jit(solution)/shard_map/ppermute | solution.py:421
  15.5 9.1 %collective-permute-start = (bf16[304,128]{1,0:T(8,128)(2,1)S(1)}, bf16[304,128]{1,0:T(8,128)(2,1)S(1)}, u32[]{:S(2)}, u32[]{:S(2)}) collective-permute-start(bf16[304,128]{1,0:T(8,128)(2,1)S(1)} %copy-done.11), channel_id=1, source_target_pairs={{8,0},{16,8},{24,16},{32,24},{40,32},{48,40},{56,48},{64,56},{72,6... | collective-permute-start | bytes 233480 | tf_op jit(solution)/shard_map/ppermute | solution.py:420
  24.6 0.0 copy-start.8
  24.6 0.0 copy-start.9
  24.6 0.0 copy-start.5
  24.7 0.0 copy-start.6
  24.7 0.0 copy-start.7
  24.7 0.0 copy-done.1
  24.7 0.6 %copy-done.8 = f32[256]{0:T(256)S(1)} copy-done((f32[256]{0:T(256)S(1)}, f32[256]{0:T(256)}, u32[]{:S(2)}) %copy-start.8) | copy-done | bytes 1048
  25.3 0.0 copy-done.9
  25.3 0.0 copy-done.5
  25.3 0.0 copy-done.6
  25.3 0.0 copy-done.7
  25.4 0.0 copy-start.2
  25.4 0.0 copy-start.3
  25.4 0.0 copy-start.4
  25.4 1.8 %norm.1 = (f32[64,2048]{1,0:T(8,128)S(1)}, f32[16,2048]{1,0:T(8,128)}, f32[8,128]{1,0:T(8,128)S(1)}) custom-call(s32[64]{0:T(128)S(1)} %copy-done.6, bf16[1024,128]{1,0:T(8,128)(2,1)S(1)} %bitcast.29, f32[16,128]{1,0:T(8,128)S(1)} %bitcast.30, f32[2,128]{1,0:T(2,128)S(1)} %bitcast.31, f32[2,128]{1,0:T(2,128)S(1)} %bitcast.32, f32[2,128]{1,0:T(2,128)S(1)} %bitcast.33), custom_call_target="tpu_custom_call" | custom-call | bytes 4194304 | tf_op jit(solution)/shard_map/norm/pallas_call | solution.py:428
  27.2 0.0 collective-permute-done.1.refs_3_
  27.2 0.0 collective-permute-done.refs_2_
  27.2 0.0 all-to-all-done.refs_8_
  27.2 0.0 copy-done.2
  27.2 0.0 copy-done.3
  27.2 0.0 copy-done.4
  27.2 4.2 %main.1 = (bf16[1024,128]{1,0:T(8,128)(2,1)S(1)}, f32[80,256]{1,0:T(8,128)S(1)}, f32[64,256]{1,0:T(8,128)S(1)}) custom-call(s32[64]{0:T(128)S(1)} %copy-done.6, f32[2048,128]{1,0:T(8,128)} %bitcast.27, f32[64,2048]{1,0:T(8,128)S(1)} %get-tuple-element.13.refs_0_, f32[16,2048]{1,0:T(8,128)S(1)} %copy-done.2, ...), custom_call_target="tpu_custom_call" | custom-call | flops 268435456 | bytes 8388608 | tf_op jit(solution)/shard_map/main/pallas_call | solution.py:444
  31.4 2.2 %all-gather = bf16[2048,128]{1,0:T(8,128)(2,1)S(1)} all-gather(bf16[1024,128]{1,0:T(8,128)(2,1)S(1)} %get-tuple-element.17), channel_id=2, replica_groups={{0,1},{2,3},{4,5},{6,7},{8,9},{10,11},{12,13},{14,15},{16,17},{18,19},{..., dimensions={0}, use_global_device_ids=true | all-gather | bytes 786432 | tf_op jit(solution)/shard_map/all_gather | solution.py:476
  33.6 0.0 copy-start
  33.7 0.9 %broadcast_in_dim.21 = bf16[4,512,128]{2,1,0:T(8,128)(2,1)} broadcast(bf16[512,128]{1,0:T(8,128)(2,1)S(1)} %dynamic-slice_reduce_fusion), dimensions={1,2} | broadcast | bytes 655360 | tf_op jit(solution)/shard_map/broadcast_in_dim | solution.py:479
  34.5 0.0 copy-start.10
  34.5 4.6 %all-to-all-start.1 = ((bf16[4,512,128]{2,1,0:T(8,128)(2,1)}), bf16[4,512,128]{2,1,0:T(8,128)(2,1)S(1)}, u32[]{:S(2)}, u32[]{:S(2)}) async-start(bf16[4,512,128]{2,1,0:T(8,128)(2,1)} %broadcast_in_dim.21), calls=%async_computation.1 | async-start | bytes 1048576 | tf_op jit(solution)/shard_map/all_to_all | solution.py:478
  39.1 0.0 copy-done.10
  39.1 0.1 iota_compare_fusion
  39.2 0.0 copy-done
  39.2 2.9 %update.1 = f32[2048,128]{1,0:T(8,128)} custom-call(s32[64]{0:T(128)S(1)} %copy-done.6, f32[2048,128]{1,0:T(8,128)S(1)} %bitcast.28, f32[80,256]{1,0:T(8,128)S(1)} %get-tuple-element.18.refs_0_, f32[64,256]{1,0:T(8,128)S(1)} %get-tuple-element.19.refs_1_, bf16[304,128]{1,0:T(8,128)(2,1)S(1)} %collective-permute-done.refs_2_, ...), custom_call_target="tpu_custom_call" | custom-call | flops 16777216 | bytes 8388608 | tf_op jit(solution)/shard_map/update/pallas_call | solution.py:460
  42.1 5.9 %all-to-all-done.1 = bf16[4,512,128]{2,1,0:T(8,128)(2,1)S(1)} async-done(((bf16[4,512,128]{2,1,0:T(8,128)(2,1)}), bf16[4,512,128]{2,1,0:T(8,128)(2,1)S(1)}, u32[]{:S(2)}, u32[]{:S(2)}) %all-to-all-start.1) | async-done | bytes 524320 | tf_op jit(solution)/shard_map/all_to_all | solution.py:478
  48.0 0.1 reduce_sum.25
  48.1 3.2 %all_gather.11 = bf16[16,4,2048]{2,1,0:T(4,128)(2,1)S(1)} all-gather(bf16[8,4,2048]{2,1,0:T(4,128)(2,1)S(1)} %bitcast.36), channel_id=1, replica_groups={{0,1},{2,3},{4,5},{6,7},{8,9},{10,11},{12,13},{14,15},{16,17},{18,19},{..., dimensions={0}, use_global_device_ids=true | all-gather | bytes 393216 | tf_op jit(solution)/shard_map/all_gather | solution.py:482
  51.2 1.0 %select_convert_fusion = bf16[16,4,2048]{2,1,0:T(4,128)(2,1)} fusion(bf16[16,4,2048]{2,1,0:T(4,128)(2,1)S(1)} %all_gather.11, bf16[16,4,2048]{2,1,0:T(4,128)(2,1)S(1)} %copy-done.1, pred[16,4]{1,0:T(8,128)(4,1)S(1)} %iota_compare_fusion), kind=kLoop, calls=%fused_computation | loop fusion | flops 655360 | bytes 786496 | tf_op jit(solution)/shard_map/convert_element_type | solution.py:484
  (1 shorter events, 0.0 us)
Async XLA Ops:
  3.2 10.4 %copy-start.11 = (bf16[304,128]{1,0:T(8,128)(2,1)S(1)}, bf16[304,128]{1,0:T(8,128)(2,1)}, u32[]{:S(2)}) copy-start(bf16[304,128]{1,0:T(8,128)(2,1)} %get-tuple-element.14) | copy-start | bytes 233476
  3.2 21.4 %copy-start.1 = (bf16[16,4,2048]{2,1,0:T(4,128)(2,1)S(1)}, bf16[16,4,2048]{2,1,0:T(4,128)(2,1)}, u32[]{:S(2)}) copy-start(bf16[16,4,2048]{2,1,0:T(4,128)(2,1)} %param.16) | copy-start | bytes 786436
  3.2 24.0 %all-to-all-start = ((bf16[8,64,256]{2,1,0:T(8,128)(2,1)}), bf16[8,64,256]{2,1,0:T(8,128)(2,1)S(1)}, u32[]{:S(2)}, u32[]{:S(2)}) async-start(bf16[8,64,256]{2,1,0:T(8,128)(2,1)} %get-tuple-element.15), calls=%async_computation | async-start | bytes 524288 | tf_op jit(solution)/shard_map/all_to_all | solution.py:422
  13.6 13.6 %collective-permute-start.1 = (bf16[304,128]{1,0:T(8,128)(2,1)S(1)}, bf16[304,128]{1,0:T(8,128)(2,1)S(1)}, u32[]{:S(2)}, u32[]{:S(2)}) collective-permute-start(bf16[304,128]{1,0:T(8,128)(2,1)S(1)} %copy-done.11), channel_id=1, source_target_pairs={{0,8},{8,16},{16,24},{24,32},{32,40},{40,48},{48,56},{56,64},{64,7... | collective-permute-start | bytes 233480 | tf_op jit(solution)/shard_map/ppermute | solution.py:421
  15.5 11.7 %collective-permute-start = (bf16[304,128]{1,0:T(8,128)(2,1)S(1)}, bf16[304,128]{1,0:T(8,128)(2,1)S(1)}, u32[]{:S(2)}, u32[]{:S(2)}) collective-permute-start(bf16[304,128]{1,0:T(8,128)(2,1)S(1)} %copy-done.11), channel_id=1, source_target_pairs={{8,0},{16,8},{24,16},{32,24},{40,32},{48,40},{56,48},{64,56},{72,6... | collective-permute-start | bytes 233480 | tf_op jit(solution)/shard_map/ppermute | solution.py:420
  24.6 0.7 %copy-start.8 = (f32[256]{0:T(256)S(1)}, f32[256]{0:T(256)}, u32[]{:S(2)}) copy-start(f32[256]{0:T(256)} %param.29) | copy-start | bytes 3076
  24.6 0.7 %copy-start.9 = (f32[256]{0:T(256)S(1)}, f32[256]{0:T(256)}, u32[]{:S(2)}) copy-start(f32[256]{0:T(256)} %param.30) | copy-start | bytes 3076
  24.6 0.7 %copy-start.5 = (f32[2048]{0:T(1024)S(1)}, f32[2048]{0:T(1024)}, u32[]{:S(2)}) copy-start(f32[2048]{0:T(1024)} %param.21) | copy-start | bytes 24580
  24.7 0.7 %copy-start.6 = (s32[64]{0:T(128)S(1)}, s32[64]{0:T(128)}, u32[]{:S(2)}) copy-start(s32[64]{0:T(128)} %get-tuple-element.12.meta_ref) | copy-start | bytes 772
  24.7 0.7 %copy-start.7 = (f32[256]{0:T(256)S(1)}, f32[256]{0:T(256)}, u32[]{:S(2)}) copy-start(f32[256]{0:T(256)} %param.28) | copy-start | bytes 3076
  25.4 1.9 %copy-start.2 = (f32[16,2048]{1,0:T(8,128)S(1)}, f32[16,2048]{1,0:T(8,128)}, u32[]{:S(2)}) copy-start(f32[16,2048]{1,0:T(8,128)} %refs_1_.1) | copy-start | bytes 393220
  25.4 1.9 %copy-start.3 = (f32[4,2048]{1,0:T(4,128)S(1)}, f32[4,2048]{1,0:T(4,128)}, u32[]{:S(2)}) copy-start(f32[4,2048]{1,0:T(4,128)} %refs_4_.1) | copy-start | bytes 98308
  25.4 1.9 %copy-start.4 = (bf16[64,256]{1,0:T(8,128)(2,1)S(1)}, bf16[64,256]{1,0:T(8,128)(2,1)}, u32[]{:S(2)}) copy-start(bf16[64,256]{1,0:T(8,128)(2,1)} %refs_9_.1) | copy-start | bytes 98308
  33.6 5.5 %copy-start = (f32[16,4,4096]{2,1,0:T(4,128)S(1)}, f32[16,4,4096]{2,1,0:T(4,128)}, u32[]{:S(2)}) copy-start(f32[16,4,4096]{2,1,0:T(4,128)} %param.19) | copy-start | bytes 3145732
  34.5 4.6 %copy-start.10 = (s32[16]{0:T(128)S(1)}, s32[16]{0:T(128)}, u32[]{:S(2)}) copy-start(s32[16]{0:T(128)} %tally_hbm.1) | copy-start | bytes 196
  34.5 13.5 %all-to-all-start.1 = ((bf16[4,512,128]{2,1,0:T(8,128)(2,1)}), bf16[4,512,128]{2,1,0:T(8,128)(2,1)S(1)}, u32[]{:S(2)}, u32[]{:S(2)}) async-start(bf16[4,512,128]{2,1,0:T(8,128)(2,1)} %broadcast_in_dim.21), calls=%async_computation.1 | async-start | bytes 1048576 | tf_op jit(solution)/shard_map/all_to_all | solution.py:478

commit v11 on v10

--- a/solution.py
+++ b/solution.py
@@ -82,7 +82,7 @@
     loads = copies(
         (lookup_hbm, prev_hbm, mem_hbm, left_hbm, tally_hbm), (lookup_ref, prev, mem, left, tally_ref), sems
     )
-    start(loads)
+    start([loads[n] for n in (3, 0, 1, 2, 4)])
     me, behind = place()
     first = me * SLOTS
     loads[3].wait()
@@ -143,6 +143,12 @@
     return a[t * SLOTS : (t + 1) * SLOTS, :]
 
 
+def reorder_matrix():
+    row, col = iota((LOCAL, LOCAL), 0), iota((LOCAL, LOCAL), 1)
+    source = (col % HEADS) * HEAD + ((col // HEADS) % (HEAD // 2)) * 2 + col // 128
+    return (row == source).astype(BF16)
+
+
 def place_received(meta_ref, received, state):
     for n, recv_ref in enumerate(received):
         begin = pl.multiple_of(meta_ref[CAME + 4 + n] * STATE_ROWS, STATE_ROWS)
@@ -227,8 +233,7 @@
     decay = jnp.exp(-jnp.exp(row_of(small_ref[0:2, :]) + dot(lora, right_ref[...])))
     row256, col256 = iota((LOCAL, LOCAL), 0), iota((LOCAL, LOCAL), 1)
     same_head = (row256 // HEAD == col256 // HEAD).astype(BF16)
-    source = (col256 % HEADS) * HEAD + ((col256 // HEADS) % (HEAD // 2)) * 2 + col256 // 128
-    reorder = (row256 == source).astype(BF16)
+    reorder = reorder_matrix()
     rkv = []
     for n in range(3):
         loads[5 + n].wait()
@@ -263,8 +268,8 @@
         term = cut(sums, n) * v[s]
         within[t] = term if within[t] is None else within[t] + term
 
-    moved = dot_split(jnp.concatenate(reach + coefs + [run], axis=0), reorder)
-    moved_ref[...] = moved[STEPS * SLOTS :, :]
+    moved = dot(jnp.concatenate(reach, axis=0).astype(BF16), reorder)
+    moved_ref[...] = jnp.concatenate(coefs + [run], axis=0)
     vals_ref[...] = rkv[2]
 
     lane = iota((SLOTS, 128), 1)
@@ -323,6 +328,7 @@
     moved_ref, vals_ref, from_after, from_before = bufs
     loads[0].wait()
     loads[1].wait()
+    moved = dot_split(moved_ref[...], reorder_matrix())
     rowd, cold = iota((LOCAL, HEADS * 128), 0), iota((LOCAL, HEADS * 128), 1)
     double = (rowd == (cold // 128) * HEAD + cold % HEAD).astype(BF16)
     doubled = dot(vals_ref[...].astype(BF16), double)
@@ -334,9 +340,9 @@
             cols = slice(p * 128, (p + 1) * 128)
             for t in range(STEPS):
                 at = pl.ds(t * 8 + p * HEADS + h, SLOTS, stride=STEPS * 8)
-                keys[at, :] = jnp.where(head_lane, cut(moved_ref, t)[:, cols], 0.0)
+                keys[at, :] = jnp.where(head_lane, cut(moved, t)[:, cols], 0.0)
                 vals[at, :] = jnp.where(half, cut(doubled, t)[:, h * 128 : (h + 1) * 128], 0.0)
-            whole = jnp.where(head_lane, cut(moved_ref, STEPS)[:, cols], 0.0)
+            whole = jnp.where(head_lane, cut(moved, STEPS)[:, cols], 0.0)
             high = whole.astype(BF16).astype(F32)
             decays[pl.ds(p * HEADS + h, SLOTS, stride=16), :] = high
             decays[pl.ds(8 + p * HEADS + h, SLOTS, stride=16), :] = whole - high

time: 52.6 us -> 52.2 us (level)
  no operation moved by 1% of the time
where the time goes in v11:
time: 52.2 us; the launch traced here: 51.8 us
  starting transfers between devices  25.9 us (50%)
  Pallas kernels  11.1 us (21%)
  waiting for transfers between devices  5.93 us (11%)
  blocking collectives  5.34 us (10%)
  local copies, waits for them, and re-layouts  1.58 us (3%)
  other arithmetic  1.15 us (2%)
  between operations  0.83 us (2%)
    all_to_all x1, starting transfers between devices, shards(): left = lax.all_to_all(left, 'tensor', 0, 0)  10.3 us
    ppermute x1, starting transfers between devices, shards(): lax.ppermute(packed, 'seq', [((i + 1) % rings, i) for i in range(rings)])  9.1 us
    all_to_all x1, waiting for transfers between devices, shards(): lax.all_to_all(jnp.broadcast_to(mine[None], (teams // 2,) + mine.shape),...  5.92 us
    all_to_all x1, starting transfers between devices, shards(): lax.all_to_all(jnp.broadcast_to(mine[None], (teams // 2,) + mine.shape),...  4.56 us
    pallas_call x1, Pallas kernels, shards(): pl.pallas_call(main_kernel, out_shape=[shape((ROWS * TILES, 128), BF16),...  4.19 us
    all_gather x1, blocking collectives, shards(): proj = lax.all_gather(total, 'tensor', axis_index_groups=pairs, tiled=True)  3.16 us
    pallas_call x1, Pallas kernels, shards(): pl.pallas_call(update_kernel, out_shape=shape((SLOTS * STATE_ROWS, 128),...  2.9 us
    pallas_call x1, Pallas kernels, shards(): pl.pallas_call(pack_kernel, out_shape=[shape((PACK_ROWS, 128), BF16), sha...  2.2 us
  transfers between devices with their start and end apart: 4, of which 1 were waited for; matrix products, arithmetic and copies ran while one was open for 0% of the time, Pallas kernels for 9%

profile of v11, /device:TPU:1, one launch (start us, length us, event | category | flops | bytes accessed | tf_op | source)
XLA Modules:
  0.0 51.8 jit_solution(3130427488221358647)
XLA Ops:
  0.6 2.2 %pack.1 = (bf16[304,128]{1,0:T(8,128)(2,1)}, bf16[8,64,256]{2,1,0:T(8,128)(2,1)}, s32[64]{0:T(128)}) custom-call(s32[16]{0:T(128)} %lookup_hbm.1, s32[16]{0:T(128)} %tally_hbm.1, f32[16,2048]{1,0:T(8,128)} %refs_1_.1, f32[2048,128]{1,0:T(8,128)} %bitcast.26, bf16[64,256]{1,0:T(8,128)(2,1)} %bitcast.37), custom_call_target="tpu_custom_call" | custom-call | bytes 1048576 | tf_op jit(solution)/shard_map/pack/pallas_call | solution.py:412
  2.8 0.0 copy-start.11
  2.9 0.0 copy-start.1
  2.9 10.3 %all-to-all-start = ((bf16[8,64,256]{2,1,0:T(8,128)(2,1)}), bf16[8,64,256]{2,1,0:T(8,128)(2,1)S(1)}, u32[]{:S(2)}, u32[]{:S(2)}) async-start(bf16[8,64,256]{2,1,0:T(8,128)(2,1)} %get-tuple-element.15), calls=%async_computation | async-start | bytes 524288 | tf_op jit(solution)/shard_map/all_to_all | solution.py:428
  13.2 0.0 copy-done.11
  13.2 1.9 %collective-permute-start.1 = (bf16[304,128]{1,0:T(8,128)(2,1)S(1)}, bf16[304,128]{1,0:T(8,128)(2,1)S(1)}, u32[]{:S(2)}, u32[]{:S(2)}) collective-permute-start(bf16[304,128]{1,0:T(8,128)(2,1)S(1)} %copy-done.11), channel_id=1, source_target_pairs={{0,8},{8,16},{16,24},{24,32},{32,40},{40,48},{48,56},{56,64},{64,7... | collective-permute-start | bytes 233480 | tf_op jit(solution)/shard_map/ppermute | solution.py:427
  15.1 9.1 %collective-permute-start = (bf16[304,128]{1,0:T(8,128)(2,1)S(1)}, bf16[304,128]{1,0:T(8,128)(2,1)S(1)}, u32[]{:S(2)}, u32[]{:S(2)}) collective-permute-start(bf16[304,128]{1,0:T(8,128)(2,1)S(1)} %copy-done.11), channel_id=1, source_target_pairs={{8,0},{16,8},{24,16},{32,24},{40,32},{48,40},{56,48},{64,56},{72,6... | collective-permute-start | bytes 233480 | tf_op jit(solution)/shard_map/ppermute | solution.py:426
  24.2 0.0 copy-start.8
  24.2 0.0 copy-start.9
  24.3 0.0 copy-start.5
  24.3 0.0 copy-start.6
  24.3 0.0 copy-start.7
  24.3 0.0 copy-done.1
  24.3 0.6 %copy-done.8 = f32[256]{0:T(256)S(1)} copy-done((f32[256]{0:T(256)S(1)}, f32[256]{0:T(256)}, u32[]{:S(2)}) %copy-start.8) | copy-done | bytes 1048
  24.9 0.0 copy-done.9
  24.9 0.0 copy-done.5
  25.0 0.0 copy-done.6
  25.0 0.0 copy-done.7
  25.0 0.0 copy-start.2
  25.0 0.0 copy-start.3
  25.0 0.0 copy-start.4
  25.0 1.8 %norm.1 = (f32[64,2048]{1,0:T(8,128)S(1)}, f32[16,2048]{1,0:T(8,128)}, f32[8,128]{1,0:T(8,128)S(1)}) custom-call(s32[64]{0:T(128)S(1)} %copy-done.6, bf16[1024,128]{1,0:T(8,128)(2,1)S(1)} %bitcast.29, f32[16,128]{1,0:T(8,128)S(1)} %bitcast.30, f32[2,128]{1,0:T(2,128)S(1)} %bitcast.31, f32[2,128]{1,0:T(2,128)S(1)} %bitcast.32, f32[2,128]{1,0:T(2,128)S(1)} %bitcast.33), custom_call_target="tpu_custom_call" | custom-call | bytes 4194304 | tf_op jit(solution)/shard_map/norm/pallas_call | solution.py:434
  26.8 0.0 collective-permute-done.1.refs_3_
  26.8 0.0 collective-permute-done.refs_2_
  26.8 0.0 all-to-all-done.refs_8_
  26.8 0.0 copy-done.2
  26.8 0.0 copy-done.3
  26.9 0.0 copy-done.4
  26.9 4.2 %main.1 = (bf16[1024,128]{1,0:T(8,128)(2,1)S(1)}, f32[80,256]{1,0:T(8,128)S(1)}, f32[64,256]{1,0:T(8,128)S(1)}) custom-call(s32[64]{0:T(128)S(1)} %copy-done.6, f32[2048,128]{1,0:T(8,128)} %bitcast.27, f32[64,2048]{1,0:T(8,128)S(1)} %get-tuple-element.13.refs_0_, f32[16,2048]{1,0:T(8,128)S(1)} %copy-done.2, ...), custom_call_target="tpu_custom_call" | custom-call | flops 268435456 | bytes 8388608 | tf_op jit(solution)/shard_map/main/pallas_call | solution.py:450
  31.1 2.2 %all-gather = bf16[2048,128]{1,0:T(8,128)(2,1)S(1)} all-gather(bf16[1024,128]{1,0:T(8,128)(2,1)S(1)} %get-tuple-element.17), channel_id=2, replica_groups={{0,1},{2,3},{4,5},{6,7},{8,9},{10,11},{12,13},{14,15},{16,17},{18,19},{..., dimensions={0}, use_global_device_ids=true | all-gather | bytes 786432 | tf_op jit(solution)/shard_map/all_gather | solution.py:482
  33.2 0.0 copy-start
  33.3 0.9 %broadcast_in_dim.21 = bf16[4,512,128]{2,1,0:T(8,128)(2,1)} broadcast(bf16[512,128]{1,0:T(8,128)(2,1)S(1)} %dynamic-slice_reduce_fusion), dimensions={1,2} | broadcast | bytes 655360 | tf_op jit(solution)/shard_map/broadcast_in_dim | solution.py:485
  34.1 0.0 copy-start.10
  34.1 4.6 %all-to-all-start.1 = ((bf16[4,512,128]{2,1,0:T(8,128)(2,1)}), bf16[4,512,128]{2,1,0:T(8,128)(2,1)S(1)}, u32[]{:S(2)}, u32[]{:S(2)}) async-start(bf16[4,512,128]{2,1,0:T(8,128)(2,1)} %broadcast_in_dim.21), calls=%async_computation.1 | async-start | bytes 1048576 | tf_op jit(solution)/shard_map/all_to_all | solution.py:484
  38.7 0.0 copy-done.10
  38.7 0.1 iota_compare_fusion
  38.8 0.0 copy-done
  38.8 2.9 %update.1 = f32[2048,128]{1,0:T(8,128)} custom-call(s32[64]{0:T(128)S(1)} %copy-done.6, f32[2048,128]{1,0:T(8,128)S(1)} %bitcast.28, f32[80,256]{1,0:T(8,128)S(1)} %get-tuple-element.18.refs_0_, f32[64,256]{1,0:T(8,128)S(1)} %get-tuple-element.19.refs_1_, bf16[304,128]{1,0:T(8,128)(2,1)S(1)} %collective-permute-done.refs_2_, ...), custom_call_target="tpu_custom_call" | custom-call | flops 16777216 | bytes 8388608 | tf_op jit(solution)/shard_map/update/pallas_call | solution.py:466
  41.7 5.9 %all-to-all-done.1 = bf16[4,512,128]{2,1,0:T(8,128)(2,1)S(1)} async-done(((bf16[4,512,128]{2,1,0:T(8,128)(2,1)}), bf16[4,512,128]{2,1,0:T(8,128)(2,1)S(1)}, u32[]{:S(2)}, u32[]{:S(2)}) %all-to-all-start.1) | async-done | bytes 524320 | tf_op jit(solution)/shard_map/all_to_all | solution.py:484
  47.6 0.1 reduce_sum.25
  47.7 3.2 %all_gather.11 = bf16[16,4,2048]{2,1,0:T(4,128)(2,1)S(1)} all-gather(bf16[8,4,2048]{2,1,0:T(4,128)(2,1)S(1)} %bitcast.36), channel_id=1, replica_groups={{0,1},{2,3},{4,5},{6,7},{8,9},{10,11},{12,13},{14,15},{16,17},{18,19},{..., dimensions={0}, use_global_device_ids=true | all-gather | bytes 393216 | tf_op jit(solution)/shard_map/all_gather | solution.py:488
  50.9 1.0 %select_convert_fusion = bf16[16,4,2048]{2,1,0:T(4,128)(2,1)} fusion(bf16[16,4,2048]{2,1,0:T(4,128)(2,1)S(1)} %all_gather.11, bf16[16,4,2048]{2,1,0:T(4,128)(2,1)S(1)} %copy-done.1, pred[16,4]{1,0:T(8,128)(4,1)S(1)} %iota_compare_fusion), kind=kLoop, calls=%fused_computation | loop fusion | flops 655360 | bytes 786496 | tf_op jit(solution)/shard_map/convert_element_type | solution.py:490
  (1 shorter events, 0.0 us)
Async XLA Ops:
  2.8 10.4 %copy-start.11 = (bf16[304,128]{1,0:T(8,128)(2,1)S(1)}, bf16[304,128]{1,0:T(8,128)(2,1)}, u32[]{:S(2)}) copy-start(bf16[304,128]{1,0:T(8,128)(2,1)} %get-tuple-element.14) | copy-start | bytes 233476
  2.9 21.4 %copy-start.1 = (bf16[16,4,2048]{2,1,0:T(4,128)(2,1)S(1)}, bf16[16,4,2048]{2,1,0:T(4,128)(2,1)}, u32[]{:S(2)}) copy-start(bf16[16,4,2048]{2,1,0:T(4,128)(2,1)} %param.16) | copy-start | bytes 786436
  2.9 24.0 %all-to-all-start = ((bf16[8,64,256]{2,1,0:T(8,128)(2,1)}), bf16[8,64,256]{2,1,0:T(8,128)(2,1)S(1)}, u32[]{:S(2)}, u32[]{:S(2)}) async-start(bf16[8,64,256]{2,1,0:T(8,128)(2,1)} %get-tuple-element.15), calls=%async_computation | async-start | bytes 524288 | tf_op jit(solution)/shard_map/all_to_all | solution.py:428
  13.2 13.6 %collective-permute-start.1 = (bf16[304,128]{1,0:T(8,128)(2,1)S(1)}, bf16[304,128]{1,0:T(8,128)(2,1)S(1)}, u32[]{:S(2)}, u32[]{:S(2)}) collective-permute-start(bf16[304,128]{1,0:T(8,128)(2,1)S(1)} %copy-done.11), channel_id=1, source_target_pairs={{0,8},{8,16},{16,24},{24,32},{32,40},{40,48},{48,56},{56,64},{64,7... | collective-permute-start | bytes 233480 | tf_op jit(solution)/shard_map/ppermute | solution.py:427
  15.1 11.7 %collective-permute-start = (bf16[304,128]{1,0:T(8,128)(2,1)S(1)}, bf16[304,128]{1,0:T(8,128)(2,1)S(1)}, u32[]{:S(2)}, u32[]{:S(2)}) collective-permute-start(bf16[304,128]{1,0:T(8,128)(2,1)S(1)} %copy-done.11), channel_id=1, source_target_pairs={{8,0},{16,8},{24,16},{32,24},{40,32},{48,40},{56,48},{64,56},{72,6... | collective-permute-start | bytes 233480 | tf_op jit(solution)/shard_map/ppermute | solution.py:426
  24.2 0.7 %copy-start.8 = (f32[256]{0:T(256)S(1)}, f32[256]{0:T(256)}, u32[]{:S(2)}) copy-start(f32[256]{0:T(256)} %param.29) | copy-start | bytes 3076
  24.2 0.7 %copy-start.9 = (f32[256]{0:T(256)S(1)}, f32[256]{0:T(256)}, u32[]{:S(2)}) copy-start(f32[256]{0:T(256)} %param.30) | copy-start | bytes 3076
  24.3 0.7 %copy-start.5 = (f32[2048]{0:T(1024)S(1)}, f32[2048]{0:T(1024)}, u32[]{:S(2)}) copy-start(f32[2048]{0:T(1024)} %param.21) | copy-start | bytes 24580
  24.3 0.7 %copy-start.6 = (s32[64]{0:T(128)S(1)}, s32[64]{0:T(128)}, u32[]{:S(2)}) copy-start(s32[64]{0:T(128)} %get-tuple-element.12.meta_ref) | copy-start | bytes 772
  24.3 0.7 %copy-start.7 = (f32[256]{0:T(256)S(1)}, f32[256]{0:T(256)}, u32[]{:S(2)}) copy-start(f32[256]{0:T(256)} %param.28) | copy-start | bytes 3076
  25.0 1.9 %copy-start.2 = (f32[16,2048]{1,0:T(8,128)S(1)}, f32[16,2048]{1,0:T(8,128)}, u32[]{:S(2)}) copy-start(f32[16,2048]{1,0:T(8,128)} %refs_1_.1) | copy-start | bytes 393220
  25.0 1.9 %copy-start.3 = (f32[4,2048]{1,0:T(4,128)S(1)}, f32[4,2048]{1,0:T(4,128)}, u32[]{:S(2)}) copy-start(f32[4,2048]{1,0:T(4,128)} %refs_4_.1) | copy-start | bytes 98308
  25.0 1.9 %copy-start.4 = (bf16[64,256]{1,0:T(8,128)(2,1)S(1)}, bf16[64,256]{1,0:T(8,128)(2,1)}, u32[]{:S(2)}) copy-start(bf16[64,256]{1,0:T(8,128)(2,1)} %refs_9_.1) | copy-start | bytes 98308
  33.2 5.5 %copy-start = (f32[16,4,4096]{2,1,0:T(4,128)S(1)}, f32[16,4,4096]{2,1,0:T(4,128)}, u32[]{:S(2)}) copy-start(f32[16,4,4096]{2,1,0:T(4,128)} %param.19) | copy-start | bytes 3145732
  34.1 4.6 %copy-start.10 = (s32[16]{0:T(128)S(1)}, s32[16]{0:T(128)}, u32[]{:S(2)}) copy-start(s32[16]{0:T(128)} %tally_hbm.1) | copy-start | bytes 196
  34.1 13.5 %all-to-all-start.1 = ((bf16[4,512,128]{2,1,0:T(8,128)(2,1)}), bf16[4,512,128]{2,1,0:T(8,128)(2,1)S(1)}, u32[]{:S(2)}, u32[]{:S(2)}) async-start(bf16[4,512,128]{2,1,0:T(8,128)(2,1)} %broadcast_in_dim.21), calls=%async_computation.1 | async-start | bytes 1048576 | tf_op jit(solution)/shard_map/all_to_all | solution.py:484

commit v12 on v11

--- a/solution.py
+++ b/solution.py
@@ -484,10 +484,13 @@
     spread = lax.all_to_all(
         jnp.broadcast_to(mine[None], (teams // 2,) + mine.shape), "tensor", 0, 0, axis_index_groups=chips
     )
-    total = tiles_back(spread.astype(F32).sum(0).astype(BF16), SLOTS // 2, STEPS, WIDTH)
-    proj = lax.all_gather(total, "tensor", axis_index_groups=pairs, tiled=True)
-    valid = tally[:, None, None] > jnp.arange(STEPS, dtype=jnp.int32)[None, :, None]
-    mixed = jnp.where(valid, layer_entry_vectors.astype(F32) + proj.astype(F32), 0.0).astype(BF16)
+    mine_rows = SLOTS // 2
+    residual = lax.dynamic_slice_in_dim(layer_entry_vectors, core * mine_rows, mine_rows, 0).astype(F32)
+    counts = lax.dynamic_slice_in_dim(tally, core * mine_rows, mine_rows, 0)
+    valid = counts[:, None, None] > jnp.arange(STEPS, dtype=jnp.int32)[None, :, None]
+    total = residual + tiles_back(spread.astype(F32).sum(0), mine_rows, STEPS, WIDTH)
+    mixed = jnp.where(valid, total, 0.0).astype(BF16)
+    mixed = lax.all_gather(mixed, "tensor", axis_index_groups=pairs, tiled=True)
     return (
         mixed,
         tiles_back(new_states, SLOTS, HEADS, HEAD * HEAD),

time: 52.2 us -> 51.9 us (level)
  local copies, waits for them, and re-layouts: 1.58 us -> 3 us
  other arithmetic: 1.15 us -> 0.3 us
  waiting for transfers between devices: 5.93 us -> 5.2 us
    unnamed x24 -> x25, local copies, waits for them, and re-layouts: 0.72 us -> 2.07 us
    convert_element_type x1, other arithmetic: 0.96 us -> 0.12 us  [shards(): mixed = jnp.where(valid, total, 0.0).astype(BF16)]
    all_to_all x1, waiting for transfers between devices: 5.92 us -> 5.2 us  [shards(): lax.all_to_all(jnp.broadcast_to(mine[None], (teams // 2,) + mine.shape),...]
where the time goes in v12:
time: 51.9 us; the launch traced here: 51.5 us
  starting transfers between devices  25.8 us (50%)
  Pallas kernels  11.1 us (21%)
  blocking collectives  5.34 us (10%)
  waiting for transfers between devices  5.2 us (10%)
  local copies, waits for them, and re-layouts  3 us (6%)
  between operations  0.83 us (2%)
    all_to_all x1, starting transfers between devices, shards(): left = lax.all_to_all(left, 'tensor', 0, 0)  10.3 us
    ppermute x1, starting transfers between devices, shards(): lax.ppermute(packed, 'seq', [((i + 1) % rings, i) for i in range(rings)])  9.1 us
    all_to_all x1, waiting for transfers between devices, shards(): lax.all_to_all(jnp.broadcast_to(mine[None], (teams // 2,) + mine.shape),...  5.2 us
    all_to_all x1, starting transfers between devices, shards(): lax.all_to_all(jnp.broadcast_to(mine[None], (teams // 2,) + mine.shape),...  4.43 us
    pallas_call x1, Pallas kernels, shards(): pl.pallas_call(main_kernel, out_shape=[shape((ROWS * TILES, 128), BF16),...  4.19 us
    all_gather x1, blocking collectives, shards(): mixed = lax.all_gather(mixed, 'tensor', axis_index_groups=pairs, tiled=True)  3.16 us
    pallas_call x1, Pallas kernels, shards(): pl.pallas_call(update_kernel, out_shape=shape((SLOTS * STATE_ROWS, 128),...  2.89 us
    pallas_call x1, Pallas kernels, shards(): pl.pallas_call(pack_kernel, out_shape=[shape((PACK_ROWS, 128), BF16), sha...  2.2 us
  transfers between devices with their start and end apart: 4, of which 1 were waited for; matrix products, arithmetic and copies ran while one was open for 0% of the time, Pallas kernels for 9%

profile of v12, /device:TPU:1, one launch (start us, length us, event | category | flops | bytes accessed | tf_op | source)
XLA Modules:
  0.0 51.5 jit_solution(12734227259261508015)
XLA Ops:
  0.6 2.2 %pack.1 = (bf16[304,128]{1,0:T(8,128)(2,1)}, bf16[8,64,256]{2,1,0:T(8,128)(2,1)}, s32[64]{0:T(128)}) custom-call(s32[16]{0:T(128)} %lookup_hbm.1, s32[16]{0:T(128)} %tally_hbm.1, f32[16,2048]{1,0:T(8,128)} %refs_1_.1, f32[2048,128]{1,0:T(8,128)} %bitcast.26, bf16[64,256]{1,0:T(8,128)(2,1)} %bitcast.37), custom_call_target="tpu_custom_call" | custom-call | bytes 1048576 | tf_op jit(solution)/shard_map/pack/pallas_call | solution.py:412
  2.8 0.0 copy-start.11
  2.9 0.0 copy-start.1
  2.9 10.3 %all-to-all-start = ((bf16[8,64,256]{2,1,0:T(8,128)(2,1)}), bf16[8,64,256]{2,1,0:T(8,128)(2,1)S(1)}, u32[]{:S(2)}, u32[]{:S(2)}) async-start(bf16[8,64,256]{2,1,0:T(8,128)(2,1)} %get-tuple-element.15), calls=%async_computation | async-start | bytes 524288 | tf_op jit(solution)/shard_map/all_to_all | solution.py:428
  13.2 0.0 copy-done.11
  13.2 1.9 %collective-permute-start.1 = (bf16[304,128]{1,0:T(8,128)(2,1)S(1)}, bf16[304,128]{1,0:T(8,128)(2,1)S(1)}, u32[]{:S(2)}, u32[]{:S(2)}) collective-permute-start(bf16[304,128]{1,0:T(8,128)(2,1)S(1)} %copy-done.11), channel_id=1, source_target_pairs={{0,8},{8,16},{16,24},{24,32},{32,40},{40,48},{48,56},{56,64},{64,7... | collective-permute-start | bytes 233480 | tf_op jit(solution)/shard_map/ppermute | solution.py:427
  15.1 9.1 %collective-permute-start = (bf16[304,128]{1,0:T(8,128)(2,1)S(1)}, bf16[304,128]{1,0:T(8,128)(2,1)S(1)}, u32[]{:S(2)}, u32[]{:S(2)}) collective-permute-start(bf16[304,128]{1,0:T(8,128)(2,1)S(1)} %copy-done.11), channel_id=1, source_target_pairs={{8,0},{16,8},{24,16},{32,24},{40,32},{48,40},{56,48},{64,56},{72,6... | collective-permute-start | bytes 233480 | tf_op jit(solution)/shard_map/ppermute | solution.py:426
  24.2 0.0 copy-start.8
  24.2 0.0 copy-start.9
  24.3 0.0 copy-start.5
  24.3 0.0 copy-start.6
  24.3 0.0 copy-start.7
  24.3 0.0 copy-done.1
  24.3 0.6 %copy-done.8 = f32[256]{0:T(256)S(1)} copy-done((f32[256]{0:T(256)S(1)}, f32[256]{0:T(256)}, u32[]{:S(2)}) %copy-start.8) | copy-done | bytes 1048
  24.9 0.0 copy-done.9
  24.9 0.0 copy-done.5
  25.0 0.0 copy-done.6
  25.0 0.0 copy-done.7
  25.0 0.0 copy-start.2
  25.0 0.0 copy-start.3
  25.0 0.0 copy-start.4
  25.0 1.8 %norm.1 = (f32[64,2048]{1,0:T(8,128)S(1)}, f32[16,2048]{1,0:T(8,128)}, f32[8,128]{1,0:T(8,128)S(1)}) custom-call(s32[64]{0:T(128)S(1)} %copy-done.6, bf16[1024,128]{1,0:T(8,128)(2,1)S(1)} %bitcast.29, f32[16,128]{1,0:T(8,128)S(1)} %bitcast.30, f32[2,128]{1,0:T(2,128)S(1)} %bitcast.31, f32[2,128]{1,0:T(2,128)S(1)} %bitcast.32, f32[2,128]{1,0:T(2,128)S(1)} %bitcast.33), custom_call_target="tpu_custom_call" | custom-call | bytes 4194304 | tf_op jit(solution)/shard_map/norm/pallas_call | solution.py:434
  26.8 0.0 collective-permute-done.1.refs_3_
  26.8 0.0 collective-permute-done.refs_2_
  26.8 0.0 all-to-all-done.refs_8_
  26.8 0.0 copy-done.2
  26.8 0.0 copy-done.3
  26.9 0.0 copy-done.4
  26.9 4.2 %main.1 = (bf16[1024,128]{1,0:T(8,128)(2,1)S(1)}, f32[80,256]{1,0:T(8,128)S(1)}, f32[64,256]{1,0:T(8,128)S(1)}) custom-call(s32[64]{0:T(128)S(1)} %copy-done.6, f32[2048,128]{1,0:T(8,128)} %bitcast.27, f32[64,2048]{1,0:T(8,128)S(1)} %get-tuple-element.13.refs_0_, f32[16,2048]{1,0:T(8,128)S(1)} %copy-done.2, ...), custom_call_target="tpu_custom_call" | custom-call | flops 268435456 | bytes 8388608 | tf_op jit(solution)/shard_map/main/pallas_call | solution.py:450
  31.1 2.2 %all-gather = bf16[2048,128]{1,0:T(8,128)(2,1)S(1)} all-gather(bf16[1024,128]{1,0:T(8,128)(2,1)S(1)} %get-tuple-element.17), channel_id=2, replica_groups={{0,1},{2,3},{4,5},{6,7},{8,9},{10,11},{12,13},{14,15},{16,17},{18,19},{..., dimensions={0}, use_global_device_ids=true | all-gather | bytes 786432 | tf_op jit(solution)/shard_map/all_gather | solution.py:482
  33.2 0.0 copy-start
  33.3 0.9 %broadcast_in_dim.21 = bf16[4,512,128]{2,1,0:T(8,128)(2,1)} broadcast(bf16[512,128]{1,0:T(8,128)(2,1)S(1)} %dynamic-slice_reduce_fusion), dimensions={1,2} | broadcast | bytes 655360 | tf_op jit(solution)/shard_map/broadcast_in_dim | solution.py:485
  34.1 4.4 %all-to-all-start.1 = ((bf16[4,512,128]{2,1,0:T(8,128)(2,1)}), bf16[4,512,128]{2,1,0:T(8,128)(2,1)S(1)}, u32[]{:S(2)}, u32[]{:S(2)}) async-start(bf16[4,512,128]{2,1,0:T(8,128)(2,1)} %broadcast_in_dim.21), calls=%async_computation.1 | async-start | bytes 1048576 | tf_op jit(solution)/shard_map/all_to_all | solution.py:484
  38.6 0.0 copy-start.10
  38.6 0.7 %copy-done.10 = s32[16]{0:T(128)S(1)} copy-done((s32[16]{0:T(128)S(1)}, s32[16]{0:T(128)}, u32[]{:S(2)}) %copy-start.10) | copy-done | bytes 88
  39.2 0.1 dynamic_slice.9
  39.3 0.1 iota_compare_fusion
  39.4 0.0 copy-done
  39.4 2.9 %update.1 = f32[2048,128]{1,0:T(8,128)} custom-call(s32[64]{0:T(128)S(1)} %copy-done.6, f32[2048,128]{1,0:T(8,128)S(1)} %bitcast.28, f32[80,256]{1,0:T(8,128)S(1)} %get-tuple-element.18.refs_0_, f32[64,256]{1,0:T(8,128)S(1)} %get-tuple-element.19.refs_1_, bf16[304,128]{1,0:T(8,128)(2,1)S(1)} %collective-permute-done.refs_2_, ...), custom_call_target="tpu_custom_call" | custom-call | flops 16777216 | bytes 8388608 | tf_op jit(solution)/shard_map/update/pallas_call | solution.py:466
  42.3 5.2 %all-to-all-done.1 = bf16[4,512,128]{2,1,0:T(8,128)(2,1)S(1)} async-done(((bf16[4,512,128]{2,1,0:T(8,128)(2,1)}), bf16[4,512,128]{2,1,0:T(8,128)(2,1)S(1)}, u32[]{:S(2)}, u32[]{:S(2)}) %all-to-all-start.1) | async-done | bytes 524320 | tf_op jit(solution)/shard_map/all_to_all | solution.py:484
  47.5 0.1 convert_reduce_fusion
  47.5 0.1 select_convert_fusion
  47.7 3.2 %all_gather.11 = bf16[16,4,2048]{2,1,0:T(4,128)(2,1)S(1)} all-gather(bf16[8,4,2048]{2,1,0:T(4,128)(2,1)S(1)} %select_convert_fusion), channel_id=1, replica_groups={{0,1},{2,3},{4,5},{6,7},{8,9},{10,11},{12,13},{14,15},{16,17},{18,19},{..., dimensions={0}, use_global_device_ids=true | all-gather | bytes 393216 | tf_op jit(solution)/shard_map/all_gather | solution.py:493
  50.8 0.7 %copy.32 = bf16[16,4,2048]{2,1,0:T(4,128)(2,1)} copy(bf16[16,4,2048]{2,1,0:T(4,128)(2,1)S(1)} %all_gather.11) | data formatting | bytes 524288
  (1 shorter events, 0.0 us)
Async XLA Ops:
  2.8 10.4 %copy-start.11 = (bf16[304,128]{1,0:T(8,128)(2,1)S(1)}, bf16[304,128]{1,0:T(8,128)(2,1)}, u32[]{:S(2)}) copy-start(bf16[304,128]{1,0:T(8,128)(2,1)} %get-tuple-element.14) | copy-start | bytes 233476
  2.9 21.5 %copy-start.1 = (bf16[16,4,2048]{2,1,0:T(4,128)(2,1)S(1)}, bf16[16,4,2048]{2,1,0:T(4,128)(2,1)}, u32[]{:S(2)}) copy-start(bf16[16,4,2048]{2,1,0:T(4,128)(2,1)} %param.16) | copy-start | bytes 786436
  2.9 24.0 %all-to-all-start = ((bf16[8,64,256]{2,1,0:T(8,128)(2,1)}), bf16[8,64,256]{2,1,0:T(8,128)(2,1)S(1)}, u32[]{:S(2)}, u32[]{:S(2)}) async-start(bf16[8,64,256]{2,1,0:T(8,128)(2,1)} %get-tuple-element.15), calls=%async_computation | async-start | bytes 524288 | tf_op jit(solution)/shard_map/all_to_all | solution.py:428
  13.2 13.6 %collective-permute-start.1 = (bf16[304,128]{1,0:T(8,128)(2,1)S(1)}, bf16[304,128]{1,0:T(8,128)(2,1)S(1)}, u32[]{:S(2)}, u32[]{:S(2)}) collective-permute-start(bf16[304,128]{1,0:T(8,128)(2,1)S(1)} %copy-done.11), channel_id=1, source_target_pairs={{0,8},{8,16},{16,24},{24,32},{32,40},{40,48},{48,56},{56,64},{64,7... | collective-permute-start | bytes 233480 | tf_op jit(solution)/shard_map/ppermute | solution.py:427
  15.1 11.7 %collective-permute-start = (bf16[304,128]{1,0:T(8,128)(2,1)S(1)}, bf16[304,128]{1,0:T(8,128)(2,1)S(1)}, u32[]{:S(2)}, u32[]{:S(2)}) collective-permute-start(bf16[304,128]{1,0:T(8,128)(2,1)S(1)} %copy-done.11), channel_id=1, source_target_pairs={{8,0},{16,8},{24,16},{32,24},{40,32},{48,40},{56,48},{64,56},{72,6... | collective-permute-start | bytes 233480 | tf_op jit(solution)/shard_map/ppermute | solution.py:426
  24.2 0.7 %copy-start.8 = (f32[256]{0:T(256)S(1)}, f32[256]{0:T(256)}, u32[]{:S(2)}) copy-start(f32[256]{0:T(256)} %param.29) | copy-start | bytes 3076
  24.2 0.7 %copy-start.9 = (f32[256]{0:T(256)S(1)}, f32[256]{0:T(256)}, u32[]{:S(2)}) copy-start(f32[256]{0:T(256)} %param.30) | copy-start | bytes 3076
  24.3 0.7 %copy-start.5 = (f32[2048]{0:T(1024)S(1)}, f32[2048]{0:T(1024)}, u32[]{:S(2)}) copy-start(f32[2048]{0:T(1024)} %param.21) | copy-start | bytes 24580
  24.3 0.7 %copy-start.6 = (s32[64]{0:T(128)S(1)}, s32[64]{0:T(128)}, u32[]{:S(2)}) copy-start(s32[64]{0:T(128)} %get-tuple-element.12.meta_ref) | copy-start | bytes 772
  24.3 0.7 %copy-start.7 = (f32[256]{0:T(256)S(1)}, f32[256]{0:T(256)}, u32[]{:S(2)}) copy-start(f32[256]{0:T(256)} %param.28) | copy-start | bytes 3076
  25.0 1.9 %copy-start.2 = (f32[16,2048]{1,0:T(8,128)S(1)}, f32[16,2048]{1,0:T(8,128)}, u32[]{:S(2)}) copy-start(f32[16,2048]{1,0:T(8,128)} %refs_1_.1) | copy-start | bytes 393220
  25.0 1.9 %copy-start.3 = (f32[4,2048]{1,0:T(4,128)S(1)}, f32[4,2048]{1,0:T(4,128)}, u32[]{:S(2)}) copy-start(f32[4,2048]{1,0:T(4,128)} %refs_4_.1) | copy-start | bytes 98308
  25.0 1.9 %copy-start.4 = (bf16[64,256]{1,0:T(8,128)(2,1)S(1)}, bf16[64,256]{1,0:T(8,128)(2,1)}, u32[]{:S(2)}) copy-start(bf16[64,256]{1,0:T(8,128)(2,1)} %refs_9_.1) | copy-start | bytes 98308
  33.2 6.1 %copy-start = (f32[16,4,4096]{2,1,0:T(4,128)S(1)}, f32[16,4,4096]{2,1,0:T(4,128)}, u32[]{:S(2)}) copy-start(f32[16,4,4096]{2,1,0:T(4,128)} %param.19) | copy-start | bytes 3145732
  34.1 13.3 %all-to-all-start.1 = ((bf16[4,512,128]{2,1,0:T(8,128)(2,1)}), bf16[4,512,128]{2,1,0:T(8,128)(2,1)S(1)}, u32[]{:S(2)}, u32[]{:S(2)}) async-start(bf16[4,512,128]{2,1,0:T(8,128)(2,1)} %broadcast_in_dim.21), calls=%async_computation.1 | async-start | bytes 1048576 | tf_op jit(solution)/shard_map/all_to_all | solution.py:484
  38.6 0.7 %copy-start.10 = (s32[16]{0:T(128)S(1)}, s32[16]{0:T(128)}, u32[]{:S(2)}) copy-start(s32[16]{0:T(128)} %tally_hbm.1) | copy-start | bytes 196

commit v13 on v12

--- a/solution.py
+++ b/solution.py
@@ -82,7 +82,7 @@
     loads = copies(
         (lookup_hbm, prev_hbm, mem_hbm, left_hbm, tally_hbm), (lookup_ref, prev, mem, left, tally_ref), sems
     )
-    start([loads[n] for n in (3, 0, 1, 2, 4)])
+    start([loads[n] for n in (3, 0, 2, 1, 4)])
     me, behind = place()
     first = me * SLOTS
     loads[3].wait()

time: 51.9 us -> 51.9 us (level)
  no operation moved by 1% of the time
where the time goes in v13:
time: 51.9 us; the launch traced here: 51.5 us
  starting transfers between devices  25.8 us (50%)
  Pallas kernels  11.1 us (21%)
  blocking collectives  5.34 us (10%)
  waiting for transfers between devices  5.2 us (10%)
  local copies, waits for them, and re-layouts  3 us (6%)
  between operations  0.83 us (2%)
    all_to_all x1, starting transfers between devices, shards(): left = lax.all_to_all(left, 'tensor', 0, 0)  10.3 us
    ppermute x1, starting transfers between devices, shards(): lax.ppermute(packed, 'seq', [((i + 1) % rings, i) for i in range(rings)])  9.1 us
    all_to_all x1, waiting for transfers between devices, shards(): lax.all_to_all(jnp.broadcast_to(mine[None], (teams // 2,) + mine.shape),...  5.2 us
    all_to_all x1, starting transfers between devices, shards(): lax.all_to_all(jnp.broadcast_to(mine[None], (teams // 2,) + mine.shape),...  4.43 us
    pallas_call x1, Pallas kernels, shards(): pl.pallas_call(main_kernel, out_shape=[shape((ROWS * TILES, 128), BF16),...  4.19 us
    all_gather x1, blocking collectives, shards(): mixed = lax.all_gather(mixed, 'tensor', axis_index_groups=pairs, tiled=True)  3.16 us
    pallas_call x1, Pallas kernels, shards(): pl.pallas_call(update_kernel, out_shape=shape((SLOTS * STATE_ROWS, 128),...  2.89 us
    pallas_call x1, Pallas kernels, shards(): pl.pallas_call(pack_kernel, out_shape=[shape((PACK_ROWS, 128), BF16), sha...  2.2 us
  transfers between devices with their start and end apart: 4, of which 1 were waited for; matrix products, arithmetic and copies ran while one was open for 0% of the time, Pallas kernels for 9%

profile of v13, /device:TPU:1, one launch (start us, length us, event | category | flops | bytes accessed | tf_op | source)
XLA Modules:
  0.0 51.5 jit_solution(531652774338823094)
XLA Ops:
  0.6 2.2 %pack.1 = (bf16[304,128]{1,0:T(8,128)(2,1)}, bf16[8,64,256]{2,1,0:T(8,128)(2,1)}, s32[64]{0:T(128)}) custom-call(s32[16]{0:T(128)} %lookup_hbm.1, s32[16]{0:T(128)} %tally_hbm.1, f32[16,2048]{1,0:T(8,128)} %refs_1_.1, f32[2048,128]{1,0:T(8,128)} %bitcast.26, bf16[64,256]{1,0:T(8,128)(2,1)} %bitcast.37), custom_call_target="tpu_custom_call" | custom-call | bytes 1048576 | tf_op jit(solution)/shard_map/pack/pallas_call | solution.py:412
  2.8 0.0 copy-start.11
  2.9 0.0 copy-start.1
  2.9 10.3 %all-to-all-start = ((bf16[8,64,256]{2,1,0:T(8,128)(2,1)}), bf16[8,64,256]{2,1,0:T(8,128)(2,1)S(1)}, u32[]{:S(2)}, u32[]{:S(2)}) async-start(bf16[8,64,256]{2,1,0:T(8,128)(2,1)} %get-tuple-element.15), calls=%async_computation | async-start | bytes 524288 | tf_op jit(solution)/shard_map/all_to_all | solution.py:428
  13.2 0.0 copy-done.11
  13.2 1.9 %collective-permute-start.1 = (bf16[304,128]{1,0:T(8,128)(2,1)S(1)}, bf16[304,128]{1,0:T(8,128)(2,1)S(1)}, u32[]{:S(2)}, u32[]{:S(2)}) collective-permute-start(bf16[304,128]{1,0:T(8,128)(2,1)S(1)} %copy-done.11), channel_id=1, source_target_pairs={{0,8},{8,16},{16,24},{24,32},{32,40},{40,48},{48,56},{56,64},{64,7... | collective-permute-start | bytes 233480 | tf_op jit(solution)/shard_map/ppermute | solution.py:427
  15.1 9.1 %collective-permute-start = (bf16[304,128]{1,0:T(8,128)(2,1)S(1)}, bf16[304,128]{1,0:T(8,128)(2,1)S(1)}, u32[]{:S(2)}, u32[]{:S(2)}) collective-permute-start(bf16[304,128]{1,0:T(8,128)(2,1)S(1)} %copy-done.11), channel_id=1, source_target_pairs={{8,0},{16,8},{24,16},{32,24},{40,32},{48,40},{56,48},{64,56},{72,6... | collective-permute-start | bytes 233480 | tf_op jit(solution)/shard_map/ppermute | solution.py:426
  24.2 0.0 copy-start.8
  24.2 0.0 copy-start.9
  24.3 0.0 copy-start.5
  24.3 0.0 copy-start.6
  24.3 0.0 copy-start.7
  24.3 0.0 copy-done.1
  24.3 0.6 %copy-done.8 = f32[256]{0:T(256)S(1)} copy-done((f32[256]{0:T(256)S(1)}, f32[256]{0:T(256)}, u32[]{:S(2)}) %copy-start.8) | copy-done | bytes 1048
  24.9 0.0 copy-done.9
  24.9 0.0 copy-done.5
  25.0 0.0 copy-done.6
  25.0 0.0 copy-done.7
  25.0 0.0 copy-start.2
  25.0 0.0 copy-start.3
  25.0 0.0 copy-start.4
  25.0 1.8 %norm.1 = (f32[64,2048]{1,0:T(8,128)S(1)}, f32[16,2048]{1,0:T(8,128)}, f32[8,128]{1,0:T(8,128)S(1)}) custom-call(s32[64]{0:T(128)S(1)} %copy-done.6, bf16[1024,128]{1,0:T(8,128)(2,1)S(1)} %bitcast.29, f32[16,128]{1,0:T(8,128)S(1)} %bitcast.30, f32[2,128]{1,0:T(2,128)S(1)} %bitcast.31, f32[2,128]{1,0:T(2,128)S(1)} %bitcast.32, f32[2,128]{1,0:T(2,128)S(1)} %bitcast.33), custom_call_target="tpu_custom_call" | custom-call | bytes 4194304 | tf_op jit(solution)/shard_map/norm/pallas_call | solution.py:434
  26.8 0.0 collective-permute-done.1.refs_3_
  26.8 0.0 collective-permute-done.refs_2_
  26.8 0.0 all-to-all-done.refs_8_
  26.8 0.0 copy-done.2
  26.8 0.0 copy-done.3
  26.9 0.0 copy-done.4
  26.9 4.2 %main.1 = (bf16[1024,128]{1,0:T(8,128)(2,1)S(1)}, f32[80,256]{1,0:T(8,128)S(1)}, f32[64,256]{1,0:T(8,128)S(1)}) custom-call(s32[64]{0:T(128)S(1)} %copy-done.6, f32[2048,128]{1,0:T(8,128)} %bitcast.27, f32[64,2048]{1,0:T(8,128)S(1)} %get-tuple-element.13.refs_0_, f32[16,2048]{1,0:T(8,128)S(1)} %copy-done.2, ...), custom_call_target="tpu_custom_call" | custom-call | flops 268435456 | bytes 8388608 | tf_op jit(solution)/shard_map/main/pallas_call | solution.py:450
  31.1 2.2 %all-gather = bf16[2048,128]{1,0:T(8,128)(2,1)S(1)} all-gather(bf16[1024,128]{1,0:T(8,128)(2,1)S(1)} %get-tuple-element.17), channel_id=2, replica_groups={{0,1},{2,3},{4,5},{6,7},{8,9},{10,11},{12,13},{14,15},{16,17},{18,19},{..., dimensions={0}, use_global_device_ids=true | all-gather | bytes 786432 | tf_op jit(solution)/shard_map/all_gather | solution.py:482
  33.2 0.0 copy-start
  33.3 0.9 %broadcast_in_dim.21 = bf16[4,512,128]{2,1,0:T(8,128)(2,1)} broadcast(bf16[512,128]{1,0:T(8,128)(2,1)S(1)} %dynamic-slice_reduce_fusion), dimensions={1,2} | broadcast | bytes 655360 | tf_op jit(solution)/shard_map/broadcast_in_dim | solution.py:485
  34.1 4.4 %all-to-all-start.1 = ((bf16[4,512,128]{2,1,0:T(8,128)(2,1)}), bf16[4,512,128]{2,1,0:T(8,128)(2,1)S(1)}, u32[]{:S(2)}, u32[]{:S(2)}) async-start(bf16[4,512,128]{2,1,0:T(8,128)(2,1)} %broadcast_in_dim.21), calls=%async_computation.1 | async-start | bytes 1048576 | tf_op jit(solution)/shard_map/all_to_all | solution.py:484
  38.6 0.0 copy-start.10
  38.6 0.7 %copy-done.10 = s32[16]{0:T(128)S(1)} copy-done((s32[16]{0:T(128)S(1)}, s32[16]{0:T(128)}, u32[]{:S(2)}) %copy-start.10) | copy-done | bytes 88
  39.2 0.1 dynamic_slice.9
  39.3 0.1 iota_compare_fusion
  39.4 0.0 copy-done
  39.4 2.9 %update.1 = f32[2048,128]{1,0:T(8,128)} custom-call(s32[64]{0:T(128)S(1)} %copy-done.6, f32[2048,128]{1,0:T(8,128)S(1)} %bitcast.28, f32[80,256]{1,0:T(8,128)S(1)} %get-tuple-element.18.refs_0_, f32[64,256]{1,0:T(8,128)S(1)} %get-tuple-element.19.refs_1_, bf16[304,128]{1,0:T(8,128)(2,1)S(1)} %collective-permute-done.refs_2_, ...), custom_call_target="tpu_custom_call" | custom-call | flops 16777216 | bytes 8388608 | tf_op jit(solution)/shard_map/update/pallas_call | solution.py:466
  42.3 5.2 %all-to-all-done.1 = bf16[4,512,128]{2,1,0:T(8,128)(2,1)S(1)} async-done(((bf16[4,512,128]{2,1,0:T(8,128)(2,1)}), bf16[4,512,128]{2,1,0:T(8,128)(2,1)S(1)}, u32[]{:S(2)}, u32[]{:S(2)}) %all-to-all-start.1) | async-done | bytes 524320 | tf_op jit(solution)/shard_map/all_to_all | solution.py:484
  47.5 0.1 convert_reduce_fusion
  47.5 0.1 select_convert_fusion
  47.7 3.2 %all_gather.11 = bf16[16,4,2048]{2,1,0:T(4,128)(2,1)S(1)} all-gather(bf16[8,4,2048]{2,1,0:T(4,128)(2,1)S(1)} %select_convert_fusion), channel_id=1, replica_groups={{0,1},{2,3},{4,5},{6,7},{8,9},{10,11},{12,13},{14,15},{16,17},{18,19},{..., dimensions={0}, use_global_device_ids=true | all-gather | bytes 393216 | tf_op jit(solution)/shard_map/all_gather | solution.py:493
  50.8 0.7 %copy.32 = bf16[16,4,2048]{2,1,0:T(4,128)(2,1)} copy(bf16[16,4,2048]{2,1,0:T(4,128)(2,1)S(1)} %all_gather.11) | data formatting | bytes 524288
  (1 shorter events, 0.0 us)
Async XLA Ops:
  2.8 10.4 %copy-start.11 = (bf16[304,128]{1,0:T(8,128)(2,1)S(1)}, bf16[304,128]{1,0:T(8,128)(2,1)}, u32[]{:S(2)}) copy-start(bf16[304,128]{1,0:T(8,128)(2,1)} %get-tuple-element.14) | copy-start | bytes 233476
  2.9 21.5 %copy-start.1 = (bf16[16,4,2048]{2,1,0:T(4,128)(2,1)S(1)}, bf16[16,4,2048]{2,1,0:T(4,128)(2,1)}, u32[]{:S(2)}) copy-start(bf16[16,4,2048]{2,1,0:T(4,128)(2,1)} %param.16) | copy-start | bytes 786436
  2.9 24.0 %all-to-all-start = ((bf16[8,64,256]{2,1,0:T(8,128)(2,1)}), bf16[8,64,256]{2,1,0:T(8,128)(2,1)S(1)}, u32[]{:S(2)}, u32[]{:S(2)}) async-start(bf16[8,64,256]{2,1,0:T(8,128)(2,1)} %get-tuple-element.15), calls=%async_computation | async-start | bytes 524288 | tf_op jit(solution)/shard_map/all_to_all | solution.py:428
  13.2 13.6 %collective-permute-start.1 = (bf16[304,128]{1,0:T(8,128)(2,1)S(1)}, bf16[304,128]{1,0:T(8,128)(2,1)S(1)}, u32[]{:S(2)}, u32[]{:S(2)}) collective-permute-start(bf16[304,128]{1,0:T(8,128)(2,1)S(1)} %copy-done.11), channel_id=1, source_target_pairs={{0,8},{8,16},{16,24},{24,32},{32,40},{40,48},{48,56},{56,64},{64,7... | collective-permute-start | bytes 233480 | tf_op jit(solution)/shard_map/ppermute | solution.py:427
  15.1 11.7 %collective-permute-start = (bf16[304,128]{1,0:T(8,128)(2,1)S(1)}, bf16[304,128]{1,0:T(8,128)(2,1)S(1)}, u32[]{:S(2)}, u32[]{:S(2)}) collective-permute-start(bf16[304,128]{1,0:T(8,128)(2,1)S(1)} %copy-done.11), channel_id=1, source_target_pairs={{8,0},{16,8},{24,16},{32,24},{40,32},{48,40},{56,48},{64,56},{72,6... | collective-permute-start | bytes 233480 | tf_op jit(solution)/shard_map/ppermute | solution.py:426
  24.2 0.7 %copy-start.8 = (f32[256]{0:T(256)S(1)}, f32[256]{0:T(256)}, u32[]{:S(2)}) copy-start(f32[256]{0:T(256)} %param.29) | copy-start | bytes 3076
  24.2 0.7 %copy-start.9 = (f32[256]{0:T(256)S(1)}, f32[256]{0:T(256)}, u32[]{:S(2)}) copy-start(f32[256]{0:T(256)} %param.30) | copy-start | bytes 3076
  24.3 0.7 %copy-start.5 = (f32[2048]{0:T(1024)S(1)}, f32[2048]{0:T(1024)}, u32[]{:S(2)}) copy-start(f32[2048]{0:T(1024)} %param.21) | copy-start | bytes 24580
  24.3 0.7 %copy-start.6 = (s32[64]{0:T(128)S(1)}, s32[64]{0:T(128)}, u32[]{:S(2)}) copy-start(s32[64]{0:T(128)} %get-tuple-element.12.meta_ref) | copy-start | bytes 772
  24.3 0.7 %copy-start.7 = (f32[256]{0:T(256)S(1)}, f32[256]{0:T(256)}, u32[]{:S(2)}) copy-start(f32[256]{0:T(256)} %param.28) | copy-start | bytes 3076
  25.0 1.9 %copy-start.2 = (f32[16,2048]{1,0:T(8,128)S(1)}, f32[16,2048]{1,0:T(8,128)}, u32[]{:S(2)}) copy-start(f32[16,2048]{1,0:T(8,128)} %refs_1_.1) | copy-start | bytes 393220
  25.0 1.9 %copy-start.3 = (f32[4,2048]{1,0:T(4,128)S(1)}, f32[4,2048]{1,0:T(4,128)}, u32[]{:S(2)}) copy-start(f32[4,2048]{1,0:T(4,128)} %refs_4_.1) | copy-start | bytes 98308
  25.0 1.9 %copy-start.4 = (bf16[64,256]{1,0:T(8,128)(2,1)S(1)}, bf16[64,256]{1,0:T(8,128)(2,1)}, u32[]{:S(2)}) copy-start(bf16[64,256]{1,0:T(8,128)(2,1)} %refs_9_.1) | copy-start | bytes 98308
  33.2 6.1 %copy-start = (f32[16,4,4096]{2,1,0:T(4,128)S(1)}, f32[16,4,4096]{2,1,0:T(4,128)}, u32[]{:S(2)}) copy-start(f32[16,4,4096]{2,1,0:T(4,128)} %param.19) | copy-start | bytes 3145732
  34.1 13.3 %all-to-all-start.1 = ((bf16[4,512,128]{2,1,0:T(8,128)(2,1)}), bf16[4,512,128]{2,1,0:T(8,128)(2,1)S(1)}, u32[]{:S(2)}, u32[]{:S(2)}) async-start(bf16[4,512,128]{2,1,0:T(8,128)(2,1)} %broadcast_in_dim.21), calls=%async_computation.1 | async-start | bytes 1048576 | tf_op jit(solution)/shard_map/all_to_all | solution.py:484
  38.6 0.7 %copy-start.10 = (s32[16]{0:T(128)S(1)}, s32[16]{0:T(128)}, u32[]{:S(2)}) copy-start(s32[16]{0:T(128)} %tally_hbm.1) | copy-start | bytes 196
